TPU v7x, 32 devices: a whole 2x2x4 slice. The times are simulated.
32 devices in a mesh: dp: 8 (over z, core), row: 2 (over x), col: 2 (over y).
Axes of the slice: x: 2, y: 2, z: 4, core: 2. Of those that a mesh axis runs over, the one named last changes fastest.
Arguments:
- tokens: bfloat16 [40960, 1024], P(('dp', 'row'), 'col'), may hold values from -8 to 8
- key_mask: int32 [128, 256], P(('dp', 'col')), may hold values from 0 to 1, as said below
- first_gain: float32 [1024], P('col'), may hold values from 0.5 to 1.5
- first_shift: float32 [1024], P('col'), may hold values from -1 to 1
- qkv_weight: float32 [3, 16, 64, 1024], P(None, 'row', 'dp', 'col'), may hold values from -0.1875 to 0.1875
- qkv_bias: float32 [2, 16, 64], P(None, 'row', 'dp'), may hold values from -1 to 1
- out_weight: float32 [16, 64, 1024], P('row', 'dp', 'col'), may hold values from -0.75 to 0.75
- out_bias: float32 [1024], P('col'), may hold values from -1 to 1
- second_gain: float32 [1024], P('col'), may hold values from 0.5 to 1.5
- second_shift: float32 [1024], P('col'), may hold values from -1 to 1
- up_weight: float32 [4096, 1024], P(('dp', 'row'), 'col')
- up_bias: float32 [4096], P(('dp', 'row')), may hold values from -1 to 1
- down_weight: float32 [4096, 1024], P(('dp', 'row'), 'col'), may hold values from -0.09375 to 0.09375
- down_bias: float32 [1024], P('col'), may hold values from -1 to 1
- cotangent: bfloat16 [40960, 1024], P(('dp', 'row'), 'col'), may hold values from -6 to 6
Outputs:
- activations: bfloat16 [40960, 1024], P(('dp', 'row'), 'col')
- token_grad: float32 [40960, 1024], P(('dp', 'row'), 'col')
- first_gain_grad: float32 [1024], P('col')
- first_shift_grad: float32 [1024], P('col')
- qkv_weight_grad: float32 [3, 16, 64, 1024], P(None, 'row', 'dp', 'col')
- qkv_bias_grad: float32 [2, 16, 64], P(None, 'row', 'dp')
- out_weight_grad: float32 [16, 64, 1024], P('row', 'dp', 'col')
- out_bias_grad: float32 [1024], P('col')
- second_gain_grad: float32 [1024], P('col')
- second_shift_grad: float32 [1024], P('col')
- up_weight_grad: float32 [4096, 1024], P(('dp', 'row'), 'col')
- up_bias_grad: float32 [4096], P(('dp', 'row'))
- down_weight_grad: float32 [4096, 1024], P(('dp', 'row'), 'col')
- down_bias_grad: float32 [1024], P('col')
Inputs may be any that keep to these rules, and one draw needn't show every extreme that they name: `key_mask`: 1 marks a visible image token and 0 a masked one; every sequence masks some of its 256 image tokens and shows most of them; buffer tokens are always visible.
All inputs are finite; a program needn't handle non-finite values.
Results may differ from a plain program's by a relative error of at most 0.025.
Values may be sent and summed in bfloat16 or wider, within the bound.
No kernel may reach another device: no remote copies, remote signals or barrier semaphores. Data moves between devices by JAX's collectives and lax.ppermute only.
A program may use at most 320 MiB of HBM per device.

v0:
```python
import jax
import jax.numpy as jnp
from jax import lax
from jax.sharding import PartitionSpec as P

D = 1024
HD = 64
BUF = 64
LEN = 320


attn_scale = 0.125
masked_fill = -1000000000.0
norm_epsilon = 1e-06


def contract_last(left, right):
    return lax.dot_general(
        left, right, (((1,), (1,)), ((), ())), preferred_element_type=jnp.float32
    )


def contract_first(left, right):
    return lax.dot_general(
        left, right, (((0,), (0,)), ((), ())), preferred_element_type=jnp.float32
    )


def rows_in(values):
    return lax.all_gather(values, "row", axis=0, tiled=True)


def rows_sum(values):
    return lax.psum_scatter(
        values.astype(jnp.bfloat16), "row", scatter_dimension=0, tiled=True
    ).astype(jnp.float32)


def cols_in(values):
    return lax.all_gather(values, "col", axis=0, tiled=True)


def cols_sum(values):
    return lax.psum_scatter(
        values.astype(jnp.bfloat16), "col", scatter_dimension=0, tiled=True
    ).astype(jnp.float32)


def col_totals(first, second):
    return lax.psum((first, second), "col")


def norm_forward(values, gain, shift):
    center = lax.psum(jnp.sum(values, axis=1), "col") / D
    centered = values - center[:, None]
    spread = lax.psum(jnp.sum(centered * centered, axis=1), "col") / D
    inverse = lax.rsqrt(spread + norm_epsilon)
    unit = centered * inverse[:, None]
    return (unit * gain + shift, unit, inverse)


def norm_backward(grad, gain, unit, inverse):
    scaled = grad * gain
    total, paired = col_totals(jnp.sum(scaled, axis=1), jnp.sum(scaled * unit, axis=1))
    return inverse[:, None] * (scaled - total[:, None] / D - unit * paired[:, None] / D)


def attend_scores(query, keyset, visible):
    scores = (
        jnp.einsum("sqhe,skhe->shqk", query, keyset, preferred_element_type=jnp.float32)
        * attn_scale
    )
    return jnp.where(visible[:, None, None, :], scores, masked_fill)


def local(
    tokens,
    key_mask,
    first_gain,
    first_shift,
    qkv_weight,
    qkv_bias,
    out_weight,
    out_bias,
    second_gain,
    second_shift,
    up_weight,
    up_bias,
    down_weight,
    down_bias,
    cotangent,
):
    bf16 = jnp.bfloat16
    f32 = jnp.float32
    qkv_block, out_block, up_block, down_block, qkv_offset, up_offset = (
        lax.all_gather(qkv_weight.astype(bf16), "dp", axis=2, tiled=True),
        lax.all_gather(out_weight.astype(bf16), "dp", axis=1, tiled=True),
        lax.all_gather(up_weight.astype(bf16), "dp", axis=0, tiled=True),
        lax.all_gather(down_weight.astype(bf16), "dp", axis=0, tiled=True),
        lax.all_gather(qkv_bias.astype(bf16), "dp", axis=2, tiled=True),
        lax.all_gather(up_bias.astype(bf16), "dp", axis=0, tiled=True),
    )
    heads_here = qkv_block.shape[1]
    width_here = qkv_block.shape[3]
    seq_here = key_mask.shape[0]
    buffer_on = jnp.ones((seq_here, BUF), jnp.int32)
    visible = jnp.concatenate([buffer_on, key_mask], axis=1) > 0
    out_matrix = out_block.reshape(heads_here * HD, width_here)
    inputs = tokens.astype(f32)
    normed, unit_one, inverse_one = norm_forward(inputs, first_gain, first_shift)
    normed_all = rows_in(normed.astype(bf16))
    partial_value = jnp.einsum("td,ihed->tihe", normed_all, qkv_block, preferred_element_type=f32)
    group_rows = partial_value.shape[0]
    summed = cols_sum(partial_value.reshape(group_rows, 3 * heads_here * HD)).reshape(
        -1, 3, heads_here, HD
    )
    offsets = qkv_offset.astype(f32)
    query = (summed[:, 0] + offsets[0]).astype(bf16).reshape(seq_here, LEN, heads_here, HD)
    keyset = summed[:, 1].astype(bf16).reshape(seq_here, LEN, heads_here, HD)
    valset = (summed[:, 2] + offsets[1]).astype(bf16).reshape(seq_here, LEN, heads_here, HD)
    scores = attend_scores(query, keyset, visible)
    top = jnp.max(scores, axis=-1, keepdims=True)
    expanded = jnp.exp(scores - top)
    denominator = jnp.sum(expanded, axis=-1, keepdims=True)
    probs = expanded / denominator
    logsum = top + jnp.log(denominator)
    attended = jnp.einsum(
        "shqk,skhe->sqhe", probs.astype(bf16), valset, preferred_element_type=f32
    ).astype(bf16)
    attended = attended.reshape(seq_here * LEN, heads_here * HD)
    attended_all = cols_in(attended)
    branch = rows_sum(jnp.dot(attended_all, out_matrix, preferred_element_type=f32))
    middle = inputs + (branch + out_bias)
    normed_two, unit_two, inverse_two = norm_forward(middle, second_gain, second_shift)
    normed_two_all = rows_in(normed_two.astype(bf16))
    upward = cols_sum(contract_last(normed_two_all, up_block)) + up_offset.astype(f32)
    gelu_value, gelu_pull = jax.vjp(lambda value: jax.nn.gelu(value, approximate=False), upward)
    hidden = gelu_value.astype(bf16)
    hidden_all = cols_in(hidden)
    branch_two = rows_sum(jnp.dot(hidden_all, down_block, preferred_element_type=f32)) + down_bias
    activations = (middle + branch_two).astype(bf16)
    grad_out = cotangent.astype(f32)
    down_bias_sum = jnp.sum(grad_out, axis=0)
    grad_all = rows_in(cotangent)
    down_grad = contract_first(hidden_all, grad_all)
    hidden_grad = cols_sum(contract_last(grad_all, down_block))
    upward_grad = gelu_pull(hidden_grad)[0].astype(bf16)
    upward_all = cols_in(upward_grad)
    up_grad = contract_first(upward_all, normed_two_all)
    up_bias_sum = jnp.sum(upward_all, axis=0, dtype=f32)
    normed_two_grad = rows_sum(jnp.dot(upward_all, up_block, preferred_element_type=f32))
    second_gain_sum = jnp.sum(normed_two_grad * unit_two, axis=0)
    second_shift_sum = jnp.sum(normed_two_grad, axis=0)
    middle_grad = grad_out + norm_backward(normed_two_grad, second_gain, unit_two, inverse_two)
    branch_low = middle_grad.astype(bf16)
    out_bias_sum = jnp.sum(branch_low, axis=0, dtype=f32)
    branch_all = rows_in(branch_low)
    out_grad = contract_first(attended_all, branch_all).reshape(heads_here, HD, width_here)
    attended_part = contract_last(branch_all, out_matrix)
    attended_grad = cols_sum(attended_part).astype(bf16).reshape(seq_here, LEN, heads_here, HD)
    again = jnp.exp(attend_scores(query, keyset, visible) - logsum)
    value_grad = jnp.einsum(
        "shqk,sqhe->skhe", again.astype(bf16), attended_grad, preferred_element_type=f32
    ).astype(bf16)
    prob_grad = jnp.einsum("sqhe,skhe->shqk", attended_grad, valset, preferred_element_type=f32)
    score_grad = (again * (prob_grad - jnp.sum(prob_grad * again, axis=-1, keepdims=True))).astype(
        bf16
    )
    query_grad = (
        jnp.einsum("shqk,skhe->sqhe", score_grad, keyset, preferred_element_type=f32) * attn_scale
    ).astype(bf16)
    key_grad = (
        jnp.einsum("shqk,sqhe->skhe", score_grad, query, preferred_element_type=f32) * attn_scale
    ).astype(bf16)
    stacked = jnp.stack(
        [
            query_grad.reshape(-1, heads_here, HD),
            key_grad.reshape(-1, heads_here, HD),
            value_grad.reshape(-1, heads_here, HD),
        ],
        axis=1,
    )
    stacked_all = cols_in(stacked.reshape(-1, 3 * heads_here * HD)).reshape(
        group_rows, 3, heads_here, HD
    )
    qkv_grad = jnp.einsum("tihe,td->ihed", stacked_all, normed_all, preferred_element_type=f32)
    qkv_bias_sum = jnp.stack(
        [
            jnp.sum(stacked_all[:, 0], axis=0, dtype=f32),
            jnp.sum(stacked_all[:, 2], axis=0, dtype=f32),
        ],
        axis=0,
    )
    normed_grad = rows_sum(
        jnp.einsum("tihe,ihed->td", stacked_all, qkv_block, preferred_element_type=f32)
    )
    first_gain_sum = jnp.sum(normed_grad * unit_one, axis=0)
    first_shift_sum = jnp.sum(normed_grad, axis=0)
    token_grad = middle_grad + norm_backward(normed_grad, first_gain, unit_one, inverse_one)
    (
        qkv_weight_grad,
        out_weight_grad,
        up_weight_grad,
        down_weight_grad,
        qkv_bias_grad,
        up_bias_grad,
    ) = (
        lax.psum_scatter(
            qkv_grad.astype(jnp.bfloat16), "dp", scatter_dimension=2, tiled=True
        ).astype(jnp.float32),
        lax.psum_scatter(
            out_grad.astype(jnp.bfloat16), "dp", scatter_dimension=1, tiled=True
        ).astype(jnp.float32),
        lax.psum_scatter(
            up_grad.astype(jnp.bfloat16), "dp", scatter_dimension=0, tiled=True
        ).astype(jnp.float32),
        lax.psum_scatter(
            down_grad.astype(jnp.bfloat16), "dp", scatter_dimension=0, tiled=True
        ).astype(jnp.float32),
        lax.psum_scatter(
            qkv_bias_sum.astype(jnp.bfloat16), "dp", scatter_dimension=2, tiled=True
        ).astype(jnp.float32),
        lax.psum_scatter(
            up_bias_sum.astype(jnp.bfloat16), "dp", scatter_dimension=0, tiled=True
        ).astype(jnp.float32),
    )
    (
        first_gain_grad,
        first_shift_grad,
        out_bias_grad,
        second_gain_grad,
        second_shift_grad,
        down_bias_grad,
    ) = lax.psum(
        (
            first_gain_sum,
            first_shift_sum,
            out_bias_sum,
            second_gain_sum,
            second_shift_sum,
            down_bias_sum,
        ),
        ("dp", "row"),
    )
    return (
        activations,
        token_grad,
        first_gain_grad,
        first_shift_grad,
        qkv_weight_grad,
        qkv_bias_grad,
        out_weight_grad,
        out_bias_grad,
        second_gain_grad,
        second_shift_grad,
        up_weight_grad,
        up_bias_grad,
        down_weight_grad,
        down_bias_grad,
    )


def solution(mesh):
    in_specs = (
        P(("dp", "row"), "col"),
        P(("dp", "col"), None),
        P("col"),
        P("col"),
        P(None, "row", "dp", "col"),
        P(None, "row", "dp"),
        P("row", "dp", "col"),
        P("col"),
        P("col"),
        P("col"),
        P(("dp", "row"), "col"),
        P(("dp", "row")),
        P(("dp", "row"), "col"),
        P("col"),
        P(("dp", "row"), "col"),
    )
    out_specs = (
        P(("dp", "row"), "col"),
        P(("dp", "row"), "col"),
        P("col"),
        P("col"),
        P(None, "row", "dp", "col"),
        P(None, "row", "dp"),
        P("row", "dp", "col"),
        P("col"),
        P("col"),
        P("col"),
        P(("dp", "row"), "col"),
        P(("dp", "row")),
        P(("dp", "row"), "col"),
        P("col"),
    )
    return jax.shard_map(local, mesh=mesh, in_specs=in_specs, out_specs=out_specs, check_vma=False)
```

profile of v0, /device:TPU:0, one launch (start us, length us, event | category | flops | bytes accessed | tf_op | source)
XLA Modules:
  0.0 2685.5 jit_solution(3723751173984276990)
XLA Ops:
  38.0 70.2 %all-gather.13.cloned.1.call-done = bf16[5120,512]{1,0:T(8,128)(2,1)} async-done(((bf16[2560,512]{1,0:T(8,128)(2,1)}), bf16[5120,512]{1,0:T(8,128)(2,1)}) %all-gather.13.cloned.1.call-update) | async-done | bytes 5242896 | tf_op jit(solution)/shard_map/all_gather | solution.py:30
  137.5 163.5 %reduce-scatter.22.cloned.1.call-done = bf16[2560,1536]{0,1:T(8,128)(2,1)} async-done(((bf16[5120,1536]{0,1:T(8,128)(2,1)}), bf16[2560,1536]{0,1:T(8,128)(2,1)}) %reduce-scatter.22.cloned.1.call-update) | async-done | bytes 7864336 | tf_op jit(solution)/shard_map/reduce_scatter | solution.py:44
  341.0 21.3 fusion.27
  419.3 53.9 %all-gather.17.cloned.1.call-done = bf16[5120,512]{0,1:T(8,128)(2,1)} async-done(((bf16[2560,512]{0,1:T(8,128)(2,1)}), bf16[5120,512]{0,1:T(8,128)(2,1)}) %all-gather.17.cloned.1.call-update) | async-done | bytes 5242896 | tf_op jit(solution)/shard_map/all_gather | solution.py:40
  484.8 61.4 %reduce-scatter.24.cloned.1.call-done = bf16[2560,512]{1,0:T(8,128)(2,1)} async-done(((bf16[5120,512]{1,0:T(8,128)(2,1)}), bf16[2560,512]{1,0:T(8,128)(2,1)}) %reduce-scatter.24.cloned.1.call-update) | async-done | bytes 2621456 | tf_op jit(solution)/shard_map/reduce_scatter | solution.py:34
  577.5 69.7 %all-gather.27.cloned.1.call-done = bf16[5120,512]{1,0:T(8,128)(2,1)} async-done(((bf16[2560,512]{1,0:T(8,128)(2,1)}), bf16[5120,512]{1,0:T(8,128)(2,1)}) %all-gather.27.cloned.1.call-update) | async-done | bytes 5242896 | tf_op jit(solution)/shard_map/all_gather | solution.py:30
  678.6 70.3 %all-gather.19.cloned.1.call-done = bf16[5120,512]{1,0:T(8,128)(2,1)} async-done(((bf16[2560,512]{1,0:T(8,128)(2,1)}), bf16[5120,512]{1,0:T(8,128)(2,1)}) %all-gather.19.cloned.1.call-update) | async-done | bytes 5242896 | tf_op jit(solution)/shard_map/all_gather | solution.py:30
  779.4 205.9 %reduce-scatter.44.cloned.1.call-done = bf16[2560,2048]{1,0:T(8,128)(2,1)} async-done(((bf16[5120,2048]{1,0:T(8,128)(2,1)}), bf16[2560,2048]{1,0:T(8,128)(2,1)}) %reduce-scatter.44.cloned.1.call-update) | async-done | bytes 10485776
  985.4 236.7 %reduce-scatter.42.cloned.1.call-done = bf16[2560,2048]{1,0:T(8,128)(2,1)} async-done(((bf16[5120,2048]{1,0:T(8,128)(2,1)}), bf16[2560,2048]{1,0:T(8,128)(2,1)}) %reduce-scatter.42.cloned.1.call-update) | async-done | bytes 10485776
  1222.1 54.0 %fusion.7 = (bf16[2560,2048]{1,0:T(8,128)(2,1)}, f32[2560,2048]{1,0:T(8,128)}) fusion(bf16[2560,2048]{1,0:T(8,128)(2,1)} %reduce-scatter.44.cloned.1.call-done, bf16[2560,2048]{1,0:T(8,128)(2,1)} %reduce-scatter.42.cloned.1.call-done, f32[2048]{0:T(1024)S(1)} %bitcast.131), kind=kLoop, calls=%fused_computation.16 | loop fusion | flops 393216000 | bytes 52436992 | tf_op jit(solution)/shard_map/convert_element_type | solution.py:147
  1276.1 19.8 multiply_convert_fusion.1
  1295.9 227.6 %all-gather.29.cloned.1.call-done = bf16[5120,2048]{1,0:T(8,128)(2,1)} async-done(((bf16[2560,2048]{1,0:T(8,128)(2,1)}), bf16[5120,2048]{1,0:T(8,128)(2,1)}) %all-gather.29.cloned.1.call-update) | async-done | bytes 20971536 | tf_op jit(solution)/shard_map/all_gather | solution.py:40
  1541.5 231.1 %all-gather.23.cloned.1.call-done = bf16[5120,2048]{1,0:T(8,128)(2,1)} async-done(((bf16[2560,2048]{1,0:T(8,128)(2,1)}), bf16[5120,2048]{1,0:T(8,128)(2,1)}) %all-gather.23.cloned.1.call-update) | async-done | bytes 20971536 | tf_op jit(solution)/shard_map/all_gather | solution.py:40
  1790.0 51.2 %reduce-scatter.28.cloned.1.call-done = bf16[2560,512]{1,0:T(8,128)(2,1)} async-done(((bf16[5120,512]{1,0:T(8,128)(2,1)}), bf16[2560,512]{1,0:T(8,128)(2,1)}) %reduce-scatter.28.cloned.1.call-update) | async-done | bytes 2621456 | tf_op jit(solution)/shard_map/reduce_scatter | solution.py:34
  1855.1 53.9 %reduce-scatter.26.cloned.1.call-done = bf16[2560,512]{1,0:T(8,128)(2,1)} async-done(((bf16[5120,512]{1,0:T(8,128)(2,1)}), bf16[2560,512]{1,0:T(8,128)(2,1)}) %reduce-scatter.26.cloned.1.call-update) | async-done | bytes 2621456 | tf_op jit(solution)/shard_map/reduce_scatter | solution.py:34
  1919.7 68.7 %all-gather.31.cloned.1.call-done = bf16[5120,512]{1,0:T(8,128)(2,1)} async-done(((bf16[2560,512]{1,0:T(8,128)(2,1)}), bf16[5120,512]{1,0:T(8,128)(2,1)}) %all-gather.31.cloned.1.call-update) | async-done | bytes 5242896 | tf_op jit(solution)/shard_map/all_gather | solution.py:30
  1996.6 64.9 %reduce-scatter.30.cloned.1.call-done = bf16[2560,512]{1,0:T(8,128)(2,1)} async-done(((bf16[5120,512]{1,0:T(8,128)(2,1)}), bf16[2560,512]{1,0:T(8,128)(2,1)}) %reduce-scatter.30.cloned.1.call-update) | async-done | bytes 2621456 | tf_op jit(solution)/shard_map/reduce_scatter | solution.py:44
  2092.1 30.2 %multiply_reduce_fusion = (f32[8,8,320]{2,1,0:T(8,128)S(1)}, f32[8,8,320,320]{2,3,1,0:T(8,128)}) fusion(f32[8,8,320]{2,1,0:T(8,128)S(1)} %log_add_fusion, f32[8,8,320,320]{2,3,1,0:T(8,128)} %get-tuple-element.48, pred[8,320]{1,0:T(8,128)(4,1)S(1)} %copy-done.14, bf16[8,320,8,64]{1,3,2,0:T(8,128)(2,1)} %copy.65, bf16[8,320,8,64]{1,0,3,2:T(8,128)(2,1)} %add_convert_fusion.1), kind=kOutput, calls=%fused_computation.1 | convolution fusion | flops 871608320 | bytes 57838080 | tf_op jit(solution)/shard_map/sqhe,skhe->shqk/dot_general | solution.py:165
  2122.3 26.2 multiply_convert_fusion
  2251.2 142.1 %all-gather.33.cloned.1.call-done = bf16[5120,1536]{0,1:T(8,128)(2,1)} async-done(((bf16[2560,1536]{0,1:T(8,128)(2,1)}), bf16[5120,1536]{0,1:T(8,128)(2,1)}) %all-gather.33.cloned.1.call-update) | async-done | bytes 15728656 | tf_op jit(solution)/shard_map/all_gather | solution.py:40
  2437.2 30.8 %reduce-scatter.34.cloned.1.call-done = bf16[256,512]{1,0:T(8,128)(2,1)} async-done(((bf16[2048,512]{1,0:T(8,128)(2,1)}), bf16[256,512]{1,0:T(8,128)(2,1)}) %reduce-scatter.34.cloned.1.call-update) | async-done | bytes 262160 | tf_op jit(solution)/shard_map/reduce_scatter | solution.py:214
  2469.8 30.1 %reduce-scatter.40.cloned.1.call-done = bf16[8,4096]{1,0:T(8,128)(2,1)} async-done(((bf16[64,4096]{1,0:T(8,128)(2,1)}), bf16[8,4096]{1,0:T(8,128)(2,1)}) %reduce-scatter.40.cloned.1.call-update) | async-done | bytes 65552
  2536.7 64.0 %reduce-scatter.32.cloned.1.call-done = bf16[2560,512]{1,0:T(8,128)(2,1)} async-done(((bf16[5120,512]{1,0:T(8,128)(2,1)}), bf16[2560,512]{1,0:T(8,128)(2,1)}) %reduce-scatter.32.cloned.1.call-update) | async-done | bytes 2621456 | tf_op jit(solution)/shard_map/reduce_scatter | solution.py:34
  2613.3 58.2 %all-reduce.5 = (f32[512]{0:T(512)}, f32[512]{0:T(512)}, f32[512]{0:T(512)}, f32[512]{0:T(512)}, f32[512]{0:T(512)}, /*index=5*/f32[512]{0:T(512)}) all-reduce(f32[512]{0:T(512)S(1)} %get-tuple-element.18, f32[512]{0:T(512)S(1)} %get-tuple-element.23, f32[512]{0:T(512)S(1)} %copy-done.26, ...), channel_id=1, replica_groups=mesh['dp'=8,'row'=2,'col'=2] {'dp','row'}, use_global_device_ids=true, to_apply=%region_28.29 | all-reduce | flops 3072 | bytes 24576 | tf_op jit(solution)/shard_map/psum | solution.py:234
  (209 shorter events, 564.0 us)
Async XLA Ops:
  7.2 30.8 %all-gather.15.cloned.1.call-start = ((), (), s32[]{:S(2)}) async-start(), calls=%async_computation.13 | async-start | bytes 1769472 | tf_op jit(solution)/shard_map/all_gather | solution.py:96
  9.1 99.1 %all-gather.13.cloned.1.call-start = ((), (), s32[]{:S(2)}) async-start(), calls=%async_computation.12 | async-start | bytes 7864320 | tf_op jit(solution)/shard_map/all_gather | solution.py:30
  32.1 268.9 %reduce-scatter.22.cloned.1.call-start = ((), (), s32[]{:S(2)}) async-start(), calls=%async_computation.14 | async-start | bytes 23592960 | tf_op jit(solution)/shard_map/reduce_scatter | solution.py:44
  122.4 350.8 %all-gather.17.cloned.1.call-start = ((), (), s32[]{:S(2)}) async-start(), calls=%async_computation.15 | async-start | bytes 7864320 | tf_op jit(solution)/shard_map/all_gather | solution.py:40
  137.5 238.9 %copy-start.13 = (pred[8,320]{1,0:T(8,128)(4,1)}, pred[8,320]{1,0:T(8,128)(4,1)S(1)}, u32[]{:S(2)}) copy-start(pred[8,320]{1,0:T(8,128)(4,1)S(1)} %pad_compare_fusion) | copy-start | bytes 7684
  404.5 141.7 %reduce-scatter.24.cloned.1.call-start = ((), (), s32[]{:S(2)}) async-start(), calls=%async_computation.16 | async-start | bytes 7864320 | tf_op jit(solution)/shard_map/reduce_scatter | solution.py:34
  480.4 97.1 %all-gather.25.cloned.1.call-start = ((), (), s32[]{:S(2)}) async-start(), calls=%async_computation.20 | async-start | bytes 2359296 | tf_op jit(solution)/shard_map/all_gather | solution.py:99
  482.2 165.0 %all-gather.27.cloned.1.call-start = ((), (), s32[]{:S(2)}) async-start(), calls=%async_computation.22 | async-start | bytes 7864320 | tf_op jit(solution)/shard_map/all_gather | solution.py:30
  482.9 195.7 %all-gather.21.cloned.1.call-start = ((), (), s32[]{:S(2)}) async-start(), calls=%async_computation.18 | async-start | bytes 2359296 | tf_op jit(solution)/shard_map/all_gather | solution.py:98
  484.8 264.1 %all-gather.19.cloned.1.call-start = ((), (), s32[]{:S(2)}) async-start(), calls=%async_computation.17 | async-start | bytes 7864320 | tf_op jit(solution)/shard_map/all_gather | solution.py:30
  571.8 413.5 %reduce-scatter.44.cloned.1.call-start = ((), (), s32[]{:S(2)}) async-start(), calls=%async_computation.34 | async-start | bytes 31457280
  665.3 556.8 %reduce-scatter.42.cloned.1.call-start = ((), (), s32[]{:S(2)}) async-start(), calls=%async_computation.33 | async-start | bytes 31457280
  767.1 756.5 %all-gather.29.cloned.1.call-start = ((), (), s32[]{:S(2)}) async-start(), calls=%async_computation.23 | async-start | bytes 31457280 | tf_op jit(solution)/shard_map/all_gather | solution.py:40
  1276.1 496.6 %all-gather.23.cloned.1.call-start = ((), (), s32[]{:S(2)}) async-start(), calls=%async_computation.19 | async-start | bytes 31457280 | tf_op jit(solution)/shard_map/all_gather | solution.py:40
  1295.9 545.3 %reduce-scatter.28.cloned.1.call-start = ((), (), s32[]{:S(2)}) async-start(), calls=%async_computation.24 | async-start | bytes 7864320 | tf_op jit(solution)/shard_map/reduce_scatter | solution.py:34
  1541.5 367.5 %reduce-scatter.26.cloned.1.call-start = ((), (), s32[]{:S(2)}) async-start(), calls=%async_computation.21 | async-start | bytes 7864320 | tf_op jit(solution)/shard_map/reduce_scatter | solution.py:34
  1789.9 198.4 %all-gather.31.cloned.1.call-start = ((), (), s32[]{:S(2)}) async-start(), calls=%async_computation.25 | async-start | bytes 7864320 | tf_op jit(solution)/shard_map/all_gather | solution.py:30
  1919.7 141.8 %reduce-scatter.30.cloned.1.call-start = ((), (), s32[]{:S(2)}) async-start(), calls=%async_computation.26 | async-start | bytes 7864320 | tf_op jit(solution)/shard_map/reduce_scatter | solution.py:44
  1995.6 397.7 %all-gather.33.cloned.1.call-start = ((), (), s32[]{:S(2)}) async-start(), calls=%async_computation.27 | async-start | bytes 23592960 | tf_op jit(solution)/shard_map/all_gather | solution.py:40
  2206.1 229.3 %reduce-scatter.36.cloned.1.call-start = ((), (), s32[]{:S(2)}) async-start(), calls=%async_computation.30 | async-start | bytes 2359296 | tf_op jit(solution)/shard_map/reduce_scatter | solution.py:217
  2223.9 244.1 %reduce-scatter.34.cloned.1.call-start = ((), (), s32[]{:S(2)}) async-start(), calls=%async_computation.29 | async-start | bytes 2359296 | tf_op jit(solution)/shard_map/reduce_scatter | solution.py:214
  2243.1 256.8 %reduce-scatter.40.cloned.1.call-start = ((), (), s32[]{:S(2)}) async-start(), calls=%async_computation.32 | async-start | bytes 589824
  2251.1 283.8 %reduce-scatter.38.cloned.1.call-start = ((), (), s32[]{:S(2)}) async-start(), calls=%async_computation.31 | async-start | bytes 1769472
  2407.9 192.9 %reduce-scatter.32.cloned.1.call-start = ((), (), s32[]{:S(2)}) async-start(), calls=%async_computation.28 | async-start | bytes 7864320 | tf_op jit(solution)/shard_map/reduce_scatter | solution.py:34
  (34 other events, 1491.6 us)
Sparse Core Ops, SparseCore 0:
  10.2 27.7 all-gather.14
  40.1 68.0 all-gather.12
  122.6 178.3 reduce-scatter.21
  404.6 68.5 all-gather.16
  480.5 65.6 reduce-scatter.23
  548.3 29.1 all-gather.24
  579.1 68.0 all-gather.26
  649.5 29.0 all-gather.20
  680.8 68.0 all-gather.18
  751.1 234.1 reduce-scatter.43
  987.8 234.2 reduce-scatter.41
  1276.2 247.3 all-gather.28
  1525.2 247.3 all-gather.22
  1775.4 65.6 reduce-scatter.27
  1843.3 65.6 reduce-scatter.25
  1919.8 68.5 all-gather.30
  1995.7 65.6 reduce-scatter.29
  2206.2 187.0 all-gather.32
  2395.6 35.7 reduce-scatter.35
  2433.6 34.3 reduce-scatter.33
  2470.3 29.5 reduce-scatter.39
  2502.3 32.5 reduce-scatter.37
  2537.3 63.3 reduce-scatter.31
where the time goes:
time: 2690 us
  waiting for transfers between devices  1930 us (72%)
  matrix products  275 us (10%)
  other arithmetic  198 us (7%)
  blocking collectives  162 us (6%)
  local copies, waits for them, and re-layouts  99.6 us (4%)
    all_gather x4, waiting for transfers between devices, cols_in(): return lax.all_gather(values, 'col', axis=0, tiled=True)  655 us
    unnamed x27, waiting for transfers between devices  485 us
    all_gather x4, waiting for transfers between devices, rows_in(): return lax.all_gather(values, 'row', axis=0, tiled=True)  279 us
    reduce_scatter x4, waiting for transfers between devices, rows_sum(): lax.psum_scatter(values.astype(jnp.bfloat16), 'row', scatter_dimension=0,...  231 us
    reduce_scatter x2, waiting for transfers between devices, cols_sum(): lax.psum_scatter(values.astype(jnp.bfloat16), 'col', scatter_dimension=0,...  228 us
    psum x1, blocking collectives, local(): lax.psum((first_gain_sum, first_shift_sum, out_bias_sum, second_gain_sum,...  58.2 us
    convert_element_type x1, other arithmetic, local(): upward_grad = gelu_pull(hidden_grad)[0].astype(bf16)  54 us
  transfers between devices with their start and end apart: 23, of which 22 were waited for; matrix products, arithmetic and copies ran while one was open for 8% of the time, Pallas kernels for 0%

commit v1 on v0

v1 whole, which is shorter than its diff:
```python
import jax
import jax.numpy as jnp
from jax import lax
from jax.sharding import Mesh, PartitionSpec as P

HD = 64
BUF = 64
LEN = 320
attn_scale = 0.125
masked_fill = -1000000000.0
norm_epsilon = 1e-06
bf16 = jnp.bfloat16
f32 = jnp.float32


def shift(values, axis, size, step):
    return lax.ppermute(values, axis, [(i, (i + step) % size) for i in range(size)])


def contract_last(left, right):
    return lax.dot_general(left, right, (((1,), (1,)), ((), ())), preferred_element_type=f32)


def contract_first(left, right):
    return lax.dot_general(left, right, (((0,), (0,)), ((), ())), preferred_element_type=f32)


def make_local(nz, ncore, nrow, ncol):
    def axis_in(values, axis, size):
        return [values] + [shift(values, axis, size, k) for k in range(1, size)]

    def gather(shard):
        along_z = jnp.stack(axis_in(shard, "z", nz))
        along_col = jnp.stack(axis_in(along_z, "col", ncol))
        along_row = jnp.stack(axis_in(along_col, "row", nrow))
        return jnp.stack(axis_in(along_row, "core", ncore))

    def axis_out(parts, axis, size):
        total = parts[0].astype(f32)
        for k in range(1, size):
            total = total + shift(parts[k].astype(bf16), axis, size, -k).astype(f32)
        return total

    def scatter(grads):
        one = axis_out(grads, "core", ncore).astype(bf16)
        two = axis_out(one, "row", nrow).astype(bf16)
        three = axis_out(two, "col", ncol).astype(bf16)
        return axis_out(three, "z", nz)

    def tokens_in(values):
        rows = values.shape[0] // ncol
        here = lax.axis_index("col")
        parts = [lax.dynamic_slice_in_dim(values, here * rows, rows, 0)]
        for k in range(1, ncol):
            block = lax.dynamic_slice_in_dim(values, ((here + k) % ncol) * rows, rows, 0)
            parts.append(shift(block, "col", ncol, k))
        return jnp.concatenate(parts, axis=1)

    def tokens_out(values, dtype):
        rows = values.shape[0]
        width = values.shape[1] // ncol
        here = lax.axis_index("col")
        result = jnp.zeros((rows * ncol, width), dtype)
        result = lax.dynamic_update_slice_in_dim(result, values[:, :width].astype(dtype), here * rows, 0)
        for k in range(1, ncol):
            block = shift(values[:, k * width : (k + 1) * width].astype(bf16), "col", ncol, -k)
            result = lax.dynamic_update_slice_in_dim(
                result, block.astype(dtype), ((here + k) % ncol) * rows, 0
            )
        return result

    def features(vector):
        return jnp.concatenate(axis_in(vector, "col", ncol))

    def norm_forward(values, gain, first_shift):
        center = jnp.mean(values, axis=1, keepdims=True)
        centered = values - center
        spread = jnp.mean(centered * centered, axis=1, keepdims=True)
        inverse = lax.rsqrt(spread + norm_epsilon)
        unit = centered * inverse
        return unit * gain + first_shift, unit, inverse

    def norm_backward(grad, gain, unit, inverse):
        scaled = grad * gain
        total = jnp.mean(scaled, axis=1, keepdims=True)
        paired = jnp.mean(scaled * unit, axis=1, keepdims=True)
        return inverse * (scaled - total - unit * paired)

    def local(
        tokens,
        key_mask,
        first_gain,
        first_shift,
        qkv_weight,
        qkv_bias,
        out_weight,
        out_bias,
        second_gain,
        second_shift,
        up_weight,
        up_bias,
        down_weight,
        down_bias,
        cotangent,
    ):
        count = tokens.shape[0] // ncol
        seqs = count // LEN
        heads_part, hd_part, width = out_weight.shape
        heads = heads_part * nrow
        hidden_part = up_weight.shape[0]
        dim = width * ncol
        hidden_units = hidden_part * nrow * nz * ncore

        inputs = tokens_in(tokens).astype(f32)
        qkv_all = gather(qkv_weight.astype(bf16))
        small = jnp.concatenate([qkv_bias.reshape(-1), up_bias]).astype(bf16)
        vectors = jnp.stack([first_gain, first_shift, second_gain, second_shift, out_bias, down_bias])
        vectors = jnp.concatenate(axis_in(vectors, "col", ncol), axis=1)
        gain_one, shift_one, gain_two, shift_two, out_offset, down_offset = [vectors[i : i + 1] for i in range(6)]
        small_z = jnp.stack(axis_in(small, "z", nz))
        small_row = jnp.stack(axis_in(small_z, "row", nrow))
        small_all = jnp.stack(axis_in(small_row, "core", ncore)).astype(f32)
        qkv_count = qkv_bias.size
        qkv_offset = small_all[..., :qkv_count].reshape(ncore, nrow, nz, 2, heads_part, hd_part)
        qkv_offset = jnp.transpose(qkv_offset, (3, 1, 4, 0, 2, 5)).reshape(2, 1, heads * HD)
        up_offset = small_all[..., qkv_count:].reshape(1, hidden_units)
        masks = jnp.zeros((ncol,) + key_mask.shape, key_mask.dtype)
        here = lax.axis_index("col")
        for k, part in enumerate(axis_in(key_mask, "col", ncol)):
            masks = lax.dynamic_update_slice_in_dim(masks, part[None], (here - k + ncol) % ncol, 0)
        masks = masks.reshape(-1, key_mask.shape[1])
        first_seq = (lax.axis_index("row") * ncol + here) * seqs
        masks = lax.dynamic_slice_in_dim(masks, first_seq, seqs, 0)
        visible = jnp.concatenate([jnp.ones((seqs, BUF), jnp.int32), masks], axis=1) > 0

        qkv_matrix = jnp.transpose(qkv_all, (4, 1, 5, 0, 3, 6, 2, 7)).reshape(3 * heads * HD, dim)
        out_all = gather(out_weight.astype(bf16))
        out_matrix = jnp.transpose(out_all, (1, 4, 0, 3, 5, 2, 6)).reshape(heads * HD, dim)
        up_all = gather(up_weight.astype(bf16))
        up_matrix = jnp.transpose(up_all, (0, 1, 3, 4, 2, 5)).reshape(hidden_units, dim)
        down_all = gather(down_weight.astype(bf16))
        down_matrix = jnp.transpose(down_all, (0, 1, 3, 4, 2, 5)).reshape(hidden_units, dim)
        grad_low = tokens_in(cotangent)

        normed, unit_one, inverse_one = norm_forward(inputs, gain_one, shift_one)
        normed = normed.astype(bf16)
        projected = contract_last(normed, qkv_matrix).reshape(count, 3, heads * HD)
        shape = (seqs, LEN, heads, HD)
        query = (projected[:, 0] + qkv_offset[0]).astype(bf16).reshape(shape)
        keyset = projected[:, 1].astype(bf16).reshape(shape)
        valset = (projected[:, 2] + qkv_offset[1]).astype(bf16).reshape(shape)

        def attend_scores():
            scores = (
                jnp.einsum("sqhe,skhe->shqk", query, keyset, preferred_element_type=f32) * attn_scale
            )
            return jnp.where(visible[:, None, None, :], scores, masked_fill)

        scores = attend_scores()
        top = jnp.max(scores, axis=-1, keepdims=True)
        expanded = jnp.exp(scores - top)
        denominator = jnp.sum(expanded, axis=-1, keepdims=True)
        probs = expanded / denominator
        logsum = top + jnp.log(denominator)
        attended = jnp.einsum(
            "shqk,skhe->sqhe", probs.astype(bf16), valset, preferred_element_type=f32
        ).astype(bf16).reshape(count, heads * HD)
        branch = jnp.dot(attended, out_matrix, preferred_element_type=f32)
        middle = inputs + (branch + out_offset)
        normed_two, unit_two, inverse_two = norm_forward(middle, gain_two, shift_two)
        normed_two = normed_two.astype(bf16)
        upward = contract_last(normed_two, up_matrix) + up_offset
        gelu_value, gelu_pull = jax.vjp(lambda value: jax.nn.gelu(value, approximate=False), upward)
        hidden = gelu_value.astype(bf16)
        branch_two = jnp.dot(hidden, down_matrix, preferred_element_type=f32) + down_offset
        activations = tokens_out(middle + branch_two, bf16)

        grad_out = grad_low.astype(f32)
        down_bias_sum = jnp.sum(grad_out, axis=0)
        hidden_shape = (ncore, nrow, nz, hidden_part, ncol, width)

        def ffn_scatter(grad):
            return scatter(jnp.transpose(grad.reshape(hidden_shape), (0, 1, 4, 2, 3, 5)))

        hidden_grad = contract_last(grad_low, down_matrix)
        down_grad = ffn_scatter(contract_first(hidden, grad_low).astype(bf16))
        upward_grad = gelu_pull(hidden_grad)[0].astype(bf16)
        up_grad = ffn_scatter(contract_first(upward_grad, normed_two).astype(bf16))
        up_bias_sum = jnp.sum(upward_grad, axis=0, dtype=f32)
        normed_two_grad = jnp.dot(upward_grad, up_matrix, preferred_element_type=f32)
        second_gain_sum = jnp.sum(normed_two_grad * unit_two, axis=0)
        second_shift_sum = jnp.sum(normed_two_grad, axis=0)
        middle_grad = grad_out + norm_backward(normed_two_grad, gain_two, unit_two, inverse_two)
        branch_low = middle_grad.astype(bf16)
        out_bias_sum = jnp.sum(branch_low, axis=0, dtype=f32)
        out_grad = contract_first(attended, branch_low).astype(bf16)
        out_grad = out_grad.reshape(nrow, heads_part, ncore, nz, hd_part, ncol, width)
        out_grad = scatter(jnp.transpose(out_grad, (2, 0, 5, 3, 1, 4, 6)))
        attended_grad = contract_last(branch_low, out_matrix).astype(bf16).reshape(shape)
        again = jnp.exp(attend_scores() - logsum)
        value_grad = jnp.einsum(
            "shqk,sqhe->skhe", again.astype(bf16), attended_grad, preferred_element_type=f32
        ).astype(bf16)
        prob_grad = jnp.einsum("sqhe,skhe->shqk", attended_grad, valset, preferred_element_type=f32)
        score_grad = (
            again * (prob_grad - jnp.sum(prob_grad * again, axis=-1, keepdims=True))
        ).astype(bf16)
        query_grad = (
            jnp.einsum("shqk,skhe->sqhe", score_grad, keyset, preferred_element_type=f32) * attn_scale
        ).astype(bf16)
        key_grad = (
            jnp.einsum("shqk,sqhe->skhe", score_grad, query, preferred_element_type=f32) * attn_scale
        ).astype(bf16)
        flat = (count, heads * HD)
        stacked = jnp.concatenate(
            [query_grad.reshape(flat), key_grad.reshape(flat), value_grad.reshape(flat)], axis=1
        )
        qkv_grad = contract_first(stacked, normed).astype(bf16)
        qkv_grad = qkv_grad.reshape(3, nrow, heads_part, ncore, nz, hd_part, ncol, width)
        qkv_grad = scatter(jnp.transpose(qkv_grad, (3, 1, 6, 4, 0, 2, 5, 7)))
        bias_sum = jnp.sum(stacked, axis=0, dtype=f32).reshape(3, nrow, heads_part, ncore, nz, hd_part)
        bias_sum = jnp.stack([bias_sum[0], bias_sum[2]])
        bias_sum = jnp.transpose(bias_sum, (3, 1, 4, 0, 2, 5)).reshape(ncore, nrow, nz, qkv_count)
        normed_grad = jnp.dot(stacked, qkv_matrix, preferred_element_type=f32)
        first_gain_sum = jnp.sum(normed_grad * unit_one, axis=0)
        first_shift_sum = jnp.sum(normed_grad, axis=0)
        token_grad = tokens_out(
            middle_grad + norm_backward(normed_grad, gain_one, unit_one, inverse_one), f32
        )

        def wide_out(parts, axis, size):
            total = parts[0]
            for k in range(1, size):
                total = total + shift(parts[k], axis, size, -k)
            return total

        def wide_all(values, axis, size):
            total = values
            for k in range(1, size):
                total = total + shift(values, axis, size, k)
            return total

        bias_all = jnp.concatenate(
            [bias_sum, up_bias_sum.reshape(ncore, nrow, nz, hidden_part)], axis=-1
        )
        bias_all = wide_out(bias_all, "core", ncore)
        bias_all = wide_out(bias_all, "row", nrow)
        bias_all = wide_all(bias_all, "col", ncol)
        bias_all = wide_out(bias_all, "z", nz)
        qkv_bias_grad = bias_all[:qkv_count].reshape(qkv_bias.shape)
        up_bias_grad = bias_all[qkv_count:]
        sums = jnp.stack(
            [
                first_gain_sum,
                first_shift_sum,
                out_bias_sum,
                second_gain_sum,
                second_shift_sum,
                down_bias_sum,
            ]
        )
        sums = [sums[:, k * width : (k + 1) * width] for k in range(ncol)]
        sums = wide_out(sums, "col", ncol)
        sums = wide_all(sums, "core", ncore)
        sums = wide_all(sums, "row", nrow)
        sums = wide_all(sums, "z", nz)
        return (
            activations,
            token_grad,
            sums[0],
            sums[1],
            qkv_grad,
            qkv_bias_grad,
            out_grad,
            sums[2],
            sums[3],
            sums[4],
            up_grad,
            up_bias_grad,
            down_grad,
            sums[5],
        )

    return local


def solution(mesh):
    devices = mesh.devices
    nz, ncore = devices.shape[0] // 2, 2
    nrow, ncol = devices.shape[1], devices.shape[2]
    fine = Mesh(devices.reshape(nz, ncore, nrow, ncol), ("z", "core", "row", "col"))
    dp = ("z", "core")
    in_specs = (
        P(("z", "core", "row"), "col"),
        P(("z", "core", "col"), None),
        P("col"),
        P("col"),
        P(None, "row", dp, "col"),
        P(None, "row", dp),
        P("row", dp, "col"),
        P("col"),
        P("col"),
        P("col"),
        P(("z", "core", "row"), "col"),
        P(("z", "core", "row")),
        P(("z", "core", "row"), "col"),
        P("col"),
        P(("z", "core", "row"), "col"),
    )
    out_specs = (
        P(("z", "core", "row"), "col"),
        P(("z", "core", "row"), "col"),
        P("col"),
        P("col"),
        P(None, "row", dp, "col"),
        P(None, "row", dp),
        P("row", dp, "col"),
        P("col"),
        P("col"),
        P("col"),
        P(("z", "core", "row"), "col"),
        P(("z", "core", "row")),
        P(("z", "core", "row"), "col"),
        P("col"),
    )
    return jax.shard_map(
        make_local(nz, ncore, nrow, ncol),
        mesh=fine,
        in_specs=in_specs,
        out_specs=out_specs,
        check_vma=False,
    )
```

time: 2690 us -> 1210 us (0.45)
  waiting for transfers between devices: 1930 us -> 331 us
  local copies, waits for them, and re-layouts: 99.6 us -> 311 us
  blocking collectives: 162 us -> 0 us
  starting transfers between devices: 1.13 us -> 85.5 us
  other arithmetic: 198 us -> 150 us
  matrix products: 275 us -> 319 us
    all_gather x11 -> x0, waiting for transfers between devices: 958 us -> none  [the longest x4 655 us: cols_in(): return lax.all_gather(values, 'col', axis=0, tiled=True)]
    reduce_scatter x8 -> x0, waiting for transfers between devices: 490 us -> none  [the longest x4 231 us: rows_sum(): lax.psum_scatter(values.astype(jnp.bfloat16), 'row', scatter_dimension=0,...]
    unnamed x27 -> x0, waiting for transfers between devices: 485 us -> none
    ppermute x0 -> x71, waiting for transfers between devices: none -> 331 us  [shift(): lax.ppermute(values, axis, [(i, (i + step) % size) for i in range(size)])]
    psum x7 -> x0, blocking collectives: 106 us -> none  [the longest x1 58.2 us: local(): lax.psum((first_gain_sum, first_shift_sum, out_bias_sum, second_gain_sum,...]
    ppermute x0 -> x71, starting transfers between devices: none -> 85.5 us  [shift(): lax.ppermute(values, axis, [(i, (i + step) % size) for i in range(size)])]
    dot_general x3 -> x4, matrix products: 43.4 us -> 106 us  [contract_last(): lax.dot_general(left, right, (((1,), (1,)), ((), ())), preferred_element_...]
    reshape x3 -> x16, local copies, waits for them, and re-layouts: 20.2 us -> 81.9 us  [the longest x4 46.1 us: ffn_scatter(): grad.reshape(hidden_shape)]
  transfers between devices with their start and end apart: 23 -> 71, of which waited for: 22 -> 22; matrix products, arithmetic and copies ran while one was open for 8% -> 43% of each run, Pallas kernels for 0% -> 0%
where the time goes in v1:
time: 1210 us; the launch traced here: 1200 us
  waiting for transfers between devices  331 us (27%)
  matrix products  319 us (26%)
  local copies, waits for them, and re-layouts  311 us (26%)
  other arithmetic  150 us (12%)
  starting transfers between devices  85.5 us (7%)
    ppermute x71, waiting for transfers between devices, shift(): lax.ppermute(values, axis, [(i, (i + step) % size) for i in range(size)])  331 us
    dot_general x4, matrix products, contract_last(): lax.dot_general(left, right, (((1,), (1,)), ((), ())), preferred_element_...  106 us
    ppermute x71, starting transfers between devices, shift(): lax.ppermute(values, axis, [(i, (i + step) % size) for i in range(size)])  85.5 us
    dot_general x4, matrix products, contract_first(): lax.dot_general(left, right, (((0,), (0,)), ((), ())), preferred_element_...  59.3 us
    unnamed x196, local copies, waits for them, and re-layouts  53.8 us
    reshape x4, local copies, waits for them, and re-layouts, ffn_scatter(): grad.reshape(hidden_shape)  46.1 us
    convert_element_type x1, other arithmetic, local(): score_grad = (again * (prob_grad - jnp.sum(prob_grad * again, axis=-1, ke...  26.6 us
    dot_general x1, matrix products, local(): jnp.einsum('sqhe,skhe->shqk', attended_grad, valset, preferred_element_ty...  24.6 us
  transfers between devices with their start and end apart: 71, of which 22 were waited for; matrix products, arithmetic and copies ran while one was open for 43% of the time, Pallas kernels for 0%

profile of v1, /device:TPU:0, one launch (start us, length us, event | category | flops | bytes accessed | tf_op | source)
XLA Modules:
  0.0 1198.6 jit_solution(2648227615621747601)
XLA Ops:
  98.9 29.6 %collective-permute-done.13 = s32[8,256]{1,0:T(8,128)S(1)} collective-permute-done((s32[8,256]{1,0:T(8,128)S(1)}, s32[8,256]{1,0:T(8,128)S(1)}, u32[]{:S(2)}, u32[]{:S(2)}) %collective-permute-start.13) | collective-permute-done | bytes 8224 | tf_op jit(solution)/shard_map/ppermute | solution.py:17
  168.7 26.3 %collective-permute-done.24 = bf16[2,4,256,512]{3,2,1,0:T(8,128)(2,1)} collective-permute-done((bf16[2,4,256,512]{3,2,1,0:T(8,128)(2,1)}, bf16[2,4,256,512]{3,2,1,0:T(8,128)(2,1)}, u32[]{:S(2)}, u32[]{:S(2)}) %collective-permute-start.24) | collective-permute-done | bytes 2097184 | tf_op jit(solution)/shard_map/ppermute | solution.py:17
  200.1 39.4 %collective-permute-done.30 = bf16[2,4,256,512]{3,2,1,0:T(8,128)(2,1)} collective-permute-done((bf16[2,4,256,512]{3,2,1,0:T(8,128)(2,1)}, bf16[2,4,256,512]{3,2,1,0:T(8,128)(2,1)}, u32[]{:S(2)}, u32[]{:S(2)}) %collective-permute-start.30) | collective-permute-done | bytes 2097184 | tf_op jit(solution)/shard_map/ppermute | solution.py:17
  327.3 21.6 %fusion.12 = (f32[4,16,320]{2,1,0:T(8,128)S(1)}, f32[4,16,320,320]{2,3,1,0:T(8,128)}) fusion(pred[4,320]{1,0:T(4,128)(4,1)S(1)} %pad_compare_fusion, bf16[4,320,16,64]{1,3,2,0:T(8,128)(2,1)} %copy.111, bf16[4,320,16,64]{1,0,3,2:T(4,128)(2,1)} %add_convert_fusion.1), kind=kOutput, calls=%fused_computation.30 | convolution fusion | flops 858501120 | bytes 31540480 | tf_op jit(solution)/shard_map/sqhe,skhe->shqk/dot_general | solution.py:155
  366.2 15.9 %convert_bitcast_fusion.1 = bf16[4,320,16,64]{1,3,2,0:T(8,128)(2,1)S(1)} fusion(f32[4,16,320]{2,1,0:T(8,128)S(1)} %fusion, f32[4,16,320]{2,1,0:T(8,128)S(1)} %get-tuple-element.94, f32[4,16,320,320]{2,3,1,0:T(8,128)} %get-tuple-element.95, pred[4,320]{1,0:T(4,128)(4,1)S(1)} %pad_compare_fusion, bf16[4,320,16,64]{1,0,3,2:T(4,128)(2,1)} %add_convert_fusion.2), kind=kOutput, calls=%fused_computation.98 | convolution fusion | flops 872939520 | bytes 31622400 | tf_op jit(solution)/shard_map/shqk,skhe->sqhe/dot_general | solution.py:165
  421.1 16.5 %copy.116 = bf16[2,2,4,256,2,512]{5,4,3,2,1,0:T(2,128)(2,1)} copy(bf16[2,2,4,256,2,512]{5,3,2,4,1,0:T(8,128)(2,1)} %maximum_bitcast_fusion) | data formatting | bytes 16777216 | tf_op jit(solution)/shard_map/transpose | solution.py:140
  446.9 60.8 %multiply_convert_fusion.1 = (bf16[1280,4096]{1,0:T(8,128)(2,1)}, f32[1280,4096]{1,0:T(8,128)}, f32[1280,4096]{1,0:T(8,128)}) fusion(f32[4096]{0:T(1024)S(1)} %bitcast.380, bf16[4096,1024]{1,0:T(8,128)(2,1)} %bitcast.343, bf16[1280,1024]{0,1:T(8,128)(2,1)} %add_convert_fusion.6.clone.4), kind=kOutput, calls=%fused_computation.12 | convolution fusion | flops 11083448320 | bytes 63455232 | tf_op jit(solution)/shard_map/dot_general | solution.py:21
  514.0 16.4 %copy.117 = bf16[2,2,4,256,2,512]{5,4,3,2,1,0:T(2,128)(2,1)} copy(bf16[2,2,4,256,2,512]{5,3,2,4,1,0:T(8,128)(2,1)} %maximum_bitcast_fusion.1) | data formatting | bytes 16777216 | tf_op jit(solution)/shard_map/transpose | solution.py:142
  540.0 29.4 %convert_reduce_fusion = (f32[4096]{0:T(1024)}, bf16[1280,4096]{1,0:T(8,128)(2,1)}) fusion(f32[1280,4096]{1,0:T(8,128)} %get-tuple-element.27, bf16[4096,1024]{1,0:T(8,128)(2,1)} %bitcast.341, bf16[1280,512]{0,1:T(8,128)(2,1)} %collective-permute-done.33, bf16[1280,512]{0,1:T(8,128)(2,1)S(1)} %copy-done.41, f32[1280,4096]{1,0:T(8,128)} %get-tuple-element.96, ...), kind=kOutput, calls=%fused_computation.10 | convolution fusion | flops 10831785984 | bytes 63471616 | tf_op jit(solution)/shard_map/dot_general | solution.py:21
  569.4 19.2 %convolution_convert_fusion.1 = bf16[4096,1024]{1,0:T(8,128)(2,1)} fusion(bf16[1280,4096]{1,0:T(8,128)(2,1)} %get-tuple-element.104, f32[1280,1024]{0,1:T(8,128)} %copy-done.1, f32[1024]{0:T(1024)S(1)} %bitcast.377, f32[1024]{0:T(1024)S(1)} %bitcast.370, f32[1280]{0:T(1024)S(1)} %copy-done.58, f32[1280]{0:T(1024)S(1)} %copy-done.54), kind=kOutput, calls=%fused_computation.43 | convolution fusion | flops 10748166144 | bytes 24135680 | tf_op jit(solution)/shard_map/dot_general | solution.py:25
  588.6 15.8 %fusion.98 = (f32[1024]{0:T(1024)}, f32[1280,1024]{1,0:T(8,128)}) fusion(bf16[1280,4096]{1,0:T(8,128)(2,1)S(1)} %copy-done.83, bf16[4096,1024]{1,0:T(8,128)(2,1)} %bitcast.344), kind=kOutput, calls=%fused_computation.261 | convolution fusion | flops 10738727936 | bytes 24121344 | tf_op jit(solution)/shard_map/dot_general | solution.py:190
  615.9 22.6 %convert_reduce_fusion.4 = (f32[1024]{0:T(1024)}, f32[1280,1024]{0,1:T(8,128)}, bf16[1280,1024]{0,1:T(8,128)(2,1)}, f32[1024]{0:T(1024)}) fusion(f32[1280]{0:T(1024)S(1)} %broadcast_multiply_fusion.2, f32[1280,1024]{0,1:T(8,128)} %copy-done.1, f32[1280]{0:T(1024)S(1)} %copy-done.54, f32[1280]{0:T(1024)S(1)} %broadcast_multiply_fusion.3, ...), kind=kOutput, calls=%fused_computation.71 | convolution fusion | flops 10762319872 | bytes 39882752 | tf_op jit(solution)/shard_map/dot_general | solution.py:175
  661.4 16.3 %convert_bitcast_fusion = bf16[4,320,16,64]{1,3,2,0:T(8,128)(2,1)} fusion(bf16[4,320,16,64]{1,3,2,0:T(8,128)(2,1)} %copy.125, f32[4,16,320]{2,1,0:T(8,128)S(1)} %copy-done.45, f32[4,16,320,320]{2,3,1,0:T(8,128)} %get-tuple-element.95, pred[4,320]{1,0:T(4,128)(4,1)S(1)} %copy-done.50), kind=kOutput, calls=%fused_computation.97 | convolution fusion | flops 866385920 | bytes 31540480 | tf_op jit(solution)/shard_map/shqk,sqhe->skhe/dot_general | solution.py:201
  677.8 24.6 %multiply_reduce_fusion = (f32[4,16,320]{2,1,0:T(8,128)S(1)}, f32[4,16,320,320]{2,3,1,0:T(8,128)}) fusion(f32[4,16,320]{2,1,0:T(8,128)S(1)} %copy-done.45, f32[4,16,320,320]{2,3,1,0:T(8,128)} %get-tuple-element.95, pred[4,320]{1,0:T(4,128)(4,1)S(1)} %copy-done.50, bf16[4,320,16,64]{1,3,2,0:T(8,128)(2,1)} %copy.125, bf16[4,320,16,64]{1,0,3,2:T(4,128)(2,1)S(1)} %copy-done.14), kind=kOutput, calls=%fused_computation.1 | convolution fusion | flops 871608320 | bytes 57836800 | tf_op jit(solution)/shard_map/sqhe,skhe->shqk/dot_general | solution.py:204
  702.4 26.6 %multiply_convert_fusion = bf16[4,16,320,320]{2,3,1,0:T(8,128)(2,1)} fusion(f32[4,16,320,320]{2,3,1,0:T(8,128)} %get-tuple-element.98, f32[4,16,320]{2,1,0:T(8,128)S(1)} %get-tuple-element.97, f32[4,16,320]{2,1,0:T(8,128)S(1)} %copy-done.45, f32[4,16,320,320]{2,3,1,0:T(8,128)} %get-tuple-element.95, pred[4,320]{1,0:T(4,128)(4,1)S(1)} %copy-done.50), kind=kLoop, calls=%fused_computation | loop fusion | flops 39321600 | bytes 65701120 | tf_op jit(solution)/shard_map/convert_element_type | solution.py:207
  748.8 18.1 %convolution_convert_fusion = bf16[4096,1024]{1,0:T(8,128)(2,1)} fusion(bf16[1280,4096]{1,0:T(8,128)(2,1)} %get-tuple-element.26, bf16[1280,512]{0,1:T(8,128)(2,1)} %collective-permute-done.33, bf16[1280,512]{0,1:T(8,128)(2,1)S(1)} %copy-done.42), kind=kOutput, calls=%fused_computation.42 | convolution fusion | flops 10746855424 | bytes 21495808 | tf_op jit(solution)/shard_map/dot_general | solution.py:25
  947.9 17.2 %collective-permute-done.34 = bf16[1280,512]{0,1:T(8,128)(2,1)} collective-permute-done((bf16[1280,512]{0,1:T(8,128)(2,1)}, bf16[1280,512]{0,1:T(8,128)(2,1)}, u32[]{:S(2)}, u32[]{:S(2)}) %collective-permute-start.34) | collective-permute-done | bytes 1310752 | tf_op jit(solution)/shard_map/ppermute | solution.py:17
  967.9 24.6 %collective-permute-done.32 = bf16[1280,512]{0,1:T(8,128)(2,1)} collective-permute-done((bf16[1280,512]{0,1:T(8,128)(2,1)}, bf16[1280,512]{0,1:T(8,128)(2,1)}, u32[]{:S(2)}, u32[]{:S(2)}) %collective-permute-start.32) | collective-permute-done | bytes 1310752 | tf_op jit(solution)/shard_map/ppermute | solution.py:17
  1015.5 24.9 %collective-permute-done.42 = bf16[2,4,3,8,8,512]{5,4,3,2,1,0:T(8,128)(2,1)} collective-permute-done((bf16[2,4,3,8,8,512]{5,4,3,2,1,0:T(8,128)(2,1)}, bf16[2,4,3,8,8,512]{5,4,3,2,1,0:T(8,128)(2,1)}, u32[]{:S(2)}, u32[]{:S(2)}) %collective-permute-start.42) | collective-permute-done | bytes 1572896 | tf_op jit(solution)/shard_map/ppermute | solution.py:17
  1045.8 18.5 %collective-permute-done.55 = bf16[4,8,8,512]{3,2,1,0:T(8,128)(2,1)S(1)} collective-permute-done((bf16[4,8,8,512]{3,2,1,0:T(8,128)(2,1)S(1)}, bf16[4,8,8,512]{3,2,1,0:T(8,128)(2,1)S(1)}, u32[]{:S(2)}, u32[]{:S(2)}) %collective-permute-start.55) | collective-permute-done | bytes 262176 | tf_op jit(solution)/shard_map/ppermute | solution.py:17
  1068.4 16.9 %collective-permute-done.66 = bf16[2,4,256,512]{3,2,1,0:T(8,128)(2,1)} collective-permute-done((bf16[2,4,256,512]{3,2,1,0:T(8,128)(2,1)}, bf16[2,4,256,512]{3,2,1,0:T(8,128)(2,1)}, u32[]{:S(2)}, u32[]{:S(2)}) %collective-permute-start.66) | collective-permute-done | bytes 2097184 | tf_op jit(solution)/shard_map/ppermute | solution.py:17
  1088.1 40.4 %collective-permute-done.60 = bf16[2,4,256,512]{3,2,1,0:T(8,128)(2,1)S(1)} collective-permute-done((bf16[2,4,256,512]{3,2,1,0:T(8,128)(2,1)S(1)}, bf16[2,4,256,512]{3,2,1,0:T(8,128)(2,1)S(1)}, u32[]{:S(2)}, u32[]{:S(2)}) %collective-permute-start.60) | collective-permute-done | bytes 2097184 | tf_op jit(solution)/shard_map/ppermute | solution.py:17
  1159.7 16.2 %collective-permute-done.69 = bf16[256,512]{1,0:T(8,128)(2,1)S(1)} collective-permute-done((bf16[256,512]{1,0:T(8,128)(2,1)S(1)}, bf16[256,512]{1,0:T(8,128)(2,1)S(1)}, u32[]{:S(2)}, u32[]{:S(2)}) %collective-permute-start.69) | collective-permute-done | bytes 262176 | tf_op jit(solution)/shard_map/ppermute | solution.py:17
  1176.9 20.6 %collective-permute-done.63 = bf16[256,512]{1,0:T(8,128)(2,1)S(1)} collective-permute-done((bf16[256,512]{1,0:T(8,128)(2,1)S(1)}, bf16[256,512]{1,0:T(8,128)(2,1)S(1)}, u32[]{:S(2)}, u32[]{:S(2)}) %collective-permute-start.63) | collective-permute-done | bytes 262176 | tf_op jit(solution)/shard_map/ppermute | solution.py:17
  (512 shorter events, 617.9 us)
Async XLA Ops:
  43.2 49.6 %collective-permute-start.6 = (bf16[2,4,3,8,8,512]{5,4,3,2,1,0:T(8,128)(2,1)}, bf16[2,4,3,8,8,512]{5,4,3,2,1,0:T(8,128)(2,1)}, u32[]{:S(2)}, u32[]{:S(2)}) collective-permute-start(bf16[2,4,3,8,8,512]{5,4,3,2,1,0:T(8,128)(2,1)} %get-tuple-element.51), channel_id=1, source_target_pairs={{0,2},{2,0},{1,3},{3,1},{4,6},{6,4},{5,7},{7,5},{8,10},{10,8},{9,1... | collective-permute-start | bytes 4718600 | tf_op jit(solution)/shard_map/ppermute | solution.py:17
  79.7 55.3 %collective-permute-start.23 = (bf16[4,256,512]{2,1,0:T(8,128)(2,1)S(1)}, bf16[4,256,512]{2,1,0:T(8,128)(2,1)S(1)}, u32[]{:S(2)}, u32[]{:S(2)}) collective-permute-start(bf16[4,256,512]{2,1,0:T(8,128)(2,1)S(1)} %get-tuple-element.61), channel_id=1, source_target_pairs={{0,1},{1,0},{2,3},{3,2},{4,5},{5,4},{6,7},{7,6},{8,9},{9,8},{10,11... | collective-permute-start | bytes 3145736 | tf_op jit(solution)/shard_map/ppermute | solution.py:17
  89.9 47.9 %collective-permute-start.29 = (bf16[4,256,512]{2,1,0:T(8,128)(2,1)S(1)}, bf16[4,256,512]{2,1,0:T(8,128)(2,1)S(1)}, u32[]{:S(2)}, u32[]{:S(2)}) collective-permute-start(bf16[4,256,512]{2,1,0:T(8,128)(2,1)S(1)} %get-tuple-element.59), channel_id=1, source_target_pairs={{0,1},{1,0},{2,3},{3,2},{4,5},{5,4},{6,7},{7,6},{8,9},{9,8},{10,11... | collective-permute-start | bytes 3145736 | tf_op jit(solution)/shard_map/ppermute | solution.py:17
  92.7 41.4 %collective-permute-start.17 = (bf16[4,8,8,512]{3,2,1,0:T(8,128)(2,1)S(1)}, bf16[4,8,8,512]{3,2,1,0:T(8,128)(2,1)S(1)}, u32[]{:S(2)}, u32[]{:S(2)}) collective-permute-start(bf16[4,8,8,512]{3,2,1,0:T(8,128)(2,1)S(1)} %get-tuple-element.75), channel_id=1, source_target_pairs={{0,1},{1,0},{2,3},{3,2},{4,5},{5,4},{6,7},{7,6},{8,9},{9,8},{10,11... | collective-permute-start | bytes 786440 | tf_op jit(solution)/shard_map/ppermute | solution.py:17
  98.9 145.7 %collective-permute-start.7 = (bf16[2,2,4,3,8,8,512]{6,5,4,3,2,1,0:T(8,128)(2,1)}, bf16[2,2,4,3,8,8,512]{6,5,4,3,2,1,0:T(8,128)(2,1)}, u32[]{:S(2)}, u32[]{:S(2)}) collective-permute-start(bf16[2,2,4,3,8,8,512]{6,5,4,3,2,1,0:T(8,128)(2,1)} %get-tuple-element.38), channel_id=1, source_target_pairs={{0,4},{4,0},{1,5},{5,1},{2,6},{6,2},{3,7},{7,3},{8,12},{12,8},{9,1... | collective-permute-start | bytes 9437192 | tf_op jit(solution)/shard_map/ppermute | solution.py:17
  137.9 57.1 %collective-permute-start.24 = (bf16[2,4,256,512]{3,2,1,0:T(8,128)(2,1)}, bf16[2,4,256,512]{3,2,1,0:T(8,128)(2,1)}, u32[]{:S(2)}, u32[]{:S(2)}) collective-permute-start(bf16[2,4,256,512]{3,2,1,0:T(8,128)(2,1)} %get-tuple-element.49), channel_id=1, source_target_pairs={{0,2},{2,0},{1,3},{3,1},{4,6},{6,4},{5,7},{7,5},{8,10},{10,8},{9,1... | collective-permute-start | bytes 6291464 | tf_op jit(solution)/shard_map/ppermute | solution.py:17
  141.6 98.0 %collective-permute-start.30 = (bf16[2,4,256,512]{3,2,1,0:T(8,128)(2,1)}, bf16[2,4,256,512]{3,2,1,0:T(8,128)(2,1)}, u32[]{:S(2)}, u32[]{:S(2)}) collective-permute-start(bf16[2,4,256,512]{3,2,1,0:T(8,128)(2,1)} %get-tuple-element.47), channel_id=1, source_target_pairs={{0,2},{2,0},{1,3},{3,1},{4,6},{6,4},{5,7},{7,5},{8,10},{10,8},{9,1... | collective-permute-start | bytes 6291464 | tf_op jit(solution)/shard_map/ppermute | solution.py:17
  160.2 379.7 %collective-permute-start.33 = (bf16[1280,512]{0,1:T(8,128)(2,1)}, bf16[1280,512]{0,1:T(8,128)(2,1)}, u32[]{:S(2)}, u32[]{:S(2)}) collective-permute-start(bf16[1280,512]{0,1:T(8,128)(2,1)} %copy.161), channel_id=1, source_target_pairs={{0,1},{1,0},{2,3},{3,2},{4,5},{5,4},{6,7},{7,6},{8,9},{9,8},{10,11... | collective-permute-start | bytes 3932168 | tf_op jit(solution)/shard_map/ppermute | solution.py:17
  200.1 213.5 %collective-permute-start.25 = (bf16[2,2,4,256,512]{4,3,2,1,0:T(8,128)(2,1)}, bf16[2,2,4,256,512]{4,3,2,1,0:T(8,128)(2,1)}, u32[]{:S(2)}, u32[]{:S(2)}) collective-permute-start(bf16[2,2,4,256,512]{4,3,2,1,0:T(8,128)(2,1)} %get-tuple-element.36), channel_id=1, source_target_pairs={{0,4},{4,0},{1,5},{5,1},{2,6},{6,2},{3,7},{7,3},{8,12},{12,8},{9,1... | collective-permute-start | bytes 12582920 | tf_op jit(solution)/shard_map/ppermute | solution.py:17
  244.5 263.2 %collective-permute-start.31 = (bf16[2,2,4,256,512]{4,3,2,1,0:T(8,128)(2,1)}, bf16[2,2,4,256,512]{4,3,2,1,0:T(8,128)(2,1)}, u32[]{:S(2)}, u32[]{:S(2)}) collective-permute-start(bf16[2,2,4,256,512]{4,3,2,1,0:T(8,128)(2,1)} %get-tuple-element.34), channel_id=1, source_target_pairs={{0,4},{4,0},{1,5},{5,1},{2,6},{6,2},{3,7},{7,3},{8,12},{12,8},{9,1... | collective-permute-start | bytes 12582920 | tf_op jit(solution)/shard_map/ppermute | solution.py:17
  794.8 209.1 %collective-permute-start.65 = (bf16[2,2,4,256,512]{4,3,2,1,0:T(8,128)(2,1)}, bf16[2,2,4,256,512]{4,3,2,1,0:T(8,128)(2,1)}, u32[]{:S(2)}, u32[]{:S(2)}) collective-permute-start(bf16[2,2,4,256,512]{4,3,2,1,0:T(8,128)(2,1)} %slice_bitcast_fusion), channel_id=1, source_target_pairs={{0,4},{4,0},{1,5},{5,1},{2,6},{6,2},{3,7},{7,3},{8,12},{12,8},{9,1... | collective-permute-start | bytes 12582920 | tf_op jit(solution)/shard_map/ppermute | solution.py:17
  827.7 47.3 %collective-permute-start.47 = (f32[2,4,384]{2,1,0:T(4,128)S(1)}, f32[2,4,384]{2,1,0:T(4,128)S(1)}, u32[]{:S(2)}, u32[]{:S(2)}) collective-permute-start(f32[2,4,384]{2,1,0:T(4,128)S(1)} %slice_bitcast_fusion.40), channel_id=1, source_target_pairs={{0,4},{4,0},{1,5},{5,1},{2,6},{6,2},{3,7},{7,3},{8,12},{12,8},{9,1... | collective-permute-start | bytes 36872 | tf_op jit(solution)/shard_map/ppermute | solution.py:17
  916.9 79.9 %collective-permute-start.41 = (bf16[2,2,4,3,8,8,512]{6,5,4,3,2,1,0:T(8,128)(2,1)}, bf16[2,2,4,3,8,8,512]{6,5,4,3,2,1,0:T(8,128)(2,1)}, u32[]{:S(2)}, u32[]{:S(2)}) collective-permute-start(bf16[2,2,4,3,8,8,512]{6,5,4,3,2,1,0:T(8,128)(2,1)} %slice_bitcast_fusion.4), channel_id=1, source_target_pairs={{0,4},{4,0},{1,5},{5,1},{2,6},{6,2},{3,7},{7,3},{8,12},{12,8},{9,1... | collective-permute-start | bytes 9437192 | tf_op jit(solution)/shard_map/ppermute | solution.py:17
  925.3 85.3 %collective-permute-start.59 = (bf16[2,2,4,256,512]{4,3,2,1,0:T(8,128)(2,1)}, bf16[2,2,4,256,512]{4,3,2,1,0:T(8,128)(2,1)}, u32[]{:S(2)}, u32[]{:S(2)}) collective-permute-start(bf16[2,2,4,256,512]{4,3,2,1,0:T(8,128)(2,1)} %slice_bitcast_fusion.2), channel_id=1, source_target_pairs={{0,4},{4,0},{1,5},{5,1},{2,6},{6,2},{3,7},{7,3},{8,12},{12,8},{9,1... | collective-permute-start | bytes 12582920 | tf_op jit(solution)/shard_map/ppermute | solution.py:17
  939.0 53.4 %collective-permute-start.32 = (bf16[1280,512]{0,1:T(8,128)(2,1)}, bf16[1280,512]{0,1:T(8,128)(2,1)}, u32[]{:S(2)}, u32[]{:S(2)}) collective-permute-start(bf16[1280,512]{0,1:T(8,128)(2,1)} %get-tuple-element.42), channel_id=1, source_target_pairs={{0,1},{1,0},{2,3},{3,2},{4,5},{5,4},{6,7},{7,6},{8,9},{9,8},{10,11... | collective-permute-start | bytes 3932168 | tf_op jit(solution)/shard_map/ppermute | solution.py:17
  1002.8 37.6 %collective-permute-start.42 = (bf16[2,4,3,8,8,512]{5,4,3,2,1,0:T(8,128)(2,1)}, bf16[2,4,3,8,8,512]{5,4,3,2,1,0:T(8,128)(2,1)}, u32[]{:S(2)}, u32[]{:S(2)}) collective-permute-start(bf16[2,4,3,8,8,512]{5,4,3,2,1,0:T(8,128)(2,1)} %slice_bitcast_fusion.10), channel_id=1, source_target_pairs={{0,2},{2,0},{1,3},{3,1},{4,6},{6,4},{5,7},{7,5},{8,10},{10,8},{9,1... | collective-permute-start | bytes 4718600 | tf_op jit(solution)/shard_map/ppermute | solution.py:17
  1009.7 75.7 %collective-permute-start.66 = (bf16[2,4,256,512]{3,2,1,0:T(8,128)(2,1)}, bf16[2,4,256,512]{3,2,1,0:T(8,128)(2,1)}, u32[]{:S(2)}, u32[]{:S(2)}) collective-permute-start(bf16[2,4,256,512]{3,2,1,0:T(8,128)(2,1)} %slice_bitcast_fusion.6), channel_id=1, source_target_pairs={{0,2},{2,0},{1,3},{3,1},{4,6},{6,4},{5,7},{7,5},{8,10},{10,8},{9,1... | collective-permute-start | bytes 6291464 | tf_op jit(solution)/shard_map/ppermute | solution.py:17
  1014.4 114.1 %collective-permute-start.60 = (bf16[2,4,256,512]{3,2,1,0:T(8,128)(2,1)S(1)}, bf16[2,4,256,512]{3,2,1,0:T(8,128)(2,1)S(1)}, u32[]{:S(2)}, u32[]{:S(2)}) collective-permute-start(bf16[2,4,256,512]{3,2,1,0:T(8,128)(2,1)S(1)} %slice_bitcast_fusion.8), channel_id=1, source_target_pairs={{0,2},{2,0},{1,3},{3,1},{4,6},{6,4},{5,7},{7,5},{8,10},{10,8},{9,1... | collective-permute-start | bytes 6291464 | tf_op jit(solution)/shard_map/ppermute | solution.py:17
  1064.4 65.4 %collective-permute-start.56 = (bf16[8,8,512]{2,1,0:T(8,128)(2,1)S(1)}, bf16[8,8,512]{2,1,0:T(8,128)(2,1)S(1)}, u32[]{:S(2)}, u32[]{:S(2)}) collective-permute-start(bf16[8,8,512]{2,1,0:T(8,128)(2,1)S(1)} %get-tuple-element.71), channel_id=1, source_target_pairs={{0,24},{8,0},{16,8},{24,16},{1,25},{9,1},{17,9},{25,17},{2,26},{10... | collective-permute-start | bytes 196616 | tf_op jit(solution)/shard_map/ppermute | solution.py:17
  1066.4 65.4 %collective-permute-start.57 = (bf16[8,8,512]{2,1,0:T(8,128)(2,1)S(1)}, bf16[8,8,512]{2,1,0:T(8,128)(2,1)S(1)}, u32[]{:S(2)}, u32[]{:S(2)}) collective-permute-start(bf16[8,8,512]{2,1,0:T(8,128)(2,1)S(1)} %get-tuple-element.73), channel_id=1, source_target_pairs={{0,16},{8,24},{16,0},{24,8},{1,17},{9,25},{17,1},{25,9},{2,18},{10... | collective-permute-start | bytes 196616 | tf_op jit(solution)/shard_map/ppermute | solution.py:17
  1067.1 65.5 %collective-permute-start.58 = (bf16[8,8,512]{2,1,0:T(8,128)(2,1)S(1)}, bf16[8,8,512]{2,1,0:T(8,128)(2,1)S(1)}, u32[]{:S(2)}, u32[]{:S(2)}) collective-permute-start(bf16[8,8,512]{2,1,0:T(8,128)(2,1)S(1)} %get-tuple-element.72), channel_id=1, source_target_pairs={{0,8},{8,16},{16,24},{24,0},{1,9},{9,17},{17,25},{25,1},{2,10},{10... | collective-permute-start | bytes 196616 | tf_op jit(solution)/shard_map/ppermute | solution.py:17
  1087.7 61.3 %collective-permute-start.67 = (bf16[4,256,512]{2,1,0:T(8,128)(2,1)S(1)}, bf16[4,256,512]{2,1,0:T(8,128)(2,1)S(1)}, u32[]{:S(2)}, u32[]{:S(2)}) collective-permute-start(bf16[4,256,512]{2,1,0:T(8,128)(2,1)S(1)} %slice_bitcast_fusion.12), channel_id=1, source_target_pairs={{0,1},{1,0},{2,3},{3,2},{4,5},{5,4},{6,7},{7,6},{8,9},{9,8},{10,11... | collective-permute-start | bytes 3145736 | tf_op jit(solution)/shard_map/ppermute | solution.py:17
  1156.0 41.5 %collective-permute-start.63 = (bf16[256,512]{1,0:T(8,128)(2,1)S(1)}, bf16[256,512]{1,0:T(8,128)(2,1)S(1)}, u32[]{:S(2)}, u32[]{:S(2)}) collective-permute-start(bf16[256,512]{1,0:T(8,128)(2,1)S(1)} %get-tuple-element.57), channel_id=1, source_target_pairs={{0,16},{8,24},{16,0},{24,8},{1,17},{9,25},{17,1},{25,9},{2,18},{10... | collective-permute-start | bytes 786440 | tf_op jit(solution)/shard_map/ppermute | solution.py:17
  1156.5 41.0 %collective-permute-start.64 = (bf16[256,512]{1,0:T(8,128)(2,1)S(1)}, bf16[256,512]{1,0:T(8,128)(2,1)S(1)}, u32[]{:S(2)}, u32[]{:S(2)}) collective-permute-start(bf16[256,512]{1,0:T(8,128)(2,1)S(1)} %get-tuple-element.56), channel_id=1, source_target_pairs={{0,8},{8,16},{16,24},{24,0},{1,9},{9,17},{17,25},{25,1},{2,10},{10... | collective-permute-start | bytes 786440 | tf_op jit(solution)/shard_map/ppermute | solution.py:17
  (140 other events, 3512.3 us)

commit v2 on v1

v2 whole, which is shorter than its diff:
```python
import functools

import jax
import jax.numpy as jnp
from jax import lax
from jax.experimental import pallas as pl
from jax.experimental.pallas import tpu as pltpu
from jax.sharding import Mesh, PartitionSpec as P

HD = 64
PAIR = 2 * HD
BUF = 64
LEN = 320
masked_fill = -1000000000.0
norm_epsilon = 1e-06
attn_scale = 0.125
exp2_scale = attn_scale * 1.4426950408889634
root_half = 0.7071067811865476
density = 0.3989422804014327
bf16 = jnp.bfloat16
f32 = jnp.float32
MIB = 1 << 20


def shift(values, axis, size, step):
    return lax.ppermute(values, axis, [(i, (i + step) % size) for i in range(size)])


def contract_last(left, right):
    return lax.dot_general(left, right, (((1,), (1,)), ((), ())), preferred_element_type=f32)


def contract_first(left, right):
    return lax.dot_general(left, right, (((0,), (0,)), ((), ())), preferred_element_type=f32)


def matmul(left, right):
    return lax.dot_general(left, right, (((1,), (0,)), ((), ())), preferred_element_type=f32)


def whole(shape):
    return pl.BlockSpec(shape, lambda *_: (0,) * len(shape), pipeline_mode=pl.Buffered(1))


def summed(shape):
    return pl.BlockSpec(shape, lambda *_: (0,) * len(shape))


def call(kernel, grid, in_specs, out_specs, out_shape, flops, moved, name, vmem=48, scratch=()):
    return pl.pallas_call(
        kernel,
        grid=grid,
        in_specs=in_specs,
        out_specs=out_specs,
        out_shape=out_shape,
        scratch_shapes=scratch,
        name=name,
        compiler_params=pltpu.CompilerParams(vmem_limit_bytes=vmem * MIB),
        cost_estimate=pl.CostEstimate(flops=flops, bytes_accessed=moved, transcendentals=0),
    )


def unit_norm(values):
    center = jnp.mean(values, axis=1, keepdims=True)
    centered = values - center
    spread = jnp.mean(centered * centered, axis=1, keepdims=True)
    inverse = lax.rsqrt(spread + norm_epsilon)
    return centered * inverse, inverse


def norm_pull(grad, gain, unit, inverse):
    scaled = grad * gain
    total = jnp.mean(scaled, axis=1, keepdims=True)
    paired = jnp.mean(scaled * unit, axis=1, keepdims=True)
    return inverse * (scaled - total - unit * paired)


def qkv_kernel(x_ref, gain_ref, shift_ref, w_ref, bias_ref, a_ref, out_ref):
    unit, _ = unit_norm(x_ref[...].astype(f32))
    a = (unit * gain_ref[...] + shift_ref[...]).astype(bf16)
    a_ref[...] = a
    for i in range(3):
        value = contract_last(a, w_ref[i])
        if i != 1:
            value = value + bias_ref[i // 2 : i // 2 + 1]
        out_ref[i] = value.astype(bf16)


def split_heads(pair):
    first = lax.broadcasted_iota(jnp.int32, pair.shape, 1) < HD
    zero = jnp.zeros_like(pair)
    return jnp.concatenate([jnp.where(first, pair, zero), jnp.where(first, zero, pair)], axis=0)


def join_heads(both):
    rows = both.shape[0] // 2
    first = lax.broadcasted_iota(jnp.int32, (rows, both.shape[1]), 1) < HD
    return jnp.where(first, both[:rows], both[rows:])


def attend_kernel(qkv_ref, mask_ref, out_ref):
    seen = mask_ref[0] > 0
    scores = contract_last(split_heads(qkv_ref[0]), qkv_ref[1])
    scores = jnp.where(seen, scores, masked_fill / attn_scale)
    top = jnp.max(scores, axis=1, keepdims=True)
    grown = jnp.exp2((scores - top) * exp2_scale)
    total = jnp.sum(grown, axis=1, keepdims=True)
    mixed = matmul(grown.astype(bf16), qkv_ref[2]) / total
    out_ref[...] = join_heads(mixed).astype(bf16)


def attend_pull_kernel(qkv_ref, mask_ref, do_ref, out_ref):
    seen = mask_ref[0] > 0
    both = split_heads(qkv_ref[0])
    keys = qkv_ref[1]
    vals = qkv_ref[2]
    pulled = split_heads(do_ref[...])
    scores = contract_last(keys, both)
    scores = jnp.where(seen, scores, masked_fill / attn_scale)
    top = jnp.max(scores, axis=0, keepdims=True)
    grown = jnp.exp2((scores - top) * exp2_scale)
    probs = grown * (1.0 / jnp.sum(grown, axis=0, keepdims=True))
    prob_grad = contract_last(vals, pulled)
    out_ref[2] = matmul(probs.astype(bf16), pulled).astype(bf16)
    inner = jnp.sum(prob_grad * probs, axis=0, keepdims=True)
    score_grad = (probs * (prob_grad - inner)).astype(bf16)
    out_ref[1] = (matmul(score_grad, both) * attn_scale).astype(bf16)
    query_grad = contract_first(score_grad, keys) * attn_scale
    out_ref[0] = join_heads(query_grad).astype(bf16)


def out_kernel(x_ref, o_ref, w_ref, bias_ref, gain_ref, shift_ref, middle_ref, a_ref):
    middle = x_ref[...].astype(f32) + (matmul(o_ref[...], w_ref[...]) + bias_ref[...])
    middle_ref[...] = middle
    unit, _ = unit_norm(middle)
    a_ref[...] = (unit * gain_ref[...] + shift_ref[...]).astype(bf16)


def up_kernel(ncol, blocks, a_ref, bias_ref, *refs):
    w_refs, (hid_ref, slope_ref) = refs[: blocks * ncol], refs[blocks * ncol :]
    width = a_ref.shape[1] // ncol
    step = w_refs[0].shape[0]
    for b in range(blocks):
        value = bias_ref[:, b * step : (b + 1) * step]
        for c in range(ncol):
            value = value + contract_last(a_ref[:, c * width : (c + 1) * width], w_refs[b * ncol + c][...])
        cdf = 0.5 + 0.5 * lax.erf(value * root_half)
        pdf = jnp.exp(-0.5 * value * value) * density
        hid_ref[:, b * step : (b + 1) * step] = (value * cdf).astype(bf16)
        slope_ref[:, b * step : (b + 1) * step] = (cdf + value * pdf).astype(bf16)


def down_kernel(ncol, blocks, hid_ref, middle_ref, bias_ref, *refs):
    w_refs, (own_ref, other_ref) = refs[: blocks * ncol], refs[blocks * ncol :]
    step, width = w_refs[0].shape
    for c in range(ncol):
        lanes = slice(c * width, (c + 1) * width)
        value = middle_ref[:, lanes] + bias_ref[:, lanes]
        for b in range(blocks):
            value = value + matmul(hid_ref[:, b * step : (b + 1) * step], w_refs[b * ncol + c][...])
        if c == 0:
            own_ref[...] = value.astype(bf16)
        else:
            other_ref[c - 1] = value.astype(bf16)


def hidden_pull_kernel(ncol, blocks, g_ref, slope_ref, *refs):
    w_refs, (du_ref, sum_ref) = refs[: blocks * ncol], refs[blocks * ncol :]
    step, width = w_refs[0].shape

    @pl.when(pl.program_id(0) == 0)
    def _():
        sum_ref[...] = jnp.zeros_like(sum_ref)

    for b in range(blocks):
        rows = slice(b * step, (b + 1) * step)
        value = contract_last(g_ref[:, :width], w_refs[b * ncol][...])
        for c in range(1, ncol):
            value = value + contract_last(g_ref[:, c * width : (c + 1) * width], w_refs[b * ncol + c][...])
        low = (value * slope_ref[:, rows].astype(f32)).astype(bf16)
        du_ref[:, rows] = low
        sum_ref[:, rows] += jnp.sum(low.astype(f32), axis=0, keepdims=True)


def middle_pull_kernel(ncol, blocks, du_ref, middle_ref, g_ref, gain_ref, wo_ref, *refs):
    w_refs, (grad_ref, low_ref, do_ref, sum_ref) = refs[: blocks * ncol], refs[blocks * ncol :]
    step, width = w_refs[0].shape

    @pl.when(pl.program_id(0) == 0)
    def _():
        sum_ref[...] = jnp.zeros_like(sum_ref)

    parts = []
    for c in range(ncol):
        value = matmul(du_ref[:, :step], w_refs[c][...])
        for b in range(1, blocks):
            value = value + matmul(du_ref[:, b * step : (b + 1) * step], w_refs[b * ncol + c][...])
        parts.append(value)
    grad = jnp.concatenate(parts, axis=1)
    unit, inverse = unit_norm(middle_ref[...])
    out_grad = g_ref[...].astype(f32)
    total = out_grad + norm_pull(grad, gain_ref[...], unit, inverse)
    grad_ref[...] = total
    low = total.astype(bf16)
    low_ref[...] = low
    do_ref[...] = contract_last(low, wo_ref[...]).astype(bf16)
    sum_ref[0:1] += jnp.sum(low.astype(f32), axis=0, keepdims=True)
    sum_ref[1:2] += jnp.sum(grad * unit, axis=0, keepdims=True)
    sum_ref[2:3] += jnp.sum(grad, axis=0, keepdims=True)
    sum_ref[3:4] += jnp.sum(out_grad, axis=0, keepdims=True)


def token_pull_kernel(ncol, dqkv_ref, x_ref, grad_ref, gain_ref, w_ref, own_ref, other_ref, sum_ref):
    @pl.when(pl.program_id(0) == 0)
    def _():
        sum_ref[...] = jnp.zeros_like(sum_ref)

    grad = matmul(dqkv_ref[0], w_ref[0])
    for i in range(1, 3):
        grad = grad + matmul(dqkv_ref[i], w_ref[i])
    unit, inverse = unit_norm(x_ref[...].astype(f32))
    total = grad_ref[...] + norm_pull(grad, gain_ref[...], unit, inverse)
    width = total.shape[1] // ncol
    own_ref[...] = total[:, :width]
    for c in range(1, ncol):
        other_ref[c - 1] = total[:, c * width : (c + 1) * width].astype(bf16)
    sum_ref[0:1] += jnp.sum(grad * unit, axis=0, keepdims=True)
    sum_ref[1:2] += jnp.sum(grad, axis=0, keepdims=True)


def ffn_grad_kernel(ncol, l_ref, r_ref, out_ref):
    width = r_ref.shape[1] // ncol
    left = l_ref[...]
    for c in range(ncol):
        out_ref[0, c] = contract_first(left, r_ref[:, c * width : (c + 1) * width]).astype(bf16)


def head_grad_kernel(dims, l_ref, r_ref, out_ref, *sums):
    ncore, ncol, nz, part, piece = dims
    width = r_ref.shape[1] // ncol
    left = l_ref[0]
    for c in range(ncol):
        value = contract_first(left, r_ref[:, c * width : (c + 1) * width]).astype(bf16)
        value = value.reshape(part, ncore, nz, piece, width)
        for core in range(ncore):
            for z in range(nz):
                out_ref[core, 0, c, z, 0] = value[:, core, z]
    if sums:
        sums[0][0] = jnp.sum(left.astype(f32), axis=0, keepdims=True)


def make_local(nz, ncore, nrow, ncol):
    blocks = ncore * nrow

    def axis_in(values, axis, size):
        return [values] + [shift(values, axis, size, k) for k in range(1, size)]

    def gather(shard):
        along_z = jnp.stack(axis_in(shard, "z", nz))
        along_col = axis_in(along_z, "col", ncol)
        by_col = [axis_in(piece, "row", nrow) for piece in along_col]
        by_row = [by_col[c][r] for r in range(nrow) for c in range(ncol)]
        by_core = [axis_in(piece, "core", ncore) for piece in by_row]
        return [by_core[i][k] for k in range(ncore) for i in range(len(by_row))]

    def scatter(mine, sent):
        held = [mine] + [shift(part, "core", ncore, -(k + 1)) for k, part in enumerate(sent)]

        def total(parts, index):
            value = parts[0][index].astype(f32)
            for part in parts[1:]:
                value = value + part[index].astype(f32)
            return value

        got = [
            shift(total(held, (k,)).astype(bf16), "row", nrow, -k) for k in range(1, nrow)
        ]
        held = [part[0] for part in held] + got
        got = [
            shift(total(held, (k,)).astype(bf16), "col", ncol, -k) for k in range(1, ncol)
        ]
        held = [part[0] for part in held] + got
        got = [shift(total(held, (k,)).astype(bf16), "z", nz, -k) for k in range(1, nz)]
        value = total(held, (0,))
        for part in got:
            value = value + part.astype(f32)
        return value

    def tokens_in(values):
        rows = values.shape[0] // ncol
        here = lax.axis_index("col")
        parts = [lax.dynamic_slice_in_dim(values, here * rows, rows, 0)]
        for k in range(1, ncol):
            block = lax.dynamic_slice_in_dim(values, ((here + k) % ncol) * rows, rows, 0)
            parts.append(shift(block, "col", ncol, k))
        return jnp.concatenate(parts, axis=1)

    def tokens_out(own, other):
        rows = own.shape[0]
        here = lax.axis_index("col")
        result = jnp.zeros((rows * ncol, own.shape[1]), own.dtype)
        result = lax.dynamic_update_slice_in_dim(result, own, here * rows, 0)
        for k in range(1, ncol):
            block = shift(other[k - 1], "col", ncol, -k).astype(own.dtype)
            result = lax.dynamic_update_slice_in_dim(result, block, ((here + k) % ncol) * rows, 0)
        return result

    def local(
        tokens,
        key_mask,
        first_gain,
        first_shift,
        qkv_weight,
        qkv_bias,
        out_weight,
        out_bias,
        second_gain,
        second_shift,
        up_weight,
        up_bias,
        down_weight,
        down_bias,
        cotangent,
    ):
        count = tokens.shape[0] // ncol
        seqs = count // LEN
        part, piece, width = out_weight.shape
        heads = part * nrow
        flat = heads * HD
        hidden_part = up_weight.shape[0]
        step = nz * hidden_part
        dim = width * ncol
        hidden = step * blocks
        pairs = heads // 2
        moved = count * dim

        def tile(shape, index=None):
            return pl.BlockSpec(shape, index or (lambda t: (t,) + (0,) * (len(shape) - 1)))

        inputs = tokens_in(tokens)
        qkv_pieces = gather(qkv_weight.astype(bf16))
        small = jnp.concatenate([qkv_bias.reshape(-1), up_bias]).astype(bf16)
        vectors = jnp.stack([first_gain, first_shift, second_gain, second_shift, out_bias, down_bias])
        vectors = jnp.concatenate(axis_in(vectors, "col", ncol), axis=1)
        gain_one, shift_one, gain_two, shift_two, out_offset, down_offset = [vectors[i : i + 1] for i in range(6)]
        small_z = jnp.stack(axis_in(small, "z", nz))
        small_row = jnp.stack(axis_in(small_z, "row", nrow))
        small_all = jnp.stack(axis_in(small_row, "core", ncore)).astype(f32)
        qkv_count = qkv_bias.size
        qkv_offset = small_all[..., :qkv_count].reshape(ncore, nrow, nz, 2, part, piece)
        qkv_offset = jnp.transpose(qkv_offset, (3, 1, 4, 0, 2, 5)).reshape(2, flat)
        up_offset = small_all[..., qkv_count:].reshape(1, hidden)
        masks = jnp.zeros((ncol,) + key_mask.shape, key_mask.dtype)
        here = lax.axis_index("col")
        for k, mask in enumerate(axis_in(key_mask, "col", ncol)):
            masks = lax.dynamic_update_slice_in_dim(masks, mask[None], (here - k + ncol) % ncol, 0)
        masks = masks.reshape(-1, key_mask.shape[1])
        first_seq = (lax.axis_index("row") * ncol + here) * seqs
        masks = lax.dynamic_slice_in_dim(masks, first_seq, seqs, 0)
        visible = jnp.concatenate([jnp.ones((seqs, BUF), jnp.int32), masks], axis=1)

        grid_shape = (ncore, nrow, ncol, nz)
        qkv_all = jnp.stack(qkv_pieces).reshape(grid_shape + qkv_weight.shape)
        qkv_matrix = jnp.transpose(qkv_all, (4, 1, 5, 0, 3, 6, 2, 7)).reshape(3, flat, dim)
        out_all = jnp.stack(gather(out_weight.astype(bf16))).reshape(grid_shape + out_weight.shape)
        out_matrix = jnp.transpose(out_all, (1, 4, 0, 3, 5, 2, 6)).reshape(flat, dim)
        up_pieces = [w.reshape(step, width) for w in gather(up_weight.astype(bf16))]
        down_pieces = [w.reshape(step, width) for w in gather(down_weight.astype(bf16))]
        grad_low = tokens_in(cotangent)

        tokens_spec = tile((LEN, dim))
        hidden_spec = tile((LEN, hidden))
        piece_specs = [whole((step, width))] * (blocks * ncol)
        vector_spec = whole((1, dim))
        three = pl.BlockSpec((3, LEN, flat), lambda t: (0, t, 0))
        pair_spec = pl.BlockSpec((3, LEN, PAIR), lambda s, p: (0, s, p))
        one_pair = pl.BlockSpec((LEN, PAIR), lambda s, p: (s, p))
        own_spec = tile((LEN, width))
        other_spec = pl.BlockSpec((ncol - 1, LEN, width), lambda t: (0, t, 0))

        def out_of(*shape, dtype=bf16):
            return jax.ShapeDtypeStruct(shape, dtype)

        normed, qkv = call(
            qkv_kernel,
            (seqs,),
            [tokens_spec, vector_spec, vector_spec, whole((3, flat, dim)), whole((2, flat))],
            [tokens_spec, three],
            [out_of(count, dim), out_of(3, count, flat)],
            6 * moved * flat,
            6 * flat * dim + 10 * moved,
            "qkv",
        )(inputs, gain_one, shift_one, qkv_matrix, qkv_offset)
        attended = call(
            attend_kernel,
            (seqs, pairs),
            [pair_spec, pl.BlockSpec((1, 1, LEN), lambda s, p: (s, 0, 0))],
            one_pair,
            out_of(count, flat),
            16 * count * LEN * flat,
            8 * moved,
            "attend",
        )(qkv, visible[:, None, :])
        middle, normed_two = call(
            out_kernel,
            (seqs,),
            [tokens_spec, tile((LEN, flat)), whole((flat, dim)), vector_spec, vector_spec, vector_spec],
            [tokens_spec, tokens_spec],
            [out_of(count, dim, dtype=f32), out_of(count, dim)],
            2 * moved * flat,
            2 * flat * dim + 10 * moved,
            "out",
        )(inputs, attended, out_matrix, out_offset, gain_two, shift_two)
        hid, slope = call(
            functools.partial(up_kernel, ncol, blocks),
            (seqs,),
            [tokens_spec, whole((1, hidden))] + piece_specs,
            [hidden_spec, hidden_spec],
            [out_of(count, hidden), out_of(count, hidden)],
            8 * moved * hidden,
            2 * hidden * dim + 4 * count * hidden,
            "up",
        )(normed_two, up_offset, *up_pieces)

        def ffn_grad(left, right, core, name):
            halves = 2
            rows = step // halves
            return call(
                functools.partial(ffn_grad_kernel, ncol),
                (nrow, halves),
                [
                    pl.BlockSpec((count, rows), lambda r, h: (0, (core * nrow + r) * halves + h)),
                    whole((count, dim)),
                ],
                pl.BlockSpec((1, ncol, rows, width), lambda r, h: (r, 0, h, 0)),
                out_of(nrow, ncol, step, width),
                2 * moved * hidden // ncore,
                2 * (hidden * dim + count * hidden) // ncore + 2 * moved,
                name,
            )(left, right).reshape(nrow, ncol, nz, hidden_part, width)

        def ffn_scatter(left, right, name):
            sent = [ffn_grad(left, right, core, name) for core in range(1, ncore)]
            return scatter(ffn_grad(left, right, 0, name), sent)

        def head_grad(left, right, kinds, name, sums=False):
            dims = (ncore, ncol, nz, part, piece)
            out = call(
                functools.partial(head_grad_kernel, dims),
                (kinds, nrow),
                [
                    pl.BlockSpec((1, count, part * HD), lambda i, r: (i, 0, r)),
                    whole((count, dim)),
                ],
                [
                    pl.BlockSpec(
                        (ncore, 1, ncol, nz, 1, part, piece, width), lambda i, r: (0, r, 0, 0, i, 0, 0, 0)
                    )
                ]
                + [pl.BlockSpec((1, 1, part * HD), lambda i, r: (i, 0, r))] * sums,
                [out_of(ncore, nrow, ncol, nz, kinds, part, piece, width)]
                + [out_of(kinds, 1, flat, dtype=f32)] * sums,
                2 * moved * flat * kinds,
                2 * kinds * (flat * dim + moved) + 2 * moved,
                name,
            )(left, right)
            grads = out[0]
            return scatter(grads[0], [grads[k] for k in range(1, ncore)]), out[1:]

        down_grad = ffn_scatter(hid, grad_low, "down_grad")
        own, other = call(
            functools.partial(down_kernel, ncol, blocks),
            (seqs,),
            [hidden_spec, tokens_spec, vector_spec] + piece_specs,
            [own_spec, other_spec],
            [out_of(count, width), out_of(ncol - 1, count, width)],
            2 * moved * hidden,
            2 * hidden * dim + 2 * count * hidden + 6 * moved,
            "down",
        )(hid, middle, down_offset, *down_pieces)
        activations = tokens_out(own, other)
        upward_grad, up_bias_sum = call(
            functools.partial(hidden_pull_kernel, ncol, blocks),
            (seqs,),
            [tokens_spec, hidden_spec] + piece_specs,
            [hidden_spec, summed((1, hidden))],
            [out_of(count, hidden), out_of(1, hidden, dtype=f32)],
            2 * moved * hidden,
            2 * hidden * dim + 4 * count * hidden,
            "hidden_pull",
        )(grad_low, slope, *down_pieces)
        up_grad = ffn_scatter(upward_grad, normed_two, "up_grad")
        middle_grad, branch_low, attended_grad, sums_two = call(
            functools.partial(middle_pull_kernel, ncol, blocks),
            (seqs,),
            [hidden_spec, tokens_spec, tokens_spec, vector_spec, whole((flat, dim))] + piece_specs,
            [tokens_spec, tokens_spec, tile((LEN, flat)), summed((4, dim))],
            [
                out_of(count, dim, dtype=f32),
                out_of(count, dim),
                out_of(count, flat),
                out_of(4, dim, dtype=f32),
            ],
            2 * moved * (hidden + flat),
            2 * hidden * dim + 2 * count * hidden + 14 * moved,
            "middle_pull",
        )(upward_grad, middle, grad_low, gain_two, out_matrix, *up_pieces)
        out_grad, _ = head_grad(attended[None], branch_low, 1, "out_grad")
        stacked = call(
            attend_pull_kernel,
            (seqs, pairs),
            [pair_spec, pl.BlockSpec((1, LEN, 1), lambda s, p: (s, 0, 0)), one_pair],
            pair_spec,
            out_of(3, count, flat),
            30 * count * LEN * flat,
            14 * moved,
            "attend_pull",
        )(qkv, visible[:, :, None], attended_grad)
        qkv_grad, (head_sums,) = head_grad(stacked, normed, 3, "qkv_grad", True)
        own, other, sums_one = call(
            functools.partial(token_pull_kernel, ncol),
            (seqs,),
            [three, tokens_spec, tokens_spec, vector_spec, whole((3, flat, dim))],
            [own_spec, other_spec, summed((2, dim))],
            [
                out_of(count, width, dtype=f32),
                out_of(ncol - 1, count, width),
                out_of(2, dim, dtype=f32),
            ],
            6 * moved * flat,
            6 * flat * dim + 14 * moved,
            "token_pull",
        )(stacked, inputs, middle_grad, gain_one, qkv_matrix)
        token_grad = tokens_out(own, other)

        bias_sum = jnp.stack([head_sums[0, 0], head_sums[2, 0]]).reshape(2, nrow, part, ncore, nz, piece)
        bias_sum = jnp.transpose(bias_sum, (3, 1, 4, 0, 2, 5)).reshape(ncore, nrow, nz, qkv_count)
        bias_sum = jnp.concatenate([bias_sum, up_bias_sum.reshape(ncore, nrow, nz, hidden_part)], axis=-1)
        sums = jnp.concatenate([sums_one, sums_two])
        own_sums = sums[:, :width].reshape(-1)
        size = own_sums.size
        flat_bias = bias_sum.reshape(-1)
        pack = jnp.concatenate([own_sums, flat_bias])
        for k in range(1, ncol):
            sent = jnp.concatenate([sums[:, k * width : (k + 1) * width].reshape(-1), flat_bias])
            pack = pack + shift(sent, "col", ncol, -k)
        for axis, count_along in (("core", ncore), ("row", nrow), ("z", nz)):
            both = pack[:size]
            rest = pack[size:].reshape(count_along, -1)
            pack = jnp.concatenate([both, rest[0]])
            for k in range(1, count_along):
                pack = pack + shift(jnp.concatenate([both, rest[k]]), axis, count_along, -k)
        sums = pack[:size].reshape(-1, width)
        bias_sum = pack[size:]
        return (
            activations,
            token_grad,
            sums[0],
            sums[1],
            qkv_grad,
            bias_sum[:qkv_count].reshape(qkv_bias.shape),
            out_grad[0],
            sums[2],
            sums[3],
            sums[4],
            up_grad,
            bias_sum[qkv_count:],
            down_grad,
            sums[5],
        )

    return local


def solution(mesh):
    devices = mesh.devices
    nz, ncore = devices.shape[0] // 2, 2
    nrow, ncol = devices.shape[1], devices.shape[2]
    fine = Mesh(devices.reshape(nz, ncore, nrow, ncol), ("z", "core", "row", "col"))
    dp = ("z", "core")
    rows = P(("z", "core", "row"), "col")
    qkv_weight = P(None, "row", dp, "col")
    qkv_bias = P(None, "row", dp)
    out_weight = P("row", dp, "col")
    feature = P("col")
    unit = P(("z", "core", "row"))
    in_specs = (
        rows,
        P(("z", "core", "col"), None),
        feature,
        feature,
        qkv_weight,
        qkv_bias,
        out_weight,
        feature,
        feature,
        feature,
        rows,
        unit,
        rows,
        feature,
        rows,
    )
    out_specs = (
        rows,
        rows,
        feature,
        feature,
        qkv_weight,
        qkv_bias,
        out_weight,
        feature,
        feature,
        feature,
        rows,
        unit,
        rows,
        feature,
    )
    return jax.shard_map(
        make_local(nz, ncore, nrow, ncol),
        mesh=fine,
        in_specs=in_specs,
        out_specs=out_specs,
        check_vma=False,
    )
```

time: 1210 us -> 743 us (0.61)
  matrix products: 319 us -> 0 us
  local copies, waits for them, and re-layouts: 311 us -> 52.9 us
  Pallas kernels: 0 us -> 232 us
  other arithmetic: 150 us -> 49.3 us
  waiting for transfers between devices: 331 us -> 294 us
  starting transfers between devices: 85.5 us -> 104 us
    dot_general x18 -> x0, matrix products: 319 us -> none  [the longest x4 106 us: contract_last(): lax.dot_general(left, right, (((1,), (1,)), ((), ())), preferred_element_...]
    pallas_call x0 -> x15, Pallas kernels: none -> 232 us  [the longest x4 35.8 us: ffn_grad(): call(functools.partial(ffn_grad_kernel, ncol), (nrow, halves), [pl.BlockS...]
    reshape x13 -> x9, local copies, waits for them, and re-layouts: 81.7 us -> 7.06 us  [the longest x1 6.39 us: local(): qkv_all = jnp.stack(qkv_pieces).reshape(grid_shape + qkv_weight.shape)]
    transpose x6 -> x0, local copies, waits for them, and re-layouts: 43.1 us -> none  [the longest x1 16.5 us: local(): jnp.transpose(up_all, (0, 1, 3, 4, 2, 5)).reshape(hidden_units, dim)]
    ppermute x71 -> x81, waiting for transfers between devices: 331 us -> 294 us  [shift(): lax.ppermute(values, axis, [(i, (i + step) % size) for i in range(size)])]
    convert_element_type x7 -> x0, local copies, waits for them, and re-layouts: 33.2 us -> none  [the longest x2 15.6 us: local(): keyset = projected[:, 1].astype(bf16).reshape(shape)]
    convert_element_type x20 -> x16, other arithmetic: 62.1 us -> 29.8 us  [the longest x12 25.3 us: scatter(): total(held, (k,)).astype(bf16)]
    slice x21 -> x15, local copies, waits for them, and re-layouts: 34.7 us -> 3.45 us  [the longest x6 2.16 us: total(): value = parts[0][index].astype(f32)]
  transfers between devices with their start and end apart: 71 -> 81, of which waited for: 22 -> 25; matrix products, arithmetic and copies ran while one was open for 43% -> 11% of each run, Pallas kernels for 0% -> 32%
where the time goes in v2:
time: 743 us; the launch traced here: 734 us
  waiting for transfers between devices  294 us (40%)
  Pallas kernels  232 us (31%)
  starting transfers between devices  104 us (14%)
  local copies, waits for them, and re-layouts  52.9 us (7%)
  other arithmetic  49.3 us (7%)
    ppermute x81, waiting for transfers between devices, shift(): lax.ppermute(values, axis, [(i, (i + step) % size) for i in range(size)])  294 us
    ppermute x81, starting transfers between devices, shift(): lax.ppermute(values, axis, [(i, (i + step) % size) for i in range(size)])  104 us
    pallas_call x4, Pallas kernels, ffn_grad(): call(functools.partial(ffn_grad_kernel, ncol), (nrow, halves), [pl.BlockS...  35.8 us
    pallas_call x1, Pallas kernels, local(): call(attend_pull_kernel, (seqs, pairs), [pair_spec, pl.BlockSpec((1, LEN,...  35 us
    pallas_call x1, Pallas kernels, local(): call(attend_kernel, (seqs, pairs), [pair_spec, pl.BlockSpec((1, 1, LEN),...  26 us
    convert_element_type x12, other arithmetic, scatter(): total(held, (k,)).astype(bf16)  25.3 us
    unnamed x106, local copies, waits for them, and re-layouts  24.3 us
    pallas_call x1, Pallas kernels, local(): call(functools.partial(up_kernel, ncol, blocks), (seqs,), [tokens_spec, w...  23.5 us
  transfers between devices with their start and end apart: 81, of which 25 were waited for; matrix products, arithmetic and copies ran while one was open for 11% of the time, Pallas kernels for 32%

profile of v2, /device:TPU:0, one launch (start us, length us, event | category | flops | bytes accessed | tf_op | source)
XLA Modules:
  0.0 734.2 jit_solution(10786560616604757726)
XLA Ops:
  62.9 12.8 %collective-permute-done.29 = bf16[256,512]{1,0:T(8,128)(2,1)S(1)} collective-permute-done((bf16[256,512]{1,0:T(8,128)(2,1)}, bf16[256,512]{1,0:T(8,128)(2,1)S(1)}, u32[]{:S(2)}, u32[]{:S(2)}) %collective-permute-start.29) | collective-permute-done | bytes 262176 | tf_op jit(solution)/shard_map/ppermute | solution.py:26
  89.0 22.8 %collective-permute-done.21 = bf16[4,8,8,512]{3,2,1,0:T(8,128)(2,1)S(1)} collective-permute-done((bf16[4,8,8,512]{3,2,1,0:T(8,128)(2,1)S(1)}, bf16[4,8,8,512]{3,2,1,0:T(8,128)(2,1)S(1)}, u32[]{:S(2)}, u32[]{:S(2)}) %collective-permute-start.21) | collective-permute-done | bytes 262176 | tf_op jit(solution)/shard_map/ppermute | solution.py:26
  122.3 21.9 %collective-permute-done.5 = bf16[4,3,8,8,512]{4,3,2,1,0:T(8,128)(2,1)S(1)} collective-permute-done((bf16[4,3,8,8,512]{4,3,2,1,0:T(8,128)(2,1)S(1)}, bf16[4,3,8,8,512]{4,3,2,1,0:T(8,128)(2,1)S(1)}, u32[]{:S(2)}, u32[]{:S(2)}) %collective-permute-start.5) | collective-permute-done | bytes 786464 | tf_op jit(solution)/shard_map/ppermute | solution.py:26
  150.6 12.8 %collective-permute-done.7 = bf16[4,3,8,8,512]{4,3,2,1,0:T(8,128)(2,1)S(1)} collective-permute-done((bf16[4,3,8,8,512]{4,3,2,1,0:T(8,128)(2,1)S(1)}, bf16[4,3,8,8,512]{4,3,2,1,0:T(8,128)(2,1)S(1)}, u32[]{:S(2)}, u32[]{:S(2)}) %collective-permute-start.7) | collective-permute-done | bytes 786464 | tf_op jit(solution)/shard_map/ppermute | solution.py:26
  179.8 9.8 %collective-permute-done.32 = bf16[4,256,512]{2,1,0:T(8,128)(2,1)} collective-permute-done((bf16[4,256,512]{2,1,0:T(8,128)(2,1)S(1)}, bf16[4,256,512]{2,1,0:T(8,128)(2,1)}, u32[]{:S(2)}, u32[]{:S(2)}) %collective-permute-start.32) | collective-permute-done | bytes 1048608 | tf_op jit(solution)/shard_map/ppermute | solution.py:26
  192.5 19.5 %collective-permute-done.33 = bf16[4,256,512]{2,1,0:T(8,128)(2,1)} collective-permute-done((bf16[4,256,512]{2,1,0:T(8,128)(2,1)}, bf16[4,256,512]{2,1,0:T(8,128)(2,1)}, u32[]{:S(2)}, u32[]{:S(2)}) %collective-permute-start.33) | collective-permute-done | bytes 1048608 | tf_op jit(solution)/shard_map/ppermute | solution.py:26
  212.0 14.4 %qkv.1 = (bf16[1280,1024]{1,0:T(8,128)(2,1)S(1)}, bf16[3,1280,1024]{2,1,0:T(8,128)(2,1)}) custom-call(bf16[1280,1024]{1,0:T(8,128)(2,1)S(1)} %pad_maximum_fusion.x_ref, f32[1,1024]{1,0:T(1,128)S(1)} %get-tuple-element.77.gain_ref, f32[1,1024]{1,0:T(1,128)S(1)} %get-tuple-element.76.shift_ref, bf16[3,1024,1024]{2,1,0:T(8,128)(2,1)} %bitcast.536, ...), custom_call_target="tpu_custom_call" | custom-call | flops 8053063680 | bytes 19398656 | tf_op jit(solution)/shard_map/qkv/pallas_call | solution.py:384
  226.5 26.0 %attend.1.o_ref = bf16[1280,1024]{1,0:T(8,128)(2,1)S(1)} custom-call(bf16[3,1280,1024]{2,1,0:T(8,128)(2,1)} %get-tuple-element.33.qkv_ref, s32[4,1,320]{2,1,0:T(1,128)S(1)} %broadcast_in_dim.29.mask_ref), custom_call_target="tpu_custom_call" | custom-call | flops 6710886400 | bytes 10485760 | tf_op jit(solution)/shard_map/attend/pallas_call | solution.py:394
  264.6 23.5 %up.1 = (bf16[1280,4096]{1,0:T(8,128)(2,1)}, bf16[1280,4096]{1,0:T(8,128)(2,1)}) custom-call(bf16[1280,1024]{1,0:T(8,128)(2,1)} %copy-done.16, f32[1,4096]{1,0:T(1,128)S(1)} %reshape.857.bias_ref, bf16[1024,512]{1,0:T(8,128)(2,1)S(1)} %bitcast.524, bf16[1024,512]{1,0:T(8,128)(2,1)} %bitcast.49.refs_1_, bf16[1024,512]{1,0:T(8,128)(2,1)} %bitcast.50.refs_2_, ...), custom_call_target="tpu_custom_call" | custom-call | flops 42949672960 | bytes 29360128 | tf_op jit(solution)/shard_map/up/pallas_call | solution.py:414
  288.1 8.8 %down_grad.3 = bf16[2,2,1024,512]{3,2,1,0:T(8,128)(2,1)} custom-call(bf16[1280,4096]{1,0:T(8,128)(2,1)} %get-tuple-element.35.hid_ref.l_ref, bf16[1280,1024]{1,0:T(8,128)(2,1)S(1)} %pad_maximum_fusion.1.g_ref.r_ref), custom_call_target="tpu_custom_call" | custom-call | flops 5368709120 | bytes 12058624 | tf_op jit(solution)/shard_map/down_grad/pallas_call | solution.py:428
  299.1 17.7 %hidden_pull.1 = (bf16[1280,4096]{1,0:T(8,128)(2,1)}, f32[1,4096]{1,0:T(1,128)S(1)}) custom-call(bf16[1280,1024]{1,0:T(8,128)(2,1)} %copy-done, bf16[1280,4096]{1,0:T(8,128)(2,1)} %get-tuple-element.39.slope_ref, bf16[1024,512]{1,0:T(8,128)(2,1)S(1)} %bitcast.522, bf16[1024,512]{1,0:T(8,128)(2,1)S(1)} %bitcast.527, bf16[1024,512]{1,0:T(8,128)(2,1)} %bitcast.62.refs_2_, ...), custom_call_target="tpu_custom_call" | custom-call | flops 10737418240 | bytes 29360128 | tf_op jit(solution)/shard_map/hidden_pull/pallas_call | solution.py:482
  316.8 9.0 %up_grad.3 = bf16[2,2,1024,512]{3,2,1,0:T(8,128)(2,1)} custom-call(bf16[1280,4096]{1,0:T(8,128)(2,1)} %get-tuple-element.40.du_ref.l_ref, bf16[1280,1024]{1,0:T(8,128)(2,1)S(1)} %copy-done.17), custom_call_target="tpu_custom_call" | custom-call | flops 5368709120 | bytes 12058624 | tf_op jit(solution)/shard_map/up_grad/pallas_call | solution.py:428
  325.8 22.8 %middle_pull.1 = (f32[1280,1024]{1,0:T(8,128)}, bf16[1280,1024]{1,0:T(8,128)(2,1)}, bf16[1280,1024]{1,0:T(8,128)(2,1)}, f32[4,1024]{1,0:T(4,128)S(1)}) custom-call(bf16[1280,4096]{1,0:T(8,128)(2,1)} %get-tuple-element.40.du_ref.l_ref, f32[1280,1024]{1,0:T(8,128)} %get-tuple-element.36.middle_ref, bf16[1280,1024]{1,0:T(8,128)(2,1)} %copy-done, ...), custom_call_target="tpu_custom_call" | custom-call | flops 13421772800 | bytes 37224448 | tf_op jit(solution)/shard_map/middle_pull/pallas_call | solution.py:493
  350.4 35.0 %attend_pull.1.dqkv_ref.l_ref = bf16[3,1280,1024]{2,1,0:T(8,128)(2,1)} custom-call(bf16[3,1280,1024]{2,1,0:T(8,128)(2,1)} %get-tuple-element.33.qkv_ref, s32[4,320,1]{2,1,0:T(8,128)S(1)} %copy.42.mask_ref, bf16[1280,1024]{1,0:T(8,128)(2,1)S(1)} %copy-done.21), custom_call_target="tpu_custom_call" | custom-call | flops 12582912000 | bytes 18350080 | tf_op jit(solution)/shard_map/attend_pull/pallas_call | solution.py:509
  385.4 12.0 %qkv_grad.1 = (bf16[2,2,2,4,3,8,8,512]{7,6,5,4,3,2,1,0:T(8,128)(2,1)}, f32[3,1,1024]{2,1,0:T(1,128)S(1)}) custom-call(bf16[3,1280,1024]{2,1,0:T(8,128)(2,1)} %attend_pull.1.dqkv_ref.l_ref, bf16[1280,1024]{1,0:T(8,128)(2,1)S(1)} %copy-done.20), custom_call_target="tpu_custom_call" | custom-call | flops 8053063680 | bytes 16777216 | tf_op jit(solution)/shard_map/qkv_grad/pallas_call | solution.py:448
  401.8 15.4 %token_pull.1 = (f32[1280,512]{1,0:T(8,128)S(1)}, bf16[1,1280,512]{2,1,0:T(8,128)(2,1)S(1)}, f32[2,1024]{1,0:T(2,128)S(1)}) custom-call(bf16[3,1280,1024]{2,1,0:T(8,128)(2,1)} %attend_pull.1.dqkv_ref.l_ref, bf16[1280,1024]{1,0:T(8,128)(2,1)} %copy-done.2, f32[1280,1024]{1,0:T(8,128)} %get-tuple-element.42.grad_ref, ...), custom_call_target="tpu_custom_call" | custom-call | flops 8053063680 | bytes 24641536 | tf_op jit(solution)/shard_map/token_pull/pallas_call | solution.py:520
  425.3 16.3 %down.1 = (bf16[1280,512]{1,0:T(8,128)(2,1)}, bf16[1,1280,512]{2,1,0:T(8,128)(2,1)}) custom-call(bf16[1280,4096]{1,0:T(8,128)(2,1)} %get-tuple-element.35.hid_ref.l_ref, f32[1280,1024]{1,0:T(8,128)} %get-tuple-element.36.middle_ref, f32[1,1024]{1,0:T(1,128)S(1)} %get-tuple-element.72.bias_ref, bf16[1024,512]{1,0:T(8,128)(2,1)S(1)} %bitcast.523, ...), custom_call_target="tpu_custom_call" | custom-call | flops 10737418240 | bytes 26738688 | tf_op jit(solution)/shard_map/down/pallas_call | solution.py:471
  441.6 9.3 %down_grad.2 = bf16[2,2,1024,512]{3,2,1,0:T(8,128)(2,1)} custom-call(bf16[1280,4096]{1,0:T(8,128)(2,1)} %get-tuple-element.35.hid_ref.l_ref, bf16[1280,1024]{1,0:T(8,128)(2,1)S(1)} %copy-done.1), custom_call_target="tpu_custom_call" | custom-call | flops 5368709120 | bytes 12058624 | tf_op jit(solution)/shard_map/down_grad/pallas_call | solution.py:428
  468.5 11.0 %collective-permute-start.54 = (f32[3456]{0:T(1024)S(1)}, f32[3456]{0:T(1024)S(1)}, u32[]{:S(2)}, u32[]{:S(2)}) collective-permute-start(f32[3456]{0:T(1024)S(1)} %get-tuple-element.89), channel_id=1, source_target_pairs={{0,24},{8,0},{16,8},{24,16},{1,25},{9,1},{17,9},{25,17},{2,26},{10... | collective-permute-start | bytes 41480 | tf_op jit(solution)/shard_map/ppermute | solution.py:26
  509.0 39.9 %collective-permute-done.48 = bf16[1280,512]{1,0:T(8,128)(2,1)} collective-permute-done((bf16[1280,512]{1,0:T(8,128)(2,1)}, bf16[1280,512]{1,0:T(8,128)(2,1)}, u32[]{:S(2)}, u32[]{:S(2)}) %collective-permute-start.48) | collective-permute-done | bytes 1310752 | tf_op jit(solution)/shard_map/ppermute | solution.py:26
  556.0 76.8 %collective-permute-done.64 = bf16[2,4,1,8,8,512]{5,4,3,2,1,0:T(8,128)(2,1)S(1)} collective-permute-done((bf16[2,4,1,8,8,512]{5,4,3,2,1,0:T(8,128)(2,1)S(1)}, bf16[2,4,1,8,8,512]{5,4,3,2,1,0:T(8,128)(2,1)S(1)}, u32[]{:S(2)}, u32[]{:S(2)}) %collective-permute-start.64) | collective-permute-done | bytes 524320 | tf_op jit(solution)/shard_map/ppermute | solution.py:26
  649.9 10.1 %collective-permute-done.59 = bf16[4,3,8,8,512]{4,3,2,1,0:T(8,128)(2,1)S(1)} collective-permute-done((bf16[4,3,8,8,512]{4,3,2,1,0:T(8,128)(2,1)S(1)}, bf16[4,3,8,8,512]{4,3,2,1,0:T(8,128)(2,1)S(1)}, u32[]{:S(2)}, u32[]{:S(2)}) %collective-permute-start.59) | collective-permute-done | bytes 786464 | tf_op jit(solution)/shard_map/ppermute | solution.py:26
  691.0 11.9 %collective-permute-done.71 = bf16[4,256,512]{2,1,0:T(8,128)(2,1)S(1)} collective-permute-done((bf16[4,256,512]{2,1,0:T(8,128)(2,1)S(1)}, bf16[4,256,512]{2,1,0:T(8,128)(2,1)S(1)}, u32[]{:S(2)}, u32[]{:S(2)}) %collective-permute-start.71) | collective-permute-done | bytes 1048608 | tf_op jit(solution)/shard_map/ppermute | solution.py:26
  715.7 16.0 %collective-permute-done.73 = bf16[256,512]{1,0:T(8,128)(2,1)S(1)} collective-permute-done((bf16[256,512]{1,0:T(8,128)(2,1)S(1)}, bf16[256,512]{1,0:T(8,128)(2,1)S(1)}, u32[]{:S(2)}, u32[]{:S(2)}) %collective-permute-start.73) | collective-permute-done | bytes 262176 | tf_op jit(solution)/shard_map/ppermute | solution.py:26
  (370 shorter events, 256.7 us)
Async XLA Ops:
  1.8 41.7 %collective-permute-start.2 = (bf16[3,8,8,512]{3,2,1,0:T(8,128)(2,1)S(1)}, bf16[3,8,8,512]{3,2,1,0:T(8,128)(2,1)S(1)}, u32[]{:S(2)}, u32[]{:S(2)}) collective-permute-start(bf16[3,8,8,512]{3,2,1,0:T(8,128)(2,1)S(1)} %convert_element_type.834), channel_id=1, source_target_pairs={{0,8},{8,16},{16,24},{24,0},{1,9},{9,17},{17,25},{25,1},{2,10},{10... | collective-permute-start | bytes 589832 | tf_op jit(solution)/shard_map/ppermute | solution.py:26
  4.9 42.2 %collective-permute-start.3 = (bf16[3,8,8,512]{3,2,1,0:T(8,128)(2,1)S(1)}, bf16[3,8,8,512]{3,2,1,0:T(8,128)(2,1)S(1)}, u32[]{:S(2)}, u32[]{:S(2)}) collective-permute-start(bf16[3,8,8,512]{3,2,1,0:T(8,128)(2,1)S(1)} %convert_element_type.834), channel_id=1, source_target_pairs={{0,16},{8,24},{16,0},{24,8},{1,17},{9,25},{17,1},{25,9},{2,18},{10... | collective-permute-start | bytes 589832 | tf_op jit(solution)/shard_map/ppermute | solution.py:26
  75.8 72.5 %collective-permute-start = (bf16[1280,512]{1,0:T(8,128)(2,1)}, bf16[1280,512]{1,0:T(8,128)(2,1)S(1)}, u32[]{:S(2)}, u32[]{:S(2)}) collective-permute-start(bf16[1280,512]{1,0:T(8,128)(2,1)} %get-tuple-element.69), channel_id=1, source_target_pairs={{0,1},{1,0},{2,3},{3,2},{4,5},{5,4},{6,7},{7,6},{8,9},{9,8},{10,11... | collective-permute-start | bytes 3932168 | tf_op jit(solution)/shard_map/ppermute | solution.py:26
  76.3 35.5 %collective-permute-start.21 = (bf16[4,8,8,512]{3,2,1,0:T(8,128)(2,1)S(1)}, bf16[4,8,8,512]{3,2,1,0:T(8,128)(2,1)S(1)}, u32[]{:S(2)}, u32[]{:S(2)}) collective-permute-start(bf16[4,8,8,512]{3,2,1,0:T(8,128)(2,1)S(1)} %pad_maximum_fusion.5), channel_id=1, source_target_pairs={{0,1},{1,0},{2,3},{3,2},{4,5},{5,4},{6,7},{7,6},{8,9},{9,8},{10,11... | collective-permute-start | bytes 786440 | tf_op jit(solution)/shard_map/ppermute | solution.py:26
  78.9 69.3 %collective-permute-start.49 = (bf16[1280,512]{1,0:T(8,128)(2,1)S(1)}, bf16[1280,512]{1,0:T(8,128)(2,1)S(1)}, u32[]{:S(2)}, u32[]{:S(2)}) collective-permute-start(bf16[1280,512]{1,0:T(8,128)(2,1)S(1)} %copy-done.34), channel_id=1, source_target_pairs={{0,1},{1,0},{2,3},{3,2},{4,5},{5,4},{6,7},{7,6},{8,9},{9,8},{10,11... | collective-permute-start | bytes 3932168 | tf_op jit(solution)/shard_map/ppermute | solution.py:26
  121.9 44.0 %collective-permute-start.8 = (bf16[4,3,8,8,512]{4,3,2,1,0:T(8,128)(2,1)S(1)}, bf16[4,3,8,8,512]{4,3,2,1,0:T(8,128)(2,1)S(1)}, u32[]{:S(2)}, u32[]{:S(2)}) collective-permute-start(bf16[4,3,8,8,512]{4,3,2,1,0:T(8,128)(2,1)S(1)} %pad_maximum_fusion.4), channel_id=1, source_target_pairs={{0,4},{4,0},{1,5},{5,1},{2,6},{6,2},{3,7},{7,3},{8,12},{12,8},{9,1... | collective-permute-start | bytes 2359304 | tf_op jit(solution)/shard_map/ppermute | solution.py:26
  167.4 44.6 %collective-permute-start.33 = (bf16[4,256,512]{2,1,0:T(8,128)(2,1)}, bf16[4,256,512]{2,1,0:T(8,128)(2,1)}, u32[]{:S(2)}, u32[]{:S(2)}) collective-permute-start(bf16[4,256,512]{2,1,0:T(8,128)(2,1)} %collective-permute-done.31), channel_id=1, source_target_pairs={{0,2},{2,0},{1,3},{3,1},{4,6},{6,4},{5,7},{7,5},{8,10},{10,8},{9,1... | collective-permute-start | bytes 3145736 | tf_op jit(solution)/shard_map/ppermute | solution.py:26
  170.9 92.2 %collective-permute-start.42 = (bf16[4,256,512]{2,1,0:T(8,128)(2,1)S(1)}, bf16[4,256,512]{2,1,0:T(8,128)(2,1)}, u32[]{:S(2)}, u32[]{:S(2)}) collective-permute-start(bf16[4,256,512]{2,1,0:T(8,128)(2,1)S(1)} %pad_maximum_fusion.3), channel_id=1, source_target_pairs={{0,2},{2,0},{1,3},{3,1},{4,6},{6,4},{5,7},{7,5},{8,10},{10,8},{9,1... | collective-permute-start | bytes 3145736 | tf_op jit(solution)/shard_map/ppermute | solution.py:26
  189.6 74.0 %collective-permute-start.35 = (bf16[4,256,512]{2,1,0:T(8,128)(2,1)}, bf16[4,256,512]{2,1,0:T(8,128)(2,1)S(1)}, u32[]{:S(2)}, u32[]{:S(2)}) collective-permute-start(bf16[4,256,512]{2,1,0:T(8,128)(2,1)} %collective-permute-done.31), channel_id=1, source_target_pairs={{0,4},{4,0},{1,5},{5,1},{2,6},{6,2},{3,7},{7,3},{8,12},{12,8},{9,1... | collective-permute-start | bytes 3145736 | tf_op jit(solution)/shard_map/ppermute | solution.py:26
  190.5 73.1 %collective-permute-start.36 = (bf16[4,256,512]{2,1,0:T(8,128)(2,1)}, bf16[4,256,512]{2,1,0:T(8,128)(2,1)}, u32[]{:S(2)}, u32[]{:S(2)}) collective-permute-start(bf16[4,256,512]{2,1,0:T(8,128)(2,1)} %collective-permute-done.32), channel_id=1, source_target_pairs={{0,4},{4,0},{1,5},{5,1},{2,6},{6,2},{3,7},{7,3},{8,12},{12,8},{9,1... | collective-permute-start | bytes 3145736 | tf_op jit(solution)/shard_map/ppermute | solution.py:26
  191.4 72.7 %collective-permute-start.43 = (bf16[4,256,512]{2,1,0:T(8,128)(2,1)S(1)}, bf16[4,256,512]{2,1,0:T(8,128)(2,1)}, u32[]{:S(2)}, u32[]{:S(2)}) collective-permute-start(bf16[4,256,512]{2,1,0:T(8,128)(2,1)S(1)} %collective-permute-done.41), channel_id=1, source_target_pairs={{0,2},{2,0},{1,3},{3,1},{4,6},{6,4},{5,7},{7,5},{8,10},{10,8},{9,1... | collective-permute-start | bytes 3145736 | tf_op jit(solution)/shard_map/ppermute | solution.py:26
  212.0 52.6 %collective-permute-start.37 = (bf16[4,256,512]{2,1,0:T(8,128)(2,1)}, bf16[4,256,512]{2,1,0:T(8,128)(2,1)}, u32[]{:S(2)}, u32[]{:S(2)}) collective-permute-start(bf16[4,256,512]{2,1,0:T(8,128)(2,1)} %collective-permute-done.33), channel_id=1, source_target_pairs={{0,4},{4,0},{1,5},{5,1},{2,6},{6,2},{3,7},{7,3},{8,12},{12,8},{9,1... | collective-permute-start | bytes 3145736 | tf_op jit(solution)/shard_map/ppermute | solution.py:26
  296.9 198.5 %collective-permute-start.75 = (bf16[2,2,4,256,512]{4,3,2,1,0:T(8,128)(2,1)}, bf16[2,2,4,256,512]{4,3,2,1,0:T(8,128)(2,1)}, u32[]{:S(2)}, u32[]{:S(2)}) collective-permute-start(bf16[2,2,4,256,512]{4,3,2,1,0:T(8,128)(2,1)} %bitcast.571), channel_id=1, source_target_pairs={{0,4},{4,0},{1,5},{5,1},{2,6},{6,2},{3,7},{7,3},{8,12},{12,8},{9,1... | collective-permute-start | bytes 12582920 | tf_op jit(solution)/shard_map/ppermute | solution.py:26
  325.8 174.6 %collective-permute-start.69 = (bf16[2,2,4,256,512]{4,3,2,1,0:T(8,128)(2,1)}, bf16[2,2,4,256,512]{4,3,2,1,0:T(8,128)(2,1)}, u32[]{:S(2)}, u32[]{:S(2)}) collective-permute-start(bf16[2,2,4,256,512]{4,3,2,1,0:T(8,128)(2,1)} %bitcast.572), channel_id=1, source_target_pairs={{0,4},{4,0},{1,5},{5,1},{2,6},{6,2},{3,7},{7,3},{8,12},{12,8},{9,1... | collective-permute-start | bytes 12582920 | tf_op jit(solution)/shard_map/ppermute | solution.py:26
  401.4 88.7 %collective-permute-start.57 = (bf16[2,2,4,3,8,8,512]{6,5,4,3,2,1,0:T(8,128)(2,1)}, bf16[2,2,4,3,8,8,512]{6,5,4,3,2,1,0:T(8,128)(2,1)}, u32[]{:S(2)}, u32[]{:S(2)}) collective-permute-start(bf16[2,2,4,3,8,8,512]{6,5,4,3,2,1,0:T(8,128)(2,1)} %slice_bitcast_fusion), channel_id=1, source_target_pairs={{0,4},{4,0},{1,5},{5,1},{2,6},{6,2},{3,7},{7,3},{8,12},{12,8},{9,1... | collective-permute-start | bytes 9437192 | tf_op jit(solution)/shard_map/ppermute | solution.py:26
  420.0 39.7 %collective-permute-start.51 = (f32[9216]{0:T(1024)S(1)}, f32[9216]{0:T(1024)S(1)}, u32[]{:S(2)}, u32[]{:S(2)}) collective-permute-start(f32[9216]{0:T(1024)S(1)} %pad_maximum_fusion.6), channel_id=1, source_target_pairs={{0,1},{1,0},{2,3},{3,2},{4,5},{5,4},{6,7},{7,6},{8,9},{9,8},{10,11... | collective-permute-start | bytes 110600 | tf_op jit(solution)/shard_map/ppermute | solution.py:26
  489.5 63.3 %collective-permute-start.50 = (bf16[1280,512]{1,0:T(8,128)(2,1)S(1)}, bf16[1280,512]{1,0:T(8,128)(2,1)}, u32[]{:S(2)}, u32[]{:S(2)}) collective-permute-start(bf16[1280,512]{1,0:T(8,128)(2,1)S(1)} %bitcast.526), channel_id=1, source_target_pairs={{0,1},{1,0},{2,3},{3,2},{4,5},{5,4},{6,7},{7,6},{8,9},{9,8},{10,11... | collective-permute-start | bytes 3932168 | tf_op jit(solution)/shard_map/ppermute | solution.py:26
  490.1 58.8 %collective-permute-start.48 = (bf16[1280,512]{1,0:T(8,128)(2,1)}, bf16[1280,512]{1,0:T(8,128)(2,1)}, u32[]{:S(2)}, u32[]{:S(2)}) collective-permute-start(bf16[1280,512]{1,0:T(8,128)(2,1)} %bitcast.68), channel_id=1, source_target_pairs={{0,1},{1,0},{2,3},{3,2},{4,5},{5,4},{6,7},{7,6},{8,9},{9,8},{10,11... | collective-permute-start | bytes 3932168 | tf_op jit(solution)/shard_map/ppermute | solution.py:26
  495.3 139.1 %collective-permute-start.58 = (bf16[2,4,3,8,8,512]{5,4,3,2,1,0:T(8,128)(2,1)}, bf16[2,4,3,8,8,512]{5,4,3,2,1,0:T(8,128)(2,1)}, u32[]{:S(2)}, u32[]{:S(2)}) collective-permute-start(bf16[2,4,3,8,8,512]{5,4,3,2,1,0:T(8,128)(2,1)} %fusion.2), channel_id=1, source_target_pairs={{0,2},{2,0},{1,3},{3,1},{4,6},{6,4},{5,7},{7,5},{8,10},{10,8},{9,1... | collective-permute-start | bytes 4718600 | tf_op jit(solution)/shard_map/ppermute | solution.py:26
  500.4 137.6 %collective-permute-start.76 = (bf16[2,4,256,512]{3,2,1,0:T(8,128)(2,1)}, bf16[2,4,256,512]{3,2,1,0:T(8,128)(2,1)}, u32[]{:S(2)}, u32[]{:S(2)}) collective-permute-start(bf16[2,4,256,512]{3,2,1,0:T(8,128)(2,1)} %fusion), channel_id=1, source_target_pairs={{0,2},{2,0},{1,3},{3,1},{4,6},{6,4},{5,7},{7,5},{8,10},{10,8},{9,1... | collective-permute-start | bytes 6291464 | tf_op jit(solution)/shard_map/ppermute | solution.py:26
  504.5 136.1 %collective-permute-start.70 = (bf16[2,4,256,512]{3,2,1,0:T(8,128)(2,1)}, bf16[2,4,256,512]{3,2,1,0:T(8,128)(2,1)}, u32[]{:S(2)}, u32[]{:S(2)}) collective-permute-start(bf16[2,4,256,512]{3,2,1,0:T(8,128)(2,1)} %fusion.1), channel_id=1, source_target_pairs={{0,2},{2,0},{1,3},{3,1},{4,6},{6,4},{5,7},{7,5},{8,10},{10,8},{9,1... | collective-permute-start | bytes 6291464 | tf_op jit(solution)/shard_map/ppermute | solution.py:26
  548.9 83.9 %collective-permute-start.64 = (bf16[2,4,1,8,8,512]{5,4,3,2,1,0:T(8,128)(2,1)S(1)}, bf16[2,4,1,8,8,512]{5,4,3,2,1,0:T(8,128)(2,1)S(1)}, u32[]{:S(2)}, u32[]{:S(2)}) collective-permute-start(bf16[2,4,1,8,8,512]{5,4,3,2,1,0:T(8,128)(2,1)S(1)} %fusion.7), channel_id=1, source_target_pairs={{0,2},{2,0},{1,3},{3,1},{4,6},{6,4},{5,7},{7,5},{8,10},{10,8},{9,1... | collective-permute-start | bytes 1572872 | tf_op jit(solution)/shard_map/ppermute | solution.py:26
  640.0 44.6 %collective-permute-start.77 = (bf16[4,256,512]{2,1,0:T(8,128)(2,1)S(1)}, bf16[4,256,512]{2,1,0:T(8,128)(2,1)S(1)}, u32[]{:S(2)}, u32[]{:S(2)}) collective-permute-start(bf16[4,256,512]{2,1,0:T(8,128)(2,1)S(1)} %fusion.3), channel_id=1, source_target_pairs={{0,1},{1,0},{2,3},{3,2},{4,5},{5,4},{6,7},{7,6},{8,9},{9,8},{10,11... | collective-permute-start | bytes 3145736 | tf_op jit(solution)/shard_map/ppermute | solution.py:26
  642.5 60.4 %collective-permute-start.71 = (bf16[4,256,512]{2,1,0:T(8,128)(2,1)S(1)}, bf16[4,256,512]{2,1,0:T(8,128)(2,1)S(1)}, u32[]{:S(2)}, u32[]{:S(2)}) collective-permute-start(bf16[4,256,512]{2,1,0:T(8,128)(2,1)S(1)} %fusion.4), channel_id=1, source_target_pairs={{0,1},{1,0},{2,3},{3,2},{4,5},{5,4},{6,7},{7,6},{8,9},{9,8},{10,11... | collective-permute-start | bytes 3145736 | tf_op jit(solution)/shard_map/ppermute | solution.py:26
  (106 other events, 2084.3 us)

commit v3 on v2

v3 whole, which is shorter than its diff:
```python
import functools
import itertools

import jax
import jax.numpy as jnp
from jax import lax
from jax.experimental import pallas as pl
from jax.experimental.pallas import tpu as pltpu
from jax.sharding import Mesh, PartitionSpec as P

HD = 64
PAIR = 2 * HD
BUF = 64
LEN = 320
masked_fill = -1000000000.0
norm_epsilon = 1e-06
attn_scale = 0.125
exp2_scale = attn_scale * 1.4426950408889634
root_half = 0.7071067811865476
density = 0.3989422804014327
bf16 = jnp.bfloat16
f32 = jnp.float32
MIB = 1 << 20


def contract_last(left, right):
    return lax.dot_general(left, right, (((1,), (1,)), ((), ())), preferred_element_type=f32)


def contract_first(left, right):
    return lax.dot_general(left, right, (((0,), (0,)), ((), ())), preferred_element_type=f32)


def matmul(left, right):
    return lax.dot_general(left, right, (((1,), (0,)), ((), ())), preferred_element_type=f32)


def whole(shape):
    return pl.BlockSpec(shape, lambda *_: (0,) * len(shape), pipeline_mode=pl.Buffered(1))


def summed(shape):
    return pl.BlockSpec(shape, lambda *_: (0,) * len(shape))


def call(kernel, grid, in_specs, out_specs, out_shape, flops, moved, name, vmem=48, scratch=()):
    return pl.pallas_call(
        kernel,
        grid=grid,
        in_specs=in_specs,
        out_specs=out_specs,
        out_shape=out_shape,
        scratch_shapes=scratch,
        name=name,
        compiler_params=pltpu.CompilerParams(vmem_limit_bytes=vmem * MIB),
        cost_estimate=pl.CostEstimate(flops=flops, bytes_accessed=moved, transcendentals=0),
    )


def unit_norm(values):
    center = jnp.mean(values, axis=1, keepdims=True)
    centered = values - center
    spread = jnp.mean(centered * centered, axis=1, keepdims=True)
    inverse = lax.rsqrt(spread + norm_epsilon)
    return centered * inverse, inverse


def norm_pull(grad, gain, unit, inverse):
    scaled = grad * gain
    total = jnp.mean(scaled, axis=1, keepdims=True)
    paired = jnp.mean(scaled * unit, axis=1, keepdims=True)
    return inverse * (scaled - total - unit * paired)


def head_weight(layout, refs):
    if layout is None:
        return refs[1:], lambda: None, lambda i: refs[0][i]
    places, kinds = layout
    held, sem = refs[-2:]
    operands = 1 + max(place[0] for place in places)

    def copies(kind):
        for operand, index, head, row, lane in places:
            source = refs[operand].at[index + (kind,)]
            part, piece, width = source.shape
            target = held.at[kind, pl.ds(head, part), pl.ds(row, piece), pl.ds(lane, width)]
            yield pltpu.make_async_copy(source, target, sem.at[kind])

    def fetch():
        @pl.when(pl.program_id(0) == 0)
        def _():
            for kind in range(kinds):
                for copy in copies(kind):
                    copy.start()

    def read(kind):
        @pl.when(pl.program_id(0) == 0)
        def _():
            for copy in copies(kind):
                copy.wait()

        return held[kind].reshape(held.shape[1] * held.shape[2], held.shape[3])

    return refs[operands:-2], fetch, read


def qkv_kernel(layout, x_ref, gain_ref, shift_ref, bias_ref, *refs):
    (a_ref, out_ref), fetch, read = head_weight(layout, refs)
    fetch()
    unit, _ = unit_norm(x_ref[...].astype(f32))
    a = (unit * gain_ref[...] + shift_ref[...]).astype(bf16)
    a_ref[...] = a
    for i in range(3):
        value = contract_last(a, read(i))
        if i != 1:
            value = value + bias_ref[i // 2 : i // 2 + 1]
        out_ref[i] = value.astype(bf16)


def split_heads(pair):
    first = lax.broadcasted_iota(jnp.int32, pair.shape, 1) < HD
    zero = jnp.zeros_like(pair)
    return jnp.concatenate([jnp.where(first, pair, zero), jnp.where(first, zero, pair)], axis=0)


def join_heads(both):
    rows = both.shape[0] // 2
    first = lax.broadcasted_iota(jnp.int32, (rows, both.shape[1]), 1) < HD
    return jnp.where(first, both[:rows], both[rows:])


def attend_kernel(qkv_ref, mask_ref, out_ref):
    seen = mask_ref[0] > 0
    scores = contract_last(split_heads(qkv_ref[0]), qkv_ref[1])
    scores = jnp.where(seen, scores, masked_fill / attn_scale)
    top = jnp.max(scores, axis=1, keepdims=True)
    grown = jnp.exp2((scores - top) * exp2_scale)
    total = jnp.sum(grown, axis=1, keepdims=True)
    mixed = matmul(grown.astype(bf16), qkv_ref[2]) / total
    out_ref[...] = join_heads(mixed).astype(bf16)


def attend_pull_kernel(qkv_ref, mask_ref, do_ref, out_ref):
    seen = mask_ref[0] > 0
    both = split_heads(qkv_ref[0])
    keys = qkv_ref[1]
    vals = qkv_ref[2]
    pulled = split_heads(do_ref[...])
    scores = contract_last(keys, both)
    scores = jnp.where(seen, scores, masked_fill / attn_scale)
    top = jnp.max(scores, axis=0, keepdims=True)
    grown = jnp.exp2((scores - top) * exp2_scale)
    probs = grown * (1.0 / jnp.sum(grown, axis=0, keepdims=True))
    prob_grad = contract_last(vals, pulled)
    out_ref[2] = matmul(probs.astype(bf16), pulled).astype(bf16)
    inner = jnp.sum(prob_grad * probs, axis=0, keepdims=True)
    score_grad = (probs * (prob_grad - inner)).astype(bf16)
    out_ref[1] = (matmul(score_grad, both) * attn_scale).astype(bf16)
    query_grad = contract_first(score_grad, keys) * attn_scale
    out_ref[0] = join_heads(query_grad).astype(bf16)


def out_kernel(layout, x_ref, o_ref, bias_ref, gain_ref, shift_ref, *refs):
    (middle_ref, a_ref), fetch, read = head_weight(layout, refs)
    fetch()
    middle = x_ref[...].astype(f32) + (matmul(o_ref[...], read(0)) + bias_ref[...])
    middle_ref[...] = middle
    unit, _ = unit_norm(middle)
    a_ref[...] = (unit * gain_ref[...] + shift_ref[...]).astype(bf16)


def pieces_of(dims, refs):
    ncol, nrow, ncore, places = dims
    w_refs, rest = refs[: len(places)], refs[len(places) :]

    def piece(block, col):
        core, within = divmod(block, 2 * nrow)
        row, half = divmod(within, 2)
        lead, second = (row, col) if half else (col, row)
        for ref, (in_core, in_half, first) in zip(w_refs, places):
            if (in_core, in_half) == (core, half) and first <= lead < first + ref.shape[0]:
                return ref[lead - first, second]

    return piece, 2 * ncore * nrow, w_refs[0].shape[2], w_refs[0].shape[3], rest


def up_kernel(dims, a_ref, bias_ref, *refs):
    piece, blocks, step, width, (hid_ref, slope_ref) = pieces_of(dims, refs)
    for b in range(blocks):
        rows = slice(b * step, (b + 1) * step)
        value = bias_ref[:, rows]
        for c in range(dims[0]):
            value = value + contract_last(a_ref[:, c * width : (c + 1) * width], piece(b, c))
        cdf = 0.5 + 0.5 * lax.erf(value * root_half)
        pdf = jnp.exp(-0.5 * value * value) * density
        hid_ref[:, rows] = (value * cdf).astype(bf16)
        slope_ref[:, rows] = (cdf + value * pdf).astype(bf16)


def down_kernel(dims, hid_ref, middle_ref, bias_ref, *refs):
    piece, blocks, step, width, (own_ref, other_ref) = pieces_of(dims, refs)
    for c in range(dims[0]):
        lanes = slice(c * width, (c + 1) * width)
        value = middle_ref[:, lanes] + bias_ref[:, lanes]
        for b in range(blocks):
            value = value + matmul(hid_ref[:, b * step : (b + 1) * step], piece(b, c))
        if c == 0:
            own_ref[...] = value.astype(bf16)
        else:
            other_ref[c - 1] = value.astype(bf16)


def hidden_pull_kernel(dims, g_ref, slope_ref, *refs):
    piece, blocks, step, width, (du_ref, sum_ref) = pieces_of(dims, refs)

    @pl.when(pl.program_id(0) == 0)
    def _():
        sum_ref[...] = jnp.zeros_like(sum_ref)

    for b in range(blocks):
        rows = slice(b * step, (b + 1) * step)
        value = contract_last(g_ref[:, :width], piece(b, 0))
        for c in range(1, dims[0]):
            value = value + contract_last(g_ref[:, c * width : (c + 1) * width], piece(b, c))
        low = (value * slope_ref[:, rows].astype(f32)).astype(bf16)
        du_ref[:, rows] = low
        sum_ref[:, rows] += jnp.sum(low.astype(f32), axis=0, keepdims=True)


def middle_pull_kernel(dims, layout, du_ref, middle_ref, g_ref, gain_ref, *refs):
    piece, blocks, step, width, rest = pieces_of(dims, refs)
    (grad_ref, low_ref, do_ref, sum_ref), fetch, read = head_weight(layout, rest)
    fetch()

    @pl.when(pl.program_id(0) == 0)
    def _():
        sum_ref[...] = jnp.zeros_like(sum_ref)

    parts = []
    for c in range(dims[0]):
        value = matmul(du_ref[:, :step], piece(0, c))
        for b in range(1, blocks):
            value = value + matmul(du_ref[:, b * step : (b + 1) * step], piece(b, c))
        parts.append(value)
    grad = jnp.concatenate(parts, axis=1)
    unit, inverse = unit_norm(middle_ref[...])
    out_grad = g_ref[...].astype(f32)
    total = out_grad + norm_pull(grad, gain_ref[...], unit, inverse)
    grad_ref[...] = total
    low = total.astype(bf16)
    low_ref[...] = low
    do_ref[...] = contract_last(low, read(0)).astype(bf16)
    sum_ref[0:1] += jnp.sum(low.astype(f32), axis=0, keepdims=True)
    sum_ref[1:2] += jnp.sum(grad * unit, axis=0, keepdims=True)
    sum_ref[2:3] += jnp.sum(grad, axis=0, keepdims=True)
    sum_ref[3:4] += jnp.sum(out_grad, axis=0, keepdims=True)


def token_pull_kernel(ncol, layout, near_ref, far_ref, x_ref, grad_ref, gain_ref, *refs):
    (own_ref, other_ref, sum_ref), fetch, read = head_weight(layout, refs)
    fetch()

    @pl.when(pl.program_id(0) == 0)
    def _():
        sum_ref[...] = jnp.zeros_like(sum_ref)

    grad = None
    for i in range(3):
        weight = read(i)
        middle = weight.shape[0] // 2
        value = matmul(near_ref[i], weight[:middle]) + matmul(far_ref[i], weight[middle:])
        grad = value if grad is None else grad + value
    unit, inverse = unit_norm(x_ref[...].astype(f32))
    total = grad_ref[...] + norm_pull(grad, gain_ref[...], unit, inverse)
    width = total.shape[1] // ncol
    own_ref[...] = total[:, :width]
    for c in range(1, ncol):
        other_ref[c - 1] = total[:, c * width : (c + 1) * width].astype(bf16)
    sum_ref[0:1] += jnp.sum(grad * unit, axis=0, keepdims=True)
    sum_ref[1:2] += jnp.sum(grad, axis=0, keepdims=True)


def ffn_sent_kernel(ncol, l_ref, r_ref, out_ref):
    width = r_ref.shape[1] // ncol
    left = l_ref[...]
    for c in range(ncol):
        out_ref[0, 0, c] = contract_first(left, r_ref[:, c * width : (c + 1) * width]).astype(bf16)


def ffn_kept_kernel(ncol, nrow, l_ref, r_ref, got_ref, *out_refs):
    by_col, by_row = out_refs[:ncol], out_refs[ncol:]
    width = r_ref.shape[1] // ncol
    left = l_ref[...]
    half, row = pl.program_id(0), pl.program_id(1)
    values = []
    for c in range(ncol):
        value = contract_first(left, r_ref[:, c * width : (c + 1) * width])
        values.append((value + got_ref[0, 0, c].astype(f32)).astype(bf16))

    @pl.when(half == 0)
    def _():
        for c in range(ncol):
            by_col[c][0] = values[c]

    for r in range(nrow):

        @pl.when((half == 1) & (row == r))
        def _(r=r):
            for c in range(ncol):
                by_row[r][c] = values[c]


def head_grad_kernel(sizes, l_ref, r_ref, *refs):
    ncore, ncol, nz, part, piece = sizes
    width = r_ref.shape[1] // ncol
    left = l_ref[0]
    for c in range(ncol):
        value = contract_first(left, r_ref[:, c * width : (c + 1) * width]).astype(bf16)
        value = value.reshape(part, ncore, nz, piece, width)
        for core in range(ncore):
            for z in range(nz):
                refs[core][0, c, z, 0] = value[:, core, z]
    for sum_ref in refs[ncore:]:
        sum_ref[0] = jnp.sum(left.astype(f32), axis=0, keepdims=True)


def make_local(nz, ncore, nrow, ncol):
    blocks = ncore * nrow
    sizes = {"z": nz, "core": ncore, "row": nrow, "col": ncol}

    def bits(axis):
        return [1 << k for k in range(sizes[axis].bit_length() - 1)]

    def exchange(values, axis, bit):
        return lax.ppermute(values, axis, [(i, i ^ bit) for i in range(sizes[axis])])

    class Slots:
        def __init__(self):
            self.before, self.now = [], []

        def advance(self):
            self.before, self.now = self.now, []

        def note(self, *values):
            self.now.extend(values)

        def gate(self, *values):
            if not self.before:
                return values
            return lax.optimization_barrier((*values, *self.before))[: len(values)]

        def move(self, values, axis, bit):
            got = exchange(values, axis, bit)
            self.now.append(got)
            return got

        def send(self, values, axis, bit):
            return self.move(self.gate(values)[0], axis, bit)

        def widen(self, parts, axis, lead=True):
            parts = list(self.gate(*parts))
            if lead:
                parts = [joined(parts)[None]]
            for bit in bits(axis):
                values = joined(parts)
                parts = [values, self.move(values, axis, bit)]
            return parts

        def fold(self, held, axis, dim):
            arrays = self.gate(*[view[0] for view in held])
            held = [(array, view[1]) for array, view in zip(arrays, held)]
            for bit in [bit for bit in reversed(bits(axis)) if bit < held[0][1][dim][1]]:
                got = self.move(total([half_of(view, dim, 1) for view in held]).astype(bf16), axis, bit)
                held = [half_of(view, dim, 0) for view in held] + [view_of(got)]
            return held

    def joined(parts):
        return parts[0] if len(parts) == 1 else jnp.concatenate(parts)

    def view_of(array):
        return (array, tuple((0, n) for n in array.shape[:3]))

    def half_of(view, dim, which):
        array, spans = view
        start, size = spans[dim]
        size //= 2
        return (array, spans[:dim] + ((start + which * size, size),) + spans[dim + 1 :])

    def total(held):
        value = None
        for array, spans in held:
            part = array[tuple(slice(start, start + size) for start, size in spans)].astype(f32)
            value = part if value is None else value + part
        return value

    class Gather:
        def __init__(self, name, slots, shard):
            self.name, self.slots, self.low = name, slots, [shard[None]]

        def z_all(self):
            (values,) = self.slots.gate(*self.low)
            near = nz // 2
            parts = [values] + [self.slots.move(values, "z", k) for k in range(1, nz)]
            self.low, self.high = parts[:near], parts[near:]

        def z_low(self):
            parts = list(self.slots.gate(*self.low))
            for bit in bits("z")[:-1]:
                values = joined(parts)
                parts = [values, self.slots.move(values, "z", bit)]
            self.low = parts

        def z_high(self):
            values = joined(list(self.slots.gate(*self.low)))
            self.low = [values]
            self.high = [self.slots.move(values, "z", bits("z")[-1])]

        def z_high_first(self):
            values = joined(list(self.slots.gate(*self.low)))
            half = values.shape[0] // 2
            self.low = [values[:half], values[half:]]
            self.high = [self.slots.move(self.low[0], "z", bits("z")[-1])]

        def z_high_second(self):
            (values,) = self.slots.gate(self.low[1])
            self.high.append(self.slots.move(values, "z", bits("z")[-1]))

        def x_low(self):
            self.low_row = self.slots.widen(self.low, "row")

        def y_high(self):
            self.high_col = self.slots.widen(self.high, "col")

        def y_low(self):
            self.low_all = self.slots.widen(self.low_row, "col")

        def x_high(self):
            self.high_all = self.slots.widen(self.high_col, "row")

        def y(self):
            self.all_col = self.slots.widen(self.low + self.high, "col")

        def x(self):
            self.all_row = self.slots.widen(self.all_col, "row")

        def core(self):
            if hasattr(self, "all_row"):
                lists = [(2, self.all_row)]
            else:
                lists = [(0, self.low_all), (1, self.high_all)]
            self.places, self.pieces = [], []
            for half, parts in lists:
                parts = self.slots.gate(*parts)
                for k in range(ncore):
                    first = 0
                    for values in parts:
                        self.places.append((k, half, first))
                        self.pieces.append(self.slots.move(values, "core", k) if k else values)
                        first += values.shape[0]

    class Scatter:
        def __init__(self, name, slots):
            self.name, self.slots, self.low, self.high = name, slots, [], []

        def halve(self, arrays):
            views = [view_of(array) for array in arrays]
            self.low = self.low + [half_of(view, 2, 0) for view in views]
            self.high = self.high + [half_of(view, 2, 1) for view in views]

        def first_fold(self, parts, axis, dim):
            parts = list(self.slots.gate(*parts))
            held = []
            for bit in reversed(bits(axis)):
                value = parts[bit] if bit == 1 else jnp.concatenate(parts[bit : 2 * bit], axis=dim)
                if held:
                    value = (value.astype(f32) + total([half_of(view, dim, 1) for view in held])).astype(bf16)
                got = self.slots.move(value, axis, bit)
                held = [half_of(view, dim, 0) for view in held] + [view_of(got)]
            return [view_of(parts[0])] + held

        def x_high_first(self, by_row):
            self.high = self.first_fold(by_row, "row", 0)

        def y_low_first(self, by_col):
            self.low = self.first_fold(by_col, "col", 1)

        def x_high(self):
            self.high = self.slots.fold(self.high, "row", 0)

        def y_low(self):
            self.low = self.slots.fold(self.low, "col", 1)

        def y_high(self):
            self.high = self.slots.fold(self.high, "col", 1)

        def x_low(self):
            self.low = self.slots.fold(self.low, "row", 0)

        def z_high(self):
            arrays = self.slots.gate(*[view[0] for view in self.high])
            value = total([(array, view[1]) for array, view in zip(arrays, self.high)])
            self.low = self.low + [view_of(self.slots.move(value.astype(bf16), "z", nz // 2))]

        def z_low(self):
            arrays = self.slots.gate(*[view[0] for view in self.low])
            held = [(array, view[1]) for array, view in zip(arrays, self.low)]
            for bit in reversed(bits("z")[:-1]):
                got = self.slots.move(total([half_of(view, 2, 1) for view in held]).astype(bf16), "z", bit)
                held = [half_of(view, 2, 0) for view in held] + [view_of(got)]
            self.low = held

        def result(self):
            arrays = self.slots.gate(*[view[0] for view in self.low])
            return total([(array, view[1]) for array, view in zip(arrays, self.low)])[0, 0, 0]

    class TokensIn:
        def __init__(self, name, slots, values):
            self.name, self.slots, self.values, self.parts = name, slots, values, []

        def step(self, which, steps):
            rows = self.values.shape[0] // ncol
            here = lax.axis_index("col")
            (values,) = self.slots.gate(self.values)
            size = rows // steps
            parts = [lax.dynamic_slice_in_dim(values, here * rows + which * size, size, 0)]
            for k in range(1, ncol):
                block = lax.dynamic_slice_in_dim(values, (here ^ k) * rows + which * size, size, 0)
                parts.append(self.slots.move(block, "col", k))
            self.parts.append(parts)

        def first(self):
            self.step(0, 2)

        def second(self):
            self.step(1, 2)

        def end(self):
            count = len(self.parts[0])
            flat = self.slots.gate(*[part for parts in self.parts for part in parts])
            rows = [jnp.concatenate(flat[i : i + count], axis=1) for i in range(0, len(flat), count)]
            return jnp.concatenate(rows)

    def do(job, *stages):
        for stage in stages:
            with jax.named_scope(job.name + "_" + stage):
                getattr(job, stage)()

    class TokensOut:
        def __init__(self, name, slots, own, other):
            self.name, self.slots, self.own, self.other = name, slots, own, other

        def send(self):
            self.blocks = [self.slots.send(self.other[k - 1], "col", k) for k in range(1, ncol)]

        def end(self):
            rows = self.own.shape[0]
            here = lax.axis_index("col")
            first, *rest = self.slots.gate(self.own, *self.blocks)
            result = jnp.zeros((rows * ncol, self.own.shape[1]), self.own.dtype)
            result = lax.dynamic_update_slice_in_dim(result, first, here * rows, 0)
            for k, block in enumerate(rest):
                result = lax.dynamic_update_slice_in_dim(
                    result, block.astype(self.own.dtype), (here ^ (k + 1)) * rows, 0
                )
            return result

    def local(
        tokens,
        key_mask,
        first_gain,
        first_shift,
        qkv_weight,
        qkv_bias,
        out_weight,
        out_bias,
        second_gain,
        second_shift,
        up_weight,
        up_bias,
        down_weight,
        down_bias,
        cotangent,
    ):
        count = tokens.shape[0] // ncol
        seqs = count // LEN
        part, piece, width = out_weight.shape
        heads = part * nrow
        flat = heads * HD
        hidden_part = up_weight.shape[0]
        step = nz * hidden_part
        dim = width * ncol
        hidden = step * blocks
        pairs = heads // 2
        moved = count * dim

        def tile(shape, index=None):
            return pl.BlockSpec(shape, index or (lambda t: (t,) + (0,) * (len(shape) - 1)))

        slots = Slots()
        q = Gather("qkv", slots, qkv_weight.astype(bf16))
        o = Gather("out", slots, out_weight[None].astype(bf16))
        u = Gather("up", slots, up_weight.astype(bf16))
        d = Gather("down", slots, down_weight.astype(bf16))
        tok = TokensIn("tokens", slots, tokens)
        cot = TokensIn("cotangent", slots, cotangent)
        small = [jnp.concatenate([qkv_bias.reshape(-1), up_bias]).astype(bf16)[None]]
        vectors = jnp.stack([first_gain, first_shift, second_gain, second_shift, out_bias, down_bias])

        do(q, "z_all")
        do(tok, "first")
        vectors = slots.widen([vectors], "col")
        slots.advance()
        do(q, "x_low", "y_high")
        do(o, "z_low")
        do(u, "z_low")
        small = slots.widen(small, "z", False)
        slots.advance()
        do(q, "y_low", "x_high")
        do(o, "z_high")
        do(u, "z_high_first")
        small = slots.widen(small, "row")
        nearby = slots.widen([key_mask], "col")
        slots.advance()
        do(q, "core")
        do(u, "z_high_second", "x_low")
        do(tok, "second")
        do(d, "z_low")
        do(o, "y")
        small = slots.widen(small, "core")
        slots.advance()
        inputs = tok.end()
        vectors = jnp.transpose(joined(list(slots.gate(*vectors))), (1, 0, 2)).reshape(6, dim)
        gain_one, shift_one, gain_two, shift_two, out_offset, down_offset = [vectors[i : i + 1] for i in range(6)]
        small_all = joined(list(slots.gate(*small))).astype(f32)
        qkv_count = qkv_bias.size
        qkv_offset = small_all[..., :qkv_count].reshape(ncore, nrow, nz, 2, part, piece)
        qkv_offset = jnp.transpose(qkv_offset, (3, 1, 4, 0, 2, 5)).reshape(2, flat)
        up_offset = small_all[..., qkv_count:].reshape(1, hidden)
        here = lax.axis_index("col")
        nearby = joined(nearby)
        masks = jnp.zeros_like(nearby)
        for k in range(ncol):
            masks = lax.dynamic_update_slice_in_dim(masks, nearby[k : k + 1], here ^ k, 0)
        masks = masks.reshape(-1, key_mask.shape[1])
        first_seq = (lax.axis_index("row") * ncol + here) * seqs
        masks = lax.dynamic_slice_in_dim(masks, first_seq, seqs, 0)
        visible = jnp.concatenate([jnp.ones((seqs, BUF), jnp.int32), masks], axis=1)

        def head_operands(w, kinds):
            half = nz // 2
            places = []
            for k, r, c, z in itertools.product(range(ncore), range(nrow), range(ncol), range(nz)):
                for n, ((in_core, in_half, first), values) in enumerate(zip(w.places, w.pieces)):
                    lead, second, inner = (c, r, z) if in_half == 0 else (r, c, z - half * (in_half == 1))
                    held = in_half == 2 or in_half == z // half
                    if held and in_core == k and first <= lead < first + values.shape[0]:
                        index = (lead - first, second, inner)
                        places.append((n, index, r * part, (k * nz + z) * piece, c * width))
            if piece % 8 == 0:
                specs = [pl.BlockSpec(memory_space=pl.ANY)] * len(w.pieces)
                scratch = [pltpu.VMEM((kinds, heads, HD, dim), bf16), pltpu.SemaphoreType.DMA((kinds,))]
                return w.pieces, specs, scratch, (tuple(places), kinds)
            matrix = jnp.zeros((kinds, heads, HD, dim), bf16)
            for n, index, head, row, lane in places:
                matrix = lax.dynamic_update_slice(matrix, w.pieces[n][index], (0, head, row, lane))
            return [matrix.reshape(kinds, flat, dim)], [whole((kinds, flat, dim))], [], None

        qkv_ops, qkv_specs, qkv_scratch, qkv_layout = head_operands(q, 3)

        tokens_spec = tile((LEN, dim))
        hidden_spec = tile((LEN, hidden))
        half_step = step // 2
        vector_spec = whole((1, dim))
        three = pl.BlockSpec((3, LEN, flat), lambda t: (0, t, 0))
        pair_spec = pl.BlockSpec((3, LEN, PAIR), lambda s, p: (0, s, p))
        one_pair = pl.BlockSpec((LEN, PAIR), lambda s, p: (s, p))
        own_spec = tile((LEN, width))
        other_spec = pl.BlockSpec((ncol - 1, LEN, width), lambda t: (0, t, 0))

        def out_of(*shape, dtype=bf16):
            return jax.ShapeDtypeStruct(shape, dtype)

        def ffn_operands(w):
            operands = [p.reshape(p.shape[0], p.shape[1], half_step, width) for p in w.pieces]
            return operands, [whole(p.shape) for p in operands], (ncol, nrow, ncore, tuple(w.places))

        do(u, "y_high")
        do(o, "x")
        do(d, "z_high_first")
        do(cot, "first")
        normed, qkv = call(
            functools.partial(qkv_kernel, qkv_layout),
            (seqs,),
            [tokens_spec, vector_spec, vector_spec, whole((2, flat))] + qkv_specs,
            [tokens_spec, three],
            [out_of(count, dim), out_of(3, count, flat)],
            6 * moved * flat,
            6 * flat * dim + 10 * moved,
            "qkv",
            scratch=qkv_scratch,
        )(inputs, gain_one, shift_one, qkv_offset, *qkv_ops)
        slots.note(qkv)
        slots.advance()

        do(u, "y_low", "x_high")
        do(d, "z_high_second")
        do(o, "core")
        attended = call(
            attend_kernel,
            (seqs, pairs),
            [pair_spec, pl.BlockSpec((1, 1, LEN), lambda s, p: (s, 0, 0))],
            one_pair,
            out_of(count, flat),
            16 * count * LEN * flat,
            8 * moved,
            "attend",
        )(slots.gate(qkv)[0], visible[:, None, :])
        slots.note(attended)
        slots.advance()

        do(u, "core")
        do(d, "x_low", "y_high")
        do(cot, "second")
        out_ops, out_specs, out_scratch, out_layout = head_operands(o, 1)
        middle, normed_two = call(
            functools.partial(out_kernel, out_layout),
            (seqs,),
            [tokens_spec, tile((LEN, flat)), vector_spec, vector_spec, vector_spec] + out_specs,
            [tokens_spec, tokens_spec],
            [out_of(count, dim, dtype=f32), out_of(count, dim)],
            2 * moved * flat,
            2 * flat * dim + 10 * moved,
            "out",
            scratch=out_scratch,
        )(inputs, slots.gate(attended)[0], out_offset, gain_two, shift_two, *out_ops)
        up_ops, up_specs, up_dims = ffn_operands(u)
        hid, slope = call(
            functools.partial(up_kernel, up_dims),
            (seqs,),
            [tokens_spec, whole((1, hidden))] + up_specs,
            [hidden_spec, hidden_spec],
            [out_of(count, hidden), out_of(count, hidden)],
            8 * moved * hidden,
            2 * hidden * dim + 4 * count * hidden,
            "up",
        )(normed_two, up_offset, *up_ops)
        slots.note(hid)
        slots.advance()

        def ffn_sent(left, right, name):
            return call(
                functools.partial(ffn_sent_kernel, ncol),
                (2, nrow),
                [
                    pl.BlockSpec((count, half_step), lambda h, r: (0, (nrow + r) * 2 + h)),
                    whole((count, dim)),
                ],
                pl.BlockSpec((1, 1, ncol, half_step, width), lambda h, r: (h, r, 0, 0, 0)),
                out_of(2, nrow, ncol, half_step, width),
                2 * moved * hidden // ncore,
                2 * (hidden * dim + count * hidden) // ncore + 2 * moved,
                name,
            )(slots.gate(left)[0], right)

        def ffn_kept(left, right, got, name):
            by_col = pl.BlockSpec((1, half_step, width), lambda h, r: (jnp.where(h == 0, r, nrow - 1), 0, 0))
            out = call(
                functools.partial(ffn_kept_kernel, ncol, nrow),
                (2, nrow),
                [
                    pl.BlockSpec((count, half_step), lambda h, r: (0, r * 2 + h)),
                    whole((count, dim)),
                    pl.BlockSpec((1, 1, ncol, half_step, width), lambda h, r: (h, r, 0, 0, 0)),
                ],
                [by_col] * ncol + [summed((ncol, half_step, width))] * nrow,
                [out_of(nrow, half_step, width)] * ncol + [out_of(ncol, half_step, width)] * nrow,
                2 * moved * hidden // ncore,
                3 * (hidden * dim + count * hidden) // ncore + 2 * moved,
                name,
            )(left, right, got)
            shape = (nz // 2, hidden_part, width)
            slots.note(out[0])
            low = [values.reshape((nrow, 1) + shape) for values in out[:ncol]]
            return low, [values.reshape((1, ncol) + shape) for values in out[ncol:]]

        def head_grad(left, right, first, name, sums=False):
            kinds, _, lanes = left.shape
            rows = lanes // (part * HD)
            out = call(
                functools.partial(head_grad_kernel, (ncore, ncol, nz, part, piece)),
                (kinds, rows),
                [
                    pl.BlockSpec((1, count, part * HD), lambda i, r: (i, 0, r)),
                    whole((count, dim)),
                ],
                [pl.BlockSpec((1, ncol, nz, 1, part, piece, width), lambda i, r: (r, 0, 0, i, 0, 0, 0))] * ncore
                + [pl.BlockSpec((1, 1, part * HD), lambda i, r: (i, 0, r))] * sums,
                [out_of(rows, ncol, nz, kinds, part, piece, width)] * ncore
                + [out_of(kinds, 1, lanes, dtype=f32)] * sums,
                2 * moved * lanes * kinds,
                2 * kinds * (lanes * dim + count * lanes) + 2 * moved,
                name,
            )(left, right)
            slots.note(out[0])
            return out[:ncore], out[ncore:]

        def core_fold(name, sums):
            with jax.named_scope(name + "_core"):
                return [sums[0]] + [slots.send(sums[k], "core", k) for k in range(1, ncore)]

        def pull(first, rows):
            low = first * part // 2
            high = rows * part // 2
            return call(
                attend_pull_kernel,
                (seqs, high),
                [
                    pl.BlockSpec((3, LEN, PAIR), lambda s, p: (0, s, low + p)),
                    pl.BlockSpec((1, LEN, 1), lambda s, p: (s, 0, 0)),
                    pl.BlockSpec((LEN, PAIR), lambda s, p: (s, low + p)),
                ],
                pair_spec,
                out_of(3, count, rows * part * HD),
                30 * count * LEN * rows * part * HD,
                14 * moved * rows // nrow,
                "attend_pull",
            )(qkv, visible[:, :, None], slots.gate(attended_grad)[0])

        do(d, "y_low", "x_high")
        grad_low = cot.end()
        sent = ffn_sent(hid, grad_low, "down_grad")
        (got,) = core_fold("down_grad", [sent, sent])[1:]
        down_low, down_high = ffn_kept(hid, grad_low, got, "down_grad")
        slots.advance()

        dg, ug, og, qg = [Scatter(name, slots) for name in ("down_grad", "up_grad", "out_grad", "qkv_grad")]
        do(d, "core")
        with jax.named_scope("down_grad_first"):
            dg.x_high_first(down_high)
            dg.y_low_first(down_low)
        down_ops, down_specs, down_dims = ffn_operands(d)
        upward_grad, up_bias_sum = call(
            functools.partial(hidden_pull_kernel, down_dims),
            (seqs,),
            [tokens_spec, hidden_spec] + down_specs,
            [hidden_spec, summed((1, hidden))],
            [out_of(count, hidden), out_of(1, hidden, dtype=f32)],
            2 * moved * hidden,
            2 * hidden * dim + 4 * count * hidden,
            "hidden_pull",
        )(grad_low, slope, *down_ops)
        slots.note(upward_grad)
        slots.advance()

        do(dg, "y_high", "x_low")
        sent = ffn_sent(upward_grad, normed_two, "up_grad")
        (got,) = core_fold("up_grad", [sent, sent])[1:]
        own, other = call(
            functools.partial(down_kernel, down_dims),
            (seqs,),
            [hidden_spec, tokens_spec, vector_spec] + down_specs,
            [own_spec, other_spec],
            [out_of(count, width), out_of(ncol - 1, count, width)],
            2 * moved * hidden,
            2 * hidden * dim + 2 * count * hidden + 6 * moved,
            "down",
        )(slots.gate(hid)[0], middle, down_offset, *down_ops)
        slots.note(own)
        up_low, up_high = ffn_kept(upward_grad, normed_two, got, "up_grad")
        slots.advance()

        with jax.named_scope("up_grad_first"):
            ug.x_high_first(up_high)
            ug.y_low_first(up_low)
        do(dg, "z_high")
        middle_grad, branch_low, attended_grad, sums_two = call(
            functools.partial(middle_pull_kernel, up_dims, out_layout),
            (seqs,),
            [hidden_spec, tokens_spec, tokens_spec, vector_spec] + up_specs + out_specs,
            [tokens_spec, tokens_spec, tile((LEN, flat)), summed((4, dim))],
            [
                out_of(count, dim, dtype=f32),
                out_of(count, dim),
                out_of(count, flat),
                out_of(4, dim, dtype=f32),
            ],
            2 * moved * (hidden + flat),
            2 * hidden * dim + 2 * count * hidden + 14 * moved,
            "middle_pull",
            scratch=out_scratch,
        )(slots.gate(upward_grad)[0], middle, grad_low, gain_two, *up_ops, *out_ops)
        slots.note(attended_grad)
        slots.advance()

        do(ug, "y_high", "x_low")
        do(dg, "z_low")
        far = pull(nrow // 2, nrow // 2)
        slots.note(far)
        slots.advance()

        do(ug, "z_high")
        activations = TokensOut("activations", slots, own, other)
        do(activations, "send")
        far_sums, (far_own,) = head_grad(slots.gate(far)[0], normed, nrow // 2, "qkv_grad", True)
        far_held = core_fold("qkv_grad_far", far_sums)
        near = pull(0, nrow // 2)
        slots.note(near)
        slots.advance()

        with jax.named_scope("qkv_grad_x"):
            arrays = slots.gate(*far_held)
            got = slots.move(total([view_of(array) for array in arrays]).astype(bf16), "row", nrow // 2)
        do(ug, "z_low")
        near_sums, (near_own,) = head_grad(slots.gate(near)[0], normed, 0, "qkv_grad", True)
        near_held = core_fold("qkv_grad_near", near_sums)
        out_sums, _ = head_grad(slots.gate(attended)[0][None], branch_low, 0, "out_grad")
        out_held = core_fold("out_grad", out_sums)
        slots.advance()

        qg.halve(near_held + [got])
        if nrow > 2:
            do(qg, "x_high", "x_low")
        do(qg, "y_high", "y_low")
        og.halve(out_held)
        do(og, "x_high", "x_low")
        own_grad, other_grad, sums_one = call(
            functools.partial(token_pull_kernel, ncol, qkv_layout),
            (seqs,),
            [pl.BlockSpec((3, LEN, flat // 2), lambda t: (0, t, 0))] * 2
            + [tokens_spec, tokens_spec, vector_spec]
            + qkv_specs,
            [own_spec, other_spec, summed((2, dim))],
            [
                out_of(count, width, dtype=f32),
                out_of(ncol - 1, count, width),
                out_of(2, dim, dtype=f32),
            ],
            6 * moved * flat,
            6 * flat * dim + 14 * moved,
            "token_pull",
            scratch=qkv_scratch,
        )(slots.gate(near)[0], far, inputs, middle_grad, gain_one, *qkv_ops)
        slots.note(own_grad)
        slots.advance()

        bias_sum = jnp.concatenate([near_own, far_own], axis=2)[::2].reshape(2, nrow, part, ncore, nz, piece)
        bias_sum = jnp.transpose(bias_sum, (3, 1, 4, 0, 2, 5)).reshape(ncore, nrow, nz, qkv_count)
        bias_sum = jnp.concatenate([bias_sum, up_bias_sum.reshape(ncore, nrow, nz, hidden_part)], axis=-1)
        sums = jnp.concatenate([sums_one, sums_two])
        size = sums.shape[0] * width
        flat_bias = bias_sum.reshape(-1)
        packs = [jnp.concatenate([sums[:, :width].reshape(-1), flat_bias])]

        def small_sums(axis):
            (pack,) = slots.gate(packs[0])
            if axis == "col":
                for k in range(1, ncol):
                    far = sums[:, k * width : (k + 1) * width].reshape(-1)
                    packs[0] = packs[0] + slots.send(jnp.concatenate([far, flat_bias]), axis, k)
                return
            for bit in reversed(bits(axis)):
                rest = pack[size:]
                half = rest.size // 2
                got = slots.move(jnp.concatenate([pack[:size], rest[half:]]), axis, bit)
                pack = pack[: size + half] + got
            packs[0] = pack

        token_grad = TokensOut("token_grad", slots, own_grad, other_grad)
        do(qg, "z_high")
        do(og, "y_high", "y_low")
        do(token_grad, "send")
        small_sums("col")
        slots.advance()

        do(qg, "z_low")
        do(og, "z_high")
        small_sums("core")
        slots.advance()

        do(og, "z_low")
        small_sums("row")
        slots.advance()

        small_sums("z")
        activations, token_grad = activations.end(), token_grad.end()
        down_grad, up_grad, out_grad, qkv_grad = dg.result(), ug.result(), og.result(), qg.result()

        pack = packs[0]
        sums = pack[:size].reshape(-1, width)
        bias_sum = pack[size:]
        return (
            activations,
            token_grad,
            sums[0],
            sums[1],
            qkv_grad,
            bias_sum[:qkv_count].reshape(qkv_bias.shape),
            out_grad[0],
            sums[2],
            sums[3],
            sums[4],
            up_grad,
            bias_sum[qkv_count:],
            down_grad,
            sums[5],
        )

    return local


def solution(mesh):
    devices = mesh.devices
    nz, ncore = devices.shape[0] // 2, 2
    nrow, ncol = devices.shape[1], devices.shape[2]
    fine = Mesh(devices.reshape(nz, ncore, nrow, ncol), ("z", "core", "row", "col"))
    dp = ("z", "core")
    rows = P(("z", "core", "row"), "col")
    qkv_weight = P(None, "row", dp, "col")
    qkv_bias = P(None, "row", dp)
    out_weight = P("row", dp, "col")
    feature = P("col")
    unit = P(("z", "core", "row"))
    in_specs = (
        rows,
        P(("z", "core", "col"), None),
        feature,
        feature,
        qkv_weight,
        qkv_bias,
        out_weight,
        feature,
        feature,
        feature,
        rows,
        unit,
        rows,
        feature,
        rows,
    )
    out_specs = (
        rows,
        rows,
        feature,
        feature,
        qkv_weight,
        qkv_bias,
        out_weight,
        feature,
        feature,
        feature,
        rows,
        unit,
        rows,
        feature,
    )
    return jax.shard_map(
        make_local(nz, ncore, nrow, ncol),
        mesh=fine,
        in_specs=in_specs,
        out_specs=out_specs,
        check_vma=False,
    )
```

time: 743 us -> 543 us (0.73)
  waiting for transfers between devices: 294 us -> 134 us
  starting transfers between devices: 104 us -> 76.9 us
  local copies, waits for them, and re-layouts: 52.9 us -> 33.5 us
  Pallas kernels: 232 us -> 242 us
    ppermute x81 -> x84, waiting for transfers between devices: 294 us -> 134 us  [exchange(): lax.ppermute(values, axis, [(i, i ^ bit) for i in range(sizes[axis])])]
    ppermute x81 -> x84, starting transfers between devices: 104 us -> 76.9 us  [exchange(): lax.ppermute(values, axis, [(i, i ^ bit) for i in range(sizes[axis])])]
    unnamed x106 -> x178, local copies, waits for them, and re-layouts: 24.3 us -> 12.6 us
    broadcast_in_dim x0 -> x20, other arithmetic: none -> 11.1 us  [the longest x16 9.31 us: widen(): parts = [joined(parts)[None]]]
    pallas_call x14 -> x16, Pallas kernels: 206 us -> 216 us  [the longest x2 36.6 us: pull(): call(attend_pull_kernel, (seqs, high), [pl.BlockSpec((3, LEN, PAIR), lamb...]
    convert_element_type x17 -> x18, other arithmetic: 29.8 us -> 23.1 us  [the longest x8 11.3 us: fold(): total([half_of(view, dim, 1) for view in held]).astype(bf16)]
  transfers between devices with their start and end apart: 81 -> 84, of which waited for: 25 -> 30; matrix products, arithmetic and copies ran while one was open for 11% -> 10% of each run, Pallas kernels for 32% -> 40%
where the time goes in v3:
time: 543 us; the launch traced here: 536 us
  Pallas kernels  242 us (45%)
  waiting for transfers between devices  134 us (25%)
  starting transfers between devices  76.9 us (14%)
  other arithmetic  47.6 us (9%)
  local copies, waits for them, and re-layouts  33.5 us (6%)
    ppermute x84, waiting for transfers between devices, exchange(): lax.ppermute(values, axis, [(i, i ^ bit) for i in range(sizes[axis])])  134 us
    ppermute x84, starting transfers between devices, exchange(): lax.ppermute(values, axis, [(i, i ^ bit) for i in range(sizes[axis])])  76.9 us
    pallas_call x2, Pallas kernels, pull(): call(attend_pull_kernel, (seqs, high), [pl.BlockSpec((3, LEN, PAIR), lamb...  36.6 us
    pallas_call x1, Pallas kernels, local(): call(attend_kernel, (seqs, pairs), [pair_spec, pl.BlockSpec((1, 1, LEN),...  25.7 us
    pallas_call x1, Pallas kernels, local(): call(functools.partial(middle_pull_kernel, up_dims, out_layout), (seqs,),...  25.3 us
    pallas_call x1, Pallas kernels, local(): call(functools.partial(up_kernel, up_dims), (seqs,), [tokens_spec, whole(...  24.3 us
    pallas_call x3, Pallas kernels, head_grad(): call(functools.partial(head_grad_kernel, (ncore, ncol, nz, part, piece)),...  19.3 us
    pallas_call x2, Pallas kernels, ffn_kept(): call(functools.partial(ffn_kept_kernel, ncol, nrow), (2, nrow), [pl.Block...  18.8 us
  transfers between devices with their start and end apart: 84, of which 30 were waited for; matrix products, arithmetic and copies ran while one was open for 10% of the time, Pallas kernels for 40%

profile of v3, /device:TPU:0, one launch (start us, length us, event | category | flops | bytes accessed | tf_op | source)
XLA Modules:
  0.0 536.4 jit_solution(12876425481499365102)
XLA Ops:
  11.9 9.2 %collective-permute-done.4 = f32[1,6,512]{2,0,1:T(1,128)S(1)} collective-permute-done((f32[1,6,512]{2,0,1:T(1,128)S(1)}, f32[1,6,512]{2,0,1:T(1,128)S(1)}, u32[]{:S(2)}, u32[]{:S(2)}) %collective-permute-start.4) | collective-permute-done | bytes 12320 | tf_op jit(solution)/shard_map/ppermute | solution.py:335
  47.2 9.7 %collective-permute-done.15 = bf16[1,4,384]{2,1,0:T(4,128)(2,1)S(1)} collective-permute-done((bf16[1,4,384]{2,1,0:T(4,128)(2,1)S(1)}, bf16[1,4,384]{2,1,0:T(4,128)(2,1)S(1)}, u32[]{:S(2)}, u32[]{:S(2)}) %collective-permute-start.15) | collective-permute-done | bytes 3104 | tf_op jit(solution)/shard_map/ppermute | solution.py:335
  77.8 16.5 %collective-permute-done.17 = bf16[640,512]{1,0:T(8,128)(2,1)} collective-permute-done((bf16[640,512]{1,0:T(8,128)(2,1)}, bf16[640,512]{1,0:T(8,128)(2,1)}, u32[]{:S(2)}, u32[]{:S(2)}) %collective-permute-start.17) | collective-permute-done | bytes 655392 | tf_op jit(solution)/shard_map/tokens_second/ppermute | solution.py:335
  106.9 16.1 %qkv.1 = (bf16[1280,1024]{1,0:T(8,128)(2,1)}, bf16[3,1280,1024]{2,1,0:T(8,128)(2,1)}) custom-call(bf16[1280,1024]{1,0:T(8,128)(2,1)} %maximum_maximum_fusion.x_ref, f32[1,1024]{1,0:T(1,128)S(1)} %bitcast.140, f32[1,1024]{1,0:T(1,128)S(1)} %bitcast.144, f32[2,1024]{1,0:T(2,128)S(1)} %reshape.195.bias_ref, ...), custom_call_target="tpu_custom_call" | custom-call | flops 8053063680 | bytes 19398656 | tf_op jit(solution)/shard_map/qkv/pallas_call | solution.py:691
  129.2 25.7 %attend.1.o_ref = bf16[1280,1024]{1,0:T(8,128)(2,1)S(1)} custom-call(bf16[3,1280,1024]{2,1,0:T(8,128)(2,1)} %get-tuple-element.277.qkv_ref, s32[4,1,320]{2,1,0:T(1,128)S(1)} %broadcast_in_dim.106.mask_ref), custom_call_target="tpu_custom_call" | custom-call | flops 6710886400 | bytes 10485760 | tf_op jit(solution)/shard_map/attend/pallas_call | solution.py:708
  164.4 7.7 %out.1 = (f32[1280,1024]{1,0:T(8,128)}, bf16[1280,1024]{1,0:T(8,128)(2,1)S(1)}) custom-call(bf16[1280,1024]{1,0:T(8,128)(2,1)} %maximum_maximum_fusion.x_ref, bf16[1280,1024]{1,0:T(8,128)(2,1)} %copy-done.35, f32[1,1024]{1,0:T(1,128)S(1)} %bitcast.145, f32[1,1024]{1,0:T(1,128)S(1)} %bitcast.142, f32[1,1024]{1,0:T(1,128)S(1)} %bitcast.146, ...), custom_call_target="tpu_custom_call" | custom-call | flops 2684354560 | bytes 15204352 | tf_op jit(solution)/shard_map/out/pallas_call | solution.py:725
  175.6 24.3 %up.1 = (bf16[1280,4096]{1,0:T(8,128)(2,1)}, bf16[1280,4096]{1,0:T(8,128)(2,1)}) custom-call(bf16[1280,1024]{1,0:T(8,128)(2,1)} %copy-done.37, f32[1,4096]{1,0:T(1,128)S(1)} %reshape.197.bias_ref, bf16[1,2,512,512]{3,2,1,0:T(8,128)(2,1)S(1)} %bitcast.128, bf16[1,2,512,512]{3,2,1,0:T(8,128)(2,1)} %bitcast.27.refs_1_, ...), custom_call_target="tpu_custom_call" | custom-call | flops 42949672960 | bytes 29360128 | tf_op jit(solution)/shard_map/up/pallas_call | solution.py:737
  201.6 9.7 %down_grad.2 = bf16[2,2,2,512,512]{4,3,2,1,0:T(8,128)(2,1)} custom-call(bf16[1280,4096]{1,0:T(8,128)(2,1)} %get-tuple-element.320.l_ref.hid_ref, bf16[1280,1024]{1,0:T(8,128)(2,1)S(1)} %maximum_maximum_fusion.1.r_ref.g_ref), custom_call_target="tpu_custom_call" | custom-call | flops 5368709120 | bytes 12058624 | tf_op jit(solution)/shard_map/down_grad/pallas_call | solution.py:751
  220.7 9.4 %down_grad.3 = (bf16[2,512,512]{2,1,0:T(8,128)(2,1)S(1)}, bf16[2,512,512]{2,1,0:T(8,128)(2,1)S(1)}, bf16[2,512,512]{2,1,0:T(8,128)(2,1)S(1)}, bf16[2,512,512]{2,1,0:T(8,128)(2,1)S(1)}) custom-call(bf16[1280,4096]{1,0:T(8,128)(2,1)} %get-tuple-element.320.l_ref.hid_ref, bf16[1280,1024]{1,0:T(8,128)(2,1)} %copy-done, bf16[2,2,2,512,512]{4,3,2,1,0:T(8,128)(2,1)} %copy-done.80), custom_call_target="tpu_custom_call" | custom-call | flops 5368709120 | bytes 16777216 | tf_op jit(solution)/shard_map/down_grad/pallas_call | solution.py:767
  230.2 6.9 %collective-permute-done.43 = bf16[1,2,2,256,512]{4,3,2,1,0:T(8,128)(2,1)S(1)} collective-permute-done((bf16[1,2,2,256,512]{4,3,2,1,0:T(8,128)(2,1)S(1)}, bf16[1,2,2,256,512]{4,3,2,1,0:T(8,128)(2,1)S(1)}, u32[]{:S(2)}, u32[]{:S(2)}) %collective-permute-start.43) | collective-permute-done | bytes 1048608 | tf_op jit(solution)/shard_map/down_y_low/ppermute | solution.py:335
  246.6 17.5 %hidden_pull.1 = (bf16[1280,4096]{1,0:T(8,128)(2,1)}, f32[1,4096]{1,0:T(1,128)S(1)}) custom-call(bf16[1280,1024]{1,0:T(8,128)(2,1)} %copy-done, bf16[1280,4096]{1,0:T(8,128)(2,1)} %get-tuple-element.318.slope_ref, bf16[1,2,512,512]{3,2,1,0:T(8,128)(2,1)S(1)} %bitcast.134, bf16[1,2,512,512]{3,2,1,0:T(8,128)(2,1)S(1)} %bitcast.148, ...), custom_call_target="tpu_custom_call" | custom-call | flops 10737418240 | bytes 29360128 | tf_op jit(solution)/shard_map/hidden_pull/pallas_call | solution.py:842
  266.3 9.1 %up_grad.2 = bf16[2,2,2,512,512]{4,3,2,1,0:T(8,128)(2,1)} custom-call(bf16[1280,4096]{1,0:T(8,128)(2,1)} %get-tuple-element.342.l_ref.du_ref, bf16[1280,1024]{1,0:T(8,128)(2,1)S(1)} %copy-done.38), custom_call_target="tpu_custom_call" | custom-call | flops 5368709120 | bytes 12058624 | tf_op jit(solution)/shard_map/up_grad/pallas_call | solution.py:751
  282.7 15.3 %down.1 = (bf16[1280,512]{1,0:T(8,128)(2,1)}, bf16[1,1280,512]{2,1,0:T(8,128)(2,1)}) custom-call(bf16[1280,4096]{1,0:T(8,128)(2,1)} %get-tuple-element.320.l_ref.hid_ref, f32[1280,1024]{1,0:T(8,128)} %get-tuple-element.321.middle_ref, f32[1,1024]{1,0:T(1,128)S(1)} %bitcast.147, bf16[1,2,512,512]{3,2,1,0:T(8,128)(2,1)S(1)} %bitcast.135, ...), custom_call_target="tpu_custom_call" | custom-call | flops 10737418240 | bytes 26738688 | tf_op jit(solution)/shard_map/down/pallas_call | solution.py:858
  298.1 9.4 %up_grad.3 = (bf16[2,512,512]{2,1,0:T(8,128)(2,1)S(1)}, bf16[2,512,512]{2,1,0:T(8,128)(2,1)S(1)}, bf16[2,512,512]{2,1,0:T(8,128)(2,1)S(1)}, bf16[2,512,512]{2,1,0:T(8,128)(2,1)S(1)}) custom-call(bf16[1280,4096]{1,0:T(8,128)(2,1)} %get-tuple-element.342.l_ref.du_ref, bf16[1280,1024]{1,0:T(8,128)(2,1)} %copy-done.37, ...), custom_call_target="tpu_custom_call" | custom-call | flops 5368709120 | bytes 16777216 | tf_op jit(solution)/shard_map/up_grad/pallas_call | solution.py:767
  312.1 25.3 %middle_pull.1 = (f32[1280,1024]{1,0:T(8,128)}, bf16[1280,1024]{1,0:T(8,128)(2,1)}, bf16[1280,1024]{1,0:T(8,128)(2,1)}, f32[4,1024]{1,0:T(4,128)S(1)}) custom-call(bf16[1280,4096]{1,0:T(8,128)(2,1)} %get-tuple-element.342.l_ref.du_ref, f32[1280,1024]{1,0:T(8,128)} %get-tuple-element.321.middle_ref, bf16[1280,1024]{1,0:T(8,128)(2,1)} %copy-done, ...), custom_call_target="tpu_custom_call" | custom-call | flops 13421772800 | bytes 37224448 | tf_op jit(solution)/shard_map/middle_pull/pallas_call | solution.py:876
  343.7 18.3 %attend_pull.2.l_ref.far_ref = bf16[3,1280,512]{2,1,0:T(8,128)(2,1)} custom-call(bf16[3,1280,1024]{2,1,0:T(8,128)(2,1)} %get-tuple-element.277.qkv_ref, s32[4,320,1]{2,1,0:T(8,128)S(1)} %copy-done.12, bf16[1280,1024]{1,0:T(8,128)(2,1)S(1)} %copy-done.39), custom_call_target="tpu_custom_call" | custom-call | flops 6291456000 | bytes 9175040 | tf_op jit(solution)/shard_map/attend_pull/pallas_call | solution.py:814
  362.1 6.4 %qkv_grad.2 = (bf16[1,2,4,3,8,8,512]{6,5,4,3,2,1,0:T(8,128)(2,1)S(1)}, bf16[1,2,4,3,8,8,512]{6,5,4,3,2,1,0:T(8,128)(2,1)S(1)}, f32[3,1,512]{2,1,0:T(1,128)S(1)}) custom-call(bf16[3,1280,512]{2,1,0:T(8,128)(2,1)} %attend_pull.2.l_ref.far_ref, bf16[1280,1024]{1,0:T(8,128)(2,1)S(1)} %copy-done.40), custom_call_target="tpu_custom_call" | custom-call | flops 4026531840 | bytes 9699328 | tf_op jit(solution)/shard_map/qkv_grad/pallas_call | solution.py:789
  372.8 18.3 %attend_pull.3.l_ref.near_ref = bf16[3,1280,512]{2,1,0:T(8,128)(2,1)} custom-call(bf16[3,1280,1024]{2,1,0:T(8,128)(2,1)} %get-tuple-element.277.qkv_ref, s32[4,320,1]{2,1,0:T(8,128)S(1)} %copy-done.12, bf16[1280,1024]{1,0:T(8,128)(2,1)S(1)} %copy-done.39), custom_call_target="tpu_custom_call" | custom-call | flops 6291456000 | bytes 9175040 | tf_op jit(solution)/shard_map/attend_pull/pallas_call | solution.py:814
  391.0 6.6 %collective-permute-done.62 = bf16[1,1,2,256,512]{4,3,2,1,0:T(8,128)(2,1)S(1)} collective-permute-done((bf16[1,1,2,256,512]{4,3,2,1,0:T(8,128)(2,1)S(1)}, bf16[1,1,2,256,512]{4,3,2,1,0:T(8,128)(2,1)S(1)}, u32[]{:S(2)}, u32[]{:S(2)}) %collective-permute-start.62) | collective-permute-done | bytes 524320 | tf_op jit(solution)/shard_map/up_grad_z_high/ppermute | solution.py:335
  402.5 7.0 %qkv_grad.3 = (bf16[1,2,4,3,8,8,512]{6,5,4,3,2,1,0:T(8,128)(2,1)S(1)}, bf16[1,2,4,3,8,8,512]{6,5,4,3,2,1,0:T(8,128)(2,1)}, f32[3,1,512]{2,1,0:T(1,128)S(1)}) custom-call(bf16[3,1280,512]{2,1,0:T(8,128)(2,1)} %attend_pull.3.l_ref.near_ref, bf16[1280,1024]{1,0:T(8,128)(2,1)S(1)} %copy-done.41), custom_call_target="tpu_custom_call" | custom-call | flops 4026531840 | bytes 9699328 | tf_op jit(solution)/shard_map/qkv_grad/pallas_call | solution.py:789
  409.5 5.9 %out_grad.1 = (bf16[2,2,4,1,8,8,512]{6,5,4,3,2,1,0:T(8,128)(2,1)S(1)}, bf16[2,2,4,1,8,8,512]{6,5,4,3,2,1,0:T(8,128)(2,1)}) custom-call(bf16[1,1280,1024]{2,1,0:T(8,128)(2,1)S(1)} %bitcast.158, bf16[1280,1024]{1,0:T(8,128)(2,1)} %get-tuple-element.365.r_ref), custom_call_target="tpu_custom_call" | custom-call | flops 2684354560 | bytes 7340032 | tf_op jit(solution)/shard_map/out_grad/pallas_call | solution.py:789
  428.6 9.4 %collective-permute-done.65 = bf16[1,2,4,3,8,8,512]{6,5,4,3,2,1,0:T(8,128)(2,1)} collective-permute-done((bf16[1,2,4,3,8,8,512]{6,5,4,3,2,1,0:T(8,128)(2,1)}, bf16[1,2,4,3,8,8,512]{6,5,4,3,2,1,0:T(8,128)(2,1)}, u32[]{:S(2)}, u32[]{:S(2)}) %collective-permute-start.65) | collective-permute-done | bytes 1572896 | tf_op jit(solution)/shard_map/qkv_grad_x/ppermute | solution.py:335
  446.8 16.2 %token_pull.1 = (f32[1280,512]{1,0:T(8,128)}, bf16[1,1280,512]{2,1,0:T(8,128)(2,1)}, f32[2,1024]{1,0:T(2,128)S(1)}) custom-call(bf16[3,1280,512]{2,1,0:T(8,128)(2,1)} %attend_pull.3.l_ref.near_ref, bf16[3,1280,512]{2,1,0:T(8,128)(2,1)} %attend_pull.2.l_ref.far_ref, bf16[1280,1024]{1,0:T(8,128)(2,1)} %maximum_maximum_fusion.x_ref, ...), custom_call_target="tpu_custom_call" | custom-call | flops 8053063680 | bytes 24641536 | tf_op jit(solution)/shard_map/token_pull/pallas_call | solution.py:926
  472.3 25.9 %collective-permute-done.76 = f32[9216]{0:T(1024)S(1)} collective-permute-done((f32[9216]{0:T(1024)S(1)}, f32[9216]{0:T(1024)S(1)}, u32[]{:S(2)}, u32[]{:S(2)}) %collective-permute-start.76) | collective-permute-done | bytes 36896 | tf_op jit(solution)/shard_map/ppermute | solution.py:335
  (448 shorter events, 208.3 us)
Async XLA Ops:
  95.8 27.2 %collective-permute-start.27 = (bf16[1,2,256,512]{3,2,1,0:T(8,128)(2,1)S(1)}, bf16[1,2,256,512]{3,2,1,0:T(8,128)(2,1)S(1)}, u32[]{:S(2)}, u32[]{:S(2)}) collective-permute-start(bf16[1,2,256,512]{3,2,1,0:T(8,128)(2,1)S(1)} %maximum_bitcast_fusion.7), channel_id=1, source_target_pairs={{0,1},{1,0},{2,3},{3,2},{4,5},{5,4},{6,7},{7,6},{8,9},{9,8},{10,11... | collective-permute-start | bytes 1572872 | tf_op jit(solution)/shard_map/up_y_high/ppermute | solution.py:335
  124.8 33.2 %collective-permute-start.31 = (bf16[1,2,2,256,512]{4,3,2,1,0:T(8,128)(2,1)S(1)}, bf16[1,2,2,256,512]{4,3,2,1,0:T(8,128)(2,1)}, u32[]{:S(2)}, u32[]{:S(2)}) collective-permute-start(bf16[1,2,2,256,512]{4,3,2,1,0:T(8,128)(2,1)S(1)} %maximum_bitcast_fusion), channel_id=1, source_target_pairs={{0,1},{1,0},{2,3},{3,2},{4,5},{5,4},{6,7},{7,6},{8,9},{9,8},{10,11... | collective-permute-start | bytes 3145736 | tf_op jit(solution)/shard_map/up_y_low/ppermute | solution.py:335
  125.5 32.6 %collective-permute-start.32 = (bf16[1,2,2,256,512]{4,3,2,1,0:T(8,128)(2,1)S(1)}, bf16[1,2,2,256,512]{4,3,2,1,0:T(8,128)(2,1)}, u32[]{:S(2)}, u32[]{:S(2)}) collective-permute-start(bf16[1,2,2,256,512]{4,3,2,1,0:T(8,128)(2,1)S(1)} %maximum_bitcast_fusion.1), channel_id=1, source_target_pairs={{0,2},{2,0},{1,3},{3,1},{4,6},{6,4},{5,7},{7,5},{8,10},{10,8},{9,1... | collective-permute-start | bytes 3145736 | tf_op jit(solution)/shard_map/up_x_high/ppermute | solution.py:335
  126.8 29.6 %collective-permute-start.33 = (bf16[1,256,512]{2,1,0:T(8,128)(2,1)}, bf16[1,256,512]{2,1,0:T(8,128)(2,1)S(1)}, u32[]{:S(2)}, u32[]{:S(2)}) collective-permute-start(bf16[1,256,512]{2,1,0:T(8,128)(2,1)} %collective-permute-done.24), channel_id=1, source_target_pairs={{0,16},{8,24},{16,0},{24,8},{1,17},{9,25},{17,1},{25,9},{2,18},{10... | collective-permute-start | bytes 786440 | tf_op jit(solution)/shard_map/down_z_high_second/ppermute | solution.py:335
  128.7 27.8 %collective-permute-start.34 = (bf16[1,2,4,1,8,8,512]{6,5,4,3,2,1,0:T(8,128)(2,1)S(1)}, bf16[1,2,4,1,8,8,512]{6,5,4,3,2,1,0:T(8,128)(2,1)S(1)}, u32[]{:S(2)}, u32[]{:S(2)}) collective-permute-start(bf16[1,2,4,1,8,8,512]{6,5,4,3,2,1,0:T(8,128)(2,1)S(1)} %maximum_bitcast_fusion.8.refs_0_.refs_8_), channel_id=1, source_target_pairs={{0,4},{4,0},{1,5},{5,1},{2,6},{6,2},{3,7},{7,3},{8,12},{12,8},{9,1... | collective-permute-start | bytes 1572872 | tf_op jit(solution)/shard_map/out_core/ppermute | solution.py:335
  128.7 28.6 %collective-permute-start.35 = (bf16[1,2,4,1,8,8,512]{6,5,4,3,2,1,0:T(8,128)(2,1)S(1)}, bf16[1,2,4,1,8,8,512]{6,5,4,3,2,1,0:T(8,128)(2,1)S(1)}, u32[]{:S(2)}, u32[]{:S(2)}) collective-permute-start(bf16[1,2,4,1,8,8,512]{6,5,4,3,2,1,0:T(8,128)(2,1)S(1)} %collective-permute-done.28.refs_1_.refs_9_), channel_id=1, source_target_pairs={{0,4},{4,0},{1,5},{5,1},{2,6},{6,2},{3,7},{7,3},{8,12},{12,8},{9,1... | collective-permute-start | bytes 1572872 | tf_op jit(solution)/shard_map/out_core/ppermute | solution.py:335
  160.3 39.5 %collective-permute-start.40 = (bf16[1,2,256,512]{3,2,1,0:T(8,128)(2,1)S(1)}, bf16[1,2,256,512]{3,2,1,0:T(8,128)(2,1)S(1)}, u32[]{:S(2)}, u32[]{:S(2)}) collective-permute-start(bf16[1,2,256,512]{3,2,1,0:T(8,128)(2,1)S(1)} %maximum_bitcast_fusion.9), channel_id=1, source_target_pairs={{0,2},{2,0},{1,3},{3,1},{4,6},{6,4},{5,7},{7,5},{8,10},{10,8},{9,1... | collective-permute-start | bytes 1572872 | tf_op jit(solution)/shard_map/down_x_low/ppermute | solution.py:335
  173.5 26.4 %collective-permute-start.41 = (bf16[1,2,256,512]{3,2,1,0:T(8,128)(2,1)S(1)}, bf16[1,2,256,512]{3,2,1,0:T(8,128)(2,1)S(1)}, u32[]{:S(2)}, u32[]{:S(2)}) collective-permute-start(bf16[1,2,256,512]{3,2,1,0:T(8,128)(2,1)S(1)} %maximum_bitcast_fusion.10), channel_id=1, source_target_pairs={{0,1},{1,0},{2,3},{3,2},{4,5},{5,4},{6,7},{7,6},{8,9},{9,8},{10,11... | collective-permute-start | bytes 1572872 | tf_op jit(solution)/shard_map/down_y_high/ppermute | solution.py:335
  175.1 26.2 %collective-permute-start.42 = (bf16[640,512]{1,0:T(8,128)(2,1)S(1)}, bf16[640,512]{1,0:T(8,128)(2,1)S(1)}, u32[]{:S(2)}, u32[]{:S(2)}) collective-permute-start(bf16[640,512]{1,0:T(8,128)(2,1)S(1)} %get-tuple-element.451), channel_id=1, source_target_pairs={{0,1},{1,0},{2,3},{3,2},{4,5},{5,4},{6,7},{7,6},{8,9},{9,8},{10,11... | collective-permute-start | bytes 1966088 | tf_op jit(solution)/shard_map/cotangent_second/ppermute | solution.py:335
  277.9 29.6 %collective-permute-start.53 = (bf16[1,1,2,256,512]{4,3,2,1,0:T(8,128)(2,1)S(1)}, bf16[1,1,2,256,512]{4,3,2,1,0:T(8,128)(2,1)S(1)}, u32[]{:S(2)}, u32[]{:S(2)}) collective-permute-start(bf16[1,1,2,256,512]{4,3,2,1,0:T(8,128)(2,1)S(1)} %add_convert_fusion.6), channel_id=1, source_target_pairs={{0,1},{1,0},{2,3},{3,2},{4,5},{5,4},{6,7},{7,6},{8,9},{9,8},{10,11... | collective-permute-start | bytes 1572872 | tf_op jit(solution)/shard_map/down_grad_y_high/ppermute | solution.py:335
  279.6 27.9 %collective-permute-start.54 = (bf16[1,1,2,256,512]{4,3,2,1,0:T(8,128)(2,1)S(1)}, bf16[1,1,2,256,512]{4,3,2,1,0:T(8,128)(2,1)S(1)}, u32[]{:S(2)}, u32[]{:S(2)}) collective-permute-start(bf16[1,1,2,256,512]{4,3,2,1,0:T(8,128)(2,1)S(1)} %add_convert_fusion.5), channel_id=1, source_target_pairs={{0,2},{2,0},{1,3},{3,1},{4,6},{6,4},{5,7},{7,5},{8,10},{10,8},{9,1... | collective-permute-start | bytes 1572872 | tf_op jit(solution)/shard_map/down_grad_x_low/ppermute | solution.py:335
  307.5 30.0 %collective-permute-start.55 = (bf16[1,2,2,256,512]{4,3,2,1,0:T(8,128)(2,1)S(1)}, bf16[1,2,2,256,512]{4,3,2,1,0:T(8,128)(2,1)}, u32[]{:S(2)}, u32[]{:S(2)}) collective-permute-start(bf16[1,2,2,256,512]{4,3,2,1,0:T(8,128)(2,1)S(1)} %bitcast.156), channel_id=1, source_target_pairs={{0,2},{2,0},{1,3},{3,1},{4,6},{6,4},{5,7},{7,5},{8,10},{10,8},{9,1... | collective-permute-start | bytes 3145736 | tf_op jit(solution)/shard_map/up_grad_first/ppermute | solution.py:335
  309.1 28.4 %collective-permute-start.56 = (bf16[2,1,2,256,512]{4,3,2,1,0:T(8,128)(2,1)S(1)}, bf16[2,1,2,256,512]{4,3,2,1,0:T(8,128)(2,1)S(1)}, u32[]{:S(2)}, u32[]{:S(2)}) collective-permute-start(bf16[2,1,2,256,512]{4,3,2,1,0:T(8,128)(2,1)S(1)} %bitcast.154), channel_id=1, source_target_pairs={{0,1},{1,0},{2,3},{3,2},{4,5},{5,4},{6,7},{7,6},{8,9},{9,8},{10,11... | collective-permute-start | bytes 3145736 | tf_op jit(solution)/shard_map/up_grad_first/ppermute | solution.py:335
  311.6 25.9 %collective-permute-start.57 = (bf16[1,1,2,256,512]{4,3,2,1,0:T(8,128)(2,1)}, bf16[1,1,2,256,512]{4,3,2,1,0:T(8,128)(2,1)S(1)}, u32[]{:S(2)}, u32[]{:S(2)}) collective-permute-start(bf16[1,1,2,256,512]{4,3,2,1,0:T(8,128)(2,1)} %add_convert_fusion.4), channel_id=1, source_target_pairs={{0,16},{8,24},{16,0},{24,8},{1,17},{9,25},{17,1},{25,9},{2,18},{10... | collective-permute-start | bytes 1572872 | tf_op jit(solution)/shard_map/down_grad_z_high/ppermute | solution.py:335
  368.6 31.5 %collective-permute-start.63 = (bf16[1,2,4,3,8,8,512]{6,5,4,3,2,1,0:T(8,128)(2,1)S(1)}, bf16[1,2,4,3,8,8,512]{6,5,4,3,2,1,0:T(8,128)(2,1)S(1)}, u32[]{:S(2)}, u32[]{:S(2)}) collective-permute-start(bf16[1,2,4,3,8,8,512]{6,5,4,3,2,1,0:T(8,128)(2,1)S(1)} %get-tuple-element.362), channel_id=1, source_target_pairs={{0,4},{4,0},{1,5},{5,1},{2,6},{6,2},{3,7},{7,3},{8,12},{12,8},{9,1... | collective-permute-start | bytes 4718600 | tf_op jit(solution)/shard_map/qkv_grad_far_core/ppermute | solution.py:335
  368.7 31.4 %collective-permute-start.61 = (bf16[1280,512]{1,0:T(8,128)(2,1)}, bf16[1280,512]{1,0:T(8,128)(2,1)S(1)}, u32[]{:S(2)}, u32[]{:S(2)}) collective-permute-start(bf16[1280,512]{1,0:T(8,128)(2,1)} %bitcast.51), channel_id=1, source_target_pairs={{0,1},{1,0},{2,3},{3,2},{4,5},{5,4},{6,7},{7,6},{8,9},{9,8},{10,11... | collective-permute-start | bytes 3932168 | tf_op jit(solution)/shard_map/activations_send/ppermute | solution.py:335
  371.5 26.2 %collective-permute-start.62 = (bf16[1,1,2,256,512]{4,3,2,1,0:T(8,128)(2,1)S(1)}, bf16[1,1,2,256,512]{4,3,2,1,0:T(8,128)(2,1)S(1)}, u32[]{:S(2)}, u32[]{:S(2)}) collective-permute-start(bf16[1,1,2,256,512]{4,3,2,1,0:T(8,128)(2,1)S(1)} %add_convert_fusion.1), channel_id=1, source_target_pairs={{0,16},{8,24},{16,0},{24,8},{1,17},{9,25},{17,1},{25,9},{2,18},{10... | collective-permute-start | bytes 1572872 | tf_op jit(solution)/shard_map/up_grad_z_high/ppermute | solution.py:335
  401.8 36.3 %collective-permute-start.65 = (bf16[1,2,4,3,8,8,512]{6,5,4,3,2,1,0:T(8,128)(2,1)}, bf16[1,2,4,3,8,8,512]{6,5,4,3,2,1,0:T(8,128)(2,1)}, u32[]{:S(2)}, u32[]{:S(2)}) collective-permute-start(bf16[1,2,4,3,8,8,512]{6,5,4,3,2,1,0:T(8,128)(2,1)} %add_convert_fusion), channel_id=1, source_target_pairs={{0,2},{2,0},{1,3},{3,1},{4,6},{6,4},{5,7},{7,5},{8,10},{10,8},{9,1... | collective-permute-start | bytes 4718600 | tf_op jit(solution)/shard_map/qkv_grad_x/ppermute | solution.py:335
  409.5 28.6 %collective-permute-start.67 = (bf16[1,2,4,3,8,8,512]{6,5,4,3,2,1,0:T(8,128)(2,1)}, bf16[1,2,4,3,8,8,512]{6,5,4,3,2,1,0:T(8,128)(2,1)}, u32[]{:S(2)}, u32[]{:S(2)}) collective-permute-start(bf16[1,2,4,3,8,8,512]{6,5,4,3,2,1,0:T(8,128)(2,1)} %get-tuple-element.378), channel_id=1, source_target_pairs={{0,4},{4,0},{1,5},{5,1},{2,6},{6,2},{3,7},{7,3},{8,12},{12,8},{9,1... | collective-permute-start | bytes 4718600 | tf_op jit(solution)/shard_map/qkv_grad_near_core/ppermute | solution.py:335
  463.2 35.1 %collective-permute-start.75 = (bf16[1280,512]{1,0:T(8,128)(2,1)}, bf16[1280,512]{1,0:T(8,128)(2,1)}, u32[]{:S(2)}, u32[]{:S(2)}) collective-permute-start(bf16[1280,512]{1,0:T(8,128)(2,1)} %bitcast.169), channel_id=1, source_target_pairs={{0,1},{1,0},{2,3},{3,2},{4,5},{5,4},{6,7},{7,6},{8,9},{9,8},{10,11... | collective-permute-start | bytes 3932168 | tf_op jit(solution)/shard_map/token_grad_send/ppermute | solution.py:335
  465.8 32.3 %collective-permute-start.72 = (bf16[1,1,2,1,8,8,512]{6,5,4,3,2,1,0:T(8,128)(2,1)S(1)}, bf16[1,1,2,1,8,8,512]{6,5,4,3,2,1,0:T(8,128)(2,1)S(1)}, u32[]{:S(2)}, u32[]{:S(2)}) collective-permute-start(bf16[1,1,2,1,8,8,512]{6,5,4,3,2,1,0:T(8,128)(2,1)S(1)} %add_convert_fusion.17), channel_id=1, source_target_pairs={{0,1},{1,0},{2,3},{3,2},{4,5},{5,4},{6,7},{7,6},{8,9},{9,8},{10,11... | collective-permute-start | bytes 393224 | tf_op jit(solution)/shard_map/out_grad_y_low/ppermute | solution.py:335
  467.5 30.7 %collective-permute-start.73 = (bf16[1,1,2,1,8,8,512]{6,5,4,3,2,1,0:T(8,128)(2,1)S(1)}, bf16[1,1,2,1,8,8,512]{6,5,4,3,2,1,0:T(8,128)(2,1)S(1)}, u32[]{:S(2)}, u32[]{:S(2)}) collective-permute-start(bf16[1,1,2,1,8,8,512]{6,5,4,3,2,1,0:T(8,128)(2,1)S(1)} %add_convert_fusion.16), channel_id=1, source_target_pairs={{0,1},{1,0},{2,3},{3,2},{4,5},{5,4},{6,7},{7,6},{8,9},{9,8},{10,11... | collective-permute-start | bytes 393224 | tf_op jit(solution)/shard_map/out_grad_y_high/ppermute | solution.py:335
  469.1 29.1 %collective-permute-start.76 = (f32[9216]{0:T(1024)S(1)}, f32[9216]{0:T(1024)S(1)}, u32[]{:S(2)}, u32[]{:S(2)}) collective-permute-start(f32[9216]{0:T(1024)S(1)} %pad_maximum_fusion.1), channel_id=1, source_target_pairs={{0,1},{1,0},{2,3},{3,2},{4,5},{5,4},{6,7},{7,6},{8,9},{9,8},{10,11... | collective-permute-start | bytes 110600 | tf_op jit(solution)/shard_map/ppermute | solution.py:335
  471.0 27.2 %collective-permute-start.74 = (bf16[1,1,2,3,8,8,512]{6,5,4,3,2,1,0:T(8,128)(2,1)S(1)}, bf16[1,1,2,3,8,8,512]{6,5,4,3,2,1,0:T(8,128)(2,1)S(1)}, u32[]{:S(2)}, u32[]{:S(2)}) collective-permute-start(bf16[1,1,2,3,8,8,512]{6,5,4,3,2,1,0:T(8,128)(2,1)S(1)} %add_convert_fusion.7), channel_id=1, source_target_pairs={{0,16},{8,24},{16,0},{24,8},{1,17},{9,25},{17,1},{25,9},{2,18},{10... | collective-permute-start | bytes 1179656 | tf_op jit(solution)/shard_map/qkv_grad_z_high/ppermute | solution.py:335
  (145 other events, 2209.8 us)

commit v4 on v3

--- a/solution.py
+++ b/solution.py
@@ -9,7 +9,9 @@
 from jax.sharding import Mesh, PartitionSpec as P
 
 HD = 64
-PAIR = 2 * HD
+HELD = 4
+QUAD = HELD * HD
+STEP = 2
 BUF = 64
 LEN = 320
 masked_fill = -1000000000.0
@@ -117,47 +119,73 @@
         out_ref[i] = value.astype(bf16)
 
 
-def split_heads(pair):
-    first = lax.broadcasted_iota(jnp.int32, pair.shape, 1) < HD
-    zero = jnp.zeros_like(pair)
-    return jnp.concatenate([jnp.where(first, pair, zero), jnp.where(first, zero, pair)], axis=0)
-
-
-def join_heads(both):
-    rows = both.shape[0] // 2
-    first = lax.broadcasted_iota(jnp.int32, (rows, both.shape[1]), 1) < HD
-    return jnp.where(first, both[:rows], both[rows:])
-
-
-def attend_kernel(qkv_ref, mask_ref, out_ref):
+def split_heads(held):
+    head = lax.broadcasted_iota(jnp.int32, held.shape, 1) // HD
+    zero = jnp.zeros_like(held)
+    return jnp.concatenate([jnp.where(head == h, held, zero) for h in range(HELD)], axis=0)
+
+
+def join_heads(all_heads):
+    rows = all_heads.shape[0] // HELD
+    head = lax.broadcasted_iota(jnp.int32, (rows, all_heads.shape[1]), 1) // HD
+    value = all_heads[:rows]
+    for h in range(1, HELD):
+        value = jnp.where(head == h, all_heads[h * rows : (h + 1) * rows], value)
+    return value
+
+
+def attend_kernel(qkv_ref, mask_ref, out_ref, probs_ref):
     seen = mask_ref[0] > 0
-    scores = contract_last(split_heads(qkv_ref[0]), qkv_ref[1])
-    scores = jnp.where(seen, scores, masked_fill / attn_scale)
-    top = jnp.max(scores, axis=1, keepdims=True)
-    grown = jnp.exp2((scores - top) * exp2_scale)
-    total = jnp.sum(grown, axis=1, keepdims=True)
-    mixed = matmul(grown.astype(bf16), qkv_ref[2]) / total
-    out_ref[...] = join_heads(mixed).astype(bf16)
-
-
-def attend_pull_kernel(qkv_ref, mask_ref, do_ref, out_ref):
-    seen = mask_ref[0] > 0
-    both = split_heads(qkv_ref[0])
-    keys = qkv_ref[1]
-    vals = qkv_ref[2]
-    pulled = split_heads(do_ref[...])
-    scores = contract_last(keys, both)
-    scores = jnp.where(seen, scores, masked_fill / attn_scale)
-    top = jnp.max(scores, axis=0, keepdims=True)
-    grown = jnp.exp2((scores - top) * exp2_scale)
-    probs = grown * (1.0 / jnp.sum(grown, axis=0, keepdims=True))
-    prob_grad = contract_last(vals, pulled)
-    out_ref[2] = matmul(probs.astype(bf16), pulled).astype(bf16)
-    inner = jnp.sum(prob_grad * probs, axis=0, keepdims=True)
-    score_grad = (probs * (prob_grad - inner)).astype(bf16)
-    out_ref[1] = (matmul(score_grad, both) * attn_scale).astype(bf16)
-    query_grad = contract_first(score_grad, keys) * attn_scale
-    out_ref[0] = join_heads(query_grad).astype(bf16)
+    for n in range(STEP):
+        lanes = slice(n * QUAD, (n + 1) * QUAD)
+        scores = contract_last(qkv_ref[1, :, lanes], split_heads(qkv_ref[0, :, lanes]))
+        scores = jnp.where(seen, scores, masked_fill / attn_scale)
+        top = jnp.max(scores, axis=0, keepdims=True)
+        grown = jnp.exp2((scores - top) * exp2_scale)
+        probs = (grown * (1.0 / jnp.sum(grown, axis=0, keepdims=True))).astype(bf16)
+        probs_ref[0, n] = probs
+        out_ref[:, lanes] = join_heads(contract_first(probs, qkv_ref[2, :, lanes])).astype(bf16)
+
+
+def attend_pull_kernel(seqs, sizes, qkv_ref, probs_ref, do_ref, normed_ref, out_ref, *refs):
+    ncore, ncol, nz, part, piece = sizes
+    sum_refs, (sum_ref, held) = refs[:ncore], refs[ncore:]
+    at = pl.program_id(0)
+    rows = held.shape[2] // (part * HD)
+
+    @pl.when(at < seqs)
+    def _():
+        place = pl.ds(pl.multiple_of(at * LEN, LEN), LEN)
+        for n in range(STEP):
+            lanes = slice(n * QUAD, (n + 1) * QUAD)
+            queries = split_heads(qkv_ref[0, :, lanes])
+            keys = qkv_ref[1, :, lanes]
+            pulled = split_heads(do_ref[:, lanes])
+            low = probs_ref[0, n]
+            probs = low.astype(f32)
+            prob_grad = contract_last(qkv_ref[2, :, lanes], pulled)
+            inner = jnp.sum(prob_grad * probs, axis=0, keepdims=True)
+            score_grad = (probs * (prob_grad - inner)).astype(bf16)
+            value_grad = matmul(low, pulled).astype(bf16)
+            key_grad = (matmul(score_grad, queries) * attn_scale).astype(bf16)
+            query_grad = join_heads(contract_first(score_grad, keys) * attn_scale).astype(bf16)
+            for i, value in enumerate((query_grad, key_grad, value_grad)):
+                out_ref[i, :, lanes] = value
+                held[i, place, lanes] = value
+
+    @pl.when(at >= seqs)
+    def _():
+        width = normed_ref.shape[1] // ncol
+        kind, row = (at - seqs) // rows, (at - seqs) % rows
+        size = part * HD
+        left = held[kind, :, pl.ds(pl.multiple_of(row * size, size), size)] if rows > 1 else held[kind]
+        for c in range(ncol):
+            value = contract_first(left, normed_ref[:, c * width : (c + 1) * width]).astype(bf16)
+            value = value.reshape(part, ncore, nz, piece, width)
+            for core in range(ncore):
+                for z in range(nz):
+                    sum_refs[core][0, c, z, 0] = value[:, core, z]
+        sum_ref[0] = jnp.sum(left.astype(f32), axis=0, keepdims=True)
 
 
 def out_kernel(layout, x_ref, o_ref, bias_ref, gain_ref, shift_ref, *refs):
@@ -394,6 +422,8 @@
         return value
 
     class Gather:
+        together = None
+
         def __init__(self, name, slots, shard):
             self.name, self.slots, self.low = name, slots, [shard[None]]
 
@@ -451,6 +481,8 @@
             self.places, self.pieces = [], []
             for half, parts in lists:
                 parts = self.slots.gate(*parts)
+                if half == self.together:
+                    parts = [joined(list(parts))]
                 for k in range(ncore):
                     first = 0
                     for values in parts:
@@ -515,24 +547,24 @@
 
     class TokensIn:
         def __init__(self, name, slots, values):
-            self.name, self.slots, self.values, self.parts = name, slots, values, []
-
-        def step(self, which, steps):
-            rows = self.values.shape[0] // ncol
+            self.name, self.slots, self.parts, self.blocks = name, slots, [], []
+            rows = values.shape[0] // ncol
             here = lax.axis_index("col")
-            (values,) = self.slots.gate(self.values)
-            size = rows // steps
-            parts = [lax.dynamic_slice_in_dim(values, here * rows + which * size, size, 0)]
-            for k in range(1, ncol):
-                block = lax.dynamic_slice_in_dim(values, (here ^ k) * rows + which * size, size, 0)
-                parts.append(self.slots.move(block, "col", k))
-            self.parts.append(parts)
+            size = rows // 2
+            for which in range(2):
+                starts = [(here ^ k) * rows + which * size for k in range(ncol)]
+                self.blocks.append([lax.dynamic_slice_in_dim(values, start, size, 0) for start in starts])
+
+        def step(self, which):
+            own, *sent = self.blocks[which]
+            sent = self.slots.gate(*sent)
+            self.parts.append([own] + [self.slots.move(block, "col", k + 1) for k, block in enumerate(sent)])
 
         def first(self):
-            self.step(0, 2)
+            self.step(0)
 
         def second(self):
-            self.step(1, 2)
+            self.step(1)
 
         def end(self):
             count = len(self.parts[0])
@@ -622,9 +654,8 @@
         nearby = slots.widen([key_mask], "col")
         slots.advance()
         do(q, "core")
-        do(u, "z_high_second", "x_low")
+        do(u, "z_high_second")
         do(tok, "second")
-        do(d, "z_low")
         do(o, "y")
         small = slots.widen(small, "core")
         slots.advance()
@@ -672,8 +703,6 @@
         half_step = step // 2
         vector_spec = whole((1, dim))
         three = pl.BlockSpec((3, LEN, flat), lambda t: (0, t, 0))
-        pair_spec = pl.BlockSpec((3, LEN, PAIR), lambda s, p: (0, s, p))
-        one_pair = pl.BlockSpec((LEN, PAIR), lambda s, p: (s, p))
         own_spec = tile((LEN, width))
         other_spec = pl.BlockSpec((ncol - 1, LEN, width), lambda t: (0, t, 0))
 
@@ -684,9 +713,9 @@
             operands = [p.reshape(p.shape[0], p.shape[1], half_step, width) for p in w.pieces]
             return operands, [whole(p.shape) for p in operands], (ncol, nrow, ncore, tuple(w.places))
 
-        do(u, "y_high")
+        do(u, "x_low", "y_high")
         do(o, "x")
-        do(d, "z_high_first")
+        do(d, "z_low")
         do(cot, "first")
         normed, qkv = call(
             functools.partial(qkv_kernel, qkv_layout),
@@ -703,24 +732,33 @@
         slots.advance()
 
         do(u, "y_low", "x_high")
-        do(d, "z_high_second")
+        do(d, "z_high")
         do(o, "core")
-        attended = call(
+        quads = flat // QUAD
+        step_lanes = STEP * QUAD
+        queries = HELD * LEN
+        attended, probs = call(
             attend_kernel,
-            (seqs, pairs),
-            [pair_spec, pl.BlockSpec((1, 1, LEN), lambda s, p: (s, 0, 0))],
-            one_pair,
-            out_of(count, flat),
+            (seqs, quads // STEP),
+            [
+                pl.BlockSpec((3, LEN, step_lanes), lambda s, p: (0, s, p)),
+                pl.BlockSpec((1, LEN, 1), lambda s, p: (s, 0, 0)),
+            ],
+            [
+                pl.BlockSpec((LEN, step_lanes), lambda s, p: (s, p)),
+                pl.BlockSpec((1, STEP, LEN, queries), lambda s, p: (s, p, 0, 0)),
+            ],
+            [out_of(count, flat), out_of(seqs, quads, LEN, queries)],
             16 * count * LEN * flat,
-            8 * moved,
+            8 * moved + 2 * seqs * quads * LEN * queries,
             "attend",
-        )(slots.gate(qkv)[0], visible[:, None, :])
+        )(slots.gate(qkv)[0], visible[:, :, None])
         slots.note(attended)
         slots.advance()
 
+        u.together = 0
         do(u, "core")
         do(d, "x_low", "y_high")
-        do(cot, "second")
         out_ops, out_specs, out_scratch, out_layout = head_operands(o, 1)
         middle, normed_two = call(
             functools.partial(out_kernel, out_layout),
@@ -733,6 +771,10 @@
             "out",
             scratch=out_scratch,
         )(inputs, slots.gate(attended)[0], out_offset, gain_two, shift_two, *out_ops)
+        slots.note(normed_two)
+        slots.advance()
+
+        do(d, "y_low", "x_high")
         up_ops, up_specs, up_dims = ffn_operands(u)
         hid, slope = call(
             functools.partial(up_kernel, up_dims),
@@ -743,7 +785,7 @@
             8 * moved * hidden,
             2 * hidden * dim + 4 * count * hidden,
             "up",
-        )(normed_two, up_offset, *up_ops)
+        )(slots.gate(normed_two)[0], up_offset, *up_ops)
         slots.note(hid)
         slots.advance()
 
@@ -804,41 +846,76 @@
             slots.note(out[0])
             return out[:ncore], out[ncore:]
 
-        def core_fold(name, sums):
+        def core_fold(name, sums, gated=True):
             with jax.named_scope(name + "_core"):
-                return [sums[0]] + [slots.send(sums[k], "core", k) for k in range(1, ncore)]
+                sent = slots.gate(*sums[1:]) if gated else sums[1:]
+                return [sums[0]] + [slots.move(values, "core", k + 1) for k, values in enumerate(sent)]
 
         def pull(first, rows):
-            low = first * part // 2
-            high = rows * part // 2
-            return call(
-                attend_pull_kernel,
-                (seqs, high),
+            lanes = rows * part * HD
+            which = first // rows
+            kinds = 3
+
+            def seq(t):
+                return jnp.minimum(t, seqs - 1)
+
+            def kind_row(t):
+                step_after = jnp.maximum(t - seqs, 0)
+                return step_after // rows, step_after % rows
+
+            def sums_at(t):
+                kind, row = kind_row(t)
+                return (row, 0, 0, kind, 0, 0, 0)
+
+            def own_at(t):
+                kind, row = kind_row(t)
+                return (kind, 0, row)
+
+            out = call(
+                functools.partial(attend_pull_kernel, seqs, (ncore, ncol, nz, part, piece)),
+                (seqs + kinds * rows,),
                 [
-                    pl.BlockSpec((3, LEN, PAIR), lambda s, p: (0, s, low + p)),
-                    pl.BlockSpec((1, LEN, 1), lambda s, p: (s, 0, 0)),
-                    pl.BlockSpec((LEN, PAIR), lambda s, p: (s, low + p)),
+                    pl.BlockSpec((kinds, LEN, lanes), lambda t: (0, seq(t), which)),
+                    pl.BlockSpec((1, STEP, LEN, queries), lambda t: (seq(t), which, 0, 0)),
+                    pl.BlockSpec((LEN, lanes), lambda t: (seq(t), which)),
+                    whole((count, dim)),
                 ],
-                pair_spec,
-                out_of(3, count, rows * part * HD),
-                30 * count * LEN * rows * part * HD,
+                [pl.BlockSpec((kinds, LEN, lanes), lambda t: (0, seq(t), 0))]
+                + [pl.BlockSpec((1, ncol, nz, 1, part, piece, width), sums_at)] * ncore
+                + [pl.BlockSpec((1, 1, part * HD), own_at)],
+                [out_of(kinds, count, lanes)]
+                + [out_of(rows, ncol, nz, kinds, part, piece, width)] * ncore
+                + [out_of(kinds, 1, lanes, dtype=f32)],
+                30 * count * LEN * lanes + 2 * moved * lanes * kinds,
                 14 * moved * rows // nrow,
                 "attend_pull",
-            )(qkv, visible[:, :, None], slots.gate(attended_grad)[0])
-
-        do(d, "y_low", "x_high")
+                scratch=[pltpu.VMEM((kinds, count, lanes), bf16)],
+            )(qkv, probs, slots.gate(attended_grad)[0], normed)
+            slots.note(out[0])
+            return out[0], out[1 : 1 + ncore], out[1 + ncore]
+
+        do(d, "core")
+        do(cot, "second")
+        down_ops, down_specs, down_dims = ffn_operands(d)
+        own, other = call(
+            functools.partial(down_kernel, down_dims),
+            (seqs,),
+            [hidden_spec, tokens_spec, vector_spec] + down_specs,
+            [own_spec, other_spec],
+            [out_of(count, width), out_of(ncol - 1, count, width)],
+            2 * moved * hidden,
+            2 * hidden * dim + 2 * count * hidden + 6 * moved,
+            "down",
+        )(hid, middle, down_offset, *down_ops)
+        slots.note(own)
+        slots.advance()
+
+        dg, ug, og, qg = [Scatter(name, slots) for name in ("down_grad", "up_grad", "out_grad", "qkv_grad")]
+        activations = TokensOut("activations", slots, own, other)
+        do(activations, "send")
         grad_low = cot.end()
         sent = ffn_sent(hid, grad_low, "down_grad")
-        (got,) = core_fold("down_grad", [sent, sent])[1:]
-        down_low, down_high = ffn_kept(hid, grad_low, got, "down_grad")
-        slots.advance()
-
-        dg, ug, og, qg = [Scatter(name, slots) for name in ("down_grad", "up_grad", "out_grad", "qkv_grad")]
-        do(d, "core")
-        with jax.named_scope("down_grad_first"):
-            dg.x_high_first(down_high)
-            dg.y_low_first(down_low)
-        down_ops, down_specs, down_dims = ffn_operands(d)
+        (got,) = core_fold("down_grad", [sent, sent], False)[1:]
         upward_grad, up_bias_sum = call(
             functools.partial(hidden_pull_kernel, down_dims),
             (seqs,),
@@ -848,31 +925,16 @@
             2 * moved * hidden,
             2 * hidden * dim + 4 * count * hidden,
             "hidden_pull",
-        )(grad_low, slope, *down_ops)
+        )(slots.gate(grad_low)[0], slope, *down_ops)
         slots.note(upward_grad)
-        slots.advance()
-
-        do(dg, "y_high", "x_low")
+        down_low, down_high = ffn_kept(hid, grad_low, got, "down_grad")
+        slots.advance()
+
+        with jax.named_scope("down_grad_first"):
+            dg.x_high_first(down_high)
+            dg.y_low_first(down_low)
         sent = ffn_sent(upward_grad, normed_two, "up_grad")
-        (got,) = core_fold("up_grad", [sent, sent])[1:]
-        own, other = call(
-            functools.partial(down_kernel, down_dims),
-            (seqs,),
-            [hidden_spec, tokens_spec, vector_spec] + down_specs,
-            [own_spec, other_spec],
-            [out_of(count, width), out_of(ncol - 1, count, width)],
-            2 * moved * hidden,
-            2 * hidden * dim + 2 * count * hidden + 6 * moved,
-            "down",
-        )(slots.gate(hid)[0], middle, down_offset, *down_ops)
-        slots.note(own)
-        up_low, up_high = ffn_kept(upward_grad, normed_two, got, "up_grad")
-        slots.advance()
-
-        with jax.named_scope("up_grad_first"):
-            ug.x_high_first(up_high)
-            ug.y_low_first(up_low)
-        do(dg, "z_high")
+        (got,) = core_fold("up_grad", [sent, sent], False)[1:]
         middle_grad, branch_low, attended_grad, sums_two = call(
             functools.partial(middle_pull_kernel, up_dims, out_layout),
             (seqs,),
@@ -890,39 +952,59 @@
             scratch=out_scratch,
         )(slots.gate(upward_grad)[0], middle, grad_low, gain_two, *up_ops, *out_ops)
         slots.note(attended_grad)
-        slots.advance()
-
+        activations = activations.end()
+        slots.note(activations)
+        slots.advance()
+
+        do(dg, "y_high", "x_low")
+        up_low, up_high = ffn_kept(slots.gate(upward_grad)[0], normed_two, got, "up_grad")
+        slots.advance()
+
+        with jax.named_scope("up_grad_first"):
+            ug.x_high_first(up_high)
+            ug.y_low_first(up_low)
+        do(dg, "z_high")
+        far, far_sums, far_own = pull(nrow // 2, nrow // 2)
+        slots.note(*far_sums)
+        slots.advance()
+
+        far_held = core_fold("qkv_grad_far", far_sums)
         do(ug, "y_high", "x_low")
         do(dg, "z_low")
-        far = pull(nrow // 2, nrow // 2)
-        slots.note(far)
-        slots.advance()
-
+        out_sums, _ = head_grad(slots.gate(attended)[0][None], branch_low, 0, "out_grad")
+        slots.advance()
+
+        far_low = Scatter("qkv_grad_far", slots)
+        far_low.halve(far_held)
+        with jax.named_scope("qkv_grad_far_x"):
+            arrays = slots.gate(*[view[0] for view in far_low.high])
+            value = total([(array, view[1]) for array, view in zip(arrays, far_low.high)])
+            got_high = slots.move(value.astype(bf16), "row", nrow // 2)
+        do(far_low, "y_low")
         do(ug, "z_high")
-        activations = TokensOut("activations", slots, own, other)
-        do(activations, "send")
-        far_sums, (far_own,) = head_grad(slots.gate(far)[0], normed, nrow // 2, "qkv_grad", True)
-        far_held = core_fold("qkv_grad_far", far_sums)
-        near = pull(0, nrow // 2)
-        slots.note(near)
-        slots.advance()
-
-        with jax.named_scope("qkv_grad_x"):
-            arrays = slots.gate(*far_held)
-            got = slots.move(total([view_of(array) for array in arrays]).astype(bf16), "row", nrow // 2)
+        out_held = core_fold("out_grad", out_sums)
+        near, near_sums, near_own = pull(0, nrow // 2)
+        slots.note(*near_sums)
+        slots.advance()
+
+        near_held = core_fold("qkv_grad_near", near_sums)
+        with jax.named_scope("qkv_grad_far_x"):
+            arrays = slots.gate(*[view[0] for view in far_low.low])
+            value = total([(array, view[1]) for array, view in zip(arrays, far_low.low)])
+            got_low = slots.move(value.astype(bf16), "row", nrow // 2)
+        og.halve(out_held)
+        do(og, "x_high", "y_low")
+        down_grad = dg.result()
+        slots.note(down_grad)
+        slots.advance()
+
+        qg.halve(near_held)
+        qg.high = qg.high + [view_of(got_high)]
+        if nrow > 2:
+            do(qg, "x_high")
+        do(qg, "y_high", "y_low")
+        do(og, "y_high", "x_low")
         do(ug, "z_low")
-        near_sums, (near_own,) = head_grad(slots.gate(near)[0], normed, 0, "qkv_grad", True)
-        near_held = core_fold("qkv_grad_near", near_sums)
-        out_sums, _ = head_grad(slots.gate(attended)[0][None], branch_low, 0, "out_grad")
-        out_held = core_fold("out_grad", out_sums)
-        slots.advance()
-
-        qg.halve(near_held + [got])
-        if nrow > 2:
-            do(qg, "x_high", "x_low")
-        do(qg, "y_high", "y_low")
-        og.halve(out_held)
-        do(og, "x_high", "x_low")
         own_grad, other_grad, sums_one = call(
             functools.partial(token_pull_kernel, ncol, qkv_layout),
             (seqs,),
@@ -951,39 +1033,36 @@
         flat_bias = bias_sum.reshape(-1)
         packs = [jnp.concatenate([sums[:, :width].reshape(-1), flat_bias])]
 
-        def small_sums(axis):
+        def small_sums():
             (pack,) = slots.gate(packs[0])
-            if axis == "col":
-                for k in range(1, ncol):
-                    far = sums[:, k * width : (k + 1) * width].reshape(-1)
-                    packs[0] = packs[0] + slots.send(jnp.concatenate([far, flat_bias]), axis, k)
-                return
-            for bit in reversed(bits(axis)):
-                rest = pack[size:]
-                half = rest.size // 2
-                got = slots.move(jnp.concatenate([pack[:size], rest[half:]]), axis, bit)
-                pack = pack[: size + half] + got
+            for k in range(1, ncol):
+                far_part = sums[:, k * width : (k + 1) * width].reshape(-1)
+                pack = pack + slots.send(jnp.concatenate([far_part, flat_bias]), "col", k)
+            for axis in ("core", "row", "z"):
+                for bit in reversed(bits(axis)):
+                    rest = pack[size:]
+                    half = rest.size // 2
+                    got = slots.move(jnp.concatenate([pack[:size], rest[half:]]), axis, bit)
+                    pack = pack[: size + half] + got
             packs[0] = pack
 
         token_grad = TokensOut("token_grad", slots, own_grad, other_grad)
+        do(token_grad, "send")
+        qg.low = qg.low + [view_of(got_low)]
+        if nrow > 2:
+            do(qg, "x_low")
         do(qg, "z_high")
-        do(og, "y_high", "y_low")
-        do(token_grad, "send")
-        small_sums("col")
+        do(og, "z_high")
+        with jax.named_scope("small_sums"):
+            small_sums()
+        up_grad = ug.result()
+        slots.note(up_grad)
         slots.advance()
 
         do(qg, "z_low")
-        do(og, "z_high")
-        small_sums("core")
-        slots.advance()
-
         do(og, "z_low")
-        small_sums("row")
-        slots.advance()
-
-        small_sums("z")
-        activations, token_grad = activations.end(), token_grad.end()
-        down_grad, up_grad, out_grad, qkv_grad = dg.result(), ug.result(), og.result(), qg.result()
+        token_grad = token_grad.end()
+        out_grad, qkv_grad = og.result(), qg.result()
 
         pack = packs[0]
         sums = pack[:size].reshape(-1, width)

time: 543 us -> 511 us (0.941)
  Pallas kernels: 242 us -> 222 us
  waiting for transfers between devices: 134 us -> 121 us
    pallas_call x3 -> x1, Pallas kernels: 19.3 us -> 5.23 us  [head_grad(): call(functools.partial(head_grad_kernel, (ncore, ncol, nz, part, piece)),...]
    ppermute x84, waiting for transfers between devices: 134 us -> 121 us  [exchange(): lax.ppermute(values, axis, [(i, i ^ bit) for i in range(sizes[axis])])]
    pallas_call x3, Pallas kernels: 62.3 us -> 55.9 us  [the longest x2 37.6 us: pull(): call(functools.partial(attend_pull_kernel, seqs, (ncore, ncol, nz, part,...]
    unnamed x178 -> x182, local copies, waits for them, and re-layouts: 12.6 us -> 13.7 us
    convert_element_type x8 -> x11, other arithmetic: 11.3 us -> 11.7 us  [fold(): total([half_of(view, dim, 1) for view in held]).astype(bf16)]
  transfers between devices with their start and end apart: 84 -> 84, of which waited for: 30 -> 35; matrix products, arithmetic and copies ran while one was open for 10% -> 11% of each run, Pallas kernels for 40% -> 40%
where the time goes in v4:
time: 511 us; the launch traced here: 506 us
  Pallas kernels  222 us (43%)
  waiting for transfers between devices  121 us (24%)
  starting transfers between devices  77.9 us (15%)
  other arithmetic  52.6 us (10%)
  local copies, waits for them, and re-layouts  30.4 us (6%)
    ppermute x84, waiting for transfers between devices, exchange(): lax.ppermute(values, axis, [(i, i ^ bit) for i in range(sizes[axis])])  121 us
    ppermute x84, starting transfers between devices, exchange(): lax.ppermute(values, axis, [(i, i ^ bit) for i in range(sizes[axis])])  77.9 us
    pallas_call x2, Pallas kernels, pull(): call(functools.partial(attend_pull_kernel, seqs, (ncore, ncol, nz, part,...  37.6 us
    pallas_call x1, Pallas kernels, local(): call(functools.partial(middle_pull_kernel, up_dims, out_layout), (seqs,),...  25.5 us
    pallas_call x1, Pallas kernels, local(): call(functools.partial(up_kernel, up_dims), (seqs,), [tokens_spec, whole(...  24.6 us
    pallas_call x2, Pallas kernels, ffn_kept(): call(functools.partial(ffn_kept_kernel, ncol, nrow), (2, nrow), [pl.Block...  18.8 us
    pallas_call x2, Pallas kernels, ffn_sent(): call(functools.partial(ffn_sent_kernel, ncol), (2, nrow), [pl.BlockSpec((...  18.4 us
    pallas_call x1, Pallas kernels, local(): call(attend_kernel, (seqs, quads // STEP), [pl.BlockSpec((3, LEN, step_la...  18.3 us
  transfers between devices with their start and end apart: 84, of which 35 were waited for; matrix products, arithmetic and copies ran while one was open for 11% of the time, Pallas kernels for 40%

profile of v4, /device:TPU:0, one launch (start us, length us, event | category | flops | bytes accessed | tf_op | source)
XLA Modules:
  0.0 506.0 jit_solution(4457706952238407324)
XLA Ops:
  12.1 9.8 %collective-permute-done.4 = f32[1,6,512]{2,0,1:T(1,128)S(1)} collective-permute-done((f32[1,6,512]{2,0,1:T(1,128)S(1)}, f32[1,6,512]{2,0,1:T(1,128)S(1)}, u32[]{:S(2)}, u32[]{:S(2)}) %collective-permute-start.4) | collective-permute-done | bytes 12320 | tf_op jit(solution)/shard_map/ppermute | solution.py:363
  45.2 9.4 %collective-permute-done.15 = bf16[1,4,384]{2,1,0:T(4,128)(2,1)S(1)} collective-permute-done((bf16[1,4,384]{2,1,0:T(4,128)(2,1)S(1)}, bf16[1,4,384]{2,1,0:T(4,128)(2,1)S(1)}, u32[]{:S(2)}, u32[]{:S(2)}) %collective-permute-start.15) | collective-permute-done | bytes 3104 | tf_op jit(solution)/shard_map/ppermute | solution.py:363
  65.5 6.8 %collective-permute-done.22 = bf16[1,256,512]{2,1,0:T(8,128)(2,1)S(1)} collective-permute-done((bf16[1,256,512]{2,1,0:T(8,128)(2,1)S(1)}, bf16[1,256,512]{2,1,0:T(8,128)(2,1)S(1)}, u32[]{:S(2)}, u32[]{:S(2)}) %collective-permute-start.22) | collective-permute-done | bytes 262176 | tf_op jit(solution)/shard_map/up_z_high_second/ppermute | solution.py:363
  76.3 12.5 %collective-permute-done.17 = bf16[640,512]{1,0:T(8,128)(2,1)} collective-permute-done((bf16[640,512]{1,0:T(8,128)(2,1)}, bf16[640,512]{1,0:T(8,128)(2,1)}, u32[]{:S(2)}, u32[]{:S(2)}) %collective-permute-start.17) | collective-permute-done | bytes 655392 | tf_op jit(solution)/shard_map/tokens_second/ppermute | solution.py:363
  103.6 16.4 %qkv.1 = (bf16[1280,1024]{1,0:T(8,128)(2,1)}, bf16[3,1280,1024]{2,1,0:T(8,128)(2,1)}) custom-call(bf16[1280,1024]{1,0:T(8,128)(2,1)} %maximum_maximum_fusion.x_ref, f32[1,1024]{1,0:T(1,128)S(1)} %bitcast.134, f32[1,1024]{1,0:T(1,128)S(1)} %bitcast.140, f32[2,1024]{1,0:T(2,128)S(1)} %reshape.189.bias_ref, ...), custom_call_target="tpu_custom_call" | custom-call | flops 8053063680 | bytes 19398656 | tf_op jit(solution)/shard_map/qkv/pallas_call | solution.py:720
  132.6 18.3 %attend.1 = (bf16[1280,1024]{1,0:T(8,128)(2,1)S(1)}, bf16[4,4,320,1280]{3,2,1,0:T(8,128)(2,1)}) custom-call(bf16[3,1280,1024]{2,1,0:T(8,128)(2,1)} %get-tuple-element.277.qkv_ref, s32[4,320,1]{2,1,0:T(8,128)S(1)} %copy.39.mask_ref), custom_call_target="tpu_custom_call" | custom-call | flops 6710886400 | bytes 23592960 | tf_op jit(solution)/shard_map/attend/pallas_call | solution.py:740
  150.9 6.6 %collective-permute-done.32 = bf16[2,256,512]{2,1,0:T(8,128)(2,1)} collective-permute-done((bf16[2,256,512]{2,1,0:T(8,128)(2,1)}, bf16[2,256,512]{2,1,0:T(8,128)(2,1)}, u32[]{:S(2)}, u32[]{:S(2)}) %collective-permute-start.32) | collective-permute-done | bytes 524320 | tf_op jit(solution)/shard_map/down_z_high/ppermute | solution.py:363
  166.9 7.6 %out.1 = (f32[1280,1024]{1,0:T(8,128)}, bf16[1280,1024]{1,0:T(8,128)(2,1)S(1)}) custom-call(bf16[1280,1024]{1,0:T(8,128)(2,1)} %maximum_maximum_fusion.x_ref, bf16[1280,1024]{1,0:T(8,128)(2,1)} %copy-done.22, f32[1,1024]{1,0:T(1,128)S(1)} %bitcast.139, f32[1,1024]{1,0:T(1,128)S(1)} %bitcast.136, f32[1,1024]{1,0:T(1,128)S(1)} %bitcast.141, ...), custom_call_target="tpu_custom_call" | custom-call | flops 2684354560 | bytes 15204352 | tf_op jit(solution)/shard_map/out/pallas_call | solution.py:763
  182.4 24.6 %up.1 = (bf16[1280,4096]{1,0:T(8,128)(2,1)}, bf16[1280,4096]{1,0:T(8,128)(2,1)}) custom-call(bf16[1280,1024]{1,0:T(8,128)(2,1)} %copy-done.24, f32[1,4096]{1,0:T(1,128)S(1)} %reshape.191.bias_ref, bf16[2,2,512,512]{3,2,1,0:T(8,128)(2,1)} %bitcast.29.refs_0_, bf16[2,2,512,512]{3,2,1,0:T(8,128)(2,1)} %bitcast.30.refs_1_, ...), custom_call_target="tpu_custom_call" | custom-call | flops 42949672960 | bytes 29360128 | tf_op jit(solution)/shard_map/up/pallas_call | solution.py:779
  214.3 15.4 %down.1 = (bf16[1280,512]{1,0:T(8,128)(2,1)}, bf16[1,1280,512]{2,1,0:T(8,128)(2,1)}) custom-call(bf16[1280,4096]{1,0:T(8,128)(2,1)} %get-tuple-element.310.hid_ref.l_ref, f32[1280,1024]{1,0:T(8,128)} %get-tuple-element.297.middle_ref, f32[1,1024]{1,0:T(1,128)S(1)} %bitcast.138, bf16[1,2,512,512]{3,2,1,0:T(8,128)(2,1)S(1)} %bitcast.132, ...), custom_call_target="tpu_custom_call" | custom-call | flops 10737418240 | bytes 26738688 | tf_op jit(solution)/shard_map/down/pallas_call | solution.py:900
  231.3 9.7 %down_grad.2 = bf16[2,2,2,512,512]{4,3,2,1,0:T(8,128)(2,1)} custom-call(bf16[1280,4096]{1,0:T(8,128)(2,1)} %get-tuple-element.310.hid_ref.l_ref, bf16[1280,1024]{1,0:T(8,128)(2,1)S(1)} %maximum_maximum_fusion.1.r_ref.g_ref), custom_call_target="tpu_custom_call" | custom-call | flops 5368709120 | bytes 12058624 | tf_op jit(solution)/shard_map/down_grad/pallas_call | solution.py:793
  242.7 17.3 %hidden_pull.1 = (bf16[1280,4096]{1,0:T(8,128)(2,1)}, f32[1,4096]{1,0:T(1,128)S(1)}) custom-call(bf16[1280,1024]{1,0:T(8,128)(2,1)} %copy-done, bf16[1280,4096]{1,0:T(8,128)(2,1)} %get-tuple-element.316.slope_ref, bf16[1,2,512,512]{3,2,1,0:T(8,128)(2,1)S(1)} %bitcast.133, bf16[1,2,512,512]{3,2,1,0:T(8,128)(2,1)S(1)} %bitcast.145, ...), custom_call_target="tpu_custom_call" | custom-call | flops 10737418240 | bytes 29360128 | tf_op jit(solution)/shard_map/hidden_pull/pallas_call | solution.py:919
  260.1 9.4 %down_grad.3 = (bf16[2,512,512]{2,1,0:T(8,128)(2,1)S(1)}, bf16[2,512,512]{2,1,0:T(8,128)(2,1)S(1)}, bf16[2,512,512]{2,1,0:T(8,128)(2,1)S(1)}, bf16[2,512,512]{2,1,0:T(8,128)(2,1)S(1)}) custom-call(bf16[1280,4096]{1,0:T(8,128)(2,1)} %get-tuple-element.310.hid_ref.l_ref, bf16[1280,1024]{1,0:T(8,128)(2,1)} %copy-done, ...), custom_call_target="tpu_custom_call" | custom-call | flops 5368709120 | bytes 16777216 | tf_op jit(solution)/shard_map/down_grad/pallas_call | solution.py:809
  272.4 8.7 %up_grad.2 = bf16[2,2,2,512,512]{4,3,2,1,0:T(8,128)(2,1)} custom-call(bf16[1280,4096]{1,0:T(8,128)(2,1)} %get-tuple-element.335.du_ref.l_ref, bf16[1280,1024]{1,0:T(8,128)(2,1)S(1)} %copy-done.25), custom_call_target="tpu_custom_call" | custom-call | flops 5368709120 | bytes 12058624 | tf_op jit(solution)/shard_map/up_grad/pallas_call | solution.py:793
  286.2 25.5 %middle_pull.1 = (f32[1280,1024]{1,0:T(8,128)}, bf16[1280,1024]{1,0:T(8,128)(2,1)}, bf16[1280,1024]{1,0:T(8,128)(2,1)}, f32[4,1024]{1,0:T(4,128)S(1)}) custom-call(bf16[1280,4096]{1,0:T(8,128)(2,1)} %get-tuple-element.335.du_ref.l_ref, f32[1280,1024]{1,0:T(8,128)} %get-tuple-element.297.middle_ref, bf16[1280,1024]{1,0:T(8,128)(2,1)} %copy-done, ...), custom_call_target="tpu_custom_call" | custom-call | flops 13421772800 | bytes 37224448 | tf_op jit(solution)/shard_map/middle_pull/pallas_call | solution.py:938
  314.3 9.4 %up_grad.3 = (bf16[2,512,512]{2,1,0:T(8,128)(2,1)S(1)}, bf16[2,512,512]{2,1,0:T(8,128)(2,1)S(1)}, bf16[2,512,512]{2,1,0:T(8,128)(2,1)S(1)}, bf16[2,512,512]{2,1,0:T(8,128)(2,1)S(1)}) custom-call(bf16[1280,4096]{1,0:T(8,128)(2,1)} %get-tuple-element.335.du_ref.l_ref, bf16[1280,1024]{1,0:T(8,128)(2,1)} %copy-done.24, ...), custom_call_target="tpu_custom_call" | custom-call | flops 5368709120 | bytes 16777216 | tf_op jit(solution)/shard_map/up_grad/pallas_call | solution.py:809
  331.1 18.8 %attend_pull.2 = (bf16[3,1280,512]{2,1,0:T(8,128)(2,1)}, bf16[1,2,4,3,8,8,512]{6,5,4,3,2,1,0:T(8,128)(2,1)S(1)}, bf16[1,2,4,3,8,8,512]{6,5,4,3,2,1,0:T(8,128)(2,1)S(1)}, f32[3,1,512]{2,1,0:T(1,128)S(1)}) custom-call(bf16[3,1280,1024]{2,1,0:T(8,128)(2,1)} %get-tuple-element.277.qkv_ref, bf16[4,4,320,1280]{3,2,1,0:T(8,128)(2,1)} %get-tuple-element.321.probs_ref, ...), custom_call_target="tpu_custom_call" | custom-call | flops 10317987840 | bytes 9175040 | tf_op jit(solution)/shard_map/attend_pull/pallas_call | solution.py:874
  349.9 4.7 collective-permute-done.56
  362.1 5.2 %out_grad.1 = (bf16[2,2,4,1,8,8,512]{6,5,4,3,2,1,0:T(8,128)(2,1)S(1)}, bf16[2,2,4,1,8,8,512]{6,5,4,3,2,1,0:T(8,128)(2,1)S(1)}) custom-call(bf16[1,1280,1024]{2,1,0:T(8,128)(2,1)S(1)} %bitcast.154, bf16[1280,1024]{1,0:T(8,128)(2,1)} %get-tuple-element.362.r_ref), custom_call_target="tpu_custom_call" | custom-call | flops 2684354560 | bytes 7340032 | tf_op jit(solution)/shard_map/out_grad/pallas_call | solution.py:831
  377.7 18.9 %attend_pull.3 = (bf16[3,1280,512]{2,1,0:T(8,128)(2,1)}, bf16[1,2,4,3,8,8,512]{6,5,4,3,2,1,0:T(8,128)(2,1)S(1)}, bf16[1,2,4,3,8,8,512]{6,5,4,3,2,1,0:T(8,128)(2,1)}, f32[3,1,512]{2,1,0:T(1,128)S(1)}) custom-call(bf16[3,1280,1024]{2,1,0:T(8,128)(2,1)} %get-tuple-element.277.qkv_ref, bf16[4,4,320,1280]{3,2,1,0:T(8,128)(2,1)} %get-tuple-element.321.probs_ref, ...), custom_call_target="tpu_custom_call" | custom-call | flops 10317987840 | bytes 9175040 | tf_op jit(solution)/shard_map/attend_pull/pallas_call | solution.py:874
  414.8 11.2 %collective-permute-done.67 = bf16[1,2,2,1,8,8,512]{6,5,4,3,2,1,0:T(8,128)(2,1)S(1)} collective-permute-done((bf16[1,2,2,1,8,8,512]{6,5,4,3,2,1,0:T(8,128)(2,1)S(1)}, bf16[1,2,2,1,8,8,512]{6,5,4,3,2,1,0:T(8,128)(2,1)S(1)}, u32[]{:S(2)}, u32[]{:S(2)}) %collective-permute-start.67) | collective-permute-done | bytes 262176 | tf_op jit(solution)/shard_map/out_grad_x_high/ppermute | solution.py:363
  436.9 16.5 %token_pull.1 = (f32[1280,512]{1,0:T(8,128)}, bf16[1,1280,512]{2,1,0:T(8,128)(2,1)}, f32[2,1024]{1,0:T(2,128)S(1)}) custom-call(bf16[3,1280,512]{2,1,0:T(8,128)(2,1)} %get-tuple-element.386.near_ref, bf16[3,1280,512]{2,1,0:T(8,128)(2,1)} %get-tuple-element.348.far_ref, bf16[1280,1024]{1,0:T(8,128)(2,1)} %maximum_maximum_fusion.x_ref, ...), custom_call_target="tpu_custom_call" | custom-call | flops 8053063680 | bytes 24641536 | tf_op jit(solution)/shard_map/token_pull/pallas_call | solution.py:1008
  481.1 8.0 %collective-permute-done.75 = bf16[1,1,2,3,8,8,512]{6,5,4,3,2,1,0:T(8,128)(2,1)} collective-permute-done((bf16[1,1,2,3,8,8,512]{6,5,4,3,2,1,0:T(8,128)(2,1)}, bf16[1,1,2,3,8,8,512]{6,5,4,3,2,1,0:T(8,128)(2,1)}, u32[]{:S(2)}, u32[]{:S(2)}) %collective-permute-start.75) | collective-permute-done | bytes 393248 | tf_op jit(solution)/shard_map/qkv_grad_z_high/ppermute | solution.py:363
  489.1 5.8 %collective-permute-done.74 = bf16[1280,512]{1,0:T(8,128)(2,1)S(1)} collective-permute-done((bf16[1280,512]{1,0:T(8,128)(2,1)}, bf16[1280,512]{1,0:T(8,128)(2,1)S(1)}, u32[]{:S(2)}, u32[]{:S(2)}) %collective-permute-start.74) | collective-permute-done | bytes 1310752 | tf_op jit(solution)/shard_map/token_grad_send/ppermute | solution.py:363
  (452 shorter events, 206.9 us)
Async XLA Ops:
  62.9 25.9 %collective-permute-start.20 = (bf16[1,2,2,3,8,8,512]{6,5,4,3,2,1,0:T(8,128)(2,1)S(1)}, bf16[1,2,2,3,8,8,512]{6,5,4,3,2,1,0:T(8,128)(2,1)}, u32[]{:S(2)}, u32[]{:S(2)}) collective-permute-start(bf16[1,2,2,3,8,8,512]{6,5,4,3,2,1,0:T(8,128)(2,1)S(1)} %maximum_bitcast_fusion.5.refs_4_), channel_id=1, source_target_pairs={{0,4},{4,0},{1,5},{5,1},{2,6},{6,2},{3,7},{7,3},{8,12},{12,8},{9,1... | collective-permute-start | bytes 2359304 | tf_op jit(solution)/shard_map/qkv_core/ppermute | solution.py:363
  63.4 25.4 %collective-permute-start.21 = (bf16[1,2,2,3,8,8,512]{6,5,4,3,2,1,0:T(8,128)(2,1)S(1)}, bf16[1,2,2,3,8,8,512]{6,5,4,3,2,1,0:T(8,128)(2,1)}, u32[]{:S(2)}, u32[]{:S(2)}) collective-permute-start(bf16[1,2,2,3,8,8,512]{6,5,4,3,2,1,0:T(8,128)(2,1)S(1)} %collective-permute-done.12.refs_5_), channel_id=1, source_target_pairs={{0,4},{4,0},{1,5},{5,1},{2,6},{6,2},{3,7},{7,3},{8,12},{12,8},{9,1... | collective-permute-start | bytes 2359304 | tf_op jit(solution)/shard_map/qkv_core/ppermute | solution.py:363
  64.1 24.8 %collective-permute-start.18 = (bf16[1,2,2,3,8,8,512]{6,5,4,3,2,1,0:T(8,128)(2,1)S(1)}, bf16[1,2,2,3,8,8,512]{6,5,4,3,2,1,0:T(8,128)(2,1)}, u32[]{:S(2)}, u32[]{:S(2)}) collective-permute-start(bf16[1,2,2,3,8,8,512]{6,5,4,3,2,1,0:T(8,128)(2,1)S(1)} %maximum_bitcast_fusion.4.refs_0_), channel_id=1, source_target_pairs={{0,4},{4,0},{1,5},{5,1},{2,6},{6,2},{3,7},{7,3},{8,12},{12,8},{9,1... | collective-permute-start | bytes 2359304 | tf_op jit(solution)/shard_map/qkv_core/ppermute | solution.py:363
  88.9 31.1 %collective-permute-start.29 = (bf16[640,512]{1,0:T(8,128)(2,1)}, bf16[640,512]{1,0:T(8,128)(2,1)}, u32[]{:S(2)}, u32[]{:S(2)}) collective-permute-start(bf16[640,512]{1,0:T(8,128)(2,1)} %get-tuple-element.276), channel_id=1, source_target_pairs={{0,1},{1,0},{2,3},{3,2},{4,5},{5,4},{6,7},{7,6},{8,9},{9,8},{10,11... | collective-permute-start | bytes 1966088 | tf_op jit(solution)/shard_map/cotangent_first/ppermute | solution.py:363
  90.1 29.9 %collective-permute-start.28 = (bf16[1,256,512]{2,1,0:T(8,128)(2,1)}, bf16[1,256,512]{2,1,0:T(8,128)(2,1)}, u32[]{:S(2)}, u32[]{:S(2)}) collective-permute-start(bf16[1,256,512]{2,1,0:T(8,128)(2,1)} %convert_bitcast_fusion), channel_id=1, source_target_pairs={{0,8},{8,0},{16,24},{24,16},{1,9},{9,1},{17,25},{25,17},{2,10},{10... | collective-permute-start | bytes 786440 | tf_op jit(solution)/shard_map/down_z_low/ppermute | solution.py:363
  90.1 29.8 %collective-permute-start.27 = (bf16[1,2,4,1,8,8,512]{6,5,4,3,2,1,0:T(8,128)(2,1)S(1)}, bf16[1,2,4,1,8,8,512]{6,5,4,3,2,1,0:T(8,128)(2,1)S(1)}, u32[]{:S(2)}, u32[]{:S(2)}) collective-permute-start(bf16[1,2,4,1,8,8,512]{6,5,4,3,2,1,0:T(8,128)(2,1)S(1)} %maximum_bitcast_fusion.8.refs_0_.refs_6_), channel_id=1, source_target_pairs={{0,2},{2,0},{1,3},{3,1},{4,6},{6,4},{5,7},{7,5},{8,10},{10,8},{9,1... | collective-permute-start | bytes 1572872 | tf_op jit(solution)/shard_map/out_x/ppermute | solution.py:363
  93.8 26.2 %collective-permute-start.26 = (bf16[1,2,256,512]{3,2,1,0:T(8,128)(2,1)}, bf16[1,2,256,512]{3,2,1,0:T(8,128)(2,1)}, u32[]{:S(2)}, u32[]{:S(2)}) collective-permute-start(bf16[1,2,256,512]{3,2,1,0:T(8,128)(2,1)} %maximum_bitcast_fusion.7), channel_id=1, source_target_pairs={{0,1},{1,0},{2,3},{3,2},{4,5},{5,4},{6,7},{7,6},{8,9},{9,8},{10,11... | collective-permute-start | bytes 1572872 | tf_op jit(solution)/shard_map/up_y_high/ppermute | solution.py:363
  121.5 36.0 %collective-permute-start.31 = (bf16[1,2,2,256,512]{4,3,2,1,0:T(8,128)(2,1)S(1)}, bf16[1,2,2,256,512]{4,3,2,1,0:T(8,128)(2,1)S(1)}, u32[]{:S(2)}, u32[]{:S(2)}) collective-permute-start(bf16[1,2,2,256,512]{4,3,2,1,0:T(8,128)(2,1)S(1)} %maximum_bitcast_fusion.1), channel_id=1, source_target_pairs={{0,2},{2,0},{1,3},{3,1},{4,6},{6,4},{5,7},{7,5},{8,10},{10,8},{9,1... | collective-permute-start | bytes 3145736 | tf_op jit(solution)/shard_map/up_x_high/ppermute | solution.py:363
  125.8 31.7 %collective-permute-start.30 = (bf16[1,2,2,256,512]{4,3,2,1,0:T(8,128)(2,1)}, bf16[1,2,2,256,512]{4,3,2,1,0:T(8,128)(2,1)}, u32[]{:S(2)}, u32[]{:S(2)}) collective-permute-start(bf16[1,2,2,256,512]{4,3,2,1,0:T(8,128)(2,1)} %maximum_bitcast_fusion), channel_id=1, source_target_pairs={{0,1},{1,0},{2,3},{3,2},{4,5},{5,4},{6,7},{7,6},{8,9},{9,8},{10,11... | collective-permute-start | bytes 3145736 | tf_op jit(solution)/shard_map/up_y_low/ppermute | solution.py:363
  131.1 26.4 %collective-permute-start.32 = (bf16[2,256,512]{2,1,0:T(8,128)(2,1)}, bf16[2,256,512]{2,1,0:T(8,128)(2,1)}, u32[]{:S(2)}, u32[]{:S(2)}) collective-permute-start(bf16[2,256,512]{2,1,0:T(8,128)(2,1)} %constant_dynamic-update-slice_fusion.2), channel_id=1, source_target_pairs={{0,16},{8,24},{16,0},{24,8},{1,17},{9,25},{17,1},{25,9},{2,18},{10... | collective-permute-start | bytes 1572872 | tf_op jit(solution)/shard_map/down_z_high/ppermute | solution.py:363
  180.4 26.7 %collective-permute-start.41 = (bf16[1,2,2,256,512]{4,3,2,1,0:T(8,128)(2,1)S(1)}, bf16[1,2,2,256,512]{4,3,2,1,0:T(8,128)(2,1)S(1)}, u32[]{:S(2)}, u32[]{:S(2)}) collective-permute-start(bf16[1,2,2,256,512]{4,3,2,1,0:T(8,128)(2,1)S(1)} %maximum_bitcast_fusion.3), channel_id=1, source_target_pairs={{0,2},{2,0},{1,3},{3,1},{4,6},{6,4},{5,7},{7,5},{8,10},{10,8},{9,1... | collective-permute-start | bytes 3145736 | tf_op jit(solution)/shard_map/down_x_high/ppermute | solution.py:363
  182.0 25.1 %collective-permute-start.40 = (bf16[1,2,2,256,512]{4,3,2,1,0:T(8,128)(2,1)S(1)}, bf16[1,2,2,256,512]{4,3,2,1,0:T(8,128)(2,1)S(1)}, u32[]{:S(2)}, u32[]{:S(2)}) collective-permute-start(bf16[1,2,2,256,512]{4,3,2,1,0:T(8,128)(2,1)S(1)} %maximum_bitcast_fusion.2), channel_id=1, source_target_pairs={{0,1},{1,0},{2,3},{3,2},{4,5},{5,4},{6,7},{7,6},{8,9},{9,8},{10,11... | collective-permute-start | bytes 3145736 | tf_op jit(solution)/shard_map/down_y_low/ppermute | solution.py:363
  241.1 31.3 %collective-permute-start.47 = (bf16[1280,512]{1,0:T(8,128)(2,1)}, bf16[1280,512]{1,0:T(8,128)(2,1)S(1)}, u32[]{:S(2)}, u32[]{:S(2)}) collective-permute-start(bf16[1280,512]{1,0:T(8,128)(2,1)} %bitcast.45), channel_id=1, source_target_pairs={{0,1},{1,0},{2,3},{3,2},{4,5},{5,4},{6,7},{7,6},{8,9},{9,8},{10,11... | collective-permute-start | bytes 3932168 | tf_op jit(solution)/shard_map/activations_send/ppermute | solution.py:363
  281.0 30.6 %collective-permute-start.51 = (bf16[2,2,2,512,512]{4,3,2,1,0:T(8,128)(2,1)}, bf16[2,2,2,512,512]{4,3,2,1,0:T(8,128)(2,1)}, u32[]{:S(2)}, u32[]{:S(2)}) collective-permute-start(bf16[2,2,2,512,512]{4,3,2,1,0:T(8,128)(2,1)} %up_grad.2), channel_id=1, source_target_pairs={{0,4},{4,0},{1,5},{5,1},{2,6},{6,2},{3,7},{7,3},{8,12},{12,8},{9,1... | collective-permute-start | bytes 12582920 | tf_op jit(solution)/shard_map/up_grad_core/ppermute | solution.py:363
  281.1 30.6 %collective-permute-start.50 = (bf16[2,1,2,256,512]{4,3,2,1,0:T(8,128)(2,1)S(1)}, bf16[2,1,2,256,512]{4,3,2,1,0:T(8,128)(2,1)S(1)}, u32[]{:S(2)}, u32[]{:S(2)}) collective-permute-start(bf16[2,1,2,256,512]{4,3,2,1,0:T(8,128)(2,1)S(1)} %bitcast.151), channel_id=1, source_target_pairs={{0,1},{1,0},{2,3},{3,2},{4,5},{5,4},{6,7},{7,6},{8,9},{9,8},{10,11... | collective-permute-start | bytes 3145736 | tf_op jit(solution)/shard_map/down_grad_first/ppermute | solution.py:363
  282.7 29.0 %collective-permute-start.49 = (bf16[1,2,2,256,512]{4,3,2,1,0:T(8,128)(2,1)S(1)}, bf16[1,2,2,256,512]{4,3,2,1,0:T(8,128)(2,1)}, u32[]{:S(2)}, u32[]{:S(2)}) collective-permute-start(bf16[1,2,2,256,512]{4,3,2,1,0:T(8,128)(2,1)S(1)} %bitcast.150), channel_id=1, source_target_pairs={{0,2},{2,0},{1,3},{3,1},{4,6},{6,4},{5,7},{7,5},{8,10},{10,8},{9,1... | collective-permute-start | bytes 3145736 | tf_op jit(solution)/shard_map/down_grad_first/ppermute | solution.py:363
  327.7 26.8 %collective-permute-start.55 = (bf16[2,1,2,256,512]{4,3,2,1,0:T(8,128)(2,1)S(1)}, bf16[2,1,2,256,512]{4,3,2,1,0:T(8,128)(2,1)S(1)}, u32[]{:S(2)}, u32[]{:S(2)}) collective-permute-start(bf16[2,1,2,256,512]{4,3,2,1,0:T(8,128)(2,1)S(1)} %bitcast.153), channel_id=1, source_target_pairs={{0,1},{1,0},{2,3},{3,2},{4,5},{5,4},{6,7},{7,6},{8,9},{9,8},{10,11... | collective-permute-start | bytes 3145736 | tf_op jit(solution)/shard_map/up_grad_first/ppermute | solution.py:363
  328.1 26.5 %collective-permute-start.54 = (bf16[1,2,2,256,512]{4,3,2,1,0:T(8,128)(2,1)S(1)}, bf16[1,2,2,256,512]{4,3,2,1,0:T(8,128)(2,1)}, u32[]{:S(2)}, u32[]{:S(2)}) collective-permute-start(bf16[1,2,2,256,512]{4,3,2,1,0:T(8,128)(2,1)S(1)} %bitcast.152), channel_id=1, source_target_pairs={{0,2},{2,0},{1,3},{3,1},{4,6},{6,4},{5,7},{7,5},{8,10},{10,8},{9,1... | collective-permute-start | bytes 3145736 | tf_op jit(solution)/shard_map/up_grad_first/ppermute | solution.py:363
  373.5 27.6 %collective-permute-start.64 = (bf16[2,2,4,1,8,8,512]{6,5,4,3,2,1,0:T(8,128)(2,1)S(1)}, bf16[2,2,4,1,8,8,512]{6,5,4,3,2,1,0:T(8,128)(2,1)S(1)}, u32[]{:S(2)}, u32[]{:S(2)}) collective-permute-start(bf16[2,2,4,1,8,8,512]{6,5,4,3,2,1,0:T(8,128)(2,1)S(1)} %get-tuple-element.373), channel_id=1, source_target_pairs={{0,4},{4,0},{1,5},{5,1},{2,6},{6,2},{3,7},{7,3},{8,12},{12,8},{9,1... | collective-permute-start | bytes 3145736 | tf_op jit(solution)/shard_map/out_grad_core/ppermute | solution.py:363
  375.5 25.7 %collective-permute-start.63 = (bf16[1,1,2,256,512]{4,3,2,1,0:T(8,128)(2,1)S(1)}, bf16[1,1,2,256,512]{4,3,2,1,0:T(8,128)(2,1)S(1)}, u32[]{:S(2)}, u32[]{:S(2)}) collective-permute-start(bf16[1,1,2,256,512]{4,3,2,1,0:T(8,128)(2,1)S(1)} %add_convert_fusion.1), channel_id=1, source_target_pairs={{0,16},{8,24},{16,0},{24,8},{1,17},{9,25},{17,1},{25,9},{2,18},{10... | collective-permute-start | bytes 1572872 | tf_op jit(solution)/shard_map/up_grad_z_high/ppermute | solution.py:363
  377.0 24.1 %collective-permute-start.61 = (bf16[1,2,2,3,8,8,512]{6,5,4,3,2,1,0:T(8,128)(2,1)S(1)}, bf16[1,2,2,3,8,8,512]{6,5,4,3,2,1,0:T(8,128)(2,1)S(1)}, u32[]{:S(2)}, u32[]{:S(2)}) collective-permute-start(bf16[1,2,2,3,8,8,512]{6,5,4,3,2,1,0:T(8,128)(2,1)S(1)} %add_convert_fusion), channel_id=1, source_target_pairs={{0,2},{2,0},{1,3},{3,1},{4,6},{6,4},{5,7},{7,5},{8,10},{10,8},{9,1... | collective-permute-start | bytes 2359304 | tf_op jit(solution)/shard_map/qkv_grad_far_x/ppermute | solution.py:363
  428.1 25.4 %collective-permute-start.73 = (bf16[1,1,1,256,512]{4,3,2,1,0:T(8,128)(2,1)}, bf16[1,1,1,256,512]{4,3,2,1,0:T(8,128)(2,1)}, u32[]{:S(2)}, u32[]{:S(2)}) collective-permute-start(bf16[1,1,1,256,512]{4,3,2,1,0:T(8,128)(2,1)} %add_convert_fusion.12), channel_id=1, source_target_pairs={{0,8},{8,0},{16,24},{24,16},{1,9},{9,1},{17,25},{25,17},{2,10},{10... | collective-permute-start | bytes 786440 | tf_op jit(solution)/shard_map/up_grad_z_low/ppermute | solution.py:363
  429.8 23.7 %collective-permute-start.72 = (bf16[1,1,2,1,8,8,512]{6,5,4,3,2,1,0:T(8,128)(2,1)}, bf16[1,1,2,1,8,8,512]{6,5,4,3,2,1,0:T(8,128)(2,1)}, u32[]{:S(2)}, u32[]{:S(2)}) collective-permute-start(bf16[1,1,2,1,8,8,512]{6,5,4,3,2,1,0:T(8,128)(2,1)} %add_convert_fusion.18), channel_id=1, source_target_pairs={{0,2},{2,0},{1,3},{3,1},{4,6},{6,4},{5,7},{7,5},{8,10},{10,8},{9,1... | collective-permute-start | bytes 393224 | tf_op jit(solution)/shard_map/out_grad_x_low/ppermute | solution.py:363
  464.4 30.5 %collective-permute-start.74 = (bf16[1280,512]{1,0:T(8,128)(2,1)}, bf16[1280,512]{1,0:T(8,128)(2,1)S(1)}, u32[]{:S(2)}, u32[]{:S(2)}) collective-permute-start(bf16[1280,512]{1,0:T(8,128)(2,1)} %bitcast.165), channel_id=1, source_target_pairs={{0,1},{1,0},{2,3},{3,2},{4,5},{5,4},{6,7},{7,6},{8,9},{9,8},{10,11... | collective-permute-start | bytes 3932168 | tf_op jit(solution)/shard_map/token_grad_send/ppermute | solution.py:363
  (146 other events, 2159.6 us)

commit v5 on v4

--- a/solution.py
+++ b/solution.py
@@ -1,5 +1,6 @@
 import functools
 import itertools
+import math
 
 import jax
 import jax.numpy as jnp
@@ -77,14 +78,14 @@
 def head_weight(layout, refs):
     if layout is None:
         return refs[1:], lambda: None, lambda i: refs[0][i]
-    places, kinds = layout
+    places, kinds, part = layout
     held, sem = refs[-2:]
     operands = 1 + max(place[0] for place in places)
 
     def copies(kind):
         for operand, index, head, row, lane in places:
-            source = refs[operand].at[index + (kind,)]
-            part, piece, width = source.shape
+            source = refs[operand].at[index + (pl.ds(kind * part, part),)]
+            _, piece, width = source.shape
             target = held.at[kind, pl.ds(head, part), pl.ds(row, piece), pl.ds(lane, width)]
             yield pltpu.make_async_copy(source, target, sem.at[kind])
 
@@ -106,10 +107,20 @@
     return refs[operands:-2], fetch, read
 
 
-def qkv_kernel(layout, x_ref, gain_ref, shift_ref, bias_ref, *refs):
+def token_tile(parts, refs):
+    if parts == 1:
+        return refs[0][...].astype(f32), refs[1:]
+    half = parts // 2
+    near = jnp.concatenate([ref[...] for ref in refs[:half]], axis=1).astype(f32)
+    far = jnp.concatenate([ref[...] for ref in refs[half:parts]], axis=1).astype(f32)
+    return jnp.where(pl.program_id(0) < pl.num_programs(0) // 2, near, far), refs[parts:]
+
+
+def qkv_kernel(layout, parts, gain_ref, shift_ref, bias_ref, *refs):
+    x, refs = token_tile(parts, refs)
     (a_ref, out_ref), fetch, read = head_weight(layout, refs)
     fetch()
-    unit, _ = unit_norm(x_ref[...].astype(f32))
+    unit, _ = unit_norm(x)
     a = (unit * gain_ref[...] + shift_ref[...]).astype(bf16)
     a_ref[...] = a
     for i in range(3):
@@ -188,10 +199,11 @@
         sum_ref[0] = jnp.sum(left.astype(f32), axis=0, keepdims=True)
 
 
-def out_kernel(layout, x_ref, o_ref, bias_ref, gain_ref, shift_ref, *refs):
+def out_kernel(layout, parts, o_ref, bias_ref, gain_ref, shift_ref, *refs):
+    x, refs = token_tile(parts, refs)
     (middle_ref, a_ref), fetch, read = head_weight(layout, refs)
     fetch()
-    middle = x_ref[...].astype(f32) + (matmul(o_ref[...], read(0)) + bias_ref[...])
+    middle = x + (matmul(o_ref[...], read(0)) + bias_ref[...])
     middle_ref[...] = middle
     unit, _ = unit_norm(middle)
     a_ref[...] = (unit * gain_ref[...] + shift_ref[...]).astype(bf16)
@@ -284,7 +296,8 @@
     sum_ref[3:4] += jnp.sum(out_grad, axis=0, keepdims=True)
 
 
-def token_pull_kernel(ncol, layout, near_ref, far_ref, x_ref, grad_ref, gain_ref, *refs):
+def token_pull_kernel(ncol, layout, parts, near_ref, far_ref, grad_ref, gain_ref, *refs):
+    x, refs = token_tile(parts, refs)
     (own_ref, other_ref, sum_ref), fetch, read = head_weight(layout, refs)
     fetch()
 
@@ -298,7 +311,7 @@
         middle = weight.shape[0] // 2
         value = matmul(near_ref[i], weight[:middle]) + matmul(far_ref[i], weight[middle:])
         grad = value if grad is None else grad + value
-    unit, inverse = unit_norm(x_ref[...].astype(f32))
+    unit, inverse = unit_norm(x)
     total = grad_ref[...] + norm_pull(grad, gain_ref[...], unit, inverse)
     width = total.shape[1] // ncol
     own_ref[...] = total[:, :width]
@@ -352,6 +365,15 @@
         sum_ref[0] = jnp.sum(left.astype(f32), axis=0, keepdims=True)
 
 
+def sums_kernel(counts, *refs):
+    in_refs, out_refs = refs[: sum(counts)], refs[sum(counts) :]
+    for n, out_ref in enumerate(out_refs):
+        value = in_refs[sum(counts[:n])][...].astype(f32)
+        for ref in in_refs[sum(counts[:n]) + 1 : sum(counts[: n + 1])]:
+            value = value + ref[...].astype(f32)
+        out_ref[...] = value.astype(bf16)
+
+
 def make_local(nz, ncore, nrow, ncol):
     blocks = ncore * nrow
     sizes = {"z": nz, "core": ncore, "row": nrow, "col": ncol}
@@ -395,12 +417,51 @@
             return parts
 
         def fold(self, held, axis, dim):
-            arrays = self.gate(*[view[0] for view in held])
-            held = [(array, view[1]) for array, view in zip(arrays, held)]
             for bit in [bit for bit in reversed(bits(axis)) if bit < held[0][1][dim][1]]:
-                got = self.move(total([half_of(view, dim, 1) for view in held]).astype(bf16), axis, bit)
+                got = self.move((yield [half_of(view, dim, 1) for view in held]), axis, bit)
                 held = [half_of(view, dim, 0) for view in held] + [view_of(got)]
             return held
+
+        def together(self, *stages):
+            running = []
+            for job, name in stages:
+                stage = getattr(job, name)()
+                running.append((job.name + "_" + name, stage, next(stage)))
+            while running:
+                counts = [len(views) for _, _, views in running]
+                arrays = self.gate(*[view[0] for _, _, views in running for view in views])
+                spans = [view[1] for _, _, views in running for view in views]
+                with jax.named_scope("sums"):
+                    values = sums_of(counts, arrays, spans)
+                waiting = []
+                for (name, stage, _), value in zip(running, values):
+                    with jax.named_scope(name):
+                        try:
+                            waiting.append((name, stage, stage.send(value)))
+                        except StopIteration:
+                            pass
+                running = waiting
+
+    def sums_of(counts, arrays, spans):
+        def spec(array, span):
+            block = tuple(size for _, size in span) + array.shape[3:]
+            index = tuple(start // size for start, size in span) + (0,) * (array.ndim - 3)
+            return pl.BlockSpec(block, lambda t: index)
+
+        firsts = [sum(counts[:n]) for n in range(len(counts))]
+        shapes = [tuple(size for _, size in spans[n]) + arrays[n].shape[3:] for n in firsts]
+        moved = sum(math.prod(size for _, size in span) * math.prod(a.shape[3:]) for a, span in zip(arrays, spans))
+        return call(
+            functools.partial(sums_kernel, counts),
+            (1,),
+            [spec(array, span) for array, span in zip(arrays, spans)],
+            [summed(shape) for shape in shapes],
+            [jax.ShapeDtypeStruct(shape, bf16) for shape in shapes],
+            moved,
+            3 * moved,
+            "sums",
+            vmem=16,
+        )(*arrays)
 
     def joined(parts):
         return parts[0] if len(parts) == 1 else jnp.concatenate(parts)
@@ -422,8 +483,6 @@
         return value
 
     class Gather:
-        together = None
-
         def __init__(self, name, slots, shard):
             self.name, self.slots, self.low = name, slots, [shard[None]]
 
@@ -472,6 +531,9 @@
 
         def x(self):
             self.all_row = self.slots.widen(self.all_col, "row")
+
+        def core_near(self):
+            self.near = [[self.slots.move(p[0], "core", k) for k in range(1, ncore)] for p in (self.low_all, self.high_all)]
 
         def core(self):
             if hasattr(self, "all_row"):
@@ -481,13 +543,14 @@
             self.places, self.pieces = [], []
             for half, parts in lists:
                 parts = self.slots.gate(*parts)
-                if half == self.together:
-                    parts = [joined(list(parts))]
                 for k in range(ncore):
                     first = 0
-                    for values in parts:
+                    for n, values in enumerate(parts):
                         self.places.append((k, half, first))
-                        self.pieces.append(self.slots.move(values, "core", k) if k else values)
+                        if k and n == 0 and hasattr(self, "near"):
+                            self.pieces.append(self.near[half][k - 1])
+                        else:
+                            self.pieces.append(self.slots.move(values, "core", k) if k else values)
                         first += values.shape[0]
 
     class Scatter:
@@ -517,29 +580,35 @@
             self.low = self.first_fold(by_col, "col", 1)
 
         def x_high(self):
-            self.high = self.slots.fold(self.high, "row", 0)
+            self.high = yield from self.slots.fold(self.high, "row", 0)
 
         def y_low(self):
-            self.low = self.slots.fold(self.low, "col", 1)
+            self.low = yield from self.slots.fold(self.low, "col", 1)
 
         def y_high(self):
-            self.high = self.slots.fold(self.high, "col", 1)
+            self.high = yield from self.slots.fold(self.high, "col", 1)
 
         def x_low(self):
-            self.low = self.slots.fold(self.low, "row", 0)
+            self.low = yield from self.slots.fold(self.low, "row", 0)
 
         def z_high(self):
-            arrays = self.slots.gate(*[view[0] for view in self.high])
-            value = total([(array, view[1]) for array, view in zip(arrays, self.high)])
-            self.low = self.low + [view_of(self.slots.move(value.astype(bf16), "z", nz // 2))]
+            value = yield self.high
+            self.low = self.low + [view_of(self.slots.move(value, "z", nz // 2))]
 
         def z_low(self):
-            arrays = self.slots.gate(*[view[0] for view in self.low])
-            held = [(array, view[1]) for array, view in zip(arrays, self.low)]
+            held = self.low
             for bit in reversed(bits("z")[:-1]):
-                got = self.slots.move(total([half_of(view, 2, 1) for view in held]).astype(bf16), "z", bit)
-                held = [half_of(view, 2, 0) for view in held] + [view_of(got)]
+                value = yield [half_of(view, 2, 1) for view in held]
+                held = [half_of(view, 2, 0) for view in held] + [view_of(self.slots.move(value, "z", bit))]
             self.low = held
+
+        def far_high(self):
+            value = yield self.high
+            self.got_high = view_of(self.slots.move(value, "row", nrow // 2))
+
+        def far_low(self):
+            value = yield self.low
+            self.got_low = view_of(self.slots.move(value, "row", nrow // 2))
 
         def result(self):
             arrays = self.slots.gate(*[view[0] for view in self.low])
@@ -547,13 +616,16 @@
 
     class TokensIn:
         def __init__(self, name, slots, values):
-            self.name, self.slots, self.parts, self.blocks = name, slots, [], []
+            self.name, self.slots, self.values, self.parts, self.blocks = name, slots, values, [], {}
+
+        def slices(self, which):
+            (values,) = self.slots.gate(self.values)
             rows = values.shape[0] // ncol
             here = lax.axis_index("col")
             size = rows // 2
-            for which in range(2):
-                starts = [(here ^ k) * rows + which * size for k in range(ncol)]
-                self.blocks.append([lax.dynamic_slice_in_dim(values, start, size, 0) for start in starts])
+            starts = [(here ^ k) * rows + which * size for k in range(ncol)]
+            self.blocks[which] = [lax.dynamic_slice_in_dim(values, start, size, 0) for start in starts]
+            self.slots.note(*self.blocks[which])
 
         def step(self, which):
             own, *sent = self.blocks[which]
@@ -572,6 +644,18 @@
             rows = [jnp.concatenate(flat[i : i + count], axis=1) for i in range(0, len(flat), count)]
             return jnp.concatenate(rows)
 
+        def operands(self):
+            size = self.parts[0][0].shape[0]
+            if size % LEN:
+                values = self.end()
+                return [values], [pl.BlockSpec((LEN, values.shape[1]), lambda t: (t, 0))]
+            half = size // LEN
+            values = list(self.slots.gate(*[part for parts in self.parts for part in parts]))
+            shape = (LEN, values[0].shape[1])
+            near = pl.BlockSpec(shape, lambda t: (jnp.minimum(t, half - 1), 0))
+            far = pl.BlockSpec(shape, lambda t: (jnp.maximum(t - half, 0), 0))
+            return values, [near] * ncol + [far] * ncol
+
     def do(job, *stages):
         for stage in stages:
             with jax.named_scope(job.name + "_" + stage):
@@ -581,14 +665,19 @@
         def __init__(self, name, slots, own, other):
             self.name, self.slots, self.own, self.other = name, slots, own, other
 
+        @staticmethod
+        def space(slots, rows, width, dtype):
+            zeros = lax.optimization_barrier(jnp.zeros((rows * ncol, width), dtype))
+            slots.note(zeros)
+            return zeros
+
         def send(self):
             self.blocks = [self.slots.send(self.other[k - 1], "col", k) for k in range(1, ncol)]
 
-        def end(self):
+        def end(self, result):
             rows = self.own.shape[0]
             here = lax.axis_index("col")
             first, *rest = self.slots.gate(self.own, *self.blocks)
-            result = jnp.zeros((rows * ncol, self.own.shape[1]), self.own.dtype)
             result = lax.dynamic_update_slice_in_dim(result, first, here * rows, 0)
             for k, block in enumerate(rest):
                 result = lax.dynamic_update_slice_in_dim(
@@ -629,53 +718,62 @@
             return pl.BlockSpec(shape, index or (lambda t: (t,) + (0,) * (len(shape) - 1)))
 
         slots = Slots()
-        q = Gather("qkv", slots, qkv_weight.astype(bf16))
-        o = Gather("out", slots, out_weight[None].astype(bf16))
+        q = Gather("qkv", slots, qkv_weight.reshape(3 * part, piece, width).astype(bf16))
+        o = Gather("out", slots, out_weight.astype(bf16))
         u = Gather("up", slots, up_weight.astype(bf16))
         d = Gather("down", slots, down_weight.astype(bf16))
         tok = TokensIn("tokens", slots, tokens)
         cot = TokensIn("cotangent", slots, cotangent)
+        vectors = jnp.stack([first_gain, first_shift, second_gain, second_shift, out_bias, down_bias])
+
         small = [jnp.concatenate([qkv_bias.reshape(-1), up_bias]).astype(bf16)[None]]
-        vectors = jnp.stack([first_gain, first_shift, second_gain, second_shift, out_bias, down_bias])
-
+        features = jnp.concatenate([vectors.reshape(-1), key_mask.reshape(-1).astype(f32)])
+        tok.slices(0)
         do(q, "z_all")
         do(tok, "first")
-        vectors = slots.widen([vectors], "col")
-        slots.advance()
+        features = slots.widen([features], "col")
+        slots.advance()
+        spaces = [TokensOut.space(slots, count, width, dtype) for dtype in (bf16, f32)]
         do(q, "x_low", "y_high")
         do(o, "z_low")
         do(u, "z_low")
         small = slots.widen(small, "z", False)
+        small = slots.widen(small, "row")
+        tok.slices(1)
         slots.advance()
         do(q, "y_low", "x_high")
         do(o, "z_high")
-        do(u, "z_high_first")
-        small = slots.widen(small, "row")
-        nearby = slots.widen([key_mask], "col")
+        do(u, "z_high")
+        do(tok, "second")
+        small = slots.widen(small, "core")
         slots.advance()
         do(q, "core")
-        do(u, "z_high_second")
-        do(tok, "second")
         do(o, "y")
-        small = slots.widen(small, "core")
-        slots.advance()
-        inputs = tok.end()
-        vectors = jnp.transpose(joined(list(slots.gate(*vectors))), (1, 0, 2)).reshape(6, dim)
-        gain_one, shift_one, gain_two, shift_two, out_offset, down_offset = [vectors[i : i + 1] for i in range(6)]
+        do(d, "z_low")
+        cot.slices(0)
         small_all = joined(list(slots.gate(*small))).astype(f32)
         qkv_count = qkv_bias.size
         qkv_offset = small_all[..., :qkv_count].reshape(ncore, nrow, nz, 2, part, piece)
         qkv_offset = jnp.transpose(qkv_offset, (3, 1, 4, 0, 2, 5)).reshape(2, flat)
         up_offset = small_all[..., qkv_count:].reshape(1, hidden)
+        features = joined(list(slots.gate(*features)))
+        vectors, nearby = features[:, : vectors.size], features[:, vectors.size :]
+        vectors = jnp.transpose(vectors.reshape(ncol, 6, width), (1, 0, 2)).reshape(6, dim)
+        slots.note(vectors, qkv_offset, up_offset)
+        slots.advance()
+        inputs, input_specs = tok.operands()
+        parts = len(inputs)
+        gain_one, shift_one, gain_two, shift_two, out_offset, down_offset = [vectors[i : i + 1] for i in range(6)]
+
         here = lax.axis_index("col")
-        nearby = joined(nearby)
+        nearby = nearby.reshape((ncol,) + key_mask.shape)
         masks = jnp.zeros_like(nearby)
         for k in range(ncol):
             masks = lax.dynamic_update_slice_in_dim(masks, nearby[k : k + 1], here ^ k, 0)
         masks = masks.reshape(-1, key_mask.shape[1])
         first_seq = (lax.axis_index("row") * ncol + here) * seqs
         masks = lax.dynamic_slice_in_dim(masks, first_seq, seqs, 0)
-        visible = jnp.concatenate([jnp.ones((seqs, BUF), jnp.int32), masks], axis=1)
+        visible = jnp.concatenate([jnp.ones((seqs, BUF), f32), masks], axis=1)
 
         def head_operands(w, kinds):
             half = nz // 2
@@ -690,10 +788,11 @@
             if piece % 8 == 0:
                 specs = [pl.BlockSpec(memory_space=pl.ANY)] * len(w.pieces)
                 scratch = [pltpu.VMEM((kinds, heads, HD, dim), bf16), pltpu.SemaphoreType.DMA((kinds,))]
-                return w.pieces, specs, scratch, (tuple(places), kinds)
+                return w.pieces, specs, scratch, (tuple(places), kinds, part)
             matrix = jnp.zeros((kinds, heads, HD, dim), bf16)
             for n, index, head, row, lane in places:
-                matrix = lax.dynamic_update_slice(matrix, w.pieces[n][index], (0, head, row, lane))
+                block = w.pieces[n][index][: kinds * part].reshape(kinds, part, piece, width)
+                matrix = lax.dynamic_update_slice(matrix, block, (0, head, row, lane))
             return [matrix.reshape(kinds, flat, dim)], [whole((kinds, flat, dim))], [], None
 
         qkv_ops, qkv_specs, qkv_scratch, qkv_layout = head_operands(q, 3)
@@ -715,24 +814,23 @@
 
         do(u, "x_low", "y_high")
         do(o, "x")
-        do(d, "z_low")
+        do(d, "z_high")
         do(cot, "first")
         normed, qkv = call(
-            functools.partial(qkv_kernel, qkv_layout),
+            functools.partial(qkv_kernel, qkv_layout, parts),
             (seqs,),
-            [tokens_spec, vector_spec, vector_spec, whole((2, flat))] + qkv_specs,
+            [vector_spec, vector_spec, whole((2, flat))] + input_specs + qkv_specs,
             [tokens_spec, three],
             [out_of(count, dim), out_of(3, count, flat)],
             6 * moved * flat,
             6 * flat * dim + 10 * moved,
             "qkv",
             scratch=qkv_scratch,
-        )(inputs, gain_one, shift_one, qkv_offset, *qkv_ops)
+        )(gain_one, shift_one, qkv_offset, *inputs, *qkv_ops)
         slots.note(qkv)
         slots.advance()
 
-        do(u, "y_low", "x_high")
-        do(d, "z_high")
+        do(u, "y_low", "x_high", "core_near")
         do(o, "core")
         quads = flat // QUAD
         step_lanes = STEP * QUAD
@@ -756,25 +854,25 @@
         slots.note(attended)
         slots.advance()
 
-        u.together = 0
         do(u, "core")
         do(d, "x_low", "y_high")
         out_ops, out_specs, out_scratch, out_layout = head_operands(o, 1)
         middle, normed_two = call(
-            functools.partial(out_kernel, out_layout),
+            functools.partial(out_kernel, out_layout, parts),
             (seqs,),
-            [tokens_spec, tile((LEN, flat)), vector_spec, vector_spec, vector_spec] + out_specs,
+            [tile((LEN, flat)), vector_spec, vector_spec, vector_spec] + input_specs + out_specs,
             [tokens_spec, tokens_spec],
             [out_of(count, dim, dtype=f32), out_of(count, dim)],
             2 * moved * flat,
             2 * flat * dim + 10 * moved,
             "out",
             scratch=out_scratch,
-        )(inputs, slots.gate(attended)[0], out_offset, gain_two, shift_two, *out_ops)
+        )(slots.gate(attended)[0], out_offset, gain_two, shift_two, *inputs, *out_ops)
         slots.note(normed_two)
         slots.advance()
 
-        do(d, "y_low", "x_high")
+        do(d, "y_low", "x_high", "core_near")
+        cot.slices(1)
         up_ops, up_specs, up_dims = ffn_operands(u)
         hid, slope = call(
             functools.partial(up_kernel, up_dims),
@@ -952,64 +1050,54 @@
             scratch=out_scratch,
         )(slots.gate(upward_grad)[0], middle, grad_low, gain_two, *up_ops, *out_ops)
         slots.note(attended_grad)
-        activations = activations.end()
+        activations = activations.end(spaces[0])
         slots.note(activations)
         slots.advance()
 
-        do(dg, "y_high", "x_low")
+        slots.together((dg, "y_high"), (dg, "x_low"))
+        out_sums, _ = head_grad(slots.gate(attended)[0][None], branch_low, 0, "out_grad")
         up_low, up_high = ffn_kept(slots.gate(upward_grad)[0], normed_two, got, "up_grad")
         slots.advance()
 
         with jax.named_scope("up_grad_first"):
             ug.x_high_first(up_high)
             ug.y_low_first(up_low)
-        do(dg, "z_high")
+        slots.together((dg, "z_high"))
+        out_held = core_fold("out_grad", out_sums)
         far, far_sums, far_own = pull(nrow // 2, nrow // 2)
         slots.note(*far_sums)
         slots.advance()
 
         far_held = core_fold("qkv_grad_far", far_sums)
-        do(ug, "y_high", "x_low")
-        do(dg, "z_low")
-        out_sums, _ = head_grad(slots.gate(attended)[0][None], branch_low, 0, "out_grad")
+        slots.together((ug, "y_high"), (ug, "x_low"))
         slots.advance()
 
         far_low = Scatter("qkv_grad_far", slots)
         far_low.halve(far_held)
-        with jax.named_scope("qkv_grad_far_x"):
-            arrays = slots.gate(*[view[0] for view in far_low.high])
-            value = total([(array, view[1]) for array, view in zip(arrays, far_low.high)])
-            got_high = slots.move(value.astype(bf16), "row", nrow // 2)
-        do(far_low, "y_low")
-        do(ug, "z_high")
-        out_held = core_fold("out_grad", out_sums)
+        og.halve(out_held)
+        slots.together(
+            (far_low, "far_high"), (far_low, "y_low"), (ug, "z_high"), (og, "x_high"), (og, "y_low")
+        )
         near, near_sums, near_own = pull(0, nrow // 2)
         slots.note(*near_sums)
         slots.advance()
 
         near_held = core_fold("qkv_grad_near", near_sums)
-        with jax.named_scope("qkv_grad_far_x"):
-            arrays = slots.gate(*[view[0] for view in far_low.low])
-            value = total([(array, view[1]) for array, view in zip(arrays, far_low.low)])
-            got_low = slots.move(value.astype(bf16), "row", nrow // 2)
-        og.halve(out_held)
-        do(og, "x_high", "y_low")
+        slots.together((far_low, "far_low"), (og, "y_high"), (og, "x_low"), (dg, "z_low"))
+        slots.advance()
+
+        qg.halve(near_held)
+        qg.high = qg.high + [far_low.got_high]
+        if nrow > 2:
+            slots.together((qg, "x_high"))
+        slots.together((qg, "y_high"), (qg, "y_low"), (og, "z_high"), (ug, "z_low"))
         down_grad = dg.result()
-        slots.note(down_grad)
-        slots.advance()
-
-        qg.halve(near_held)
-        qg.high = qg.high + [view_of(got_high)]
-        if nrow > 2:
-            do(qg, "x_high")
-        do(qg, "y_high", "y_low")
-        do(og, "y_high", "x_low")
-        do(ug, "z_low")
         own_grad, other_grad, sums_one = call(
-            functools.partial(token_pull_kernel, ncol, qkv_layout),
+            functools.partial(token_pull_kernel, ncol, qkv_layout, parts),
             (seqs,),
             [pl.BlockSpec((3, LEN, flat // 2), lambda t: (0, t, 0))] * 2
-            + [tokens_spec, tokens_spec, vector_spec]
+            + [tokens_spec, vector_spec]
+            + input_specs
             + qkv_specs,
             [own_spec, other_spec, summed((2, dim))],
             [
@@ -1021,7 +1109,7 @@
             6 * flat * dim + 14 * moved,
             "token_pull",
             scratch=qkv_scratch,
-        )(slots.gate(near)[0], far, inputs, middle_grad, gain_one, *qkv_ops)
+        )(slots.gate(near)[0], far, middle_grad, gain_one, *inputs, *qkv_ops)
         slots.note(own_grad)
         slots.advance()
 
@@ -1048,20 +1136,18 @@
 
         token_grad = TokensOut("token_grad", slots, own_grad, other_grad)
         do(token_grad, "send")
-        qg.low = qg.low + [view_of(got_low)]
+        qg.low = qg.low + [far_low.got_low]
         if nrow > 2:
-            do(qg, "x_low")
-        do(qg, "z_high")
-        do(og, "z_high")
+            slots.together((qg, "x_low"))
+        slots.together((qg, "z_high"), (og, "z_low"))
         with jax.named_scope("small_sums"):
             small_sums()
         up_grad = ug.result()
         slots.note(up_grad)
         slots.advance()
 
-        do(qg, "z_low")
-        do(og, "z_low")
-        token_grad = token_grad.end()
+        slots.together((qg, "z_low"))
+        token_grad = token_grad.end(spaces[1])
         out_grad, qkv_grad = og.result(), qg.result()
 
         pack = packs[0]

time: 511 us -> 487 us (0.953)
  other arithmetic: 52.6 us -> 22.7 us
  waiting for transfers between devices: 121 us -> 100 us
  Pallas kernels: 222 us -> 237 us
  local copies, waits for them, and re-layouts: 30.4 us -> 44.3 us
    convert_element_type x21 -> x1, other arithmetic: 26.2 us -> 1.08 us  [local(): qkv_weight.reshape(3 * part, piece, width).astype(bf16)]
    ppermute x84 -> x83, waiting for transfers between devices: 121 us -> 100 us  [exchange(): lax.ppermute(values, axis, [(i, i ^ bit) for i in range(sizes[axis])])]
    pallas_call x3 -> x11, Pallas kernels: 40.5 us -> 54.7 us  [the longest x1 16.9 us: local(): call(functools.partial(token_pull_kernel, ncol, qkv_layout, parts), (seqs...]
    unnamed x182 -> x195, local copies, waits for them, and re-layouts: 13.7 us -> 18.5 us
    broadcast_in_dim x14 -> x12, other arithmetic: 10.4 us -> 7.16 us  [widen(): parts = [joined(parts)[None]]]
    ppermute x84 -> x83, starting transfers between devices: 77.9 us -> 75.4 us  [exchange(): lax.ppermute(values, axis, [(i, i ^ bit) for i in range(sizes[axis])])]
  transfers between devices with their start and end apart: 84 -> 83, of which waited for: 35 -> 26; matrix products, arithmetic and copies ran while one was open for 11% -> 9% of each run, Pallas kernels for 40% -> 44%
where the time goes in v5:
time: 487 us; the launch traced here: 482 us
  Pallas kernels  237 us (49%)
  waiting for transfers between devices  100 us (21%)
  starting transfers between devices  75.4 us (15%)
  local copies, waits for them, and re-layouts  44.3 us (9%)
  other arithmetic  22.7 us (5%)
    ppermute x83, waiting for transfers between devices, exchange(): lax.ppermute(values, axis, [(i, i ^ bit) for i in range(sizes[axis])])  100 us
    ppermute x83, starting transfers between devices, exchange(): lax.ppermute(values, axis, [(i, i ^ bit) for i in range(sizes[axis])])  75.4 us
    pallas_call x2, Pallas kernels, pull(): call(functools.partial(attend_pull_kernel, seqs, (ncore, ncol, nz, part,...  37.8 us
    pallas_call x1, Pallas kernels, local(): call(functools.partial(middle_pull_kernel, up_dims, out_layout), (seqs,),...  24.7 us
    pallas_call x1, Pallas kernels, local(): call(functools.partial(up_kernel, up_dims), (seqs,), [tokens_spec, whole(...  24.7 us
    pallas_call x2, Pallas kernels, ffn_kept(): call(functools.partial(ffn_kept_kernel, ncol, nrow), (2, nrow), [pl.Block...  19.5 us
    pallas_call x2, Pallas kernels, ffn_sent(): call(functools.partial(ffn_sent_kernel, ncol), (2, nrow), [pl.BlockSpec((...  18.6 us
    unnamed x195, local copies, waits for them, and re-layouts  18.5 us
  transfers between devices with their start and end apart: 83, of which 26 were waited for; matrix products, arithmetic and copies ran while one was open for 9% of the time, Pallas kernels for 44%

profile of v5, /device:TPU:0, one launch (start us, length us, event | category | flops | bytes accessed | tf_op | source)
XLA Modules:
  0.0 482.0 jit_solution(4944831383356210055)
XLA Ops:
  11.4 13.9 %collective-permute-done = f32[1,5120]{1,0:T(1,128)S(1)} collective-permute-done((f32[1,5120]{1,0:T(1,128)S(1)}, f32[1,5120]{1,0:T(1,128)S(1)}, u32[]{:S(2)}, u32[]{:S(2)}) %collective-permute-start) | collective-permute-done | bytes 20512 | tf_op jit(solution)/shard_map/ppermute | solution.py:385
  51.5 21.7 %collective-permute-done.14 = bf16[2,8,8,512]{3,2,1,0:T(8,128)(2,1)S(1)} collective-permute-done((bf16[2,8,8,512]{3,2,1,0:T(8,128)(2,1)S(1)}, bf16[2,8,8,512]{3,2,1,0:T(8,128)(2,1)S(1)}, u32[]{:S(2)}, u32[]{:S(2)}) %collective-permute-start.14) | collective-permute-done | bytes 131104 | tf_op jit(solution)/shard_map/out_z_high/ppermute | solution.py:385
  76.2 3.5 collective-permute-done.23
  84.0 3.4 collective-permute-done.22
  96.1 15.9 %qkv.1 = (bf16[1280,1024]{1,0:T(8,128)(2,1)}, bf16[3,1280,1024]{2,1,0:T(8,128)(2,1)}) custom-call(f32[1,1024]{1,0:T(1,128)S(1)} %bitcast.132, f32[1,1024]{1,0:T(1,128)S(1)} %bitcast.136, f32[2,1024]{1,0:T(2,128)S(1)} %reshape.220.bias_ref, bf16[640,512]{1,0:T(8,128)(2,1)S(1)} %get-tuple-element.287.refs_0_, bf16[640,512]{1,0:T(8,128)(2,1)S(1)} %copy-done.36, ...), custom_call_target="tpu_custom_call" | custom-call | flops 8053063680 | bytes 19398656 | tf_op jit(solution)/shard_map/qkv/pallas_call | solution.py:819
  112.1 3.9 collective-permute-done.24
  121.4 18.3 %attend.1 = (bf16[1280,1024]{1,0:T(8,128)(2,1)S(1)}, bf16[4,4,320,1280]{3,2,1,0:T(8,128)(2,1)}) custom-call(bf16[3,1280,1024]{2,1,0:T(8,128)(2,1)} %get-tuple-element.299.qkv_ref, f32[4,320,1]{2,1,0:T(8,128)S(1)} %copy.31.mask_ref), custom_call_target="tpu_custom_call" | custom-call | flops 6710886400 | bytes 23592960 | tf_op jit(solution)/shard_map/attend/pallas_call | solution.py:838
  146.0 9.0 %out.1 = (f32[1280,1024]{1,0:T(8,128)}, bf16[1280,1024]{1,0:T(8,128)(2,1)}) custom-call(bf16[1280,1024]{1,0:T(8,128)(2,1)} %copy-done.48, f32[1,1024]{1,0:T(1,128)S(1)} %bitcast.138, f32[1,1024]{1,0:T(1,128)S(1)} %bitcast.134, f32[1,1024]{1,0:T(1,128)S(1)} %bitcast.139, bf16[640,512]{1,0:T(8,128)(2,1)S(1)} %get-tuple-element.287.refs_0_, ...), custom_call_target="tpu_custom_call" | custom-call | flops 2684354560 | bytes 15204352 | tf_op jit(solution)/shard_map/out/pallas_call | solution.py:860
  160.7 24.7 %up.1 = (bf16[1280,4096]{1,0:T(8,128)(2,1)}, bf16[1280,4096]{1,0:T(8,128)(2,1)}) custom-call(bf16[1280,1024]{1,0:T(8,128)(2,1)} %get-tuple-element.313.a_ref.r_ref, f32[1,4096]{1,0:T(1,128)S(1)} %reshape.222.bias_ref, bf16[1,2,512,512]{3,2,1,0:T(8,128)(2,1)S(1)} %bitcast.126, bf16[1,2,512,512]{3,2,1,0:T(8,128)(2,1)} %bitcast.32.refs_1_, ...), custom_call_target="tpu_custom_call" | custom-call | flops 42949672960 | bytes 29360128 | tf_op jit(solution)/shard_map/up/pallas_call | solution.py:877
  191.0 15.6 %down.1 = (bf16[1280,512]{1,0:T(8,128)(2,1)}, bf16[1,1280,512]{2,1,0:T(8,128)(2,1)}) custom-call(bf16[1280,4096]{1,0:T(8,128)(2,1)} %get-tuple-element.331.hid_ref.l_ref, f32[1280,1024]{1,0:T(8,128)} %get-tuple-element.317.middle_ref, f32[1,1024]{1,0:T(1,128)S(1)} %bitcast.137, bf16[1,2,512,512]{3,2,1,0:T(8,128)(2,1)S(1)} %bitcast.130, ...), custom_call_target="tpu_custom_call" | custom-call | flops 10737418240 | bytes 26738688 | tf_op jit(solution)/shard_map/down/pallas_call | solution.py:998
  207.1 9.7 %down_grad.2 = bf16[2,2,2,512,512]{4,3,2,1,0:T(8,128)(2,1)} custom-call(bf16[1280,4096]{1,0:T(8,128)(2,1)} %get-tuple-element.331.hid_ref.l_ref, bf16[1280,1024]{1,0:T(8,128)(2,1)S(1)} %maximum_maximum_fusion.r_ref.g_ref), custom_call_target="tpu_custom_call" | custom-call | flops 5368709120 | bytes 12058624 | tf_op jit(solution)/shard_map/down_grad/pallas_call | solution.py:891
  218.4 17.5 %hidden_pull.1 = (bf16[1280,4096]{1,0:T(8,128)(2,1)}, f32[1,4096]{1,0:T(1,128)S(1)}) custom-call(bf16[1280,1024]{1,0:T(8,128)(2,1)} %copy-done.13, bf16[1280,4096]{1,0:T(8,128)(2,1)} %get-tuple-element.337.slope_ref, bf16[1,2,512,512]{3,2,1,0:T(8,128)(2,1)S(1)} %bitcast.131, bf16[1,2,512,512]{3,2,1,0:T(8,128)(2,1)S(1)} %bitcast.143, ...), custom_call_target="tpu_custom_call" | custom-call | flops 10737418240 | bytes 29360128 | tf_op jit(solution)/shard_map/hidden_pull/pallas_call | solution.py:1017
  235.9 9.4 %down_grad.3 = (bf16[2,512,512]{2,1,0:T(8,128)(2,1)S(1)}, bf16[2,512,512]{2,1,0:T(8,128)(2,1)S(1)}, bf16[2,512,512]{2,1,0:T(8,128)(2,1)S(1)}, bf16[2,512,512]{2,1,0:T(8,128)(2,1)S(1)}) custom-call(bf16[1280,4096]{1,0:T(8,128)(2,1)} %get-tuple-element.331.hid_ref.l_ref, bf16[1280,1024]{1,0:T(8,128)(2,1)} %copy-done.13, ...), custom_call_target="tpu_custom_call" | custom-call | flops 5368709120 | bytes 16777216 | tf_op jit(solution)/shard_map/down_grad/pallas_call | solution.py:907
  247.9 8.9 %up_grad.2 = bf16[2,2,2,512,512]{4,3,2,1,0:T(8,128)(2,1)} custom-call(bf16[1280,4096]{1,0:T(8,128)(2,1)} %get-tuple-element.361.du_ref.l_ref, bf16[1280,1024]{1,0:T(8,128)(2,1)S(1)} %copy-done.50), custom_call_target="tpu_custom_call" | custom-call | flops 5368709120 | bytes 12058624 | tf_op jit(solution)/shard_map/up_grad/pallas_call | solution.py:891
  263.3 24.7 %middle_pull.1 = (f32[1280,1024]{1,0:T(8,128)}, bf16[1280,1024]{1,0:T(8,128)(2,1)}, bf16[1280,1024]{1,0:T(8,128)(2,1)}, f32[4,1024]{1,0:T(4,128)S(1)}) custom-call(bf16[1280,4096]{1,0:T(8,128)(2,1)} %get-tuple-element.361.du_ref.l_ref, f32[1280,1024]{1,0:T(8,128)} %get-tuple-element.317.middle_ref, bf16[1280,1024]{1,0:T(8,128)(2,1)} %copy-done.13, ...), custom_call_target="tpu_custom_call" | custom-call | flops 13421772800 | bytes 37224448 | tf_op jit(solution)/shard_map/middle_pull/pallas_call | solution.py:1036
  290.1 5.7 %out_grad.1 = (bf16[2,2,4,1,8,8,512]{6,5,4,3,2,1,0:T(8,128)(2,1)S(1)}, bf16[2,2,4,1,8,8,512]{6,5,4,3,2,1,0:T(8,128)(2,1)}) custom-call(bf16[1,1280,1024]{2,1,0:T(8,128)(2,1)S(1)} %bitcast.151, bf16[1280,1024]{1,0:T(8,128)(2,1)} %get-tuple-element.359.r_ref), custom_call_target="tpu_custom_call" | custom-call | flops 2684354560 | bytes 7340032 | tf_op jit(solution)/shard_map/out_grad/pallas_call | solution.py:929
  295.8 10.1 %up_grad.3 = (bf16[2,512,512]{2,1,0:T(8,128)(2,1)S(1)}, bf16[2,512,512]{2,1,0:T(8,128)(2,1)}, bf16[2,512,512]{2,1,0:T(8,128)(2,1)S(1)}, bf16[2,512,512]{2,1,0:T(8,128)(2,1)S(1)}) custom-call(bf16[1280,4096]{1,0:T(8,128)(2,1)} %get-tuple-element.361.du_ref.l_ref, bf16[1280,1024]{1,0:T(8,128)(2,1)} %get-tuple-element.313.a_ref.r_ref, ...), custom_call_target="tpu_custom_call" | custom-call | flops 5368709120 | bytes 16777216 | tf_op jit(solution)/shard_map/up_grad/pallas_call | solution.py:907
  310.4 18.9 %attend_pull.2 = (bf16[3,1280,512]{2,1,0:T(8,128)(2,1)}, bf16[1,2,4,3,8,8,512]{6,5,4,3,2,1,0:T(8,128)(2,1)S(1)}, bf16[1,2,4,3,8,8,512]{6,5,4,3,2,1,0:T(8,128)(2,1)S(1)}, f32[3,1,512]{2,1,0:T(1,128)S(1)}) custom-call(bf16[3,1280,1024]{2,1,0:T(8,128)(2,1)} %get-tuple-element.299.qkv_ref, bf16[4,4,320,1280]{3,2,1,0:T(8,128)(2,1)} %get-tuple-element.342.probs_ref, ...), custom_call_target="tpu_custom_call" | custom-call | flops 10317987840 | bytes 9175040 | tf_op jit(solution)/shard_map/attend_pull/pallas_call | solution.py:972
  330.5 4.0 collective-permute-done.55.refs_12_
  338.1 12.2 %collective-permute-done.58.refs_6_ = bf16[1,1,2,256,512]{4,3,2,1,0:T(8,128)(2,1)S(1)} collective-permute-done((bf16[1,1,2,256,512]{4,3,2,1,0:T(8,128)(2,1)S(1)}, bf16[1,1,2,256,512]{4,3,2,1,0:T(8,128)(2,1)S(1)}, u32[]{:S(2)}, u32[]{:S(2)}) %collective-permute-start.58) | collective-permute-done | bytes 524320 | tf_op jit(solution)/shard_map/up_grad_y_high/ppermute | solution.py:385
  361.4 18.9 %attend_pull.3 = (bf16[3,1280,512]{2,1,0:T(8,128)(2,1)}, bf16[1,2,4,3,8,8,512]{6,5,4,3,2,1,0:T(8,128)(2,1)S(1)}, bf16[1,2,4,3,8,8,512]{6,5,4,3,2,1,0:T(8,128)(2,1)}, f32[3,1,512]{2,1,0:T(1,128)S(1)}) custom-call(bf16[3,1280,1024]{2,1,0:T(8,128)(2,1)} %get-tuple-element.299.qkv_ref, bf16[4,4,320,1280]{3,2,1,0:T(8,128)(2,1)} %get-tuple-element.342.probs_ref, ...), custom_call_target="tpu_custom_call" | custom-call | flops 10317987840 | bytes 9175040 | tf_op jit(solution)/shard_map/attend_pull/pallas_call | solution.py:972
  413.3 16.9 %token_pull.1 = (f32[1280,512]{1,0:T(8,128)}, bf16[1,1280,512]{2,1,0:T(8,128)(2,1)}, f32[2,1024]{1,0:T(2,128)S(1)}) custom-call(bf16[3,1280,512]{2,1,0:T(8,128)(2,1)} %get-tuple-element.425.near_ref, bf16[3,1280,512]{2,1,0:T(8,128)(2,1)} %get-tuple-element.376.far_ref, f32[1280,1024]{1,0:T(8,128)} %get-tuple-element.426.grad_ref, f32[1,1024]{1,0:T(1,128)S(1)} %bitcast.133, ...), custom_call_target="tpu_custom_call" | custom-call | flops 8053063680 | bytes 24641536 | tf_op jit(solution)/shard_map/token_pull/pallas_call | solution.py:1095
  454.5 5.1 %collective-permute-done.81 = f32[3456]{0:T(1024)S(1)} collective-permute-done((f32[3456]{0:T(1024)S(1)}, f32[3456]{0:T(1024)S(1)}, u32[]{:S(2)}, u32[]{:S(2)}) %collective-permute-start.81) | collective-permute-done | bytes 13856 | tf_op jit(solution)/shard_map/small_sums/ppermute | solution.py:385
  461.4 6.2 %collective-permute-done.75.refs_4_ = bf16[1,1,2,3,8,8,512]{6,5,4,3,2,1,0:T(8,128)(2,1)} collective-permute-done((bf16[1,1,2,3,8,8,512]{6,5,4,3,2,1,0:T(8,128)(2,1)}, bf16[1,1,2,3,8,8,512]{6,5,4,3,2,1,0:T(8,128)(2,1)}, u32[]{:S(2)}, u32[]{:S(2)}) %collective-permute-start.75) | collective-permute-done | bytes 393248 | tf_op jit(solution)/shard_map/qkv_grad_z_high/ppermute | solution.py:385
  (454 shorter events, 181.7 us)
Async XLA Ops:
  40.2 33.1 %collective-permute-start.16 = (bf16[640,512]{1,0:T(8,128)(2,1)S(1)}, bf16[640,512]{1,0:T(8,128)(2,1)S(1)}, u32[]{:S(2)}, u32[]{:S(2)}) collective-permute-start(bf16[640,512]{1,0:T(8,128)(2,1)S(1)} %get-tuple-element.272), channel_id=1, source_target_pairs={{0,1},{1,0},{2,3},{3,2},{4,5},{5,4},{6,7},{7,6},{8,9},{9,8},{10,11... | collective-permute-start | bytes 1966088 | tf_op jit(solution)/shard_map/tokens_second/ppermute | solution.py:385
  42.7 30.5 %collective-permute-start.13 = (bf16[1,2,2,24,8,512]{5,4,3,2,1,0:T(8,128)(2,1)}, bf16[1,2,2,24,8,512]{5,4,3,2,1,0:T(8,128)(2,1)}, u32[]{:S(2)}, u32[]{:S(2)}) collective-permute-start(bf16[1,2,2,24,8,512]{5,4,3,2,1,0:T(8,128)(2,1)} %maximum_bitcast_fusion.5.refs_8_), channel_id=1, source_target_pairs={{0,2},{2,0},{1,3},{3,1},{4,6},{6,4},{5,7},{7,5},{8,10},{10,8},{9,1... | collective-permute-start | bytes 2359304 | tf_op jit(solution)/shard_map/qkv_x_high/ppermute | solution.py:385
  44.3 28.9 %collective-permute-start.12 = (bf16[1,2,2,24,8,512]{5,4,3,2,1,0:T(8,128)(2,1)S(1)}, bf16[1,2,2,24,8,512]{5,4,3,2,1,0:T(8,128)(2,1)S(1)}, u32[]{:S(2)}, u32[]{:S(2)}) collective-permute-start(bf16[1,2,2,24,8,512]{5,4,3,2,1,0:T(8,128)(2,1)S(1)} %maximum_bitcast_fusion.4.refs_4_), channel_id=1, source_target_pairs={{0,1},{1,0},{2,3},{3,2},{4,5},{5,4},{6,7},{7,6},{8,9},{9,8},{10,11... | collective-permute-start | bytes 2359304 | tf_op jit(solution)/shard_map/qkv_y_low/ppermute | solution.py:385
  46.9 26.3 %collective-permute-start.15 = (bf16[2,256,512]{2,1,0:T(8,128)(2,1)S(1)}, bf16[2,256,512]{2,1,0:T(8,128)(2,1)S(1)}, u32[]{:S(2)}, u32[]{:S(2)}) collective-permute-start(bf16[2,256,512]{2,1,0:T(8,128)(2,1)S(1)} %constant_dynamic-update-slice_fusion.2), channel_id=1, source_target_pairs={{0,16},{8,24},{16,0},{24,8},{1,17},{9,25},{17,1},{25,9},{2,18},{10... | collective-permute-start | bytes 1572872 | tf_op jit(solution)/shard_map/up_z_high/ppermute | solution.py:385
  87.5 28.4 %collective-permute-start.28 = (bf16[640,512]{1,0:T(8,128)(2,1)S(1)}, bf16[640,512]{1,0:T(8,128)(2,1)S(1)}, u32[]{:S(2)}, u32[]{:S(2)}) collective-permute-start(bf16[640,512]{1,0:T(8,128)(2,1)S(1)} %get-tuple-element.298), channel_id=1, source_target_pairs={{0,1},{1,0},{2,3},{3,2},{4,5},{5,4},{6,7},{7,6},{8,9},{9,8},{10,11... | collective-permute-start | bytes 1966088 | tf_op jit(solution)/shard_map/cotangent_first/ppermute | solution.py:385
  116.1 25.1 %collective-permute-start.30 = (bf16[1,2,2,256,512]{4,3,2,1,0:T(8,128)(2,1)S(1)}, bf16[1,2,2,256,512]{4,3,2,1,0:T(8,128)(2,1)}, u32[]{:S(2)}, u32[]{:S(2)}) collective-permute-start(bf16[1,2,2,256,512]{4,3,2,1,0:T(8,128)(2,1)S(1)} %maximum_bitcast_fusion.1), channel_id=1, source_target_pairs={{0,2},{2,0},{1,3},{3,1},{4,6},{6,4},{5,7},{7,5},{8,10},{10,8},{9,1... | collective-permute-start | bytes 3145736 | tf_op jit(solution)/shard_map/up_x_high/ppermute | solution.py:385
  118.2 25.2 %collective-permute-start.29 = (bf16[1,2,2,256,512]{4,3,2,1,0:T(8,128)(2,1)S(1)}, bf16[1,2,2,256,512]{4,3,2,1,0:T(8,128)(2,1)}, u32[]{:S(2)}, u32[]{:S(2)}) collective-permute-start(bf16[1,2,2,256,512]{4,3,2,1,0:T(8,128)(2,1)S(1)} %maximum_bitcast_fusion), channel_id=1, source_target_pairs={{0,1},{1,0},{2,3},{3,2},{4,5},{5,4},{6,7},{7,6},{8,9},{9,8},{10,11... | collective-permute-start | bytes 3145736 | tf_op jit(solution)/shard_map/up_y_low/ppermute | solution.py:385
  158.7 28.1 %collective-permute-start.40 = (bf16[1,2,2,256,512]{4,3,2,1,0:T(8,128)(2,1)S(1)}, bf16[1,2,2,256,512]{4,3,2,1,0:T(8,128)(2,1)S(1)}, u32[]{:S(2)}, u32[]{:S(2)}) collective-permute-start(bf16[1,2,2,256,512]{4,3,2,1,0:T(8,128)(2,1)S(1)} %maximum_bitcast_fusion.3), channel_id=1, source_target_pairs={{0,2},{2,0},{1,3},{3,1},{4,6},{6,4},{5,7},{7,5},{8,10},{10,8},{9,1... | collective-permute-start | bytes 3145736 | tf_op jit(solution)/shard_map/down_x_high/ppermute | solution.py:385
  159.6 27.1 %collective-permute-start.42 = (bf16[1,2,2,256,512]{4,3,2,1,0:T(8,128)(2,1)S(1)}, bf16[1,2,2,256,512]{4,3,2,1,0:T(8,128)(2,1)}, u32[]{:S(2)}, u32[]{:S(2)}) collective-permute-start(bf16[1,2,2,256,512]{4,3,2,1,0:T(8,128)(2,1)S(1)} %maximum_bitcast_fusion.3), channel_id=1, source_target_pairs={{0,4},{4,0},{1,5},{5,1},{2,6},{6,2},{3,7},{7,3},{8,12},{12,8},{9,1... | collective-permute-start | bytes 3145736 | tf_op jit(solution)/shard_map/down_core_near/ppermute | solution.py:385
  159.7 27.0 %collective-permute-start.39 = (bf16[1,2,2,256,512]{4,3,2,1,0:T(8,128)(2,1)S(1)}, bf16[1,2,2,256,512]{4,3,2,1,0:T(8,128)(2,1)S(1)}, u32[]{:S(2)}, u32[]{:S(2)}) collective-permute-start(bf16[1,2,2,256,512]{4,3,2,1,0:T(8,128)(2,1)S(1)} %maximum_bitcast_fusion.2), channel_id=1, source_target_pairs={{0,1},{1,0},{2,3},{3,2},{4,5},{5,4},{6,7},{7,6},{8,9},{9,8},{10,11... | collective-permute-start | bytes 3145736 | tf_op jit(solution)/shard_map/down_y_low/ppermute | solution.py:385
  160.5 26.3 %collective-permute-start.41 = (bf16[1,2,2,256,512]{4,3,2,1,0:T(8,128)(2,1)S(1)}, bf16[1,2,2,256,512]{4,3,2,1,0:T(8,128)(2,1)S(1)}, u32[]{:S(2)}, u32[]{:S(2)}) collective-permute-start(bf16[1,2,2,256,512]{4,3,2,1,0:T(8,128)(2,1)S(1)} %maximum_bitcast_fusion.2), channel_id=1, source_target_pairs={{0,4},{4,0},{1,5},{5,1},{2,6},{6,2},{3,7},{7,3},{8,12},{12,8},{9,1... | collective-permute-start | bytes 3145736 | tf_op jit(solution)/shard_map/down_core_near/ppermute | solution.py:385
  217.0 30.9 %collective-permute-start.46 = (bf16[1280,512]{1,0:T(8,128)(2,1)S(1)}, bf16[1280,512]{1,0:T(8,128)(2,1)S(1)}, u32[]{:S(2)}, u32[]{:S(2)}) collective-permute-start(bf16[1280,512]{1,0:T(8,128)(2,1)S(1)} %bitcast.179), channel_id=1, source_target_pairs={{0,1},{1,0},{2,3},{3,2},{4,5},{5,4},{6,7},{7,6},{8,9},{9,8},{10,11... | collective-permute-start | bytes 3932168 | tf_op jit(solution)/shard_map/activations_send/ppermute | solution.py:385
  256.8 31.2 %collective-permute-start.50 = (bf16[2,2,2,512,512]{4,3,2,1,0:T(8,128)(2,1)}, bf16[2,2,2,512,512]{4,3,2,1,0:T(8,128)(2,1)}, u32[]{:S(2)}, u32[]{:S(2)}) collective-permute-start(bf16[2,2,2,512,512]{4,3,2,1,0:T(8,128)(2,1)} %up_grad.2), channel_id=1, source_target_pairs={{0,4},{4,0},{1,5},{5,1},{2,6},{6,2},{3,7},{7,3},{8,12},{12,8},{9,1... | collective-permute-start | bytes 12582920 | tf_op jit(solution)/shard_map/up_grad_core/ppermute | solution.py:385
  256.8 31.1 %collective-permute-start.49 = (bf16[2,1,2,256,512]{4,3,2,1,0:T(8,128)(2,1)S(1)}, bf16[2,1,2,256,512]{4,3,2,1,0:T(8,128)(2,1)S(1)}, u32[]{:S(2)}, u32[]{:S(2)}) collective-permute-start(bf16[2,1,2,256,512]{4,3,2,1,0:T(8,128)(2,1)S(1)} %bitcast.148), channel_id=1, source_target_pairs={{0,1},{1,0},{2,3},{3,2},{4,5},{5,4},{6,7},{7,6},{8,9},{9,8},{10,11... | collective-permute-start | bytes 3145736 | tf_op jit(solution)/shard_map/down_grad_first/ppermute | solution.py:385
  258.2 29.8 %collective-permute-start.48 = (bf16[1,2,2,256,512]{4,3,2,1,0:T(8,128)(2,1)S(1)}, bf16[1,2,2,256,512]{4,3,2,1,0:T(8,128)(2,1)S(1)}, u32[]{:S(2)}, u32[]{:S(2)}) collective-permute-start(bf16[1,2,2,256,512]{4,3,2,1,0:T(8,128)(2,1)S(1)} %bitcast.146), channel_id=1, source_target_pairs={{0,2},{2,0},{1,3},{3,1},{4,6},{6,4},{5,7},{7,5},{8,10},{10,8},{9,1... | collective-permute-start | bytes 3145736 | tf_op jit(solution)/shard_map/down_grad_first/ppermute | solution.py:385
  306.0 28.6 %collective-permute-start.56 = (bf16[2,2,4,1,8,8,512]{6,5,4,3,2,1,0:T(8,128)(2,1)}, bf16[2,2,4,1,8,8,512]{6,5,4,3,2,1,0:T(8,128)(2,1)S(1)}, u32[]{:S(2)}, u32[]{:S(2)}) collective-permute-start(bf16[2,2,4,1,8,8,512]{6,5,4,3,2,1,0:T(8,128)(2,1)} %get-tuple-element.375), channel_id=1, source_target_pairs={{0,4},{4,0},{1,5},{5,1},{2,6},{6,2},{3,7},{7,3},{8,12},{12,8},{9,1... | collective-permute-start | bytes 3145736 | tf_op jit(solution)/shard_map/out_grad_core/ppermute | solution.py:385
  306.0 28.5 %collective-permute-start.54 = (bf16[2,1,2,256,512]{4,3,2,1,0:T(8,128)(2,1)}, bf16[2,1,2,256,512]{4,3,2,1,0:T(8,128)(2,1)S(1)}, u32[]{:S(2)}, u32[]{:S(2)}) collective-permute-start(bf16[2,1,2,256,512]{4,3,2,1,0:T(8,128)(2,1)} %bitcast.58), channel_id=1, source_target_pairs={{0,1},{1,0},{2,3},{3,2},{4,5},{5,4},{6,7},{7,6},{8,9},{9,8},{10,11... | collective-permute-start | bytes 3145736 | tf_op jit(solution)/shard_map/up_grad_first/ppermute | solution.py:385
  307.3 27.2 %collective-permute-start.53 = (bf16[1,2,2,256,512]{4,3,2,1,0:T(8,128)(2,1)S(1)}, bf16[1,2,2,256,512]{4,3,2,1,0:T(8,128)(2,1)}, u32[]{:S(2)}, u32[]{:S(2)}) collective-permute-start(bf16[1,2,2,256,512]{4,3,2,1,0:T(8,128)(2,1)S(1)} %bitcast.147), channel_id=1, source_target_pairs={{0,2},{2,0},{1,3},{3,1},{4,6},{6,4},{5,7},{7,5},{8,10},{10,8},{9,1... | collective-permute-start | bytes 3145736 | tf_op jit(solution)/shard_map/up_grad_first/ppermute | solution.py:385
  308.6 25.9 %collective-permute-start.55 = (bf16[1,1,2,256,512]{4,3,2,1,0:T(8,128)(2,1)S(1)}, bf16[1,1,2,256,512]{4,3,2,1,0:T(8,128)(2,1)S(1)}, u32[]{:S(2)}, u32[]{:S(2)}) collective-permute-start(bf16[1,1,2,256,512]{4,3,2,1,0:T(8,128)(2,1)S(1)} %sums.9), channel_id=1, source_target_pairs={{0,16},{8,24},{16,0},{24,8},{1,17},{9,25},{17,1},{25,9},{2,18},{10... | collective-permute-start | bytes 1572872 | tf_op jit(solution)/shard_map/down_grad_z_high/ppermute | solution.py:385
  355.6 25.5 %collective-permute-start.60 = (bf16[1,2,2,3,8,8,512]{6,5,4,3,2,1,0:T(8,128)(2,1)}, bf16[1,2,2,3,8,8,512]{6,5,4,3,2,1,0:T(8,128)(2,1)S(1)}, u32[]{:S(2)}, u32[]{:S(2)}) collective-permute-start(bf16[1,2,2,3,8,8,512]{6,5,4,3,2,1,0:T(8,128)(2,1)} %get-tuple-element.401), channel_id=1, source_target_pairs={{0,2},{2,0},{1,3},{3,1},{4,6},{6,4},{5,7},{7,5},{8,10},{10,8},{9,1... | collective-permute-start | bytes 2359304 | tf_op jit(solution)/shard_map/qkv_grad_far_far_high/ppermute | solution.py:385
  356.4 24.7 %collective-permute-start.62 = (bf16[1,1,2,256,512]{4,3,2,1,0:T(8,128)(2,1)}, bf16[1,1,2,256,512]{4,3,2,1,0:T(8,128)(2,1)}, u32[]{:S(2)}, u32[]{:S(2)}) collective-permute-start(bf16[1,1,2,256,512]{4,3,2,1,0:T(8,128)(2,1)} %get-tuple-element.403), channel_id=1, source_target_pairs={{0,16},{8,24},{16,0},{24,8},{1,17},{9,25},{17,1},{25,9},{2,18},{10... | collective-permute-start | bytes 1572872 | tf_op jit(solution)/shard_map/up_grad_z_high/ppermute | solution.py:385
  408.1 25.6 %collective-permute-start.70 = (bf16[1,1,2,3,8,8,512]{6,5,4,3,2,1,0:T(8,128)(2,1)}, bf16[1,1,2,3,8,8,512]{6,5,4,3,2,1,0:T(8,128)(2,1)}, u32[]{:S(2)}, u32[]{:S(2)}) collective-permute-start(bf16[1,1,2,3,8,8,512]{6,5,4,3,2,1,0:T(8,128)(2,1)} %get-tuple-element.442), channel_id=1, source_target_pairs={{0,1},{1,0},{2,3},{3,2},{4,5},{5,4},{6,7},{7,6},{8,9},{9,8},{10,11... | collective-permute-start | bytes 1179656 | tf_op jit(solution)/shard_map/qkv_grad_y_high/ppermute | solution.py:385
  409.3 24.4 %collective-permute-start.71 = (bf16[1,1,2,3,8,8,512]{6,5,4,3,2,1,0:T(8,128)(2,1)}, bf16[1,1,2,3,8,8,512]{6,5,4,3,2,1,0:T(8,128)(2,1)}, u32[]{:S(2)}, u32[]{:S(2)}) collective-permute-start(bf16[1,1,2,3,8,8,512]{6,5,4,3,2,1,0:T(8,128)(2,1)} %get-tuple-element.443), channel_id=1, source_target_pairs={{0,1},{1,0},{2,3},{3,2},{4,5},{5,4},{6,7},{7,6},{8,9},{9,8},{10,11... | collective-permute-start | bytes 1179656 | tf_op jit(solution)/shard_map/qkv_grad_y_low/ppermute | solution.py:385
  440.1 30.9 %collective-permute-start.74 = (bf16[1280,512]{1,0:T(8,128)(2,1)}, bf16[1280,512]{1,0:T(8,128)(2,1)}, u32[]{:S(2)}, u32[]{:S(2)}) collective-permute-start(bf16[1280,512]{1,0:T(8,128)(2,1)} %bitcast.178), channel_id=1, source_target_pairs={{0,1},{1,0},{2,3},{3,2},{4,5},{5,4},{6,7},{7,6},{8,9},{9,8},{10,11... | collective-permute-start | bytes 3932168 | tf_op jit(solution)/shard_map/token_grad_send/ppermute | solution.py:385
  (151 other events, 2388.9 us)

commit v6 on v5

--- a/solution.py
+++ b/solution.py
@@ -1050,8 +1050,6 @@
             scratch=out_scratch,
         )(slots.gate(upward_grad)[0], middle, grad_low, gain_two, *up_ops, *out_ops)
         slots.note(attended_grad)
-        activations = activations.end(spaces[0])
-        slots.note(activations)
         slots.advance()
 
         slots.together((dg, "y_high"), (dg, "x_low"))
@@ -1069,6 +1067,8 @@
         slots.advance()
 
         far_held = core_fold("qkv_grad_far", far_sums)
+        activations = activations.end(spaces[0])
+        slots.note(activations)
         slots.together((ug, "y_high"), (ug, "x_low"))
         slots.advance()
 

time: 487 us -> 479 us (0.984)
  local copies, waits for them, and re-layouts: 44.3 us -> 37.8 us
    unnamed x195 -> x197, local copies, waits for them, and re-layouts: 18.5 us -> 16.8 us
  transfers between devices with their start and end apart: 83 -> 83, of which waited for: 26 -> 27; matrix products, arithmetic and copies ran while one was open for 9% -> 9% of each run, Pallas kernels for 44% -> 44%
where the time goes in v6:
time: 479 us; the launch traced here: 474 us
  Pallas kernels  236 us (49%)
  waiting for transfers between devices  99.9 us (21%)
  starting transfers between devices  75.4 us (16%)
  local copies, waits for them, and re-layouts  37.8 us (8%)
  other arithmetic  22.7 us (5%)
    ppermute x83, waiting for transfers between devices, exchange(): lax.ppermute(values, axis, [(i, i ^ bit) for i in range(sizes[axis])])  99.9 us
    ppermute x83, starting transfers between devices, exchange(): lax.ppermute(values, axis, [(i, i ^ bit) for i in range(sizes[axis])])  75.4 us
    pallas_call x2, Pallas kernels, pull(): call(functools.partial(attend_pull_kernel, seqs, (ncore, ncol, nz, part,...  37.7 us
    pallas_call x1, Pallas kernels, local(): call(functools.partial(up_kernel, up_dims), (seqs,), [tokens_spec, whole(...  24.9 us
    pallas_call x1, Pallas kernels, local(): call(functools.partial(middle_pull_kernel, up_dims, out_layout), (seqs,),...  24.7 us
    pallas_call x2, Pallas kernels, ffn_kept(): call(functools.partial(ffn_kept_kernel, ncol, nrow), (2, nrow), [pl.Block...  19.9 us
    pallas_call x2, Pallas kernels, ffn_sent(): call(functools.partial(ffn_sent_kernel, ncol), (2, nrow), [pl.BlockSpec((...  18.8 us
    pallas_call x1, Pallas kernels, local(): call(attend_kernel, (seqs, quads // STEP), [pl.BlockSpec((3, LEN, step_la...  18.2 us
  transfers between devices with their start and end apart: 83, of which 27 were waited for; matrix products, arithmetic and copies ran while one was open for 9% of the time, Pallas kernels for 44%

profile of v6, /device:TPU:0, one launch (start us, length us, event | category | flops | bytes accessed | tf_op | source)
XLA Modules:
  0.0 473.8 jit_solution(14913660460323761680)
XLA Ops:
  11.4 13.9 %collective-permute-done = f32[1,5120]{1,0:T(1,128)S(1)} collective-permute-done((f32[1,5120]{1,0:T(1,128)S(1)}, f32[1,5120]{1,0:T(1,128)S(1)}, u32[]{:S(2)}, u32[]{:S(2)}) %collective-permute-start) | collective-permute-done | bytes 20512 | tf_op jit(solution)/shard_map/ppermute | solution.py:385
  51.5 21.7 %collective-permute-done.14 = bf16[2,8,8,512]{3,2,1,0:T(8,128)(2,1)S(1)} collective-permute-done((bf16[2,8,8,512]{3,2,1,0:T(8,128)(2,1)S(1)}, bf16[2,8,8,512]{3,2,1,0:T(8,128)(2,1)S(1)}, u32[]{:S(2)}, u32[]{:S(2)}) %collective-permute-start.14) | collective-permute-done | bytes 131104 | tf_op jit(solution)/shard_map/out_z_high/ppermute | solution.py:385
  76.3 3.5 collective-permute-done.23
  84.1 3.4 collective-permute-done.22
  96.1 16.0 %qkv.1 = (bf16[1280,1024]{1,0:T(8,128)(2,1)}, bf16[3,1280,1024]{2,1,0:T(8,128)(2,1)}) custom-call(f32[1,1024]{1,0:T(1,128)S(1)} %bitcast.132, f32[1,1024]{1,0:T(1,128)S(1)} %bitcast.136, f32[2,1024]{1,0:T(2,128)S(1)} %reshape.220.bias_ref, bf16[640,512]{1,0:T(8,128)(2,1)S(1)} %get-tuple-element.287.refs_0_, bf16[640,512]{1,0:T(8,128)(2,1)S(1)} %copy-done.34, ...), custom_call_target="tpu_custom_call" | custom-call | flops 8053063680 | bytes 19398656 | tf_op jit(solution)/shard_map/qkv/pallas_call | solution.py:819
  112.1 3.9 collective-permute-done.24
  121.4 18.2 %attend.1 = (bf16[1280,1024]{1,0:T(8,128)(2,1)S(1)}, bf16[4,4,320,1280]{3,2,1,0:T(8,128)(2,1)}) custom-call(bf16[3,1280,1024]{2,1,0:T(8,128)(2,1)} %get-tuple-element.299.qkv_ref, f32[4,320,1]{2,1,0:T(8,128)S(1)} %copy.31.mask_ref), custom_call_target="tpu_custom_call" | custom-call | flops 6710886400 | bytes 23592960 | tf_op jit(solution)/shard_map/attend/pallas_call | solution.py:838
  146.0 9.0 %out.1 = (f32[1280,1024]{1,0:T(8,128)}, bf16[1280,1024]{1,0:T(8,128)(2,1)}) custom-call(bf16[1280,1024]{1,0:T(8,128)(2,1)} %copy-done.46, f32[1,1024]{1,0:T(1,128)S(1)} %bitcast.138, f32[1,1024]{1,0:T(1,128)S(1)} %bitcast.134, f32[1,1024]{1,0:T(1,128)S(1)} %bitcast.139, bf16[640,512]{1,0:T(8,128)(2,1)S(1)} %get-tuple-element.287.refs_0_, ...), custom_call_target="tpu_custom_call" | custom-call | flops 2684354560 | bytes 15204352 | tf_op jit(solution)/shard_map/out/pallas_call | solution.py:860
  160.7 24.9 %up.1 = (bf16[1280,4096]{1,0:T(8,128)(2,1)}, bf16[1280,4096]{1,0:T(8,128)(2,1)}) custom-call(bf16[1280,1024]{1,0:T(8,128)(2,1)} %get-tuple-element.313.a_ref.r_ref, f32[1,4096]{1,0:T(1,128)S(1)} %reshape.222.bias_ref, bf16[1,2,512,512]{3,2,1,0:T(8,128)(2,1)S(1)} %bitcast.126, bf16[1,2,512,512]{3,2,1,0:T(8,128)(2,1)} %bitcast.32.refs_1_, ...), custom_call_target="tpu_custom_call" | custom-call | flops 42949672960 | bytes 29360128 | tf_op jit(solution)/shard_map/up/pallas_call | solution.py:877
  190.0 15.6 %down.1 = (bf16[1280,512]{1,0:T(8,128)(2,1)}, bf16[1,1280,512]{2,1,0:T(8,128)(2,1)}) custom-call(bf16[1280,4096]{1,0:T(8,128)(2,1)} %get-tuple-element.338.hid_ref.l_ref, f32[1280,1024]{1,0:T(8,128)} %get-tuple-element.317.middle_ref, f32[1,1024]{1,0:T(1,128)S(1)} %bitcast.137, bf16[1,2,512,512]{3,2,1,0:T(8,128)(2,1)S(1)} %bitcast.130, ...), custom_call_target="tpu_custom_call" | custom-call | flops 10737418240 | bytes 26738688 | tf_op jit(solution)/shard_map/down/pallas_call | solution.py:998
  205.9 9.7 %down_grad.2 = bf16[2,2,2,512,512]{4,3,2,1,0:T(8,128)(2,1)} custom-call(bf16[1280,4096]{1,0:T(8,128)(2,1)} %get-tuple-element.338.hid_ref.l_ref, bf16[1280,1024]{1,0:T(8,128)(2,1)S(1)} %maximum_maximum_fusion.g_ref.r_ref), custom_call_target="tpu_custom_call" | custom-call | flops 5368709120 | bytes 12058624 | tf_op jit(solution)/shard_map/down_grad/pallas_call | solution.py:891
  217.3 17.5 %hidden_pull.1 = (bf16[1280,4096]{1,0:T(8,128)(2,1)}, f32[1,4096]{1,0:T(1,128)S(1)}) custom-call(bf16[1280,1024]{1,0:T(8,128)(2,1)} %copy-done.13, bf16[1280,4096]{1,0:T(8,128)(2,1)} %get-tuple-element.336.slope_ref, bf16[1,2,512,512]{3,2,1,0:T(8,128)(2,1)S(1)} %bitcast.131, bf16[1,2,512,512]{3,2,1,0:T(8,128)(2,1)S(1)} %bitcast.143, ...), custom_call_target="tpu_custom_call" | custom-call | flops 10737418240 | bytes 29360128 | tf_op jit(solution)/shard_map/hidden_pull/pallas_call | solution.py:1017
  234.8 9.4 %down_grad.3 = (bf16[2,512,512]{2,1,0:T(8,128)(2,1)S(1)}, bf16[2,512,512]{2,1,0:T(8,128)(2,1)S(1)}, bf16[2,512,512]{2,1,0:T(8,128)(2,1)S(1)}, bf16[2,512,512]{2,1,0:T(8,128)(2,1)S(1)}) custom-call(bf16[1280,4096]{1,0:T(8,128)(2,1)} %get-tuple-element.338.hid_ref.l_ref, bf16[1280,1024]{1,0:T(8,128)(2,1)} %copy-done.13, ...), custom_call_target="tpu_custom_call" | custom-call | flops 5368709120 | bytes 16777216 | tf_op jit(solution)/shard_map/down_grad/pallas_call | solution.py:907
  246.8 9.2 %up_grad.2 = bf16[2,2,2,512,512]{4,3,2,1,0:T(8,128)(2,1)} custom-call(bf16[1280,4096]{1,0:T(8,128)(2,1)} %get-tuple-element.347.l_ref.du_ref, bf16[1280,1024]{1,0:T(8,128)(2,1)S(1)} %copy-done.48), custom_call_target="tpu_custom_call" | custom-call | flops 5368709120 | bytes 12058624 | tf_op jit(solution)/shard_map/up_grad/pallas_call | solution.py:891
  258.5 24.7 %middle_pull.1 = (f32[1280,1024]{1,0:T(8,128)}, bf16[1280,1024]{1,0:T(8,128)(2,1)}, bf16[1280,1024]{1,0:T(8,128)(2,1)}, f32[4,1024]{1,0:T(4,128)S(1)}) custom-call(bf16[1280,4096]{1,0:T(8,128)(2,1)} %get-tuple-element.347.l_ref.du_ref, f32[1280,1024]{1,0:T(8,128)} %get-tuple-element.317.middle_ref, bf16[1280,1024]{1,0:T(8,128)(2,1)} %copy-done.13, ...), custom_call_target="tpu_custom_call" | custom-call | flops 13421772800 | bytes 37224448 | tf_op jit(solution)/shard_map/middle_pull/pallas_call | solution.py:1036
  285.3 5.8 %out_grad.1 = (bf16[2,2,4,1,8,8,512]{6,5,4,3,2,1,0:T(8,128)(2,1)S(1)}, bf16[2,2,4,1,8,8,512]{6,5,4,3,2,1,0:T(8,128)(2,1)}) custom-call(bf16[1,1280,1024]{2,1,0:T(8,128)(2,1)S(1)} %bitcast.150, bf16[1280,1024]{1,0:T(8,128)(2,1)} %get-tuple-element.359.r_ref), custom_call_target="tpu_custom_call" | custom-call | flops 2684354560 | bytes 7340032 | tf_op jit(solution)/shard_map/out_grad/pallas_call | solution.py:929
  291.1 10.5 %up_grad.3 = (bf16[2,512,512]{2,1,0:T(8,128)(2,1)S(1)}, bf16[2,512,512]{2,1,0:T(8,128)(2,1)}, bf16[2,512,512]{2,1,0:T(8,128)(2,1)S(1)}, bf16[2,512,512]{2,1,0:T(8,128)(2,1)}) custom-call(bf16[1280,4096]{1,0:T(8,128)(2,1)} %get-tuple-element.347.l_ref.du_ref, bf16[1280,1024]{1,0:T(8,128)(2,1)} %get-tuple-element.313.a_ref.r_ref, ...), custom_call_target="tpu_custom_call" | custom-call | flops 5368709120 | bytes 16777216 | tf_op jit(solution)/shard_map/up_grad/pallas_call | solution.py:907
  306.1 18.9 %attend_pull.2 = (bf16[3,1280,512]{2,1,0:T(8,128)(2,1)}, bf16[1,2,4,3,8,8,512]{6,5,4,3,2,1,0:T(8,128)(2,1)S(1)}, bf16[1,2,4,3,8,8,512]{6,5,4,3,2,1,0:T(8,128)(2,1)S(1)}, f32[3,1,512]{2,1,0:T(1,128)S(1)}) custom-call(bf16[3,1280,1024]{2,1,0:T(8,128)(2,1)} %get-tuple-element.299.qkv_ref, bf16[4,4,320,1280]{3,2,1,0:T(8,128)(2,1)} %get-tuple-element.370.probs_ref, ...), custom_call_target="tpu_custom_call" | custom-call | flops 10317987840 | bytes 9175040 | tf_op jit(solution)/shard_map/attend_pull/pallas_call | solution.py:972
  326.1 4.0 collective-permute-done.55.refs_12_
  333.2 11.7 %collective-permute-done.58.refs_6_ = bf16[1,1,2,256,512]{4,3,2,1,0:T(8,128)(2,1)S(1)} collective-permute-done((bf16[1,1,2,256,512]{4,3,2,1,0:T(8,128)(2,1)S(1)}, bf16[1,1,2,256,512]{4,3,2,1,0:T(8,128)(2,1)S(1)}, u32[]{:S(2)}, u32[]{:S(2)}) %collective-permute-start.58) | collective-permute-done | bytes 524320 | tf_op jit(solution)/shard_map/up_grad_y_high/ppermute | solution.py:385
  354.0 18.8 %attend_pull.3 = (bf16[3,1280,512]{2,1,0:T(8,128)(2,1)}, bf16[1,2,4,3,8,8,512]{6,5,4,3,2,1,0:T(8,128)(2,1)S(1)}, bf16[1,2,4,3,8,8,512]{6,5,4,3,2,1,0:T(8,128)(2,1)}, f32[3,1,512]{2,1,0:T(1,128)S(1)}) custom-call(bf16[3,1280,1024]{2,1,0:T(8,128)(2,1)} %get-tuple-element.299.qkv_ref, bf16[4,4,320,1280]{3,2,1,0:T(8,128)(2,1)} %get-tuple-element.370.probs_ref, ...), custom_call_target="tpu_custom_call" | custom-call | flops 10317987840 | bytes 9175040 | tf_op jit(solution)/shard_map/attend_pull/pallas_call | solution.py:972
  405.0 16.9 %token_pull.1 = (f32[1280,512]{1,0:T(8,128)}, bf16[1,1280,512]{2,1,0:T(8,128)(2,1)}, f32[2,1024]{1,0:T(2,128)S(1)}) custom-call(bf16[3,1280,512]{2,1,0:T(8,128)(2,1)} %get-tuple-element.425.near_ref, bf16[3,1280,512]{2,1,0:T(8,128)(2,1)} %get-tuple-element.373.far_ref, f32[1280,1024]{1,0:T(8,128)} %get-tuple-element.426.grad_ref, f32[1,1024]{1,0:T(1,128)S(1)} %bitcast.133, ...), custom_call_target="tpu_custom_call" | custom-call | flops 8053063680 | bytes 24641536 | tf_op jit(solution)/shard_map/token_pull/pallas_call | solution.py:1095
  446.2 5.1 %collective-permute-done.81 = f32[3456]{0:T(1024)S(1)} collective-permute-done((f32[3456]{0:T(1024)S(1)}, f32[3456]{0:T(1024)S(1)}, u32[]{:S(2)}, u32[]{:S(2)}) %collective-permute-start.81) | collective-permute-done | bytes 13856 | tf_op jit(solution)/shard_map/small_sums/ppermute | solution.py:385
  453.1 6.2 %collective-permute-done.75.refs_4_ = bf16[1,1,2,3,8,8,512]{6,5,4,3,2,1,0:T(8,128)(2,1)} collective-permute-done((bf16[1,1,2,3,8,8,512]{6,5,4,3,2,1,0:T(8,128)(2,1)}, bf16[1,1,2,3,8,8,512]{6,5,4,3,2,1,0:T(8,128)(2,1)}, u32[]{:S(2)}, u32[]{:S(2)}) %collective-permute-start.75) | collective-permute-done | bytes 393248 | tf_op jit(solution)/shard_map/qkv_grad_z_high/ppermute | solution.py:385
  (456 shorter events, 173.1 us)
Async XLA Ops:
  40.2 33.1 %collective-permute-start.16 = (bf16[640,512]{1,0:T(8,128)(2,1)S(1)}, bf16[640,512]{1,0:T(8,128)(2,1)S(1)}, u32[]{:S(2)}, u32[]{:S(2)}) collective-permute-start(bf16[640,512]{1,0:T(8,128)(2,1)S(1)} %get-tuple-element.272), channel_id=1, source_target_pairs={{0,1},{1,0},{2,3},{3,2},{4,5},{5,4},{6,7},{7,6},{8,9},{9,8},{10,11... | collective-permute-start | bytes 1966088 | tf_op jit(solution)/shard_map/tokens_second/ppermute | solution.py:385
  42.7 30.5 %collective-permute-start.13 = (bf16[1,2,2,24,8,512]{5,4,3,2,1,0:T(8,128)(2,1)}, bf16[1,2,2,24,8,512]{5,4,3,2,1,0:T(8,128)(2,1)}, u32[]{:S(2)}, u32[]{:S(2)}) collective-permute-start(bf16[1,2,2,24,8,512]{5,4,3,2,1,0:T(8,128)(2,1)} %maximum_bitcast_fusion.5.refs_8_), channel_id=1, source_target_pairs={{0,2},{2,0},{1,3},{3,1},{4,6},{6,4},{5,7},{7,5},{8,10},{10,8},{9,1... | collective-permute-start | bytes 2359304 | tf_op jit(solution)/shard_map/qkv_x_high/ppermute | solution.py:385
  44.4 28.9 %collective-permute-start.12 = (bf16[1,2,2,24,8,512]{5,4,3,2,1,0:T(8,128)(2,1)S(1)}, bf16[1,2,2,24,8,512]{5,4,3,2,1,0:T(8,128)(2,1)S(1)}, u32[]{:S(2)}, u32[]{:S(2)}) collective-permute-start(bf16[1,2,2,24,8,512]{5,4,3,2,1,0:T(8,128)(2,1)S(1)} %maximum_bitcast_fusion.4.refs_4_), channel_id=1, source_target_pairs={{0,1},{1,0},{2,3},{3,2},{4,5},{5,4},{6,7},{7,6},{8,9},{9,8},{10,11... | collective-permute-start | bytes 2359304 | tf_op jit(solution)/shard_map/qkv_y_low/ppermute | solution.py:385
  46.9 26.3 %collective-permute-start.15 = (bf16[2,256,512]{2,1,0:T(8,128)(2,1)S(1)}, bf16[2,256,512]{2,1,0:T(8,128)(2,1)S(1)}, u32[]{:S(2)}, u32[]{:S(2)}) collective-permute-start(bf16[2,256,512]{2,1,0:T(8,128)(2,1)S(1)} %constant_dynamic-update-slice_fusion.2), channel_id=1, source_target_pairs={{0,16},{8,24},{16,0},{24,8},{1,17},{9,25},{17,1},{25,9},{2,18},{10... | collective-permute-start | bytes 1572872 | tf_op jit(solution)/shard_map/up_z_high/ppermute | solution.py:385
  87.5 28.4 %collective-permute-start.28 = (bf16[640,512]{1,0:T(8,128)(2,1)S(1)}, bf16[640,512]{1,0:T(8,128)(2,1)S(1)}, u32[]{:S(2)}, u32[]{:S(2)}) collective-permute-start(bf16[640,512]{1,0:T(8,128)(2,1)S(1)} %get-tuple-element.298), channel_id=1, source_target_pairs={{0,1},{1,0},{2,3},{3,2},{4,5},{5,4},{6,7},{7,6},{8,9},{9,8},{10,11... | collective-permute-start | bytes 1966088 | tf_op jit(solution)/shard_map/cotangent_first/ppermute | solution.py:385
  116.1 25.0 %collective-permute-start.30 = (bf16[1,2,2,256,512]{4,3,2,1,0:T(8,128)(2,1)S(1)}, bf16[1,2,2,256,512]{4,3,2,1,0:T(8,128)(2,1)}, u32[]{:S(2)}, u32[]{:S(2)}) collective-permute-start(bf16[1,2,2,256,512]{4,3,2,1,0:T(8,128)(2,1)S(1)} %maximum_bitcast_fusion.1), channel_id=1, source_target_pairs={{0,2},{2,0},{1,3},{3,1},{4,6},{6,4},{5,7},{7,5},{8,10},{10,8},{9,1... | collective-permute-start | bytes 3145736 | tf_op jit(solution)/shard_map/up_x_high/ppermute | solution.py:385
  118.2 25.2 %collective-permute-start.29 = (bf16[1,2,2,256,512]{4,3,2,1,0:T(8,128)(2,1)S(1)}, bf16[1,2,2,256,512]{4,3,2,1,0:T(8,128)(2,1)}, u32[]{:S(2)}, u32[]{:S(2)}) collective-permute-start(bf16[1,2,2,256,512]{4,3,2,1,0:T(8,128)(2,1)S(1)} %maximum_bitcast_fusion), channel_id=1, source_target_pairs={{0,1},{1,0},{2,3},{3,2},{4,5},{5,4},{6,7},{7,6},{8,9},{9,8},{10,11... | collective-permute-start | bytes 3145736 | tf_op jit(solution)/shard_map/up_y_low/ppermute | solution.py:385
  158.7 27.0 %collective-permute-start.40 = (bf16[1,2,2,256,512]{4,3,2,1,0:T(8,128)(2,1)S(1)}, bf16[1,2,2,256,512]{4,3,2,1,0:T(8,128)(2,1)}, u32[]{:S(2)}, u32[]{:S(2)}) collective-permute-start(bf16[1,2,2,256,512]{4,3,2,1,0:T(8,128)(2,1)S(1)} %maximum_bitcast_fusion.3), channel_id=1, source_target_pairs={{0,2},{2,0},{1,3},{3,1},{4,6},{6,4},{5,7},{7,5},{8,10},{10,8},{9,1... | collective-permute-start | bytes 3145736 | tf_op jit(solution)/shard_map/down_x_high/ppermute | solution.py:385
  159.7 26.1 %collective-permute-start.42 = (bf16[1,2,2,256,512]{4,3,2,1,0:T(8,128)(2,1)S(1)}, bf16[1,2,2,256,512]{4,3,2,1,0:T(8,128)(2,1)}, u32[]{:S(2)}, u32[]{:S(2)}) collective-permute-start(bf16[1,2,2,256,512]{4,3,2,1,0:T(8,128)(2,1)S(1)} %maximum_bitcast_fusion.3), channel_id=1, source_target_pairs={{0,4},{4,0},{1,5},{5,1},{2,6},{6,2},{3,7},{7,3},{8,12},{12,8},{9,1... | collective-permute-start | bytes 3145736 | tf_op jit(solution)/shard_map/down_core_near/ppermute | solution.py:385
  159.8 26.0 %collective-permute-start.39 = (bf16[1,2,2,256,512]{4,3,2,1,0:T(8,128)(2,1)S(1)}, bf16[1,2,2,256,512]{4,3,2,1,0:T(8,128)(2,1)S(1)}, u32[]{:S(2)}, u32[]{:S(2)}) collective-permute-start(bf16[1,2,2,256,512]{4,3,2,1,0:T(8,128)(2,1)S(1)} %maximum_bitcast_fusion.2), channel_id=1, source_target_pairs={{0,1},{1,0},{2,3},{3,2},{4,5},{5,4},{6,7},{7,6},{8,9},{9,8},{10,11... | collective-permute-start | bytes 3145736 | tf_op jit(solution)/shard_map/down_y_low/ppermute | solution.py:385
  160.5 25.3 %collective-permute-start.41 = (bf16[1,2,2,256,512]{4,3,2,1,0:T(8,128)(2,1)S(1)}, bf16[1,2,2,256,512]{4,3,2,1,0:T(8,128)(2,1)S(1)}, u32[]{:S(2)}, u32[]{:S(2)}) collective-permute-start(bf16[1,2,2,256,512]{4,3,2,1,0:T(8,128)(2,1)S(1)} %maximum_bitcast_fusion.2), channel_id=1, source_target_pairs={{0,4},{4,0},{1,5},{5,1},{2,6},{6,2},{3,7},{7,3},{8,12},{12,8},{9,1... | collective-permute-start | bytes 3145736 | tf_op jit(solution)/shard_map/down_core_near/ppermute | solution.py:385
  215.9 30.9 %collective-permute-start.46 = (bf16[1280,512]{1,0:T(8,128)(2,1)S(1)}, bf16[1280,512]{1,0:T(8,128)(2,1)S(1)}, u32[]{:S(2)}, u32[]{:S(2)}) collective-permute-start(bf16[1280,512]{1,0:T(8,128)(2,1)S(1)} %bitcast.178), channel_id=1, source_target_pairs={{0,1},{1,0},{2,3},{3,2},{4,5},{5,4},{6,7},{7,6},{8,9},{9,8},{10,11... | collective-permute-start | bytes 3932168 | tf_op jit(solution)/shard_map/activations_send/ppermute | solution.py:385
  256.0 27.2 %collective-permute-start.50 = (bf16[2,2,2,512,512]{4,3,2,1,0:T(8,128)(2,1)}, bf16[2,2,2,512,512]{4,3,2,1,0:T(8,128)(2,1)}, u32[]{:S(2)}, u32[]{:S(2)}) collective-permute-start(bf16[2,2,2,512,512]{4,3,2,1,0:T(8,128)(2,1)} %up_grad.2), channel_id=1, source_target_pairs={{0,4},{4,0},{1,5},{5,1},{2,6},{6,2},{3,7},{7,3},{8,12},{12,8},{9,1... | collective-permute-start | bytes 12582920 | tf_op jit(solution)/shard_map/up_grad_core/ppermute | solution.py:385
  256.0 27.2 %collective-permute-start.49 = (bf16[2,1,2,256,512]{4,3,2,1,0:T(8,128)(2,1)S(1)}, bf16[2,1,2,256,512]{4,3,2,1,0:T(8,128)(2,1)S(1)}, u32[]{:S(2)}, u32[]{:S(2)}) collective-permute-start(bf16[2,1,2,256,512]{4,3,2,1,0:T(8,128)(2,1)S(1)} %bitcast.149), channel_id=1, source_target_pairs={{0,1},{1,0},{2,3},{3,2},{4,5},{5,4},{6,7},{7,6},{8,9},{9,8},{10,11... | collective-permute-start | bytes 3145736 | tf_op jit(solution)/shard_map/down_grad_first/ppermute | solution.py:385
  257.4 25.8 %collective-permute-start.48 = (bf16[1,2,2,256,512]{4,3,2,1,0:T(8,128)(2,1)S(1)}, bf16[1,2,2,256,512]{4,3,2,1,0:T(8,128)(2,1)S(1)}, u32[]{:S(2)}, u32[]{:S(2)}) collective-permute-start(bf16[1,2,2,256,512]{4,3,2,1,0:T(8,128)(2,1)S(1)} %bitcast.148), channel_id=1, source_target_pairs={{0,2},{2,0},{1,3},{3,1},{4,6},{6,4},{5,7},{7,5},{8,10},{10,8},{9,1... | collective-permute-start | bytes 3145736 | tf_op jit(solution)/shard_map/down_grad_first/ppermute | solution.py:385
  301.6 28.6 %collective-permute-start.56 = (bf16[2,2,4,1,8,8,512]{6,5,4,3,2,1,0:T(8,128)(2,1)}, bf16[2,2,4,1,8,8,512]{6,5,4,3,2,1,0:T(8,128)(2,1)S(1)}, u32[]{:S(2)}, u32[]{:S(2)}) collective-permute-start(bf16[2,2,4,1,8,8,512]{6,5,4,3,2,1,0:T(8,128)(2,1)} %get-tuple-element.369), channel_id=1, source_target_pairs={{0,4},{4,0},{1,5},{5,1},{2,6},{6,2},{3,7},{7,3},{8,12},{12,8},{9,1... | collective-permute-start | bytes 3145736 | tf_op jit(solution)/shard_map/out_grad_core/ppermute | solution.py:385
  301.7 28.5 %collective-permute-start.54 = (bf16[2,1,2,256,512]{4,3,2,1,0:T(8,128)(2,1)}, bf16[2,1,2,256,512]{4,3,2,1,0:T(8,128)(2,1)S(1)}, u32[]{:S(2)}, u32[]{:S(2)}) collective-permute-start(bf16[2,1,2,256,512]{4,3,2,1,0:T(8,128)(2,1)} %bitcast.58), channel_id=1, source_target_pairs={{0,1},{1,0},{2,3},{3,2},{4,5},{5,4},{6,7},{7,6},{8,9},{9,8},{10,11... | collective-permute-start | bytes 3145736 | tf_op jit(solution)/shard_map/up_grad_first/ppermute | solution.py:385
  303.0 27.2 %collective-permute-start.53 = (bf16[1,2,2,256,512]{4,3,2,1,0:T(8,128)(2,1)}, bf16[1,2,2,256,512]{4,3,2,1,0:T(8,128)(2,1)S(1)}, u32[]{:S(2)}, u32[]{:S(2)}) collective-permute-start(bf16[1,2,2,256,512]{4,3,2,1,0:T(8,128)(2,1)} %bitcast.55), channel_id=1, source_target_pairs={{0,2},{2,0},{1,3},{3,1},{4,6},{6,4},{5,7},{7,5},{8,10},{10,8},{9,1... | collective-permute-start | bytes 3145736 | tf_op jit(solution)/shard_map/up_grad_first/ppermute | solution.py:385
  304.3 25.9 %collective-permute-start.55 = (bf16[1,1,2,256,512]{4,3,2,1,0:T(8,128)(2,1)S(1)}, bf16[1,1,2,256,512]{4,3,2,1,0:T(8,128)(2,1)S(1)}, u32[]{:S(2)}, u32[]{:S(2)}) collective-permute-start(bf16[1,1,2,256,512]{4,3,2,1,0:T(8,128)(2,1)S(1)} %sums.9), channel_id=1, source_target_pairs={{0,16},{8,24},{16,0},{24,8},{1,17},{9,25},{17,1},{25,9},{2,18},{10... | collective-permute-start | bytes 1572872 | tf_op jit(solution)/shard_map/down_grad_z_high/ppermute | solution.py:385
  348.2 25.5 %collective-permute-start.60 = (bf16[1,2,2,3,8,8,512]{6,5,4,3,2,1,0:T(8,128)(2,1)}, bf16[1,2,2,3,8,8,512]{6,5,4,3,2,1,0:T(8,128)(2,1)S(1)}, u32[]{:S(2)}, u32[]{:S(2)}) collective-permute-start(bf16[1,2,2,3,8,8,512]{6,5,4,3,2,1,0:T(8,128)(2,1)} %get-tuple-element.401), channel_id=1, source_target_pairs={{0,2},{2,0},{1,3},{3,1},{4,6},{6,4},{5,7},{7,5},{8,10},{10,8},{9,1... | collective-permute-start | bytes 2359304 | tf_op jit(solution)/shard_map/qkv_grad_far_far_high/ppermute | solution.py:385
  348.9 24.8 %collective-permute-start.62 = (bf16[1,1,2,256,512]{4,3,2,1,0:T(8,128)(2,1)}, bf16[1,1,2,256,512]{4,3,2,1,0:T(8,128)(2,1)}, u32[]{:S(2)}, u32[]{:S(2)}) collective-permute-start(bf16[1,1,2,256,512]{4,3,2,1,0:T(8,128)(2,1)} %get-tuple-element.403), channel_id=1, source_target_pairs={{0,16},{8,24},{16,0},{24,8},{1,17},{9,25},{17,1},{25,9},{2,18},{10... | collective-permute-start | bytes 1572872 | tf_op jit(solution)/shard_map/up_grad_z_high/ppermute | solution.py:385
  399.7 25.7 %collective-permute-start.70 = (bf16[1,1,2,3,8,8,512]{6,5,4,3,2,1,0:T(8,128)(2,1)}, bf16[1,1,2,3,8,8,512]{6,5,4,3,2,1,0:T(8,128)(2,1)}, u32[]{:S(2)}, u32[]{:S(2)}) collective-permute-start(bf16[1,1,2,3,8,8,512]{6,5,4,3,2,1,0:T(8,128)(2,1)} %get-tuple-element.442), channel_id=1, source_target_pairs={{0,1},{1,0},{2,3},{3,2},{4,5},{5,4},{6,7},{7,6},{8,9},{9,8},{10,11... | collective-permute-start | bytes 1179656 | tf_op jit(solution)/shard_map/qkv_grad_y_high/ppermute | solution.py:385
  401.0 24.4 %collective-permute-start.71 = (bf16[1,1,2,3,8,8,512]{6,5,4,3,2,1,0:T(8,128)(2,1)}, bf16[1,1,2,3,8,8,512]{6,5,4,3,2,1,0:T(8,128)(2,1)}, u32[]{:S(2)}, u32[]{:S(2)}) collective-permute-start(bf16[1,1,2,3,8,8,512]{6,5,4,3,2,1,0:T(8,128)(2,1)} %get-tuple-element.443), channel_id=1, source_target_pairs={{0,1},{1,0},{2,3},{3,2},{4,5},{5,4},{6,7},{7,6},{8,9},{9,8},{10,11... | collective-permute-start | bytes 1179656 | tf_op jit(solution)/shard_map/qkv_grad_y_low/ppermute | solution.py:385
  431.8 30.9 %collective-permute-start.74 = (bf16[1280,512]{1,0:T(8,128)(2,1)}, bf16[1280,512]{1,0:T(8,128)(2,1)}, u32[]{:S(2)}, u32[]{:S(2)}) collective-permute-start(bf16[1280,512]{1,0:T(8,128)(2,1)} %bitcast.177), channel_id=1, source_target_pairs={{0,1},{1,0},{2,3},{3,2},{4,5},{5,4},{6,7},{7,6},{8,9},{9,8},{10,11... | collective-permute-start | bytes 3932168 | tf_op jit(solution)/shard_map/token_grad_send/ppermute | solution.py:385
  (152 other events, 2385.1 us)

commit v7 on v6

--- a/solution.py
+++ b/solution.py
@@ -747,9 +747,9 @@
         do(tok, "second")
         small = slots.widen(small, "core")
         slots.advance()
+        do(d, "z_low")
         do(q, "core")
         do(o, "y")
-        do(d, "z_low")
         cot.slices(0)
         small_all = joined(list(slots.gate(*small))).astype(f32)
         qkv_count = qkv_bias.size
@@ -812,10 +812,11 @@
             operands = [p.reshape(p.shape[0], p.shape[1], half_step, width) for p in w.pieces]
             return operands, [whole(p.shape) for p in operands], (ncol, nrow, ncore, tuple(w.places))
 
-        do(u, "x_low", "y_high")
+        do(u, "y_high")
         do(o, "x")
         do(d, "z_high")
         do(cot, "first")
+        do(u, "x_low")
         normed, qkv = call(
             functools.partial(qkv_kernel, qkv_layout, parts),
             (seqs,),
@@ -830,8 +831,8 @@
         slots.note(qkv)
         slots.advance()
 
-        do(u, "y_low", "x_high", "core_near")
         do(o, "core")
+        do(u, "x_high", "y_low", "core_near")
         quads = flat // QUAD
         step_lanes = STEP * QUAD
         queries = HELD * LEN
@@ -1135,13 +1136,13 @@
             packs[0] = pack
 
         token_grad = TokensOut("token_grad", slots, own_grad, other_grad)
-        do(token_grad, "send")
+        with jax.named_scope("small_sums"):
+            small_sums()
         qg.low = qg.low + [far_low.got_low]
         if nrow > 2:
             slots.together((qg, "x_low"))
         slots.together((qg, "z_high"), (og, "z_low"))
-        with jax.named_scope("small_sums"):
-            small_sums()
+        do(token_grad, "send")
         up_grad = ug.result()
         slots.note(up_grad)
         slots.advance()

time: 479 us -> 477 us (level)
  waiting for transfers between devices: 99.9 us -> 94.8 us
    ppermute x83, waiting for transfers between devices: 99.9 us -> 94.8 us  [exchange(): lax.ppermute(values, axis, [(i, i ^ bit) for i in range(sizes[axis])])]
    unnamed x197 -> x201, local copies, waits for them, and re-layouts: 16.8 us -> 17.4 us
  transfers between devices with their start and end apart: 83 -> 83, of which waited for: 27 -> 25; matrix products, arithmetic and copies ran while one was open for 9% -> 8% of each run, Pallas kernels for 44% -> 45%
where the time goes in v7:
time: 477 us; the launch traced here: 472 us
  Pallas kernels  236 us (49%)
  waiting for transfers between devices  94.8 us (20%)
  starting transfers between devices  78.9 us (17%)
  local copies, waits for them, and re-layouts  39.3 us (8%)
  other arithmetic  21 us (4%)
    ppermute x83, waiting for transfers between devices, exchange(): lax.ppermute(values, axis, [(i, i ^ bit) for i in range(sizes[axis])])  94.8 us
    ppermute x83, starting transfers between devices, exchange(): lax.ppermute(values, axis, [(i, i ^ bit) for i in range(sizes[axis])])  78.9 us
    pallas_call x2, Pallas kernels, pull(): call(functools.partial(attend_pull_kernel, seqs, (ncore, ncol, nz, part,...  37.8 us
    pallas_call x1, Pallas kernels, local(): call(functools.partial(up_kernel, up_dims), (seqs,), [tokens_spec, whole(...  24.9 us
    pallas_call x1, Pallas kernels, local(): call(functools.partial(middle_pull_kernel, up_dims, out_layout), (seqs,),...  24.7 us
    pallas_call x2, Pallas kernels, ffn_kept(): call(functools.partial(ffn_kept_kernel, ncol, nrow), (2, nrow), [pl.Block...  19.9 us
    pallas_call x2, Pallas kernels, ffn_sent(): call(functools.partial(ffn_sent_kernel, ncol), (2, nrow), [pl.BlockSpec((...  18.9 us
    pallas_call x1, Pallas kernels, local(): call(attend_kernel, (seqs, quads // STEP), [pl.BlockSpec((3, LEN, step_la...  18.3 us
  transfers between devices with their start and end apart: 83, of which 25 were waited for; matrix products, arithmetic and copies ran while one was open for 8% of the time, Pallas kernels for 45%

profile of v7, /device:TPU:0, one launch (start us, length us, event | category | flops | bytes accessed | tf_op | source)
XLA Modules:
  0.0 472.2 jit_solution(14100054380415343144)
XLA Ops:
  11.4 13.9 %collective-permute-done = f32[1,5120]{1,0:T(1,128)S(1)} collective-permute-done((f32[1,5120]{1,0:T(1,128)S(1)}, f32[1,5120]{1,0:T(1,128)S(1)}, u32[]{:S(2)}, u32[]{:S(2)}) %collective-permute-start) | collective-permute-done | bytes 20512 | tf_op jit(solution)/shard_map/ppermute | solution.py:385
  46.9 3.3 collective-permute-start.15
  51.5 21.7 %collective-permute-done.14 = bf16[2,8,8,512]{3,2,1,0:T(8,128)(2,1)S(1)} collective-permute-done((bf16[2,8,8,512]{3,2,1,0:T(8,128)(2,1)S(1)}, bf16[2,8,8,512]{3,2,1,0:T(8,128)(2,1)S(1)}, u32[]{:S(2)}, u32[]{:S(2)}) %collective-permute-start.14) | collective-permute-done | bytes 131104 | tf_op jit(solution)/shard_map/out_z_high/ppermute | solution.py:385
  76.5 4.0 collective-permute-done.23
  96.3 15.9 %qkv.1 = (bf16[1280,1024]{1,0:T(8,128)(2,1)}, bf16[3,1280,1024]{2,1,0:T(8,128)(2,1)}) custom-call(f32[1,1024]{1,0:T(1,128)S(1)} %bitcast.132, f32[1,1024]{1,0:T(1,128)S(1)} %bitcast.136, f32[2,1024]{1,0:T(2,128)S(1)} %reshape.220.bias_ref, bf16[640,512]{1,0:T(8,128)(2,1)S(1)} %get-tuple-element.287.refs_0_, bf16[640,512]{1,0:T(8,128)(2,1)S(1)} %copy-done.34, ...), custom_call_target="tpu_custom_call" | custom-call | flops 8053063680 | bytes 19398656 | tf_op jit(solution)/shard_map/qkv/pallas_call | solution.py:820
  118.6 18.3 %attend.1 = (bf16[1280,1024]{1,0:T(8,128)(2,1)S(1)}, bf16[4,4,320,1280]{3,2,1,0:T(8,128)(2,1)}) custom-call(bf16[3,1280,1024]{2,1,0:T(8,128)(2,1)} %get-tuple-element.299.qkv_ref, f32[4,320,1]{2,1,0:T(8,128)S(1)} %copy.31.mask_ref), custom_call_target="tpu_custom_call" | custom-call | flops 6710886400 | bytes 23592960 | tf_op jit(solution)/shard_map/attend/pallas_call | solution.py:839
  143.1 9.0 %out.1 = (f32[1280,1024]{1,0:T(8,128)}, bf16[1280,1024]{1,0:T(8,128)(2,1)}) custom-call(bf16[1280,1024]{1,0:T(8,128)(2,1)} %copy-done.46, f32[1,1024]{1,0:T(1,128)S(1)} %bitcast.138, f32[1,1024]{1,0:T(1,128)S(1)} %bitcast.134, f32[1,1024]{1,0:T(1,128)S(1)} %bitcast.139, bf16[640,512]{1,0:T(8,128)(2,1)S(1)} %get-tuple-element.287.refs_0_, ...), custom_call_target="tpu_custom_call" | custom-call | flops 2684354560 | bytes 15204352 | tf_op jit(solution)/shard_map/out/pallas_call | solution.py:861
  158.5 24.9 %up.1 = (bf16[1280,4096]{1,0:T(8,128)(2,1)}, bf16[1280,4096]{1,0:T(8,128)(2,1)}) custom-call(bf16[1280,1024]{1,0:T(8,128)(2,1)} %get-tuple-element.313.a_ref.r_ref, f32[1,4096]{1,0:T(1,128)S(1)} %reshape.222.bias_ref, bf16[1,2,512,512]{3,2,1,0:T(8,128)(2,1)S(1)} %bitcast.124, bf16[1,2,512,512]{3,2,1,0:T(8,128)(2,1)} %bitcast.32.refs_1_, ...), custom_call_target="tpu_custom_call" | custom-call | flops 42949672960 | bytes 29360128 | tf_op jit(solution)/shard_map/up/pallas_call | solution.py:878
  187.7 15.6 %down.1 = (bf16[1280,512]{1,0:T(8,128)(2,1)}, bf16[1,1280,512]{2,1,0:T(8,128)(2,1)}) custom-call(bf16[1280,4096]{1,0:T(8,128)(2,1)} %get-tuple-element.338.hid_ref.l_ref, f32[1280,1024]{1,0:T(8,128)} %get-tuple-element.317.middle_ref, f32[1,1024]{1,0:T(1,128)S(1)} %bitcast.137, bf16[1,2,512,512]{3,2,1,0:T(8,128)(2,1)S(1)} %bitcast.130, ...), custom_call_target="tpu_custom_call" | custom-call | flops 10737418240 | bytes 26738688 | tf_op jit(solution)/shard_map/down/pallas_call | solution.py:999
  203.8 9.7 %down_grad.2 = bf16[2,2,2,512,512]{4,3,2,1,0:T(8,128)(2,1)} custom-call(bf16[1280,4096]{1,0:T(8,128)(2,1)} %get-tuple-element.338.hid_ref.l_ref, bf16[1280,1024]{1,0:T(8,128)(2,1)S(1)} %maximum_maximum_fusion.g_ref.r_ref), custom_call_target="tpu_custom_call" | custom-call | flops 5368709120 | bytes 12058624 | tf_op jit(solution)/shard_map/down_grad/pallas_call | solution.py:892
  214.4 17.5 %hidden_pull.1 = (bf16[1280,4096]{1,0:T(8,128)(2,1)}, f32[1,4096]{1,0:T(1,128)S(1)}) custom-call(bf16[1280,1024]{1,0:T(8,128)(2,1)} %copy-done.13, bf16[1280,4096]{1,0:T(8,128)(2,1)} %get-tuple-element.336.slope_ref, bf16[1,2,512,512]{3,2,1,0:T(8,128)(2,1)S(1)} %bitcast.131, bf16[1,2,512,512]{3,2,1,0:T(8,128)(2,1)S(1)} %bitcast.143, ...), custom_call_target="tpu_custom_call" | custom-call | flops 10737418240 | bytes 29360128 | tf_op jit(solution)/shard_map/hidden_pull/pallas_call | solution.py:1018
  231.9 9.4 %down_grad.3 = (bf16[2,512,512]{2,1,0:T(8,128)(2,1)S(1)}, bf16[2,512,512]{2,1,0:T(8,128)(2,1)S(1)}, bf16[2,512,512]{2,1,0:T(8,128)(2,1)S(1)}, bf16[2,512,512]{2,1,0:T(8,128)(2,1)S(1)}) custom-call(bf16[1280,4096]{1,0:T(8,128)(2,1)} %get-tuple-element.338.hid_ref.l_ref, bf16[1280,1024]{1,0:T(8,128)(2,1)} %copy-done.13, ...), custom_call_target="tpu_custom_call" | custom-call | flops 5368709120 | bytes 16777216 | tf_op jit(solution)/shard_map/down_grad/pallas_call | solution.py:908
  241.3 3.3 collective-permute-done.46
  244.6 9.2 %up_grad.2 = bf16[2,2,2,512,512]{4,3,2,1,0:T(8,128)(2,1)} custom-call(bf16[1280,4096]{1,0:T(8,128)(2,1)} %get-tuple-element.347.l_ref.du_ref, bf16[1280,1024]{1,0:T(8,128)(2,1)S(1)} %copy-done.48), custom_call_target="tpu_custom_call" | custom-call | flops 5368709120 | bytes 12058624 | tf_op jit(solution)/shard_map/up_grad/pallas_call | solution.py:892
  256.0 24.7 %middle_pull.1 = (f32[1280,1024]{1,0:T(8,128)}, bf16[1280,1024]{1,0:T(8,128)(2,1)}, bf16[1280,1024]{1,0:T(8,128)(2,1)}, f32[4,1024]{1,0:T(4,128)S(1)}) custom-call(bf16[1280,4096]{1,0:T(8,128)(2,1)} %get-tuple-element.347.l_ref.du_ref, f32[1280,1024]{1,0:T(8,128)} %get-tuple-element.317.middle_ref, bf16[1280,1024]{1,0:T(8,128)(2,1)} %copy-done.13, ...), custom_call_target="tpu_custom_call" | custom-call | flops 13421772800 | bytes 37224448 | tf_op jit(solution)/shard_map/middle_pull/pallas_call | solution.py:1037
  283.0 5.7 %out_grad.1 = (bf16[2,2,4,1,8,8,512]{6,5,4,3,2,1,0:T(8,128)(2,1)S(1)}, bf16[2,2,4,1,8,8,512]{6,5,4,3,2,1,0:T(8,128)(2,1)}) custom-call(bf16[1,1280,1024]{2,1,0:T(8,128)(2,1)S(1)} %bitcast.150, bf16[1280,1024]{1,0:T(8,128)(2,1)} %get-tuple-element.359.r_ref), custom_call_target="tpu_custom_call" | custom-call | flops 2684354560 | bytes 7340032 | tf_op jit(solution)/shard_map/out_grad/pallas_call | solution.py:930
  288.7 10.5 %up_grad.3 = (bf16[2,512,512]{2,1,0:T(8,128)(2,1)S(1)}, bf16[2,512,512]{2,1,0:T(8,128)(2,1)}, bf16[2,512,512]{2,1,0:T(8,128)(2,1)S(1)}, bf16[2,512,512]{2,1,0:T(8,128)(2,1)}) custom-call(bf16[1280,4096]{1,0:T(8,128)(2,1)} %get-tuple-element.347.l_ref.du_ref, bf16[1280,1024]{1,0:T(8,128)(2,1)} %get-tuple-element.313.a_ref.r_ref, ...), custom_call_target="tpu_custom_call" | custom-call | flops 5368709120 | bytes 16777216 | tf_op jit(solution)/shard_map/up_grad/pallas_call | solution.py:908
  301.8 3.5 collective-permute-start.55
  307.0 18.9 %attend_pull.2 = (bf16[3,1280,512]{2,1,0:T(8,128)(2,1)}, bf16[1,2,4,3,8,8,512]{6,5,4,3,2,1,0:T(8,128)(2,1)S(1)}, bf16[1,2,4,3,8,8,512]{6,5,4,3,2,1,0:T(8,128)(2,1)S(1)}, f32[3,1,512]{2,1,0:T(1,128)S(1)}) custom-call(bf16[3,1280,1024]{2,1,0:T(8,128)(2,1)} %get-tuple-element.299.qkv_ref, bf16[4,4,320,1280]{3,2,1,0:T(8,128)(2,1)} %get-tuple-element.370.probs_ref, ...), custom_call_target="tpu_custom_call" | custom-call | flops 10317987840 | bytes 9175040 | tf_op jit(solution)/shard_map/attend_pull/pallas_call | solution.py:973
  331.5 11.7 %collective-permute-done.58.refs_6_ = bf16[1,1,2,256,512]{4,3,2,1,0:T(8,128)(2,1)S(1)} collective-permute-done((bf16[1,1,2,256,512]{4,3,2,1,0:T(8,128)(2,1)S(1)}, bf16[1,1,2,256,512]{4,3,2,1,0:T(8,128)(2,1)S(1)}, u32[]{:S(2)}, u32[]{:S(2)}) %collective-permute-start.58) | collective-permute-done | bytes 524320 | tf_op jit(solution)/shard_map/up_grad_y_high/ppermute | solution.py:385
  352.8 18.9 %attend_pull.3 = (bf16[3,1280,512]{2,1,0:T(8,128)(2,1)}, bf16[1,2,4,3,8,8,512]{6,5,4,3,2,1,0:T(8,128)(2,1)S(1)}, bf16[1,2,4,3,8,8,512]{6,5,4,3,2,1,0:T(8,128)(2,1)}, f32[3,1,512]{2,1,0:T(1,128)S(1)}) custom-call(bf16[3,1280,1024]{2,1,0:T(8,128)(2,1)} %get-tuple-element.299.qkv_ref, bf16[4,4,320,1280]{3,2,1,0:T(8,128)(2,1)} %get-tuple-element.370.probs_ref, ...), custom_call_target="tpu_custom_call" | custom-call | flops 10317987840 | bytes 9175040 | tf_op jit(solution)/shard_map/attend_pull/pallas_call | solution.py:973
  403.3 16.9 %token_pull.1 = (f32[1280,512]{1,0:T(8,128)}, bf16[1,1280,512]{2,1,0:T(8,128)(2,1)}, f32[2,1024]{1,0:T(2,128)S(1)}) custom-call(bf16[3,1280,512]{2,1,0:T(8,128)(2,1)} %get-tuple-element.425.near_ref, bf16[3,1280,512]{2,1,0:T(8,128)(2,1)} %get-tuple-element.373.far_ref, f32[1280,1024]{1,0:T(8,128)} %get-tuple-element.426.grad_ref, f32[1,1024]{1,0:T(1,128)S(1)} %bitcast.133, ...), custom_call_target="tpu_custom_call" | custom-call | flops 8053063680 | bytes 24641536 | tf_op jit(solution)/shard_map/token_pull/pallas_call | solution.py:1096
  444.6 5.1 %collective-permute-done.79 = f32[3456]{0:T(1024)S(1)} collective-permute-done((f32[3456]{0:T(1024)S(1)}, f32[3456]{0:T(1024)S(1)}, u32[]{:S(2)}, u32[]{:S(2)}) %collective-permute-start.79) | collective-permute-done | bytes 13856 | tf_op jit(solution)/shard_map/small_sums/ppermute | solution.py:385
  451.5 7.7 %collective-permute-done.80.refs_4_ = bf16[1,1,2,3,8,8,512]{6,5,4,3,2,1,0:T(8,128)(2,1)} collective-permute-done((bf16[1,1,2,3,8,8,512]{6,5,4,3,2,1,0:T(8,128)(2,1)}, bf16[1,1,2,3,8,8,512]{6,5,4,3,2,1,0:T(8,128)(2,1)}, u32[]{:S(2)}, u32[]{:S(2)}) %collective-permute-start.80) | collective-permute-done | bytes 393248 | tf_op jit(solution)/shard_map/qkv_grad_z_high/ppermute | solution.py:385
  (460 shorter events, 170.5 us)
Async XLA Ops:
  40.2 33.1 %collective-permute-start.16 = (bf16[640,512]{1,0:T(8,128)(2,1)S(1)}, bf16[640,512]{1,0:T(8,128)(2,1)S(1)}, u32[]{:S(2)}, u32[]{:S(2)}) collective-permute-start(bf16[640,512]{1,0:T(8,128)(2,1)S(1)} %get-tuple-element.272), channel_id=1, source_target_pairs={{0,1},{1,0},{2,3},{3,2},{4,5},{5,4},{6,7},{7,6},{8,9},{9,8},{10,11... | collective-permute-start | bytes 1966088 | tf_op jit(solution)/shard_map/tokens_second/ppermute | solution.py:385
  42.7 30.5 %collective-permute-start.13 = (bf16[1,2,2,24,8,512]{5,4,3,2,1,0:T(8,128)(2,1)}, bf16[1,2,2,24,8,512]{5,4,3,2,1,0:T(8,128)(2,1)}, u32[]{:S(2)}, u32[]{:S(2)}) collective-permute-start(bf16[1,2,2,24,8,512]{5,4,3,2,1,0:T(8,128)(2,1)} %maximum_bitcast_fusion.5.refs_8_), channel_id=1, source_target_pairs={{0,2},{2,0},{1,3},{3,1},{4,6},{6,4},{5,7},{7,5},{8,10},{10,8},{9,1... | collective-permute-start | bytes 2359304 | tf_op jit(solution)/shard_map/qkv_x_high/ppermute | solution.py:385
  44.3 29.7 %collective-permute-start.12 = (bf16[1,2,2,24,8,512]{5,4,3,2,1,0:T(8,128)(2,1)S(1)}, bf16[1,2,2,24,8,512]{5,4,3,2,1,0:T(8,128)(2,1)S(1)}, u32[]{:S(2)}, u32[]{:S(2)}) collective-permute-start(bf16[1,2,2,24,8,512]{5,4,3,2,1,0:T(8,128)(2,1)S(1)} %maximum_bitcast_fusion.4.refs_4_), channel_id=1, source_target_pairs={{0,1},{1,0},{2,3},{3,2},{4,5},{5,4},{6,7},{7,6},{8,9},{9,8},{10,11... | collective-permute-start | bytes 2359304 | tf_op jit(solution)/shard_map/qkv_y_low/ppermute | solution.py:385
  46.9 26.3 %collective-permute-start.15 = (bf16[2,256,512]{2,1,0:T(8,128)(2,1)S(1)}, bf16[2,256,512]{2,1,0:T(8,128)(2,1)S(1)}, u32[]{:S(2)}, u32[]{:S(2)}) collective-permute-start(bf16[2,256,512]{2,1,0:T(8,128)(2,1)S(1)} %constant_dynamic-update-slice_fusion.2), channel_id=1, source_target_pairs={{0,16},{8,24},{16,0},{24,8},{1,17},{9,25},{17,1},{25,9},{2,18},{10... | collective-permute-start | bytes 1572872 | tf_op jit(solution)/shard_map/up_z_high/ppermute | solution.py:385
  87.0 25.2 %collective-permute-start.28 = (bf16[1,2,256,512]{3,2,1,0:T(8,128)(2,1)S(1)}, bf16[1,2,256,512]{3,2,1,0:T(8,128)(2,1)S(1)}, u32[]{:S(2)}, u32[]{:S(2)}) collective-permute-start(bf16[1,2,256,512]{3,2,1,0:T(8,128)(2,1)S(1)} %bitcast.151), channel_id=1, source_target_pairs={{0,2},{2,0},{1,3},{3,1},{4,6},{6,4},{5,7},{7,5},{8,10},{10,8},{9,1... | collective-permute-start | bytes 1572872 | tf_op jit(solution)/shard_map/up_x_low/ppermute | solution.py:385
  88.6 25.3 %collective-permute-start.27 = (bf16[640,512]{1,0:T(8,128)(2,1)S(1)}, bf16[640,512]{1,0:T(8,128)(2,1)S(1)}, u32[]{:S(2)}, u32[]{:S(2)}) collective-permute-start(bf16[640,512]{1,0:T(8,128)(2,1)S(1)} %get-tuple-element.297), channel_id=1, source_target_pairs={{0,1},{1,0},{2,3},{3,2},{4,5},{5,4},{6,7},{7,6},{8,9},{9,8},{10,11... | collective-permute-start | bytes 1966088 | tf_op jit(solution)/shard_map/cotangent_first/ppermute | solution.py:385
  114.0 24.4 %collective-permute-start.32 = (bf16[1,2,2,256,512]{4,3,2,1,0:T(8,128)(2,1)S(1)}, bf16[1,2,2,256,512]{4,3,2,1,0:T(8,128)(2,1)}, u32[]{:S(2)}, u32[]{:S(2)}) collective-permute-start(bf16[1,2,2,256,512]{4,3,2,1,0:T(8,128)(2,1)S(1)} %maximum_bitcast_fusion.1), channel_id=1, source_target_pairs={{0,1},{1,0},{2,3},{3,2},{4,5},{5,4},{6,7},{7,6},{8,9},{9,8},{10,11... | collective-permute-start | bytes 3145736 | tf_op jit(solution)/shard_map/up_y_low/ppermute | solution.py:385
  115.5 25.2 %collective-permute-start.31 = (bf16[1,2,2,256,512]{4,3,2,1,0:T(8,128)(2,1)S(1)}, bf16[1,2,2,256,512]{4,3,2,1,0:T(8,128)(2,1)}, u32[]{:S(2)}, u32[]{:S(2)}) collective-permute-start(bf16[1,2,2,256,512]{4,3,2,1,0:T(8,128)(2,1)S(1)} %maximum_bitcast_fusion), channel_id=1, source_target_pairs={{0,2},{2,0},{1,3},{3,1},{4,6},{6,4},{5,7},{7,5},{8,10},{10,8},{9,1... | collective-permute-start | bytes 3145736 | tf_op jit(solution)/shard_map/up_x_high/ppermute | solution.py:385
  156.1 27.4 %collective-permute-start.40 = (bf16[1,2,2,256,512]{4,3,2,1,0:T(8,128)(2,1)S(1)}, bf16[1,2,2,256,512]{4,3,2,1,0:T(8,128)(2,1)}, u32[]{:S(2)}, u32[]{:S(2)}) collective-permute-start(bf16[1,2,2,256,512]{4,3,2,1,0:T(8,128)(2,1)S(1)} %maximum_bitcast_fusion.3), channel_id=1, source_target_pairs={{0,2},{2,0},{1,3},{3,1},{4,6},{6,4},{5,7},{7,5},{8,10},{10,8},{9,1... | collective-permute-start | bytes 3145736 | tf_op jit(solution)/shard_map/down_x_high/ppermute | solution.py:385
  156.7 26.8 %collective-permute-start.42 = (bf16[1,2,2,256,512]{4,3,2,1,0:T(8,128)(2,1)S(1)}, bf16[1,2,2,256,512]{4,3,2,1,0:T(8,128)(2,1)}, u32[]{:S(2)}, u32[]{:S(2)}) collective-permute-start(bf16[1,2,2,256,512]{4,3,2,1,0:T(8,128)(2,1)S(1)} %maximum_bitcast_fusion.3), channel_id=1, source_target_pairs={{0,4},{4,0},{1,5},{5,1},{2,6},{6,2},{3,7},{7,3},{8,12},{12,8},{9,1... | collective-permute-start | bytes 3145736 | tf_op jit(solution)/shard_map/down_core_near/ppermute | solution.py:385
  156.8 26.7 %collective-permute-start.39 = (bf16[1,2,2,256,512]{4,3,2,1,0:T(8,128)(2,1)S(1)}, bf16[1,2,2,256,512]{4,3,2,1,0:T(8,128)(2,1)S(1)}, u32[]{:S(2)}, u32[]{:S(2)}) collective-permute-start(bf16[1,2,2,256,512]{4,3,2,1,0:T(8,128)(2,1)S(1)} %maximum_bitcast_fusion.2), channel_id=1, source_target_pairs={{0,1},{1,0},{2,3},{3,2},{4,5},{5,4},{6,7},{7,6},{8,9},{9,8},{10,11... | collective-permute-start | bytes 3145736 | tf_op jit(solution)/shard_map/down_y_low/ppermute | solution.py:385
  158.2 25.2 %collective-permute-start.41 = (bf16[1,2,2,256,512]{4,3,2,1,0:T(8,128)(2,1)S(1)}, bf16[1,2,2,256,512]{4,3,2,1,0:T(8,128)(2,1)S(1)}, u32[]{:S(2)}, u32[]{:S(2)}) collective-permute-start(bf16[1,2,2,256,512]{4,3,2,1,0:T(8,128)(2,1)S(1)} %maximum_bitcast_fusion.2), channel_id=1, source_target_pairs={{0,4},{4,0},{1,5},{5,1},{2,6},{6,2},{3,7},{7,3},{8,12},{12,8},{9,1... | collective-permute-start | bytes 3145736 | tf_op jit(solution)/shard_map/down_core_near/ppermute | solution.py:385
  213.7 30.9 %collective-permute-start.46 = (bf16[1280,512]{1,0:T(8,128)(2,1)S(1)}, bf16[1280,512]{1,0:T(8,128)(2,1)S(1)}, u32[]{:S(2)}, u32[]{:S(2)}) collective-permute-start(bf16[1280,512]{1,0:T(8,128)(2,1)S(1)} %bitcast.178), channel_id=1, source_target_pairs={{0,1},{1,0},{2,3},{3,2},{4,5},{5,4},{6,7},{7,6},{8,9},{9,8},{10,11... | collective-permute-start | bytes 3932168 | tf_op jit(solution)/shard_map/activations_send/ppermute | solution.py:385
  253.8 26.9 %collective-permute-start.50 = (bf16[2,2,2,512,512]{4,3,2,1,0:T(8,128)(2,1)}, bf16[2,2,2,512,512]{4,3,2,1,0:T(8,128)(2,1)}, u32[]{:S(2)}, u32[]{:S(2)}) collective-permute-start(bf16[2,2,2,512,512]{4,3,2,1,0:T(8,128)(2,1)} %up_grad.2), channel_id=1, source_target_pairs={{0,4},{4,0},{1,5},{5,1},{2,6},{6,2},{3,7},{7,3},{8,12},{12,8},{9,1... | collective-permute-start | bytes 12582920 | tf_op jit(solution)/shard_map/up_grad_core/ppermute | solution.py:385
  253.8 26.9 %collective-permute-start.49 = (bf16[2,1,2,256,512]{4,3,2,1,0:T(8,128)(2,1)S(1)}, bf16[2,1,2,256,512]{4,3,2,1,0:T(8,128)(2,1)S(1)}, u32[]{:S(2)}, u32[]{:S(2)}) collective-permute-start(bf16[2,1,2,256,512]{4,3,2,1,0:T(8,128)(2,1)S(1)} %bitcast.149), channel_id=1, source_target_pairs={{0,1},{1,0},{2,3},{3,2},{4,5},{5,4},{6,7},{7,6},{8,9},{9,8},{10,11... | collective-permute-start | bytes 3145736 | tf_op jit(solution)/shard_map/down_grad_first/ppermute | solution.py:385
  254.5 26.2 %collective-permute-start.48 = (bf16[1,2,2,256,512]{4,3,2,1,0:T(8,128)(2,1)S(1)}, bf16[1,2,2,256,512]{4,3,2,1,0:T(8,128)(2,1)S(1)}, u32[]{:S(2)}, u32[]{:S(2)}) collective-permute-start(bf16[1,2,2,256,512]{4,3,2,1,0:T(8,128)(2,1)S(1)} %bitcast.148), channel_id=1, source_target_pairs={{0,2},{2,0},{1,3},{3,1},{4,6},{6,4},{5,7},{7,5},{8,10},{10,8},{9,1... | collective-permute-start | bytes 3145736 | tf_op jit(solution)/shard_map/down_grad_first/ppermute | solution.py:385
  299.3 29.2 %collective-permute-start.56 = (bf16[2,2,4,1,8,8,512]{6,5,4,3,2,1,0:T(8,128)(2,1)}, bf16[2,2,4,1,8,8,512]{6,5,4,3,2,1,0:T(8,128)(2,1)S(1)}, u32[]{:S(2)}, u32[]{:S(2)}) collective-permute-start(bf16[2,2,4,1,8,8,512]{6,5,4,3,2,1,0:T(8,128)(2,1)} %get-tuple-element.369), channel_id=1, source_target_pairs={{0,4},{4,0},{1,5},{5,1},{2,6},{6,2},{3,7},{7,3},{8,12},{12,8},{9,1... | collective-permute-start | bytes 3145736 | tf_op jit(solution)/shard_map/out_grad_core/ppermute | solution.py:385
  299.3 29.2 %collective-permute-start.54 = (bf16[2,1,2,256,512]{4,3,2,1,0:T(8,128)(2,1)}, bf16[2,1,2,256,512]{4,3,2,1,0:T(8,128)(2,1)S(1)}, u32[]{:S(2)}, u32[]{:S(2)}) collective-permute-start(bf16[2,1,2,256,512]{4,3,2,1,0:T(8,128)(2,1)} %bitcast.58), channel_id=1, source_target_pairs={{0,1},{1,0},{2,3},{3,2},{4,5},{5,4},{6,7},{7,6},{8,9},{9,8},{10,11... | collective-permute-start | bytes 3145736 | tf_op jit(solution)/shard_map/up_grad_first/ppermute | solution.py:385
  300.1 28.4 %collective-permute-start.53 = (bf16[1,2,2,256,512]{4,3,2,1,0:T(8,128)(2,1)}, bf16[1,2,2,256,512]{4,3,2,1,0:T(8,128)(2,1)S(1)}, u32[]{:S(2)}, u32[]{:S(2)}) collective-permute-start(bf16[1,2,2,256,512]{4,3,2,1,0:T(8,128)(2,1)} %bitcast.55), channel_id=1, source_target_pairs={{0,2},{2,0},{1,3},{3,1},{4,6},{6,4},{5,7},{7,5},{8,10},{10,8},{9,1... | collective-permute-start | bytes 3145736 | tf_op jit(solution)/shard_map/up_grad_first/ppermute | solution.py:385
  301.8 26.7 %collective-permute-start.55 = (bf16[1,1,2,256,512]{4,3,2,1,0:T(8,128)(2,1)S(1)}, bf16[1,1,2,256,512]{4,3,2,1,0:T(8,128)(2,1)S(1)}, u32[]{:S(2)}, u32[]{:S(2)}) collective-permute-start(bf16[1,1,2,256,512]{4,3,2,1,0:T(8,128)(2,1)S(1)} %sums.9), channel_id=1, source_target_pairs={{0,16},{8,24},{16,0},{24,8},{1,17},{9,25},{17,1},{25,9},{2,18},{10... | collective-permute-start | bytes 1572872 | tf_op jit(solution)/shard_map/down_grad_z_high/ppermute | solution.py:385
  346.5 26.1 %collective-permute-start.60 = (bf16[1,2,2,3,8,8,512]{6,5,4,3,2,1,0:T(8,128)(2,1)}, bf16[1,2,2,3,8,8,512]{6,5,4,3,2,1,0:T(8,128)(2,1)S(1)}, u32[]{:S(2)}, u32[]{:S(2)}) collective-permute-start(bf16[1,2,2,3,8,8,512]{6,5,4,3,2,1,0:T(8,128)(2,1)} %get-tuple-element.401), channel_id=1, source_target_pairs={{0,2},{2,0},{1,3},{3,1},{4,6},{6,4},{5,7},{7,5},{8,10},{10,8},{9,1... | collective-permute-start | bytes 2359304 | tf_op jit(solution)/shard_map/qkv_grad_far_far_high/ppermute | solution.py:385
  347.2 25.4 %collective-permute-start.62 = (bf16[1,1,2,256,512]{4,3,2,1,0:T(8,128)(2,1)}, bf16[1,1,2,256,512]{4,3,2,1,0:T(8,128)(2,1)}, u32[]{:S(2)}, u32[]{:S(2)}) collective-permute-start(bf16[1,1,2,256,512]{4,3,2,1,0:T(8,128)(2,1)} %get-tuple-element.403), channel_id=1, source_target_pairs={{0,16},{8,24},{16,0},{24,8},{1,17},{9,25},{17,1},{25,9},{2,18},{10... | collective-permute-start | bytes 1572872 | tf_op jit(solution)/shard_map/up_grad_z_high/ppermute | solution.py:385
  399.6 24.2 %collective-permute-start.70 = (bf16[1,1,2,3,8,8,512]{6,5,4,3,2,1,0:T(8,128)(2,1)}, bf16[1,1,2,3,8,8,512]{6,5,4,3,2,1,0:T(8,128)(2,1)}, u32[]{:S(2)}, u32[]{:S(2)}) collective-permute-start(bf16[1,1,2,3,8,8,512]{6,5,4,3,2,1,0:T(8,128)(2,1)} %get-tuple-element.442), channel_id=1, source_target_pairs={{0,1},{1,0},{2,3},{3,2},{4,5},{5,4},{6,7},{7,6},{8,9},{9,8},{10,11... | collective-permute-start | bytes 1179656 | tf_op jit(solution)/shard_map/qkv_grad_y_high/ppermute | solution.py:385
  430.1 30.9 %collective-permute-start.74 = (bf16[1280,512]{1,0:T(8,128)(2,1)}, bf16[1280,512]{1,0:T(8,128)(2,1)}, u32[]{:S(2)}, u32[]{:S(2)}) collective-permute-start(bf16[1280,512]{1,0:T(8,128)(2,1)} %bitcast.177), channel_id=1, source_target_pairs={{0,1},{1,0},{2,3},{3,2},{4,5},{5,4},{6,7},{7,6},{8,9},{9,8},{10,11... | collective-permute-start | bytes 3932168 | tf_op jit(solution)/shard_map/token_grad_send/ppermute | solution.py:385
  (154 other events, 2357.6 us)
